TPU v7x, 32 devices: a whole 2x2x4 slice. The times are simulated.
32 devices in a mesh: shard: 4 (over y, x), ctx: 2 (over core), tp: 4 (over z).
Axes of the slice: x: 2, y: 2, z: 4, core: 2. Of those that a mesh axis runs over, the one named last changes fastest.
Arguments:
- hidden: bfloat16 [3, 4, 1024, 2048], P(None, 'shard', ('ctx', 'tp')), may hold values from -6 to 6
- segments: int32 [3, 4, 1024], P(None, 'shard'), may hold values from 0 to 15, never falling along the last dimension, each value on 1 to 512 neighbouring positions
- cotangent: bfloat16 [3, 4, 1024, 2048], P(None, 'shard', ('ctx', 'tp')), may hold values from -6 to 6
- attn_gain: bfloat16 [2048], P(('shard', 'ctx', 'tp')), may hold values from 0.5 to 1.5
- q_weight: bfloat16 [2048, 3072], P(('shard', 'ctx'), 'tp'), may hold values from -0.125 to 0.125
- latent_weight: bfloat16 [2048, 576], P(('shard', 'ctx', 'tp')), may hold values from -0.125 to 0.125
- latent_gain: bfloat16 [512], P(('shard', 'ctx', 'tp')), may hold values from 0.5 to 1.5
- expand_weight: bfloat16 [512, 4096], P(('shard', 'ctx'), 'tp'), may hold values from -0.25 to 0.25
- out_weight: bfloat16 [2048, 2048], P('tp', ('shard', 'ctx')), may hold values from -0.5 to 0.5
- mlp_gain: bfloat16 [2048], P(('shard', 'ctx', 'tp')), may hold values from 0.5 to 1.5
- gate_weight: bfloat16 [2048, 10944], P(('shard', 'ctx'), 'tp'), may hold values from -0.125 to 0.125
- up_weight: bfloat16 [2048, 10944], P(('shard', 'ctx'), 'tp'), may hold values from -0.125 to 0.125
- down_weight: bfloat16 [10944, 2048], P('tp', ('shard', 'ctx')), may hold values from -0.0546875 to 0.0546875
Outputs:
- output: bfloat16 [3, 4, 1024, 2048], P(None, 'shard', ('ctx', 'tp'))
- input_grad: bfloat16 [3, 4, 1024, 2048], P(None, 'shard', ('ctx', 'tp'))
- attn_gain_grad: float32 [2048], P(('shard', 'ctx', 'tp'))
- q_weight_grad: float32 [2048, 3072], P(('shard', 'ctx'), 'tp')
- latent_weight_grad: float32 [2048, 576], P(('shard', 'ctx', 'tp'))
- latent_gain_grad: float32 [512], P(('shard', 'ctx', 'tp'))
- expand_weight_grad: float32 [512, 4096], P(('shard', 'ctx'), 'tp')
- out_weight_grad: float32 [2048, 2048], P('tp', ('shard', 'ctx'))
- mlp_gain_grad: float32 [2048], P(('shard', 'ctx', 'tp'))
- gate_weight_grad: float32 [2048, 10944], P(('shard', 'ctx'), 'tp')
- up_weight_grad: float32 [2048, 10944], P(('shard', 'ctx'), 'tp')
- down_weight_grad: float32 [10944, 2048], P('tp', ('shard', 'ctx'))
Inputs may be any that keep to these rules, and one draw needn't show every extreme that they name: `segments`: segment numbers never fall along a sequence; 0 marks padding; a segment holds at most 512 tokens.
All inputs are finite; a program needn't handle non-finite values.
Results may differ from a plain program's by a relative error of at most 0.023.
Values may be sent and summed in bfloat16 or wider, within the bound.
No kernel may reach another device: no remote copies, remote signals or barrier semaphores. Data moves between devices by JAX's collectives and lax.ppermute only.
A program may use at most 232 MiB of HBM per device.

v0:
```python
import jax
import jax.numpy as jnp
from jax import lax
from jax.sharding import PartitionSpec as P

NOPE = 128
ROPE = 64
VHEAD = 128
KVRANK = 512


EPSILON = 1e-06
THETA_BASE = 10000.0
NEG_FILL = -1e30


def norm_scale(values):
    return lax.rsqrt(jnp.mean(values * values, axis=-1, keepdims=True) + EPSILON)


def norm_back(values, factor, gain_vec, grad_out):
    scaled = grad_out * gain_vec
    grad_in = factor * scaled - values * factor**3 * jnp.mean(
        scaled * values, axis=-1, keepdims=True
    )
    return (grad_in, jnp.sum(grad_out * values * factor, axis=0))


def positions(segment_ids):
    length = segment_ids.shape[0]
    index_row = jnp.arange(length, dtype=jnp.int32)
    begins = jnp.concatenate([jnp.ones((1,), jnp.bool_), segment_ids[1:] != segment_ids[:-1]])
    return index_row - lax.cummax(jnp.where(begins, index_row, 0), axis=0)


def rotary_table(places_in):
    half_width = ROPE // 2
    freqs = THETA_BASE ** (-2.0 * jnp.arange(half_width, dtype=jnp.float32) / ROPE)
    angles = places_in.astype(jnp.float32)[:, None] * freqs[None, :]
    return (jnp.cos(angles), jnp.sin(angles))


def rotate(values, cos_table, sin_table):
    half_width = values.shape[-1] // 2
    first_half = values[..., :half_width]
    second_half = values[..., half_width:]
    return jnp.concatenate(
        [
            first_half * cos_table - second_half * sin_table,
            second_half * cos_table + first_half * sin_table,
        ],
        axis=-1,
    )


def rotate_back(grads, cos_table, sin_table):
    half_width = grads.shape[-1] // 2
    first_half = grads[..., :half_width]
    second_half = grads[..., half_width:]
    return jnp.concatenate(
        [
            first_half * cos_table + second_half * sin_table,
            second_half * cos_table - first_half * sin_table,
        ],
        axis=-1,
    )


def shards(
    hidden,
    segments,
    cotangent,
    attn_gain,
    q_weight,
    latent_weight,
    latent_gain,
    expand_weight,
    out_weight,
    mlp_gain,
    gate_weight,
    up_weight,
    down_weight,
):
    f32 = jnp.float32
    bf16 = jnp.bfloat16
    micro_count = hidden.shape[0]
    own_rows = hidden.shape[2]
    seq_length = segments.shape[2]
    span_rows = own_rows * lax.axis_size("tp")
    query_width = NOPE + ROPE
    kv_width = NOPE + VHEAD
    heads_here = q_weight.shape[1] // query_width
    span_first = lax.axis_index("ctx") * span_rows
    own_first = span_first + lax.axis_index("tp") * own_rows
    softmax_scale = query_width ** (-0.5)
    block_rows = min(512, span_rows)
    block_count = span_rows // block_rows
    key_index = jnp.arange(seq_length, dtype=jnp.int32)
    outputs_list = []
    grads_list = []
    split_total = None
    whole_total = None
    for micro_idx in range(micro_count):
        w_query, w_expand, w_gate, w_up, w_out, w_down = (
            lax.all_gather(q_weight, ("shard", "ctx"), axis=0, tiled=True),
            lax.all_gather(expand_weight, ("shard", "ctx"), axis=0, tiled=True),
            lax.all_gather(gate_weight, ("shard", "ctx"), axis=0, tiled=True),
            lax.all_gather(up_weight, ("shard", "ctx"), axis=0, tiled=True),
            lax.all_gather(out_weight, ("shard", "ctx"), axis=1, tiled=True),
            lax.all_gather(down_weight, ("shard", "ctx"), axis=1, tiled=True),
        )
        gain_attn, w_latent, gain_latent, gain_mlp = (
            lax.all_gather(attn_gain, ("shard", "ctx", "tp"), axis=0, tiled=True),
            lax.all_gather(latent_weight, ("shard", "ctx", "tp"), axis=0, tiled=True),
            lax.all_gather(latent_gain, ("shard", "ctx", "tp"), axis=0, tiled=True),
            lax.all_gather(mlp_gain, ("shard", "ctx", "tp"), axis=0, tiled=True),
        )
        gain_one = gain_attn.astype(f32)
        gain_kv = gain_latent.astype(f32)
        gain_two = gain_mlp.astype(f32)
        seg_row = segments[micro_idx, 0]
        cos_all, sin_all = rotary_table(positions(seg_row))
        cos_own = lax.dynamic_slice_in_dim(cos_all, own_first, own_rows, 0)
        sin_own = lax.dynamic_slice_in_dim(sin_all, own_first, own_rows, 0)
        cos_query = lax.dynamic_slice_in_dim(cos_all, span_first, span_rows, 0)[:, None, :]
        sin_query = lax.dynamic_slice_in_dim(sin_all, span_first, span_rows, 0)[:, None, :]
        inputs = hidden[micro_idx, 0].astype(f32)
        factor_one = norm_scale(inputs)
        normed_own = (inputs * factor_one * gain_one).astype(bf16)
        normed_span = lax.all_gather(normed_own, "tp", axis=0, tiled=True)
        latent_raw = jnp.dot(normed_own, w_latent, preferred_element_type=f32)
        latent_part = latent_raw[:, :KVRANK]
        factor_latent = norm_scale(latent_part)
        latent_own = (latent_part * factor_latent * gain_kv).astype(bf16)
        rope_own = rotate(latent_raw[:, KVRANK:], cos_own, sin_own).astype(bf16)
        latent_all, rope_all = (
            lax.all_gather(latent_own, ("ctx", "tp"), axis=0, tiled=True),
            lax.all_gather(rope_own, ("ctx", "tp"), axis=0, tiled=True),
        )
        query_lin = jnp.dot(normed_span, w_query, preferred_element_type=f32).reshape(
            span_rows, heads_here, query_width
        )
        queries = jnp.concatenate(
            [query_lin[..., :NOPE], rotate(query_lin[..., NOPE:], cos_query, sin_query)], axis=-1
        ).astype(bf16)
        expanded = (
            jnp.dot(latent_all, w_expand, preferred_element_type=f32)
            .astype(bf16)
            .reshape(seq_length, heads_here, kv_width)
        )
        values_all = expanded[..., NOPE:]
        keys_all = jnp.concatenate(
            [
                expanded[..., :NOPE],
                jnp.broadcast_to(rope_all[:, None, :], (seq_length, heads_here, ROPE)),
            ],
            axis=-1,
        )

        def block_scores(block_idx):
            block_first = span_first + block_idx * block_rows
            query_index = block_first + jnp.arange(block_rows, dtype=jnp.int32)
            seg_query = lax.dynamic_slice_in_dim(seg_row, block_first, block_rows, 0)
            same_doc = (
                (seg_query[:, None] == seg_row[None, :])
                & (key_index[None, :] <= query_index[:, None])
                & (seg_row[None, :] != 0)
            )
            allowed = same_doc | (key_index[None, :] == query_index[:, None])
            scores = (
                jnp.einsum("qhd,khd->hqk", queries, keys_all, preferred_element_type=f32)
                * softmax_scale
            )
            return (queries, jnp.where(allowed[None], scores, NEG_FILL))

        def attend(block_idx):
            scores = block_scores(block_idx)[1]
            top_score = jnp.max(scores, axis=-1, keepdims=True)
            expd = jnp.exp(scores - top_score)
            totals = jnp.sum(expd, axis=-1, keepdims=True)
            probs = expd / totals
            mixed = jnp.einsum(
                "hqk,khd->qhd", probs.astype(bf16), values_all, preferred_element_type=f32
            )
            return (mixed.astype(bf16), (top_score + jnp.log(totals))[..., 0])

        att_blocks, log_sums = lax.map(attend, jnp.arange(block_count, dtype=jnp.int32))
        att_flat = att_blocks.reshape(span_rows, heads_here * VHEAD)
        middle = inputs + lax.psum_scatter(
            jnp.dot(att_flat, w_out, preferred_element_type=f32).astype(jnp.bfloat16),
            "tp",
            scatter_dimension=0,
            tiled=True,
        ).astype(jnp.float32)
        factor_two = norm_scale(middle)
        normed_two = (middle * factor_two * gain_two).astype(bf16)
        normed_wide, grad_wide = (
            lax.all_gather(normed_two, "tp", axis=0, tiled=True),
            lax.all_gather(cotangent[micro_idx, 0], "tp", axis=0, tiled=True),
        )
        gate_val = jnp.dot(normed_wide, w_gate, preferred_element_type=f32)
        up_val = jnp.dot(normed_wide, w_up, preferred_element_type=f32)
        sigma = jax.nn.sigmoid(gate_val)
        swish = gate_val * sigma
        hidden_act = (swish * up_val).astype(bf16)
        outputs_list.append(
            (
                middle
                + lax.psum_scatter(
                    jnp.dot(hidden_act, w_down, preferred_element_type=f32).astype(jnp.bfloat16),
                    "tp",
                    scatter_dimension=0,
                    tiled=True,
                ).astype(jnp.float32)
            ).astype(bf16)
        )
        grad_wdown = jnp.dot(hidden_act.T, grad_wide, preferred_element_type=f32)
        grad_act = jnp.dot(grad_wide, w_down.T, preferred_element_type=f32)
        grad_gate = (grad_act * up_val * sigma * (1.0 + gate_val * (1.0 - sigma))).astype(bf16)
        grad_up = (grad_act * swish).astype(bf16)
        grad_wgate = jnp.dot(normed_wide.T, grad_gate, preferred_element_type=f32)
        grad_wup = jnp.dot(normed_wide.T, grad_up, preferred_element_type=f32)
        grad_normed_two = lax.psum_scatter(
            (
                jnp.dot(grad_gate, w_gate.T, preferred_element_type=f32)
                + jnp.dot(grad_up, w_up.T, preferred_element_type=f32)
            ).astype(jnp.bfloat16),
            "tp",
            scatter_dimension=0,
            tiled=True,
        ).astype(jnp.float32)
        grad_mid_norm, grad_gain_two = norm_back(middle, factor_two, gain_two, grad_normed_two)
        grad_middle = cotangent[micro_idx, 0].astype(f32) + grad_mid_norm
        grad_attn_wide = lax.all_gather(grad_middle.astype(bf16), "tp", axis=0, tiled=True)
        grad_wout = jnp.dot(att_flat.T, grad_attn_wide, preferred_element_type=f32)
        grad_mixed = (
            jnp.dot(grad_attn_wide, w_out.T, preferred_element_type=f32)
            .astype(bf16)
            .reshape(span_rows, heads_here, VHEAD)
        )

        def back_block(carry, block_idx):
            key_grad, value_grad = carry
            query_block, scores = block_scores(block_idx)
            probs = jnp.exp(scores - log_sums[block_idx][..., None])
            grad_probs = jnp.einsum(
                "qhd,khd->hqk", grad_mixed, values_all, preferred_element_type=f32
            )
            inner = jnp.sum(probs * grad_probs, axis=-1, keepdims=True)
            grad_scores = (softmax_scale * probs * (grad_probs - inner)).astype(bf16)
            grad_query = jnp.einsum(
                "hqk,khd->qhd", grad_scores, keys_all, preferred_element_type=f32
            )
            key_grad = key_grad + jnp.einsum(
                "hqk,qhd->khd", grad_scores, query_block, preferred_element_type=f32
            )
            value_grad = value_grad + jnp.einsum(
                "hqk,qhd->khd", probs.astype(bf16), grad_mixed, preferred_element_type=f32
            )
            return ((key_grad, value_grad), grad_query)

        zero_keys = jnp.zeros((seq_length, heads_here, query_width), f32)
        zero_values = jnp.zeros((seq_length, heads_here, VHEAD), f32)
        (key_grad, value_grad), grad_queries = lax.scan(
            back_block, (zero_keys, zero_values), jnp.arange(block_count, dtype=jnp.int32)
        )
        grad_queries = grad_queries.reshape(span_rows, heads_here, query_width)
        grad_qlin = (
            jnp.concatenate(
                [
                    grad_queries[..., :NOPE],
                    rotate_back(grad_queries[..., NOPE:], cos_query, sin_query),
                ],
                axis=-1,
            )
            .astype(bf16)
            .reshape(span_rows, heads_here * query_width)
        )
        grad_wquery = jnp.dot(normed_span.T, grad_qlin, preferred_element_type=f32)
        grad_expanded = (
            jnp.concatenate([key_grad[..., :NOPE], value_grad], axis=-1)
            .astype(bf16)
            .reshape(seq_length, heads_here * kv_width)
        )
        grad_rope_all = jnp.sum(key_grad[..., NOPE:], axis=1)
        grad_wexpand = jnp.dot(latent_all.T, grad_expanded, preferred_element_type=f32)
        grad_latent_all = jnp.dot(grad_expanded, w_expand.T, preferred_element_type=f32)
        grad_latent_own, grad_rope_own = (
            lax.psum_scatter(
                grad_latent_all.astype(jnp.bfloat16), ("ctx", "tp"), scatter_dimension=0, tiled=True
            ).astype(jnp.float32),
            lax.psum_scatter(
                grad_rope_all.astype(jnp.bfloat16), ("ctx", "tp"), scatter_dimension=0, tiled=True
            ).astype(jnp.float32),
        )
        grad_latent_part, grad_gain_latent = norm_back(
            latent_part, factor_latent, gain_kv, grad_latent_own
        )
        grad_raw = jnp.concatenate(
            [grad_latent_part, rotate_back(grad_rope_own, cos_own, sin_own)], axis=-1
        ).astype(bf16)
        grad_wlatent = jnp.dot(normed_own.T, grad_raw, preferred_element_type=f32)
        grad_normed_one = lax.psum_scatter(
            jnp.dot(grad_qlin, w_query.T, preferred_element_type=f32).astype(jnp.bfloat16),
            "tp",
            scatter_dimension=0,
            tiled=True,
        ).astype(jnp.float32) + jnp.dot(grad_raw, w_latent.T, preferred_element_type=f32)
        grad_in_norm, grad_gain_one = norm_back(inputs, factor_one, gain_one, grad_normed_one)
        grads_list.append((grad_middle + grad_in_norm).astype(bf16))
        split_grads = (grad_wquery, grad_wexpand, grad_wgate, grad_wup, grad_wout, grad_wdown)
        whole_grads = (grad_gain_one, grad_wlatent, grad_gain_latent, grad_gain_two)
        split_grads = (
            lax.psum_scatter(
                split_grads[0].astype(jnp.bfloat16),
                ("shard", "ctx"),
                scatter_dimension=0,
                tiled=True,
            ).astype(jnp.float32),
            lax.psum_scatter(
                split_grads[1].astype(jnp.bfloat16),
                ("shard", "ctx"),
                scatter_dimension=0,
                tiled=True,
            ).astype(jnp.float32),
            lax.psum_scatter(
                split_grads[2].astype(jnp.bfloat16),
                ("shard", "ctx"),
                scatter_dimension=0,
                tiled=True,
            ).astype(jnp.float32),
            lax.psum_scatter(
                split_grads[3].astype(jnp.bfloat16),
                ("shard", "ctx"),
                scatter_dimension=0,
                tiled=True,
            ).astype(jnp.float32),
            lax.psum_scatter(
                split_grads[4].astype(jnp.bfloat16),
                ("shard", "ctx"),
                scatter_dimension=1,
                tiled=True,
            ).astype(jnp.float32),
            lax.psum_scatter(
                split_grads[5].astype(jnp.bfloat16),
                ("shard", "ctx"),
                scatter_dimension=1,
                tiled=True,
            ).astype(jnp.float32),
        )
        split_total = (
            split_grads if split_total is None else jax.tree.map(jnp.add, split_total, split_grads)
        )
        whole_total = (
            whole_grads if whole_total is None else jax.tree.map(jnp.add, whole_total, whole_grads)
        )
    whole_total = (
        lax.psum_scatter(whole_total[0], ("shard", "ctx", "tp"), scatter_dimension=0, tiled=True),
        lax.psum_scatter(whole_total[1], ("shard", "ctx", "tp"), scatter_dimension=0, tiled=True),
        lax.psum_scatter(whole_total[2], ("shard", "ctx", "tp"), scatter_dimension=0, tiled=True),
        lax.psum_scatter(whole_total[3], ("shard", "ctx", "tp"), scatter_dimension=0, tiled=True),
    )
    output = jnp.stack(outputs_list)[:, None]
    input_grad = jnp.stack(grads_list)[:, None]
    return (
        output,
        input_grad,
        whole_total[0],
        split_total[0],
        whole_total[1],
        whole_total[2],
        split_total[1],
        split_total[4],
        whole_total[3],
        split_total[2],
        split_total[3],
        split_total[5],
    )


def solution(mesh):
    placed = (
        P(None, "shard", ("ctx", "tp"), None),
        P(None, "shard", None),
        P(None, "shard", ("ctx", "tp"), None),
        P(("shard", "ctx", "tp")),
        P(("shard", "ctx"), "tp"),
        P(("shard", "ctx", "tp"), None),
        P(("shard", "ctx", "tp")),
        P(("shard", "ctx"), "tp"),
        P("tp", ("shard", "ctx")),
        P(("shard", "ctx", "tp")),
        P(("shard", "ctx"), "tp"),
        P(("shard", "ctx"), "tp"),
        P("tp", ("shard", "ctx")),
    )
    return jax.shard_map(
        shards,
        mesh=mesh,
        in_specs=placed,
        out_specs=(
            P(None, "shard", ("ctx", "tp"), None),
            P(None, "shard", ("ctx", "tp"), None),
            P(("shard", "ctx", "tp")),
            P(("shard", "ctx"), "tp"),
            P(("shard", "ctx", "tp"), None),
            P(("shard", "ctx", "tp")),
            P(("shard", "ctx"), "tp"),
            P("tp", ("shard", "ctx")),
            P(("shard", "ctx", "tp")),
            P(("shard", "ctx"), "tp"),
            P(("shard", "ctx"), "tp"),
            P("tp", ("shard", "ctx")),
        ),
        check_vma=False,
    )
```

profile of v0, /device:TPU:0, one launch (start us, length us, event | category | flops | bytes accessed | tf_op | source)
XLA Modules:
  0.0 3161.5 jit_solution(10605002190076156074)
XLA Ops:
  10.5 42.2 %all-reduce.7 = (bf16[2048]{0:T(1024)(128)(2,1)S(1)}, bf16[512]{0:T(512)(128)(2,1)S(1)}, bf16[2048]{0:T(1024)(128)(2,1)S(1)}) all-reduce(bf16[2048]{0:T(1024)(128)(2,1)S(1)} %dynamic-update-slice, bf16[512]{0:T(512)(128)(2,1)S(1)} %dynamic-update-slice.1, ...), channel_id=1, replica_groups=mesh['shard'=4,'ctx'=2,'tp'=4] {'shard','ctx','tp'}, use_global_device_ids=true, to_apply=%add | all-reduce | flops 4608 | bytes 18432
  91.6 25.4 all_gather.124
  121.0 33.0 %all-gather.34.cloned.1.call-done = bf16[2048,768]{1,0:T(8,128)(2,1)} async-done(((bf16[256,768]{1,0:T(8,128)(2,1)}), bf16[2048,768]{1,0:T(8,128)(2,1)}) %all-gather.34.cloned.1.call-update) | async-done | bytes 3145744 | tf_op jit(solution)/shard_map/all_gather | solution.py:105
  159.3 19.9 all-gather.30.cloned.1.call-done
  179.3 26.0 all-gather.52.cloned.1.call-done
  239.0 25.2 all_gather.120
  288.8 19.7 all-gather.46.cloned.1.call-done
  322.2 24.0 all_gather.111
  362.2 19.5 all-gather.28.cloned.1.call-done
  395.2 31.8 %reduce-scatter.58.cloned.1.call-done = bf16[128,2048]{1,0:T(8,128)(2,1)} async-done(((bf16[512,2048]{1,0:T(8,128)(2,1)}), bf16[128,2048]{1,0:T(8,128)(2,1)}) %reduce-scatter.58.cloned.1.call-update) | async-done | bytes 524304 | tf_op jit(solution)/shard_map/reduce_scatter | solution.py:189
  427.1 46.0 %reduce-scatter.54.cloned.1.call-done = bf16[128,2048]{1,0:T(8,128)(2,1)} async-done(((bf16[512,2048]{1,0:T(8,128)(2,1)}), bf16[128,2048]{1,0:T(8,128)(2,1)}) %reduce-scatter.54.cloned.1.call-update) | async-done | bytes 524304 | tf_op jit(solution)/shard_map/reduce_scatter | solution.py:189
  473.1 46.1 %reduce-scatter.50.cloned.1.call-done = bf16[128,2048]{1,0:T(8,128)(2,1)} async-done(((bf16[512,2048]{1,0:T(8,128)(2,1)}), bf16[128,2048]{1,0:T(8,128)(2,1)}) %reduce-scatter.50.cloned.1.call-update) | async-done | bytes 524304 | tf_op jit(solution)/shard_map/reduce_scatter | solution.py:189
  530.8 39.2 %all-gather.38.cloned.1.call-done = bf16[512,2048]{1,0:T(8,128)(2,1)} async-done(((bf16[128,2048]{1,0:T(8,128)(2,1)}), bf16[512,2048]{1,0:T(8,128)(2,1)}) %all-gather.38.cloned.1.call-update) | async-done | bytes 2097168 | tf_op jit(solution)/shard_map/all_gather | solution.py:198
  569.9 69.1 %all-gather.40.cloned.1.call-done = bf16[2048,2736]{0,1:T(8,128)(2,1)} async-done(((bf16[256,2736]{0,1:T(8,128)(2,1)}), bf16[2048,2736]{0,1:T(8,128)(2,1)}) %all-gather.40.cloned.1.call-update) | async-done | bytes 11206672 | tf_op jit(solution)/shard_map/all_gather | solution.py:107
  651.4 58.0 %all-gather.42.cloned.1.call-done = bf16[2048,2736]{0,1:T(8,128)(2,1)} async-done(((bf16[256,2736]{0,1:T(8,128)(2,1)}), bf16[2048,2736]{0,1:T(8,128)(2,1)}) %all-gather.42.cloned.1.call-update) | async-done | bytes 11206672 | tf_op jit(solution)/shard_map/all_gather | solution.py:108
  719.8 37.6 %all-gather.64.cloned.1.call-done = bf16[1,1,512,2048]{3,2,1,0:T(8,128)(2,1)} async-done(((bf16[1,1,128,2048]{3,2,1,0:T(8,128)(2,1)}), bf16[1,1,512,2048]{3,2,1,0:T(8,128)(2,1)}) %all-gather.64.cloned.1.call-update) | async-done | bytes 2097168 | tf_op jit(solution)/shard_map/all_gather | solution.py:199
  757.4 69.1 %all-gather.44.cloned.1.call-done = bf16[2736,2048]{1,0:T(8,128)(2,1)} async-done(((bf16[2736,256]{1,0:T(8,128)(2,1)}), bf16[2736,2048]{1,0:T(8,128)(2,1)}) %all-gather.44.cloned.1.call-update) | async-done | bytes 11206672 | tf_op jit(solution)/shard_map/all_gather | solution.py:110
  897.7 23.2 all-gather.66.cloned.1.call-done
  990.8 23.3 all-gather.68.cloned.1.call-done
  1062.1 42.3 %reduce-scatter.66.cloned.1.call-done = bf16[128,2048]{1,0:T(8,128)(2,1)} async-done(((bf16[512,2048]{1,0:T(8,128)(2,1)}), bf16[128,2048]{1,0:T(8,128)(2,1)}) %reduce-scatter.66.cloned.1.call-update) | async-done | bytes 524304 | tf_op jit(solution)/shard_map/reduce_scatter | solution.py:223
  1104.4 45.6 %reduce-scatter.70.cloned.1.call-done = bf16[128,2048]{1,0:T(8,128)(2,1)} async-done(((bf16[512,2048]{1,0:T(8,128)(2,1)}), bf16[128,2048]{1,0:T(8,128)(2,1)}) %reduce-scatter.70.cloned.1.call-update) | async-done | bytes 524304 | tf_op jit(solution)/shard_map/reduce_scatter | solution.py:223
  1153.7 41.7 %reduce-scatter.60.cloned.1.call-done = bf16[128,2048]{1,0:T(8,128)(2,1)} async-done(((bf16[512,2048]{1,0:T(8,128)(2,1)}), bf16[128,2048]{1,0:T(8,128)(2,1)}) %reduce-scatter.60.cloned.1.call-update) | async-done | bytes 524304 | tf_op jit(solution)/shard_map/reduce_scatter | solution.py:209
  1203.1 41.5 %all-gather.62.cloned.1.call-done = bf16[512,2048]{1,0:T(8,128)(2,1)} async-done(((bf16[128,2048]{1,0:T(8,128)(2,1)}), bf16[512,2048]{1,0:T(8,128)(2,1)}) %all-gather.62.cloned.1.call-update) | async-done | bytes 2097168 | tf_op jit(solution)/shard_map/all_gather | solution.py:234
  1261.5 29.4 all-gather.60.cloned.1.call-done
  1307.6 30.2 all-gather.58.cloned.1.call-done
  1598.0 39.1 %reduce-scatter.84.cloned.1.call-done = bf16[64,1024]{1,0:T(8,128)(2,1)} async-done(((bf16[512,1024]{1,0:T(8,128)(2,1)}), bf16[64,1024]{1,0:T(8,128)(2,1)}) %reduce-scatter.84.cloned.1.call-update) | async-done | bytes 131088 | tf_op jit(solution)/shard_map/reduce_scatter | solution.py:320
  1637.0 39.2 %reduce-scatter.82.cloned.1.call-done = bf16[64,1024]{1,0:T(8,128)(2,1)} async-done(((bf16[512,1024]{1,0:T(8,128)(2,1)}), bf16[64,1024]{1,0:T(8,128)(2,1)}) %reduce-scatter.82.cloned.1.call-update) | async-done | bytes 131088 | tf_op jit(solution)/shard_map/reduce_scatter | solution.py:320
  1678.0 42.6 %reduce-scatter.92.cloned.1.call-done = bf16[512,256]{1,0:T(8,128)(2,1)} async-done(((bf16[512,2048]{1,0:T(8,128)(2,1)}), bf16[512,256]{1,0:T(8,128)(2,1)}) %reduce-scatter.92.cloned.1.call-update) | async-done | bytes 262160 | tf_op jit(solution)/shard_map/reduce_scatter | solution.py:338
  1720.6 45.0 %reduce-scatter.90.cloned.1.call-done = bf16[512,256]{1,0:T(8,128)(2,1)} async-done(((bf16[512,2048]{1,0:T(8,128)(2,1)}), bf16[512,256]{1,0:T(8,128)(2,1)}) %reduce-scatter.90.cloned.1.call-update) | async-done | bytes 262160 | tf_op jit(solution)/shard_map/reduce_scatter | solution.py:338
  1765.6 44.5 %reduce-scatter.88.cloned.1.call-done = bf16[512,256]{1,0:T(8,128)(2,1)} async-done(((bf16[512,2048]{1,0:T(8,128)(2,1)}), bf16[512,256]{1,0:T(8,128)(2,1)}) %reduce-scatter.88.cloned.1.call-update) | async-done | bytes 262160 | tf_op jit(solution)/shard_map/reduce_scatter | solution.py:338
  1812.1 44.3 %reduce-scatter.64.cloned.1.call-done = bf16[128,2048]{1,0:T(8,128)(2,1)} async-done(((bf16[512,2048]{1,0:T(8,128)(2,1)}), bf16[128,2048]{1,0:T(8,128)(2,1)}) %reduce-scatter.64.cloned.1.call-update) | async-done | bytes 524304 | tf_op jit(solution)/shard_map/reduce_scatter | solution.py:303
  1859.4 42.3 %reduce-scatter.68.cloned.1.call-done = bf16[128,2048]{1,0:T(8,128)(2,1)} async-done(((bf16[512,2048]{1,0:T(8,128)(2,1)}), bf16[128,2048]{1,0:T(8,128)(2,1)}) %reduce-scatter.68.cloned.1.call-update) | async-done | bytes 524304 | tf_op jit(solution)/shard_map/reduce_scatter | solution.py:303
  1905.6 41.8 %reduce-scatter.72.cloned.1.call-done = bf16[128,2048]{1,0:T(8,128)(2,1)} async-done(((bf16[512,2048]{1,0:T(8,128)(2,1)}), bf16[128,2048]{1,0:T(8,128)(2,1)}) %reduce-scatter.72.cloned.1.call-update) | async-done | bytes 524304 | tf_op jit(solution)/shard_map/reduce_scatter | solution.py:303
  1952.0 44.1 %all-reduce.6 = (f32[2048]{0:T(1024)S(1)}, f32[512]{0:T(512)S(1)}, f32[2048]{0:T(1024)S(1)}) all-reduce(f32[2048]{0:T(1024)S(1)} %add_add_fusion.2, f32[512]{0:T(512)S(1)} %add_add_fusion.3, f32[2048]{0:T(1024)S(1)} %add_add_fusion.1), channel_id=23, replica_groups=mesh['shard'=4,'ctx'=2,'tp'=4] {'shard','ctx','tp'}, use_global_device_ids=true, to_apply=%region_57.58.clone | all-reduce | flops 4608 | bytes 36864
  2004.6 34.6 %reduce-scatter.56.cloned.1.call-done = bf16[128,2048]{1,0:T(8,128)(2,1)} async-done(((bf16[512,2048]{1,0:T(8,128)(2,1)}), bf16[128,2048]{1,0:T(8,128)(2,1)}) %reduce-scatter.56.cloned.1.call-update) | async-done | bytes 524304 | tf_op jit(solution)/shard_map/reduce_scatter | solution.py:209
  2044.7 43.4 %reduce-scatter.78.cloned.1.call-done = bf16[256,768]{1,0:T(8,128)(2,1)} async-done(((bf16[2048,768]{1,0:T(8,128)(2,1)}), bf16[256,768]{1,0:T(8,128)(2,1)}) %reduce-scatter.78.cloned.1.call-update) | async-done | bytes 393232 | tf_op jit(solution)/shard_map/reduce_scatter | solution.py:314
  2088.1 49.9 %reduce-scatter.74.cloned.1.call-done = bf16[256,768]{1,0:T(8,128)(2,1)} async-done(((bf16[2048,768]{1,0:T(8,128)(2,1)}), bf16[256,768]{1,0:T(8,128)(2,1)}) %reduce-scatter.74.cloned.1.call-update) | async-done | bytes 393232 | tf_op jit(solution)/shard_map/reduce_scatter | solution.py:314
  2137.9 49.5 %reduce-scatter.76.cloned.1.call-done = bf16[256,768]{1,0:T(8,128)(2,1)} async-done(((bf16[2048,768]{1,0:T(8,128)(2,1)}), bf16[256,768]{1,0:T(8,128)(2,1)}) %reduce-scatter.76.cloned.1.call-update) | async-done | bytes 393232 | tf_op jit(solution)/shard_map/reduce_scatter | solution.py:314
  2189.7 88.0 %reduce-scatter.106.cloned.1.call-done = bf16[2736,256]{1,0:T(8,128)(2,1)} async-done(((bf16[2736,2048]{1,0:T(8,128)(2,1)}), bf16[2736,256]{1,0:T(8,128)(2,1)}) %reduce-scatter.106.cloned.1.call-update) | async-done | bytes 1400848 | tf_op jit(solution)/shard_map/reduce_scatter | solution.py:344
  2277.7 89.7 %reduce-scatter.108.cloned.1.call-done = bf16[2736,256]{1,0:T(8,128)(2,1)} async-done(((bf16[2736,2048]{1,0:T(8,128)(2,1)}), bf16[2736,256]{1,0:T(8,128)(2,1)}) %reduce-scatter.108.cloned.1.call-update) | async-done | bytes 1400848 | tf_op jit(solution)/shard_map/reduce_scatter | solution.py:344
  2367.4 90.3 %reduce-scatter.110.cloned.1.call-done = bf16[2736,256]{1,0:T(8,128)(2,1)} async-done(((bf16[2736,2048]{1,0:T(8,128)(2,1)}), bf16[2736,256]{1,0:T(8,128)(2,1)}) %reduce-scatter.110.cloned.1.call-update) | async-done | bytes 1400848 | tf_op jit(solution)/shard_map/reduce_scatter | solution.py:344
  2461.8 85.5 %reduce-scatter.100.cloned.1.call-done = bf16[256,2736]{0,1:T(8,128)(2,1)} async-done(((bf16[2048,2736]{0,1:T(8,128)(2,1)}), bf16[256,2736]{0,1:T(8,128)(2,1)}) %reduce-scatter.100.cloned.1.call-update) | async-done | bytes 1400848 | tf_op jit(solution)/shard_map/reduce_scatter | solution.py:332
  2547.3 90.3 %reduce-scatter.102.cloned.1.call-done = bf16[256,2736]{0,1:T(8,128)(2,1)} async-done(((bf16[2048,2736]{0,1:T(8,128)(2,1)}), bf16[256,2736]{0,1:T(8,128)(2,1)}) %reduce-scatter.102.cloned.1.call-update) | async-done | bytes 1400848 | tf_op jit(solution)/shard_map/reduce_scatter | solution.py:332
  2637.6 89.8 %reduce-scatter.104.cloned.1.call-done = bf16[256,2736]{0,1:T(8,128)(2,1)} async-done(((bf16[2048,2736]{0,1:T(8,128)(2,1)}), bf16[256,2736]{0,1:T(8,128)(2,1)}) %reduce-scatter.104.cloned.1.call-update) | async-done | bytes 1400848 | tf_op jit(solution)/shard_map/reduce_scatter | solution.py:332
  2731.6 86.1 %reduce-scatter.94.cloned.1.call-done = bf16[256,2736]{0,1:T(8,128)(2,1)} async-done(((bf16[2048,2736]{0,1:T(8,128)(2,1)}), bf16[256,2736]{0,1:T(8,128)(2,1)}) %reduce-scatter.94.cloned.1.call-update) | async-done | bytes 1400848 | tf_op jit(solution)/shard_map/reduce_scatter | solution.py:326
  2817.7 89.8 %reduce-scatter.96.cloned.1.call-done = bf16[256,2736]{0,1:T(8,128)(2,1)} async-done(((bf16[2048,2736]{0,1:T(8,128)(2,1)}), bf16[256,2736]{0,1:T(8,128)(2,1)}) %reduce-scatter.96.cloned.1.call-update) | async-done | bytes 1400848 | tf_op jit(solution)/shard_map/reduce_scatter | solution.py:326
  2907.5 90.1 %reduce-scatter.98.cloned.1.call-done = bf16[256,2736]{0,1:T(8,128)(2,1)} async-done(((bf16[2048,2736]{0,1:T(8,128)(2,1)}), bf16[256,2736]{0,1:T(8,128)(2,1)}) %reduce-scatter.98.cloned.1.call-update) | async-done | bytes 1400848 | tf_op jit(solution)/shard_map/reduce_scatter | solution.py:326
  3001.8 152.5 %reduce-scatter.80.cloned.1.call-done = f32[64,576]{1,0:T(8,128)} async-done(((f32[2048,576]{1,0:T(8,128)}), f32[64,576]{1,0:T(8,128)}) %reduce-scatter.80.cloned.1.call-update) | async-done | bytes 147472 | tf_op jit(solution)/shard_map/reduce_scatter | solution.py:359
  (764 shorter events, 722.0 us)
Async XLA Ops:
  82.0 201.4 %all-gather.48.cloned.1.call-start = ((), (), s32[]{:S(2)}) async-start(), calls=%async_computation.50 | async-start | bytes 2621440 | tf_op jit(solution)/shard_map/all_gather | solution.py:130
  82.8 225.7 %all-gather.46.cloned.1.call-start = ((), (), s32[]{:S(2)}) async-start(), calls=%async_computation.49 | async-start | bytes 1179648 | tf_op jit(solution)/shard_map/all_gather | solution.py:137
  83.5 274.0 %all-gather.32.cloned.1.call-start = ((), (), s32[]{:S(2)}) async-start(), calls=%async_computation.40 | async-start | bytes 2621440 | tf_op jit(solution)/shard_map/all_gather | solution.py:130
  84.3 297.4 %all-gather.28.cloned.1.call-start = ((), (), s32[]{:S(2)}) async-start(), calls=%async_computation.38 | async-start | bytes 1179648 | tf_op jit(solution)/shard_map/all_gather | solution.py:137
  117.0 310.1 %reduce-scatter.58.cloned.1.call-start = ((), (), s32[]{:S(2)}) async-start(), calls=%async_computation.56 | async-start | bytes 2621440 | tf_op jit(solution)/shard_map/reduce_scatter | solution.py:189
  238.1 235.0 %reduce-scatter.54.cloned.1.call-start = ((), (), s32[]{:S(2)}) async-start(), calls=%async_computation.51 | async-start | bytes 2621440 | tf_op jit(solution)/shard_map/reduce_scatter | solution.py:189
  322.0 197.2 %reduce-scatter.50.cloned.1.call-start = ((), (), s32[]{:S(2)}) async-start(), calls=%async_computation.43 | async-start | bytes 2621440 | tf_op jit(solution)/shard_map/reduce_scatter | solution.py:189
  525.1 184.2 %all-gather.42.cloned.1.call-start = ((), (), s32[]{:S(2)}) async-start(), calls=%async_computation.46 | async-start | bytes 12607488 | tf_op jit(solution)/shard_map/all_gather | solution.py:108
  525.7 231.7 %all-gather.64.cloned.1.call-start = ((), (), s32[]{:S(2)}) async-start(), calls=%async_computation.87 | async-start | bytes 2621440 | tf_op jit(solution)/shard_map/all_gather | solution.py:199
  527.1 299.4 %all-gather.44.cloned.1.call-start = ((), (), s32[]{:S(2)}) async-start(), calls=%async_computation.47 | async-start | bytes 12607488 | tf_op jit(solution)/shard_map/all_gather | solution.py:110
  527.7 347.0 %all-gather.50.cloned.1.call-start = ((), (), s32[]{:S(2)}) async-start(), calls=%async_computation.52 | async-start | bytes 2621440 | tf_op jit(solution)/shard_map/all_gather | solution.py:198
  528.5 392.4 %all-gather.66.cloned.1.call-start = ((), (), s32[]{:S(2)}) async-start(), calls=%async_computation.88 | async-start | bytes 2621440 | tf_op jit(solution)/shard_map/all_gather | solution.py:199
  529.1 438.7 %all-gather.56.cloned.1.call-start = ((), (), s32[]{:S(2)}) async-start(), calls=%async_computation.57 | async-start | bytes 2621440 | tf_op jit(solution)/shard_map/all_gather | solution.py:198
  529.8 484.3 %all-gather.68.cloned.1.call-start = ((), (), s32[]{:S(2)}) async-start(), calls=%async_computation.89 | async-start | bytes 2621440 | tf_op jit(solution)/shard_map/all_gather | solution.py:199
  530.5 531.5 %reduce-scatter.62.cloned.1.call-start = ((), (), s32[]{:S(2)}) async-start(), calls=%async_computation.59 | async-start | bytes 2621440 | tf_op jit(solution)/shard_map/reduce_scatter | solution.py:223
  862.5 242.0 %reduce-scatter.66.cloned.1.call-start = ((), (), s32[]{:S(2)}) async-start(), calls=%async_computation.62 | async-start | bytes 2621440 | tf_op jit(solution)/shard_map/reduce_scatter | solution.py:223
  958.8 191.2 %reduce-scatter.70.cloned.1.call-start = ((), (), s32[]{:S(2)}) async-start(), calls=%async_computation.65 | async-start | bytes 2621440 | tf_op jit(solution)/shard_map/reduce_scatter | solution.py:223
  1062.0 182.6 %all-gather.62.cloned.1.call-start = ((), (), s32[]{:S(2)}) async-start(), calls=%async_computation.66 | async-start | bytes 2621440 | tf_op jit(solution)/shard_map/all_gather | solution.py:234
  1203.0 378.7 %reduce-scatter.118.cloned.1.call-start = ((), (), s32[]{:S(2)}) async-start(), calls=%async_computation.93 | async-start | bytes 294912
  1353.7 229.2 %reduce-scatter.114.cloned.1.call-start = ((), (), s32[]{:S(2)}) async-start(), calls=%async_computation.91 | async-start | bytes 294912
  1361.0 222.7 %reduce-scatter.122.cloned.1.call-start = ((), (), s32[]{:S(2)}) async-start(), calls=%async_computation.95 | async-start | bytes 294912
  1366.3 220.5 %reduce-scatter.120.cloned.1.call-start = ((), (), s32[]{:S(2)}) async-start(), calls=%async_computation.94 | async-start | bytes 1179648
  1370.5 217.4 %reduce-scatter.116.cloned.1.call-start = ((), (), s32[]{:S(2)}) async-start(), calls=%async_computation.92 | async-start | bytes 1179648
  1381.4 207.6 %reduce-scatter.112.cloned.1.call-start = ((), (), s32[]{:S(2)}) async-start(), calls=%async_computation.90 | async-start | bytes 1179648
  1390.8 207.2 %reduce-scatter.86.cloned.1.call-start = ((), (), s32[]{:S(2)}) async-start(), calls=%async_computation.74 | async-start | bytes 1179648 | tf_op jit(solution)/shard_map/reduce_scatter | solution.py:320
  1393.2 243.8 %reduce-scatter.84.cloned.1.call-start = ((), (), s32[]{:S(2)}) async-start(), calls=%async_computation.73 | async-start | bytes 1179648 | tf_op jit(solution)/shard_map/reduce_scatter | solution.py:320
  1397.6 278.6 %reduce-scatter.82.cloned.1.call-start = ((), (), s32[]{:S(2)}) async-start(), calls=%async_computation.72 | async-start | bytes 1179648 | tf_op jit(solution)/shard_map/reduce_scatter | solution.py:320
  1400.4 320.2 %reduce-scatter.92.cloned.1.call-start = ((), (), s32[]{:S(2)}) async-start(), calls=%async_computation.77 | async-start | bytes 2359296 | tf_op jit(solution)/shard_map/reduce_scatter | solution.py:338
  1405.0 360.6 %reduce-scatter.90.cloned.1.call-start = ((), (), s32[]{:S(2)}) async-start(), calls=%async_computation.76 | async-start | bytes 2359296 | tf_op jit(solution)/shard_map/reduce_scatter | solution.py:338
  1407.7 402.4 %reduce-scatter.88.cloned.1.call-start = ((), (), s32[]{:S(2)}) async-start(), calls=%async_computation.75 | async-start | bytes 2359296 | tf_op jit(solution)/shard_map/reduce_scatter | solution.py:338
  1412.1 444.3 %reduce-scatter.64.cloned.1.call-start = ((), (), s32[]{:S(2)}) async-start(), calls=%async_computation.61 | async-start | bytes 2621440 | tf_op jit(solution)/shard_map/reduce_scatter | solution.py:303
  1421.0 480.8 %reduce-scatter.68.cloned.1.call-start = ((), (), s32[]{:S(2)}) async-start(), calls=%async_computation.64 | async-start | bytes 2621440 | tf_op jit(solution)/shard_map/reduce_scatter | solution.py:303
  1429.9 517.5 %reduce-scatter.72.cloned.1.call-start = ((), (), s32[]{:S(2)}) async-start(), calls=%async_computation.67 | async-start | bytes 2621440 | tf_op jit(solution)/shard_map/reduce_scatter | solution.py:303
  1439.0 562.0 %reduce-scatter.52.cloned.1.call-start = ((), (), s32[]{:S(2)}) async-start(), calls=%async_computation.48 | async-start | bytes 2621440 | tf_op jit(solution)/shard_map/reduce_scatter | solution.py:209
  1449.9 589.4 %reduce-scatter.56.cloned.1.call-start = ((), (), s32[]{:S(2)}) async-start(), calls=%async_computation.53 | async-start | bytes 2621440 | tf_op jit(solution)/shard_map/reduce_scatter | solution.py:209
  1460.8 627.3 %reduce-scatter.78.cloned.1.call-start = ((), (), s32[]{:S(2)}) async-start(), calls=%async_computation.70 | async-start | bytes 3538944 | tf_op jit(solution)/shard_map/reduce_scatter | solution.py:314
  1466.0 671.9 %reduce-scatter.74.cloned.1.call-start = ((), (), s32[]{:S(2)}) async-start(), calls=%async_computation.68 | async-start | bytes 3538944 | tf_op jit(solution)/shard_map/reduce_scatter | solution.py:314
  1471.3 716.2 %reduce-scatter.76.cloned.1.call-start = ((), (), s32[]{:S(2)}) async-start(), calls=%async_computation.69 | async-start | bytes 3538944 | tf_op jit(solution)/shard_map/reduce_scatter | solution.py:314
  1476.7 801.0 %reduce-scatter.106.cloned.1.call-start = ((), (), s32[]{:S(2)}) async-start(), calls=%async_computation.84 | async-start | bytes 12607488 | tf_op jit(solution)/shard_map/reduce_scatter | solution.py:344
  1488.7 878.7 %reduce-scatter.108.cloned.1.call-start = ((), (), s32[]{:S(2)}) async-start(), calls=%async_computation.85 | async-start | bytes 12607488 | tf_op jit(solution)/shard_map/reduce_scatter | solution.py:344
  1500.7 956.9 %reduce-scatter.110.cloned.1.call-start = ((), (), s32[]{:S(2)}) async-start(), calls=%async_computation.86 | async-start | bytes 12607488 | tf_op jit(solution)/shard_map/reduce_scatter | solution.py:344
  1512.8 1034.6 %reduce-scatter.100.cloned.1.call-start = ((), (), s32[]{:S(2)}) async-start(), calls=%async_computation.81 | async-start | bytes 12607488 | tf_op jit(solution)/shard_map/reduce_scatter | solution.py:332
  1524.8 1112.7 %reduce-scatter.102.cloned.1.call-start = ((), (), s32[]{:S(2)}) async-start(), calls=%async_computation.82 | async-start | bytes 12607488 | tf_op jit(solution)/shard_map/reduce_scatter | solution.py:332
  1535.7 1191.8 %reduce-scatter.104.cloned.1.call-start = ((), (), s32[]{:S(2)}) async-start(), calls=%async_computation.83 | async-start | bytes 12607488 | tf_op jit(solution)/shard_map/reduce_scatter | solution.py:332
  1546.6 1271.1 %reduce-scatter.94.cloned.1.call-start = ((), (), s32[]{:S(2)}) async-start(), calls=%async_computation.78 | async-start | bytes 12607488 | tf_op jit(solution)/shard_map/reduce_scatter | solution.py:326
  1557.1 1350.4 %reduce-scatter.96.cloned.1.call-start = ((), (), s32[]{:S(2)}) async-start(), calls=%async_computation.79 | async-start | bytes 12607488 | tf_op jit(solution)/shard_map/reduce_scatter | solution.py:326
  1569.2 1428.4 %reduce-scatter.98.cloned.1.call-start = ((), (), s32[]{:S(2)}) async-start(), calls=%async_computation.80 | async-start | bytes 12607488 | tf_op jit(solution)/shard_map/reduce_scatter | solution.py:326
  1581.5 1572.9 %reduce-scatter.80.cloned.1.call-start = ((), (), s32[]{:S(2)}) async-start(), calls=%async_computation.71 | async-start | bytes 5406720 | tf_op jit(solution)/shard_map/reduce_scatter | solution.py:359
  (209 other events, 6080.0 us)
Sparse Core Ops, SparseCore 0:
  10.9 60.7 all-gather.25
  73.8 47.1 all-gather.53
  235.4 47.9 all-gather.47
  310.6 46.9 all-gather.31
  384.6 42.4 reduce-scatter.57
  429.9 43.1 reduce-scatter.53
  476.0 43.1 reduce-scatter.49
  524.7 45.2 all-gather.37
  571.8 67.1 all-gather.39
  640.9 68.4 all-gather.41
  711.4 45.9 all-gather.63
  759.3 67.1 all-gather.43
  828.7 45.9 all-gather.49
  876.2 44.6 all-gather.65
  923.1 44.6 all-gather.55
  969.4 44.5 all-gather.67
  1016.5 42.5 reduce-scatter.61
  1061.2 43.1 reduce-scatter.65
  1106.8 43.1 reduce-scatter.69
  1152.2 43.1 reduce-scatter.59
  1199.3 45.2 all-gather.61
  1246.2 44.6 all-gather.59
  1293.1 44.6 all-gather.57
  1524.9 34.8 reduce-scatter.111
  1562.9 35.0 reduce-scatter.85
  1601.0 35.9 reduce-scatter.83
  1640.2 35.9 reduce-scatter.81
  1679.4 41.2 reduce-scatter.91
  1724.3 41.2 reduce-scatter.89
  1768.9 41.2 reduce-scatter.87
  1812.5 43.8 reduce-scatter.63
  1858.6 43.1 reduce-scatter.67
  1904.2 43.1 reduce-scatter.71
  1949.6 44.1 reduce-scatter.51
  1996.0 43.2 reduce-scatter.55
  2042.5 45.5 reduce-scatter.77
  2091.7 46.2 reduce-scatter.73
  2141.2 46.2 reduce-scatter.75
  2191.4 86.2 reduce-scatter.105
  2281.1 86.2 reduce-scatter.107
  2371.4 86.2 reduce-scatter.109
  2461.0 86.2 reduce-scatter.99
  2551.3 86.2 reduce-scatter.101
  2641.1 86.2 reduce-scatter.103
  2731.4 86.2 reduce-scatter.93
  2821.2 86.2 reduce-scatter.95
  2911.3 86.2 reduce-scatter.97
  3000.4 153.9 reduce-scatter.79
  (11 shorter events, 309.3 us)
where the time goes:
time: 3170 us; the launch traced here: 3160 us
  waiting for transfers between devices  2360 us (74%)
  matrix products  489 us (15%)
  blocking collectives  161 us (5%)
  other arithmetic  82.4 us (3%)
  local copies, waits for them, and re-layouts  50.3 us (2%)
    reduce_scatter x3, waiting for transfers between devices, shards(): lax.psum_scatter(split_grads[5].astype(jnp.bfloat16), ('shard', 'ctx'), s...  268 us
    reduce_scatter x3, waiting for transfers between devices, shards(): lax.psum_scatter(split_grads[2].astype(jnp.bfloat16), ('shard', 'ctx'), s...  266 us
    reduce_scatter x3, waiting for transfers between devices, shards(): lax.psum_scatter(split_grads[3].astype(jnp.bfloat16), ('shard', 'ctx'), s...  266 us
    reduce_scatter x1, waiting for transfers between devices, shards(): lax.psum_scatter(whole_total[1], ('shard', 'ctx', 'tp'), scatter_dimensio...  153 us
    reduce_scatter x3, waiting for transfers between devices, shards(): lax.psum_scatter(split_grads[0].astype(jnp.bfloat16), ('shard', 'ctx'), s...  143 us
    reduce_scatter x3, waiting for transfers between devices, shards(): lax.psum_scatter(split_grads[4].astype(jnp.bfloat16), ('shard', 'ctx'), s...  132 us
    reduce_scatter x3, waiting for transfers between devices, shards(): lax.psum_scatter(jnp.dot(grad_qlin, w_query.T, preferred_element_type=f32...  128 us
    reduce_scatter x3, waiting for transfers between devices, shards(): lax.psum_scatter(jnp.dot(att_flat, w_out, preferred_element_type=f32).ast...  124 us
  transfers between devices with their start and end apart: 59, of which 51 were waited for; matrix products, arithmetic and copies ran while one was open for 18% of the time, Pallas kernels for 0%

commit v1 on v0

v1 whole, which is shorter than its diff:
```python
import functools

import jax
import jax.numpy as jnp
from jax import lax
from jax.experimental import pallas as pl
from jax.experimental.pallas import tpu as pltpu
from jax.sharding import PartitionSpec as P

NOPE = 128
ROPE = 64
VHEAD = 128
KVRANK = 512
DOC_MOST = 512
LANES = 128

EPSILON = 1e-06
THETA_BASE = 10000.0
NEG_FILL = -1e30

f32 = jnp.float32
bf16 = jnp.bfloat16


def norm_scale(values):
    return lax.rsqrt(jnp.mean(values * values, axis=-1, keepdims=True) + EPSILON)


def norm_back(values, factor, gain_vec, grad_out):
    scaled = grad_out * gain_vec
    grad_in = factor * scaled - values * factor**3 * jnp.mean(
        scaled * values, axis=-1, keepdims=True
    )
    return (grad_in, jnp.sum(grad_out * values * factor, axis=0))


def rotate(values, cos_table, sin_table):
    half_width = values.shape[-1] // 2
    first_half = values[..., :half_width]
    second_half = values[..., half_width:]
    return jnp.concatenate(
        [
            first_half * cos_table - second_half * sin_table,
            second_half * cos_table + first_half * sin_table,
        ],
        axis=-1,
    )


def dot(left, right, kind=f32):
    return jnp.dot(left, right, preferred_element_type=f32).astype(kind)


def dot_rt(left, right, kind=f32):
    return lax.dot_general(
        left, right, (((1,), (1,)), ((), ())), preferred_element_type=f32
    ).astype(kind)


def dot_lt(left, right, kind=f32):
    return lax.dot_general(
        left, right, (((0,), (0,)), ((), ())), preferred_element_type=f32
    ).astype(kind)


def add16(*terms):
    total = terms[0].astype(f32)
    for term in terms[1:]:
        total = total + term.astype(f32)
    return total.astype(bf16)


def after(value, *others):
    return lax.optimization_barrier((value, *others))[0]


def swap_core(value):
    return lax.ppermute(value, "ctx", [(0, 1), (1, 0)])


def swap_x(value):
    return lax.ppermute(value, "shard", [(i, i ^ 1) for i in range(4)])


def swap_y(value):
    return lax.ppermute(value, "shard", [(i, i ^ 2) for i in range(4)])


def step_z(value):
    size = lax.axis_size("tp")
    return lax.ppermute(value, "tp", [(i, (i + 1) % size) for i in range(size)])


def gather_z(value):
    pieces = [value]
    for _ in range(lax.axis_size("tp") - 1):
        pieces.append(step_z(pieces[-1]))
    return pieces


def gather_xfirst(value):
    one = swap_x(value)
    return [value, one, swap_y(value), swap_y(one)]


def gather_yfirst(value):
    two = swap_y(value)
    return [value, swap_x(value), two, swap_x(two)]


def scatter_yfirst(blocks, last=bf16):
    three, two = swap_y(blocks[3]), swap_y(blocks[2])
    other = swap_x(add16(blocks[1], three))
    total = blocks[0].astype(f32) + two.astype(f32) + other.astype(f32)
    return total.astype(last)


def scatter_xfirst(blocks, last=bf16):
    three, one = swap_x(blocks[3]), swap_x(blocks[1])
    other = swap_y(add16(blocks[2], three))
    total = blocks[0].astype(f32) + one.astype(f32) + other.astype(f32)
    return total.astype(last)


def scatter_z(block_of, last=bf16, add=add16):
    size = lax.axis_size("tp")
    total = block_of(1)
    for j in range(2, size):
        total = add(step_z(total), block_of(j))
    return (step_z(total).astype(f32) + block_of(0).astype(f32)).astype(last)


def in_order(core, mine, other, axis):
    return jnp.where(
        core == 0,
        jnp.concatenate([mine, other], axis=axis),
        jnp.concatenate([other, mine], axis=axis),
    )


def swap_halves(values, lane):
    return jnp.where(
        lane % ROPE < ROPE // 2,
        pltpu.roll(values, LANES - ROPE // 2, 1),
        pltpu.roll(values, ROPE // 2, 1),
    )


def window_mask(start, base, rows, width, seg_query, seg_key):
    query_index = base + lax.broadcasted_iota(jnp.int32, (rows, width), 0)
    key_index = start + lax.broadcasted_iota(jnp.int32, (rows, width), 1)
    same_doc = (seg_query == seg_key) & (key_index <= query_index) & (seg_key != 0)
    return same_doc | (key_index == query_index)


def head_operands(q_ref, kv_ref, rope_key, slot, window, head, heads, cos_table, sin_table):
    rows = q_ref.shape[2]
    lane = lax.broadcasted_iota(jnp.int32, (rows, LANES), 1)
    first = heads * NOPE + head // 2 * LANES
    rope_lin = q_ref[slot, 0, :, first : first + LANES]
    turned = rope_lin * cos_table + swap_halves(rope_lin, lane) * sin_table
    turned = jnp.where(lane // ROPE == head % 2, turned, 0.0)
    plain = q_ref[slot, 0, :, head * NOPE : (head + 1) * NOPE]
    query = jnp.concatenate([plain, turned], axis=1).astype(bf16)
    at = head * (NOPE + VHEAD)
    key = jnp.concatenate([kv_ref[0, window, at : at + NOPE], rope_key], axis=1)
    value = kv_ref[0, window, at + NOPE : at + NOPE + VHEAD]
    return query, key, value


def attend_kernel(
    heads, width, scale, place, q_ref, kv_ref, kr_ref, segq_ref, segk_ref, cos_ref, sin_ref, o_ref
):
    slots, rows = q_ref.shape[0], q_ref.shape[2]
    for slot in range(slots):
        start = pl.multiple_of(place[slot, 0], rows)
        window = pl.ds(start, width)
        allowed = window_mask(
            start,
            place[slot, 1],
            rows,
            width,
            segq_ref[0, slot * rows : (slot + 1) * rows, :],
            segk_ref[0, slot : slot + 1, :],
        )
        rope_key = kr_ref[0, window, :]
        for head in range(heads):
            query, key, value = head_operands(
                q_ref, kv_ref, rope_key, slot, window, head, heads, cos_ref[slot, 0], sin_ref[slot, 0]
            )
            scores = jnp.where(allowed, dot_rt(query, key) * scale, NEG_FILL)
            expd = jnp.exp(scores - jnp.max(scores, axis=-1, keepdims=True))
            probs = expd / jnp.sum(expd, axis=-1, keepdims=True)
            o_ref[slot, 0, :, head * VHEAD : (head + 1) * VHEAD] = dot(
                probs.astype(bf16), value, bf16
            )


def attend_back_kernel(
    heads,
    width,
    scale,
    place,
    q_ref,
    kv_ref,
    kr_ref,
    segq_ref,
    segk_ref,
    cos_ref,
    sin_ref,
    do_ref,
    dq_ref,
    dkv_ref,
    dkr_ref,
    total,
):
    slots, rows = q_ref.shape[0], q_ref.shape[2]
    lane = lax.broadcasted_iota(jnp.int32, (rows, LANES), 1)

    @pl.when(pl.program_id(1) == 0)
    def _():
        dkr_ref[...] = jnp.zeros_like(dkr_ref)

    total[...] = jnp.zeros_like(total)
    for slot in range(slots):
        start = pl.multiple_of(place[slot, 0], rows)
        window = pl.ds(start, width)
        allowed = window_mask(
            start,
            place[slot, 1],
            rows,
            width,
            segq_ref[0, slot * rows : (slot + 1) * rows, :],
            segk_ref[0, slot : slot + 1, :],
        )
        rope_key = kr_ref[0, window, :]
        rope_grads = None
        for head in range(heads):
            query, key, value = head_operands(
                q_ref, kv_ref, rope_key, slot, window, head, heads, cos_ref[slot, 0], sin_ref[slot, 0]
            )
            grad_mixed = do_ref[slot, 0, :, head * VHEAD : (head + 1) * VHEAD]
            scores = jnp.where(allowed, dot_rt(query, key) * scale, NEG_FILL)
            expd = jnp.exp(scores - jnp.max(scores, axis=-1, keepdims=True))
            probs = expd / jnp.sum(expd, axis=-1, keepdims=True)
            grad_probs = dot_rt(grad_mixed, value)
            inner = jnp.sum(probs * grad_probs, axis=-1, keepdims=True)
            grad_scores = (scale * probs * (grad_probs - inner)).astype(bf16)
            grad_query = dot(grad_scores, key)
            grad_key = dot_lt(grad_scores, query)
            at = head * (NOPE + VHEAD)
            total[window, at : at + NOPE] += grad_key[:, :NOPE]
            dkr_ref[0, window, :] += grad_key[:, NOPE:]
            total[window, at + NOPE : at + NOPE + VHEAD] += dot_lt(probs.astype(bf16), grad_mixed)
            dq_ref[slot, 0, :, head * NOPE : (head + 1) * NOPE] = grad_query[:, :NOPE].astype(bf16)
            if head % 2 == 0:
                rope_grads = jnp.where(lane < ROPE, grad_query[:, NOPE:], 0.0)
            else:
                rope_grads = jnp.where(lane < ROPE, rope_grads, grad_query[:, NOPE:])
            if head % 2 == 1 or head == heads - 1:
                turned = rope_grads * cos_ref[slot, 0] - swap_halves(rope_grads, lane) * sin_ref[slot, 0]
                first = heads * NOPE + head // 2 * LANES
                dq_ref[slot, 0, :, first : first + LANES] = turned.astype(bf16)
    dkv_ref[0] = total[...].astype(bf16)


def attention_specs(heads, slots, rows, length, width, q_width):
    return [
        pl.BlockSpec((slots, 1, rows, q_width), lambda m, j, place: (0, m, 0, j)),
        pl.BlockSpec((1, length, heads * (NOPE + VHEAD)), lambda m, j, place: (m, 0, j)),
        pl.BlockSpec((1, length, LANES), lambda m, j, place: (m, 0, 0)),
        pl.BlockSpec((1, slots * rows, 1), lambda m, j, place: (m, 0, 0)),
        pl.BlockSpec((1, slots, width), lambda m, j, place: (m, 0, 0)),
        pl.BlockSpec((slots, 1, rows, LANES), lambda m, j, place: (0, m, 0, 0)),
        pl.BlockSpec((slots, 1, rows, LANES), lambda m, j, place: (0, m, 0, 0)),
    ]


def attend(heads, groups, width, scale, place, q_lin, kv, rope_keys, seg_query, seg_key, cos, sin):
    slots, micro, rows, q_all = q_lin.shape
    length = kv.shape[1]
    return pl.pallas_call(
        functools.partial(attend_kernel, heads, width, scale),
        out_shape=jax.ShapeDtypeStruct((slots, micro, rows, groups * heads * VHEAD), bf16),
        grid_spec=pltpu.PrefetchScalarGridSpec(
            num_scalar_prefetch=1,
            grid=(micro, groups),
            in_specs=attention_specs(heads, slots, rows, length, width, q_all // groups),
            out_specs=pl.BlockSpec(
                (slots, 1, rows, heads * VHEAD), lambda m, j, place: (0, m, 0, j)
            ),
        ),
        compiler_params=pltpu.CompilerParams(
            dimension_semantics=("arbitrary", "arbitrary"), vmem_limit_bytes=40 << 20
        ),
        cost_estimate=pl.CostEstimate(
            flops=2 * slots * rows * micro * groups * heads * width * 384,
            transcendentals=slots * rows * micro * groups * heads * width,
            bytes_accessed=2 * kv.size + 6 * q_lin.size,
        ),
        name="attend",
    )(place, q_lin, kv, rope_keys, seg_query, seg_key, cos, sin)


def attend_back(
    heads, groups, width, scale, place, q_lin, kv, rope_keys, seg_query, seg_key, cos, sin, d_o
):
    slots, micro, rows, q_all = q_lin.shape
    length = kv.shape[1]
    q_width = q_all // groups
    kv_width = heads * (NOPE + VHEAD)
    return pl.pallas_call(
        functools.partial(attend_back_kernel, heads, width, scale),
        out_shape=(
            jax.ShapeDtypeStruct(q_lin.shape, bf16),
            jax.ShapeDtypeStruct(kv.shape, bf16),
            jax.ShapeDtypeStruct((micro, length, LANES), f32),
        ),
        grid_spec=pltpu.PrefetchScalarGridSpec(
            num_scalar_prefetch=1,
            grid=(micro, groups),
            in_specs=attention_specs(heads, slots, rows, length, width, q_width)
            + [pl.BlockSpec((slots, 1, rows, heads * VHEAD), lambda m, j, place: (0, m, 0, j))],
            out_specs=[
                pl.BlockSpec((slots, 1, rows, q_width), lambda m, j, place: (0, m, 0, j)),
                pl.BlockSpec((1, length, kv_width), lambda m, j, place: (m, 0, j)),
                pl.BlockSpec((1, length, LANES), lambda m, j, place: (m, 0, 0)),
            ],
            scratch_shapes=[pltpu.VMEM((length, kv_width), f32)],
        ),
        compiler_params=pltpu.CompilerParams(
            dimension_semantics=("arbitrary", "arbitrary"), vmem_limit_bytes=40 << 20
        ),
        cost_estimate=pl.CostEstimate(
            flops=2 * slots * rows * micro * groups * heads * width * 1024,
            transcendentals=slots * rows * micro * groups * heads * width,
            bytes_accessed=4 * kv.size + 8 * q_lin.size,
        ),
        name="attend_back",
    )(place, q_lin, kv, rope_keys, seg_query, seg_key, cos, sin, d_o)


def shards(
    hidden,
    segments,
    cotangent,
    attn_gain,
    q_weight,
    latent_weight,
    latent_gain,
    expand_weight,
    out_weight,
    mlp_gain,
    gate_weight,
    up_weight,
    down_weight,
):
    micro, _, rows, width = hidden.shape
    length = segments.shape[2]
    tp_size, cores = lax.axis_size("tp"), lax.axis_size("ctx")
    shard, core, place_z = lax.axis_index("shard"), lax.axis_index("ctx"), lax.axis_index("tp")
    span = rows * tp_size
    own = micro * rows
    block = width // 4
    slice_rows = q_weight.shape[0]
    heads_here = q_weight.shape[1] // (NOPE + ROPE)
    split = heads_here % cores == 0
    heads = heads_here // cores if split else heads_here
    slots = cores if split else 1
    rope_width = -(-heads * ROPE // LANES) * LANES
    q_width = heads * NOPE + rope_width
    scale = (NOPE + ROPE) ** (-0.5)
    hidden_here = gate_weight.shape[1]
    part = -(-hidden_here // (cores * LANES)) * LANES
    window = min(length, -(-(DOC_MOST + rows) // LANES) * LANES)

    def features(values):
        size = values.shape[-1] // 4
        return jnp.concatenate(
            [
                lax.dynamic_slice_in_dim(values, (shard ^ k) * size, size, values.ndim - 1)
                for k in range(4)
            ],
            axis=-1,
        )

    def mine(values, axis):
        return lax.dynamic_index_in_dim(values, core, axis, keepdims=False)

    def others(values, axis):
        return lax.dynamic_index_in_dim(values, 1 - core, axis, keepdims=False)

    def halves(values, axis, pick, joined):
        del axis
        return in_order(core, mine(values, pick), swap_core(others(values, pick)), joined)

    small_rows = latent_weight.shape[0]
    gain_rows, latent_gains = attn_gain.shape[0], latent_gain.shape[0]
    kv_cols = latent_weight.shape[1]
    gains_row = jnp.concatenate([attn_gain, mlp_gain, latent_gain])
    gains_row = jnp.pad(gains_row, (0, kv_cols - gains_row.shape[0]))
    small = jnp.concatenate([latent_weight, jnp.pad(gains_row[None], ((0, 15), (0, 0)))])
    line = jnp.zeros((tp_size, small_rows + 16, kv_cols), bf16)
    for j, piece in enumerate(gather_z(small)):
        line = lax.dynamic_update_index_in_dim(line, piece, (place_z - j) % tp_size, 0)
    plane = jnp.stack(gather_xfirst(line))
    small_all = in_order(core, plane[:, None], swap_core(plane)[:, None], 1)
    w_latent = small_all[:, :, :, :small_rows].reshape(width, kv_cols)
    gain_all = small_all[:, :, :, small_rows].astype(f32)
    gain_one = gain_all[..., :gain_rows].reshape(width)
    gain_two = gain_all[..., gain_rows : 2 * gain_rows].reshape(width)
    gain_kv = features(
        gain_all[..., 2 * gain_rows : 2 * gain_rows + latent_gains].reshape(KVRANK)
    )

    down_pad = jnp.pad(down_weight, ((0, cores * part - hidden_here), (0, 0)))
    down_piece = halves(down_pad.reshape(cores, part, slice_rows), 0, 0, 1)
    half_part = part // 2 // 16 * 16
    down_top = gather_xfirst(down_piece[:half_part])
    down_low = gather_yfirst(down_piece[half_part:])
    w_down = jnp.concatenate(
        [jnp.concatenate(down_top, axis=1), jnp.concatenate(down_low, axis=1)], axis=0
    )

    def q_order(values):
        groups = values.shape[1] // (heads * (NOPE + ROPE))
        by_head = values.reshape(values.shape[0], groups, heads, NOPE + ROPE)
        plain = by_head[..., :NOPE].reshape(values.shape[0], groups, heads * NOPE)
        rope = by_head[..., NOPE:].reshape(values.shape[0], groups, heads * ROPE)
        rope = jnp.pad(rope, ((0, 0), (0, 0), (0, rope_width - heads * ROPE)))
        return jnp.concatenate([plain, rope], axis=-1)

    def q_disorder(values):
        lead = values.shape[:2]
        plain = values[..., : heads * NOPE].reshape(*lead, heads, NOPE)
        rope = values[..., heads * NOPE : heads * (NOPE + ROPE)].reshape(*lead, heads, ROPE)
        return jnp.concatenate([plain, rope], axis=-1).reshape(lead[0], -1)

    q_local = q_order(q_weight)
    expand_rows = expand_weight.shape[0]
    kv_width = heads * (NOPE + VHEAD)
    expand_local = expand_weight.reshape(expand_rows, -1, kv_width)
    out_local = out_weight.reshape(-1, heads * VHEAD, slice_rows)
    if split:
        q_piece = halves(q_local, 0, 1, 0)
        expand_piece = halves(expand_local, 0, 1, 0)
        out_piece = halves(out_local, 1, 0, 1)
    else:
        q_piece = in_order(core, q_local[:, 0], swap_core(q_local[:, 0]), 0)
        expand_piece = in_order(core, expand_local[:, 0], swap_core(expand_local[:, 0]), 0)
        out_piece = in_order(core, out_local[0], swap_core(out_local[0]), 1)
    q_line = jnp.concatenate(gather_z(q_piece), axis=1)
    expand_line = jnp.concatenate(gather_z(expand_piece), axis=1)
    out_line = jnp.concatenate(gather_z(out_piece), axis=0)
    q_blocks = gather_xfirst(q_line)
    expand_blocks = gather_yfirst(expand_line)
    out_blocks = gather_yfirst(out_line)
    w_query = jnp.concatenate(q_blocks, axis=0)
    w_expand = jnp.concatenate(expand_blocks, axis=0)
    w_expand = jnp.concatenate(
        [
            lax.dynamic_slice_in_dim(w_expand, (shard ^ k) * (KVRANK // 4), KVRANK // 4, 0)
            for k in range(4)
        ],
        axis=0,
    )
    w_out = jnp.concatenate(out_blocks, axis=1)

    def hidden_piece(weight):
        padded = jnp.pad(weight, ((0, 0), (0, cores * part - hidden_here)))
        return halves(padded.reshape(slice_rows, cores, part), 0, 1, 0)

    gate_piece, up_piece = lax.optimization_barrier(
        (hidden_piece(gate_weight), hidden_piece(up_weight), q_blocks[3], out_blocks[3])
    )[:2]
    w_gate = jnp.concatenate(gather_xfirst(gate_piece), axis=0)
    w_up = jnp.concatenate(gather_yfirst(up_piece), axis=0)

    seg_all = segments[:, 0]
    bases = [core * span + place_z * rows, (1 - core) * span + place_z * rows][:slots]
    starts = [jnp.maximum(base + rows - window, 0) for base in bases]
    place = jnp.stack([jnp.stack([a, b]) for a, b in zip(starts, bases)]).astype(jnp.int32)
    seg_query = jnp.concatenate(
        [lax.dynamic_slice_in_dim(seg_all, base, rows, 1) for base in bases], axis=1
    )
    seg_key = jnp.stack(
        [lax.dynamic_slice_in_dim(seg_all, start, window, 1) for start in starts], axis=1
    )
    query_index = jnp.concatenate([base + jnp.arange(rows, dtype=jnp.int32) for base in bases])
    first_index = jnp.sum(
        (seg_all[:, None, :] < seg_query[:, :, None]).astype(jnp.int32), axis=-1
    )
    positions = (query_index[None] - first_index).reshape(micro, slots, rows)
    positions = positions.transpose(1, 0, 2)
    freqs = THETA_BASE ** (-2.0 * jnp.arange(ROPE // 2, dtype=f32) / ROPE)
    angles = positions.astype(f32)[..., None] * freqs
    cos_rows, sin_rows = jnp.cos(angles), jnp.sin(angles)
    cos_own = cos_rows[0].reshape(own, ROPE // 2)
    sin_own = sin_rows[0].reshape(own, ROPE // 2)
    cos_lanes = jnp.concatenate([cos_rows] * 4, axis=-1)
    sin_lanes = jnp.concatenate([-sin_rows, sin_rows] * 2, axis=-1)
    attention = (heads, tp_size, window, scale, place)
    tables = (seg_query[..., None], seg_key, cos_lanes, sin_lanes)

    inputs = features(hidden.reshape(own, width)).astype(f32)
    factor_one = norm_scale(inputs)
    normed_own = (inputs * factor_one * gain_one).astype(bf16)
    normed_chip = normed_own
    if split:
        normed_chip = jnp.concatenate([normed_own, swap_core(normed_own)])
    latent_raw = dot(normed_own, w_latent)
    latent_part = latent_raw[:, :KVRANK]
    factor_latent = norm_scale(latent_part)
    latent_own = (latent_part * factor_latent * gain_kv).astype(bf16)
    rope_own = rotate(latent_raw[:, KVRANK:], cos_own, sin_own).astype(bf16)
    latent_pack = jnp.concatenate([latent_own, rope_own], axis=1).reshape(micro, rows, kv_cols)
    latent_half = jnp.zeros((micro, span, kv_cols), bf16)
    for j, piece in enumerate(gather_z(latent_pack)):
        latent_half = lax.dynamic_update_slice_in_dim(
            latent_half, piece, (place_z - j) % tp_size * rows, 1
        )
    latent_full = in_order(core, latent_half, swap_core(latent_half), 1)
    latent_all = latent_full[..., :KVRANK].reshape(micro * length, KVRANK)
    rope_keys = jnp.concatenate([latent_full[..., KVRANK:]] * 2, axis=-1)

    q_lin = dot(normed_chip, w_query).reshape(slots, micro, rows, tp_size * q_width)
    kv_all = dot(latent_all, w_expand, bf16).reshape(micro, length, tp_size * kv_width)
    mixed = attend(*attention, q_lin, kv_all, rope_keys, *tables)
    mixed = mixed.reshape(slots * own, tp_size * heads * VHEAD)
    if split:
        mixed_out = dot(mixed, w_out, bf16)
        middle = inputs + mixed_out[:own].astype(f32) + swap_core(mixed_out[own:]).astype(f32)
    else:
        middle = inputs + dot(mixed, w_out)
    factor_two = norm_scale(middle)
    normed_two = (middle * factor_two * gain_two).astype(bf16)

    def to_group(values):
        pieces = []
        for piece in gather_z(values):
            pieces += [piece, swap_core(piece)]
        return jnp.concatenate(pieces)

    grad_own = features(cotangent.reshape(own, width))
    grad_all = to_group(after(grad_own, q_line, expand_line, out_line))
    normed_all = to_group(normed_two)
    grad_act = dot_rt(grad_all, w_down)
    gate_val = dot(normed_all, w_gate)
    up_val = dot(normed_all, w_up)
    sigma = jax.nn.sigmoid(gate_val)
    swish = gate_val * sigma
    hidden_act = (swish * up_val).astype(bf16)
    grad_gate = (grad_act * up_val * sigma * (1.0 + gate_val * (1.0 - sigma))).astype(bf16)
    grad_up = (grad_act * swish).astype(bf16)

    def rows_of(values, j):
        return values[2 * own * j : 2 * own * (j + 1)]

    def from_group(product):
        def block_of(j):
            both = lax.optimization_barrier(product(j))
            return add16(both[:own], swap_core(both[own:]))

        return scatter_z(block_of, f32)

    grad_normed_two = from_group(
        lambda j: (
            dot_rt(rows_of(grad_gate, j), w_gate) + dot_rt(rows_of(grad_up, j), w_up)
        ).astype(bf16)
    )
    down_out = from_group(lambda j: dot(rows_of(hidden_act, j), w_down, bf16))
    output = (middle + down_out).astype(bf16)

    def columns(values, k):
        return values[:, block * k : block * (k + 1)]

    gate_back = scatter_yfirst(
        [dot_lt(columns(normed_all, k), grad_gate, bf16) for k in range(4)]
    )
    up_back = scatter_xfirst([dot_lt(columns(normed_all, k), grad_up, bf16) for k in range(4)])
    down_blocks = [dot_lt(hidden_act, columns(grad_all, k), bf16) for k in range(4)]
    down_back = jnp.concatenate(
        [
            scatter_yfirst([piece[:half_part] for piece in down_blocks]),
            scatter_xfirst([piece[half_part:] for piece in down_blocks]),
        ]
    )

    def hidden_grad(value):
        by_core = value.reshape(cores, slice_rows, part)
        both = in_order(core, mine(by_core, 0), swap_core(others(by_core, 0)), 1)
        return both[:, :hidden_here].astype(f32)

    grad_wgate, grad_wup = hidden_grad(gate_back), hidden_grad(up_back)
    by_core = down_back.reshape(part, cores, slice_rows)
    grad_wdown = in_order(core, mine(by_core, 1), swap_core(others(by_core, 1)), 0)
    grad_wdown = grad_wdown[:hidden_here].astype(f32)

    grad_mid_norm, grad_gain_two = norm_back(middle, factor_two, gain_two, grad_normed_two)
    grad_middle = grad_own.astype(f32) + grad_mid_norm
    grad_attn = grad_middle.astype(bf16)
    if split:
        grad_attn = jnp.concatenate([grad_attn, swap_core(grad_attn)])
    grad_mixed = dot_rt(grad_attn, w_out, bf16)
    grad_qlin, grad_kv, grad_ropes = attend_back(
        *attention,
        q_lin,
        kv_all,
        rope_keys,
        *tables,
        grad_mixed.reshape(slots, micro, rows, tp_size * heads * VHEAD),
    )
    grad_qlin = grad_qlin.reshape(slots * own, tp_size * q_width)
    grad_kv = grad_kv.reshape(micro * length, tp_size * kv_width)

    grad_latent = jnp.concatenate(
        [
            dot_rt(grad_kv, w_expand, bf16).reshape(micro, length, KVRANK),
            (grad_ropes[..., :ROPE] + grad_ropes[..., ROPE:]).astype(bf16),
        ],
        axis=-1,
    ).reshape(micro, cores, span, kv_cols)
    latent_sum = add16(mine(grad_latent, 1), swap_core(others(grad_latent, 1)))
    grad_latent_own = scatter_z(
        lambda j: lax.dynamic_slice_in_dim(latent_sum, (place_z - j) % tp_size * rows, rows, 1), f32
    ).reshape(own, kv_cols)
    grad_latent_part, grad_gain_latent = norm_back(
        latent_part, factor_latent, gain_kv, grad_latent_own[:, :KVRANK]
    )
    grad_raw = jnp.concatenate(
        [grad_latent_part, rotate(grad_latent_own[:, KVRANK:], cos_own, -sin_own)], axis=-1
    ).astype(bf16)
    grad_normed_one = dot_rt(grad_raw, w_latent)
    if split:
        query_back = dot_rt(grad_qlin, w_query, bf16)
        grad_normed_one = (
            grad_normed_one
            + query_back[:own].astype(f32)
            + swap_core(query_back[own:]).astype(f32)
        )
    else:
        grad_normed_one = grad_normed_one + dot_rt(grad_qlin, w_query)
    grad_in_norm, grad_gain_one = norm_back(inputs, factor_one, gain_one, grad_normed_one)
    input_grad = (grad_middle + grad_in_norm).astype(bf16)

    out_back = scatter_xfirst([dot_lt(mixed, columns(grad_attn, k), bf16) for k in range(4)])
    query_back = scatter_yfirst(
        [dot_lt(columns(normed_chip, k), grad_qlin, bf16) for k in range(4)]
    )
    latent_block = KVRANK // 4
    expand_back = scatter_xfirst(
        [
            dot_lt(
                lax.dynamic_slice_in_dim(latent_all, (shard ^ k) * latent_block, latent_block, 1),
                grad_kv,
                bf16,
            )
            for k in range(4)
        ]
    )
    out_here = scatter_z(
        lambda j: out_back[heads * VHEAD * j : heads * VHEAD * (j + 1)]
    )
    query_here = scatter_z(lambda j: query_back[:, q_width * j : q_width * (j + 1)])
    expand_here = scatter_z(lambda j: expand_back[:, kv_width * j : kv_width * (j + 1)])
    out_cores = out_here.reshape(heads * VHEAD, cores, slice_rows)
    query_cores = query_here.reshape(cores, slice_rows, q_width)
    expand_cores = expand_here.reshape(cores, expand_rows, kv_width)
    if split:
        grad_wout = in_order(core, mine(out_cores, 1), swap_core(others(out_cores, 1)), 0)
        grad_wquery = in_order(
            core, mine(query_cores, 0)[:, None], swap_core(others(query_cores, 0))[:, None], 1
        )
        grad_wexpand = in_order(core, mine(expand_cores, 0), swap_core(others(expand_cores, 0)), 1)
    else:
        grad_wout = mine(out_cores, 1).astype(f32) + swap_core(others(out_cores, 1)).astype(f32)
        grad_wquery = mine(query_cores, 0).astype(f32) + swap_core(others(query_cores, 0)).astype(
            f32
        )
        grad_wquery = grad_wquery[:, None]
        grad_wexpand = mine(expand_cores, 0).astype(f32) + swap_core(
            others(expand_cores, 0)
        ).astype(f32)
    grad_wquery = q_disorder(grad_wquery).astype(f32)
    grad_wout, grad_wexpand = grad_wout.astype(f32), grad_wexpand.astype(f32)

    def scatter_small(values, add):
        kept = add(mine(values, 1), swap_core(others(values, 1)))
        three, two = swap_y(kept[3]), swap_y(kept[2])
        kept = add(add(kept[0], two), swap_x(add(kept[1], three)))
        return scatter_z(
            lambda j: lax.dynamic_index_in_dim(
                kept, (place_z - j) % tp_size, 0, keepdims=False
            ),
            f32,
            add,
        )

    grad_wlatent = dot_lt(normed_own, grad_raw, bf16)
    grad_wlatent = scatter_small(
        grad_wlatent.reshape(4, cores, tp_size, small_rows, kv_cols), add16
    )
    gain_grads = scatter_small(
        jnp.concatenate(
            [
                grad_gain_one.reshape(4, cores, tp_size, gain_rows),
                grad_gain_two.reshape(4, cores, tp_size, gain_rows),
                features(grad_gain_latent).reshape(4, cores, tp_size, latent_gains),
            ],
            axis=-1,
        ),
        jnp.add,
    )
    like = (micro, 1, rows, width)
    return (
        features(output).reshape(like),
        features(input_grad).reshape(like),
        gain_grads[:gain_rows],
        grad_wquery,
        grad_wlatent,
        gain_grads[2 * gain_rows :],
        grad_wexpand,
        grad_wout,
        gain_grads[gain_rows : 2 * gain_rows],
        grad_wgate,
        grad_wup,
        grad_wdown,
    )


def solution(mesh):
    tokens = P(None, "shard", ("ctx", "tp"), None)
    everywhere = P(("shard", "ctx", "tp"))
    down_split = P(("shard", "ctx"), "tp")
    up_split = P("tp", ("shard", "ctx"))
    whole_rows = P(("shard", "ctx", "tp"), None)
    return jax.shard_map(
        shards,
        mesh=mesh,
        in_specs=(
            tokens,
            P(None, "shard", None),
            tokens,
            everywhere,
            down_split,
            whole_rows,
            everywhere,
            down_split,
            up_split,
            everywhere,
            down_split,
            down_split,
            up_split,
        ),
        out_specs=(
            tokens,
            tokens,
            everywhere,
            down_split,
            whole_rows,
            everywhere,
            down_split,
            up_split,
            everywhere,
            down_split,
            down_split,
            up_split,
        ),
        check_vma=False,
    )
```

time: 3170 us -> 1380 us (0.44)
  waiting for transfers between devices: 2360 us -> 515 us
  blocking collectives: 161 us -> 0 us
  local copies, waits for them, and re-layouts: 50.3 us -> 149 us
  matrix products: 489 us -> 411 us
  Pallas kernels: 0 us -> 71.8 us
  starting transfers between devices: 4.55 us -> 72.4 us
  other arithmetic: 82.4 us -> 148 us
    reduce_scatter x31 -> x0, waiting for transfers between devices: 1720 us -> none  [the longest x3 268 us: shards(): lax.psum_scatter(split_grads[5].astype(jnp.bfloat16), ('shard', 'ctx'), s...]
    all_gather x22 -> x0, waiting for transfers between devices: 623 us -> none  [the longest x3 101 us: shards(): lax.all_gather(grad_middle.astype(bf16), 'tp', axis=0, tiled=True)]
    ppermute x0 -> x133, waiting for transfers between devices: none -> 515 us  [the longest x45 344 us: step_z(): return lax.ppermute(value, 'tp', [(i, (i + 1) % size) for i in range(size)])]
    unnamed x2 -> x0, blocking collectives: 86.3 us -> none
    dot_general x81 -> x48, matrix products: 489 us -> 411 us  [the longest x25 155 us: dot_lt(): lax.dot_general(left, right, (((0,), (0,)), ((), ())), preferred_element_...]
    all_gather x3 -> x0, blocking collectives: 74.6 us -> none  [shards(): lax.all_gather(rope_own, ('ctx', 'tp'), axis=0, tiled=True)]
    ppermute x0 -> x133, starting transfers between devices: none -> 72.4 us  [the longest x26 30.2 us: swap_y(): return lax.ppermute(value, 'shard', [(i, i ^ 2) for i in range(4)])]
    pallas_call x0 -> x2, Pallas kernels: none -> 71.8 us  [the longest x1 44.7 us: attend_back(): pl.pallas_call(functools.partial(attend_back_kernel, heads, width, scale)...]
  transfers between devices with their start and end apart: 59 -> 133, of which waited for: 51 -> 54; matrix products, arithmetic and copies ran while one was open for 18% -> 36% of each run, Pallas kernels for 0% -> 2%
where the time goes in v1:
time: 1380 us; the launch traced here: 1370 us
  waiting for transfers between devices  515 us (37%)
  matrix products  411 us (30%)
  local copies, waits for them, and re-layouts  149 us (11%)
  other arithmetic  148 us (11%)
  starting transfers between devices  72.4 us (5%)
  Pallas kernels  71.8 us (5%)
    ppermute x45, waiting for transfers between devices, step_z(): return lax.ppermute(value, 'tp', [(i, (i + 1) % size) for i in range(size)])  344 us
    dot_general x25, matrix products, dot_lt(): lax.dot_general(left, right, (((0,), (0,)), ((), ())), preferred_element_...  155 us
    dot_general x13, matrix products, dot_rt(): lax.dot_general(left, right, (((1,), (1,)), ((), ())), preferred_element_...  131 us
    ppermute x26, waiting for transfers between devices, swap_y(): return lax.ppermute(value, 'shard', [(i, i ^ 2) for i in range(4)])  125 us
    dot_general x10, matrix products, dot(): return jnp.dot(left, right, preferred_element_type=f32).astype(kind)  125 us
    pallas_call x1, Pallas kernels, attend_back(): pl.pallas_call(functools.partial(attend_back_kernel, heads, width, scale)...  44.7 us
    unnamed x359, local copies, waits for them, and re-layouts  44.1 us
    ppermute x25, waiting for transfers between devices, swap_x(): return lax.ppermute(value, 'shard', [(i, i ^ 1) for i in range(4)])  43.5 us
  transfers between devices with their start and end apart: 133, of which 54 were waited for; matrix products, arithmetic and copies ran while one was open for 36% of the time, Pallas kernels for 2%

profile of v1, /device:TPU:0, one launch (start us, length us, event | category | flops | bytes accessed | tf_op | source)
XLA Modules:
  0.0 1371.8 jit_solution(9359835276370812703)
XLA Ops:
  71.0 8.4 collective-permute-done.9
  88.0 9.4 collective-permute-done.27
  103.5 13.1 collective-permute-done.11
  145.5 14.1 %collective-permute-done.29 = bf16[256,512]{1,0:T(8,128)(2,1)S(1)} collective-permute-done((bf16[256,512]{1,0:T(8,128)(2,1)}, bf16[256,512]{1,0:T(8,128)(2,1)S(1)}, u32[]{:S(2)}, u32[]{:S(2)}) %collective-permute-start.29) | collective-permute-done | bytes 262176 | tf_op jit(solution)/shard_map/ppermute | solution.py:91
  188.2 10.6 collective-permute-done.17
  207.0 23.9 %collective-permute-done.14 = bf16[512,1536]{1,0:T(8,128)(2,1)} collective-permute-done((bf16[512,1536]{1,0:T(8,128)(2,1)}, bf16[512,1536]{1,0:T(8,128)(2,1)}, u32[]{:S(2)}, u32[]{:S(2)}) %collective-permute-start.14) | collective-permute-done | bytes 1572896 | tf_op jit(solution)/shard_map/ppermute | solution.py:86
  232.5 13.2 fusion.3
  256.8 24.5 %collective-permute-done.31 = bf16[1024,512]{1,0:T(8,128)(2,1)} collective-permute-done((bf16[1024,512]{1,0:T(8,128)(2,1)}, bf16[1024,512]{1,0:T(8,128)(2,1)}, u32[]{:S(2)}, u32[]{:S(2)}) %collective-permute-start.31) | collective-permute-done | bytes 1048608 | tf_op jit(solution)/shard_map/ppermute | solution.py:86
  282.8 9.6 convolution_convert_fusion
  293.0 27.1 %attend.1 = bf16[2,3,128,1024]{3,2,1,0:T(8,128)(2,1)S(1)} custom-call(s32[2,2]{1,0:T(2,128)S(1)} %pad_add_fusion.2.place, f32[2,3,128,1536]{3,2,1,0:T(8,128)S(1)} %bitcast.250, bf16[3,1024,2048]{2,1,0:T(8,128)(2,1)} %bitcast.277, bf16[3,1024,128]{2,1,0:T(8,128)(2,1)S(1)} %pad_maximum_fusion.24.kr_ref, s32[3,256,1]{2,1,0:T(8,128)S(1)} %copy.204.segq_ref, ...), custom_call_target="tpu_custom_call" | custom-call | flops 3019898880 | bytes 19660800 | tf_op jit(solution)/shard_map/attend/pallas_call | solution.py:282
  323.8 7.5 convolution_convert_fusion.2
  340.0 10.7 collective-permute-done.55
  350.6 27.6 %maximum_maximum_fusion = bf16[1408,2048]{1,0:T(8,128)(2,1)} fusion(bf16[704,512]{1,0:T(8,128)(2,1)S(1)} %collective-permute-done.55, bf16[704,512]{1,0:T(8,128)(2,1)} %collective-permute-done.54, bf16[704,512]{1,0:T(8,128)(2,1)S(1)} %collective-permute-done.53, bf16[704,512]{1,0:T(8,128)(2,1)} %get-tuple-element.135, ...), kind=kLoop, calls=%fused_computation.17 | loop fusion | flops 46137344 | bytes 11534336 | tf_op jit(solution)/shard_map/concatenate | solution.py:421
  393.1 22.8 %collective-permute-done.44 = bf16[512,1408]{0,1:T(8,128)(2,1)S(1)} collective-permute-done((bf16[512,1408]{0,1:T(8,128)(2,1)S(1)}, bf16[512,1408]{0,1:T(8,128)(2,1)S(1)}, u32[]{:S(2)}, u32[]{:S(2)}) %collective-permute-start.44) | collective-permute-done | bytes 1441824 | tf_op jit(solution)/shard_map/ppermute | solution.py:86
  424.3 19.6 %collective-permute-done.47 = bf16[512,1408]{0,1:T(8,128)(2,1)S(1)} collective-permute-done((bf16[512,1408]{0,1:T(8,128)(2,1)S(1)}, bf16[512,1408]{0,1:T(8,128)(2,1)S(1)}, u32[]{:S(2)}, u32[]{:S(2)}) %collective-permute-start.47) | collective-permute-done | bytes 1441824 | tf_op jit(solution)/shard_map/ppermute | solution.py:86
  449.2 10.8 collective-permute-done.35
  463.9 8.6 collective-permute-done.45
  478.3 16.2 %collective-permute-done.37 = bf16[384,2048]{1,0:T(8,128)(2,1)S(1)} collective-permute-done((bf16[384,2048]{1,0:T(8,128)(2,1)S(1)}, bf16[384,2048]{1,0:T(8,128)(2,1)S(1)}, u32[]{:S(2)}, u32[]{:S(2)}) %collective-permute-start.37) | collective-permute-done | bytes 1572896 | tf_op jit(solution)/shard_map/ppermute | solution.py:91
  494.6 24.7 %fusion.171 = f32[3072,1408]{1,0:T(8,128)} fusion(bf16[3072,2048]{1,0:T(8,128)(2,1)} %constant_dynamic-update-slice_fusion.16, bf16[1408,2048]{1,0:T(8,128)(2,1)S(1)} %bitcast.282), kind=kOutput, calls=%fused_computation.442 | convolution fusion | flops 17716740096 | bytes 35651584 | tf_op jit(solution)/shard_map/dot_general | solution.py:55
  535.2 24.7 %fusion.170 = f32[3072,1408]{1,0:T(8,128)} fusion(bf16[3072,2048]{1,0:T(8,128)(2,1)} %constant_dynamic-update-slice_fusion, bf16[2048,1408]{0,1:T(8,128)(2,1)S(1)} %bitcast.326), kind=kOutput, calls=%fused_computation.441 | convolution fusion | flops 17716740096 | bytes 35651584 | tf_op jit(solution)/shard_map/dot_general | solution.py:51
  559.9 37.2 %multiply_convert_fusion.1 = (bf16[3072,1408]{1,0:T(8,128)(2,1)}, bf16[3072,1408]{1,0:T(8,128)(2,1)}, bf16[3072,1408]{1,0:T(8,128)(2,1)}) fusion(f32[3072,1408]{1,0:T(8,128)} %fusion.171, f32[3072,1408]{1,0:T(8,128)} %fusion.170, bf16[3072,2048]{1,0:T(8,128)(2,1)} %constant_dynamic-update-slice_fusion, bf16[2048,1408]{0,1:T(8,128)(2,1)} %constant_dynamic-update-slice_fusion.8), kind=kOutput, calls=%fused_computation.1 | convolution fusion | flops 17781620736 | bytes 78905344 | tf_op jit(solution)/shard_map/dot_general | solution.py:51
  597.2 9.2 fusion.29
  606.4 9.2 fusion.26
  628.2 10.4 convolution_convert_fusion.13
  638.7 10.2 convolution_convert_fusion.15
  656.4 7.5 fusion.23
  671.1 8.1 convolution_convert_fusion.5
  713.7 9.2 add_convert_fusion
  722.9 9.0 add_convert_fusion.1
  731.9 10.3 add_convert_fusion.3
  742.2 10.3 add_convert_fusion.2
  752.5 8.0 convolution_convert_fusion.7
  804.4 10.5 fusion.37
  823.2 19.7 %collective-permute-done.57 = bf16[384,2048]{1,0:T(8,128)(2,1)S(1)} collective-permute-done((bf16[384,2048]{1,0:T(8,128)(2,1)S(1)}, bf16[384,2048]{1,0:T(8,128)(2,1)S(1)}, u32[]{:S(2)}, u32[]{:S(2)}) %collective-permute-start.57) | collective-permute-done | bytes 1572896 | tf_op jit(solution)/shard_map/ppermute | solution.py:91
  843.0 9.2 fusion.44
  855.2 25.6 %collective-permute-done.71 = bf16[384,2048]{1,0:T(8,128)(2,1)S(1)} collective-permute-done((bf16[384,2048]{1,0:T(8,128)(2,1)S(1)}, bf16[384,2048]{1,0:T(8,128)(2,1)S(1)}, u32[]{:S(2)}, u32[]{:S(2)}) %collective-permute-start.71) | collective-permute-done | bytes 1572896 | tf_op jit(solution)/shard_map/ppermute | solution.py:91
  882.4 9.6 fusion.41
  891.9 28.0 %collective-permute-done.59 = bf16[384,2048]{1,0:T(8,128)(2,1)S(1)} collective-permute-done((bf16[384,2048]{1,0:T(8,128)(2,1)S(1)}, bf16[384,2048]{1,0:T(8,128)(2,1)S(1)}, u32[]{:S(2)}, u32[]{:S(2)}) %collective-permute-start.59) | collective-permute-done | bytes 1572896 | tf_op jit(solution)/shard_map/ppermute | solution.py:91
  922.5 28.9 %collective-permute-done.73 = bf16[384,2048]{1,0:T(8,128)(2,1)S(1)} collective-permute-done((bf16[384,2048]{1,0:T(8,128)(2,1)S(1)}, bf16[384,2048]{1,0:T(8,128)(2,1)S(1)}, u32[]{:S(2)}, u32[]{:S(2)}) %collective-permute-start.73) | collective-permute-done | bytes 1572896 | tf_op jit(solution)/shard_map/ppermute | solution.py:91
  953.5 10.3 fusion.48
  972.6 53.5 %collective-permute-done.75 = bf16[384,2048]{1,0:T(8,128)(2,1)} collective-permute-done((bf16[384,2048]{1,0:T(8,128)(2,1)}, bf16[384,2048]{1,0:T(8,128)(2,1)}, u32[]{:S(2)}, u32[]{:S(2)}) %collective-permute-start.75) | collective-permute-done | bytes 1572896 | tf_op jit(solution)/shard_map/ppermute | solution.py:91
  1058.7 44.7 %attend_back.1 = (bf16[2,3,128,1536]{3,2,1,0:T(8,128)(2,1)S(1)}, bf16[3,1024,2048]{2,1,0:T(8,128)(2,1)}, f32[3,1024,128]{2,1,0:T(8,128)S(1)}) custom-call(s32[2,2]{1,0:T(2,128)S(1)} %pad_add_fusion.2.place, f32[2,3,128,1536]{3,2,1,0:T(8,128)S(1)} %bitcast.253, bf16[3,1024,2048]{2,1,0:T(8,128)(2,1)} %bitcast.278, bf16[3,1024,128]{2,1,0:T(8,128)(2,1)S(1)} %copy-done.1, ...), custom_call_target="tpu_custom_call" | custom-call | flops 8053063680 | bytes 34603008 | tf_op jit(solution)/shard_map/attend_back/pallas_call | solution.py:312
  1114.3 11.2 convolution_convert_fusion.1
  1140.3 14.1 %convolution_convert_fusion.3 = bf16[768,2048]{1,0:T(8,128)(2,1)} fusion(bf16[768,1536]{1,0:T(8,128)(2,1)S(1)} %bitcast.260, bf16[512,1536]{1,0:T(8,128)(2,1)} %collective-permute-done.14, bf16[512,1536]{1,0:T(8,128)(2,1)} %collective-permute-done.13, bf16[512,1536]{1,0:T(8,128)(2,1)} %collective-permute-done.12, bf16[512,384]{1,0:T(8,128)(2,1)S(1)} %copy-done.102, ...), kind=kOutput, calls=%fused_computation.44 | convolution fusion | flops 4877451264 | bytes 11796480 | tf_op jit(solution)/shard_map/dot_general | solution.py:55
  1208.7 12.7 collective-permute-done.113
  1224.1 10.2 collective-permute-done.114
  1234.5 9.3 collective-permute-done.79
  1332.6 8.5 collective-permute-done.94
  (859 shorter events, 596.0 us)
Async XLA Ops:
  2.1 52.9 %collective-permute-start.19 = (bf16[64,512]{1,0:T(8,128)(2,1)S(1)}, bf16[64,512]{1,0:T(8,128)(2,1)}, u32[]{:S(2)}, u32[]{:S(2)}) collective-permute-start(bf16[64,512]{1,0:T(8,128)(2,1)S(1)} %bitcast.343), channel_id=1, source_target_pairs={{0,4},{4,0},{1,5},{5,1},{2,6},{6,2},{3,7},{7,3},{8,12},{12,8},{9,1... | collective-permute-start | bytes 196616 | tf_op jit(solution)/shard_map/ppermute | solution.py:78
  9.2 70.3 %collective-permute-start.26 = (bf16[256,256]{1,0:T(8,128)(2,1)}, bf16[256,256]{1,0:T(8,128)(2,1)}, u32[]{:S(2)}, u32[]{:S(2)}) collective-permute-start(bf16[256,256]{1,0:T(8,128)(2,1)} %get-tuple-element.151), channel_id=1, source_target_pairs={{0,4},{4,0},{1,5},{5,1},{2,6},{6,2},{3,7},{7,3},{8,12},{12,8},{9,1... | collective-permute-start | bytes 393224 | tf_op jit(solution)/shard_map/ppermute | solution.py:78
  11.7 51.1 %collective-permute-start.8 = (bf16[256,384]{1,0:T(8,128)(2,1)}, bf16[256,384]{1,0:T(8,128)(2,1)}, u32[]{:S(2)}, u32[]{:S(2)}) collective-permute-start(bf16[256,384]{1,0:T(8,128)(2,1)} %get-tuple-element.147), channel_id=1, source_target_pairs={{0,4},{4,0},{1,5},{5,1},{2,6},{6,2},{3,7},{7,3},{8,12},{12,8},{9,1... | collective-permute-start | bytes 589832 | tf_op jit(solution)/shard_map/ppermute | solution.py:78
  68.3 51.2 %collective-permute-start.6 = (bf16[4,4,80,576]{3,1,0,2:T(4,128)(2,1)}, bf16[4,4,80,576]{3,1,0,2:T(4,128)(2,1)}, u32[]{:S(2)}, u32[]{:S(2)}) collective-permute-start(bf16[4,4,80,576]{3,1,0,2:T(4,128)(2,1)} %pad_maximum_fusion.10), channel_id=1, source_target_pairs={{0,4},{4,0},{1,5},{5,1},{2,6},{6,2},{3,7},{7,3},{8,12},{12,8},{9,1... | collective-permute-start | bytes 4423688 | tf_op jit(solution)/shard_map/ppermute | solution.py:78
  86.0 54.0 %collective-permute-start.41 = (bf16[256,1408]{0,1:T(8,128)(2,1)}, bf16[256,1408]{0,1:T(8,128)(2,1)}, u32[]{:S(2)}, u32[]{:S(2)}) collective-permute-start(bf16[256,1408]{0,1:T(8,128)(2,1)} %get-tuple-element.133), channel_id=1, source_target_pairs={{0,4},{4,0},{1,5},{5,1},{2,6},{6,2},{3,7},{7,3},{8,12},{12,8},{9,1... | collective-permute-start | bytes 2162696 | tf_op jit(solution)/shard_map/ppermute | solution.py:78
  119.5 48.8 %collective-permute-start.12 = (bf16[512,1536]{1,0:T(8,128)(2,1)}, bf16[512,1536]{1,0:T(8,128)(2,1)}, u32[]{:S(2)}, u32[]{:S(2)}) collective-permute-start(bf16[512,1536]{1,0:T(8,128)(2,1)} %pad_maximum_fusion.12), channel_id=1, source_target_pairs={{0,8},{8,0},{16,24},{24,16},{1,9},{9,1},{17,25},{25,17},{2,10},{10... | collective-permute-start | bytes 4718600 | tf_op jit(solution)/shard_map/ppermute | solution.py:82
  159.6 44.4 %collective-permute-start.13 = (bf16[512,1536]{1,0:T(8,128)(2,1)}, bf16[512,1536]{1,0:T(8,128)(2,1)}, u32[]{:S(2)}, u32[]{:S(2)}) collective-permute-start(bf16[512,1536]{1,0:T(8,128)(2,1)} %pad_maximum_fusion.12), channel_id=1, source_target_pairs={{0,16},{8,24},{16,0},{24,8},{1,17},{9,25},{17,1},{25,9},{2,18},{10... | collective-permute-start | bytes 4718600 | tf_op jit(solution)/shard_map/ppermute | solution.py:86
  168.3 62.6 %collective-permute-start.14 = (bf16[512,1536]{1,0:T(8,128)(2,1)}, bf16[512,1536]{1,0:T(8,128)(2,1)}, u32[]{:S(2)}, u32[]{:S(2)}) collective-permute-start(bf16[512,1536]{1,0:T(8,128)(2,1)} %collective-permute-done.12), channel_id=1, source_target_pairs={{0,16},{8,24},{16,0},{24,8},{1,17},{9,25},{17,1},{25,9},{2,18},{10... | collective-permute-start | bytes 4718600 | tf_op jit(solution)/shard_map/ppermute | solution.py:86
  177.9 77.3 %collective-permute-start.51 = (bf16[704,512]{1,0:T(8,128)(2,1)}, bf16[704,512]{1,0:T(8,128)(2,1)}, u32[]{:S(2)}, u32[]{:S(2)}) collective-permute-start(bf16[704,512]{1,0:T(8,128)(2,1)} %get-tuple-element.134), channel_id=1, source_target_pairs={{0,16},{8,24},{16,0},{24,8},{1,17},{9,25},{17,1},{25,9},{2,18},{10... | collective-permute-start | bytes 2162696 | tf_op jit(solution)/shard_map/ppermute | solution.py:86
  201.0 44.6 %collective-permute-start.18 = (bf16[3,512,576]{1,2,0:T(8,128)(2,1)}, bf16[3,512,576]{1,2,0:T(8,128)(2,1)}, u32[]{:S(2)}, u32[]{:S(2)}) collective-permute-start(bf16[3,512,576]{1,2,0:T(8,128)(2,1)} %copy.201), channel_id=1, source_target_pairs={{0,4},{4,0},{1,5},{5,1},{2,6},{6,2},{3,7},{7,3},{8,12},{12,8},{9,1... | collective-permute-start | bytes 5308424 | tf_op jit(solution)/shard_map/ppermute | solution.py:78
  204.0 116.1 %collective-permute-start.50 = (bf16[704,512]{1,0:T(8,128)(2,1)}, bf16[704,512]{1,0:T(8,128)(2,1)}, u32[]{:S(2)}, u32[]{:S(2)}) collective-permute-start(bf16[704,512]{1,0:T(8,128)(2,1)} %get-tuple-element.134), channel_id=1, source_target_pairs={{0,8},{8,0},{16,24},{24,16},{1,9},{9,1},{17,25},{25,17},{2,10},{10... | collective-permute-start | bytes 2162696 | tf_op jit(solution)/shard_map/ppermute | solution.py:82
  205.5 115.2 %collective-permute-start.54 = (bf16[704,512]{1,0:T(8,128)(2,1)}, bf16[704,512]{1,0:T(8,128)(2,1)}, u32[]{:S(2)}, u32[]{:S(2)}) collective-permute-start(bf16[704,512]{1,0:T(8,128)(2,1)} %get-tuple-element.135), channel_id=1, source_target_pairs={{0,16},{8,24},{16,0},{24,8},{1,17},{9,25},{17,1},{25,9},{2,18},{10... | collective-permute-start | bytes 2162696 | tf_op jit(solution)/shard_map/ppermute | solution.py:86
  230.9 50.3 %collective-permute-start.31 = (bf16[1024,512]{1,0:T(8,128)(2,1)}, bf16[1024,512]{1,0:T(8,128)(2,1)}, u32[]{:S(2)}, u32[]{:S(2)}) collective-permute-start(bf16[1024,512]{1,0:T(8,128)(2,1)} %pad_maximum_fusion.23), channel_id=1, source_target_pairs={{0,16},{8,24},{16,0},{24,8},{1,17},{9,25},{17,1},{25,9},{2,18},{10... | collective-permute-start | bytes 3145736 | tf_op jit(solution)/shard_map/ppermute | solution.py:86
  245.7 75.0 %collective-permute-start.30 = (bf16[1024,512]{1,0:T(8,128)(2,1)}, bf16[1024,512]{1,0:T(8,128)(2,1)}, u32[]{:S(2)}, u32[]{:S(2)}) collective-permute-start(bf16[1024,512]{1,0:T(8,128)(2,1)} %pad_maximum_fusion.23), channel_id=1, source_target_pairs={{0,8},{8,0},{16,24},{24,16},{1,9},{9,1},{17,25},{25,17},{2,10},{10... | collective-permute-start | bytes 3145736 | tf_op jit(solution)/shard_map/ppermute | solution.py:82
  256.6 76.1 %collective-permute-start.64 = (bf16[384,2048]{1,0:T(8,128)(2,1)S(1)}, bf16[384,2048]{1,0:T(8,128)(2,1)}, u32[]{:S(2)}, u32[]{:S(2)}) collective-permute-start(bf16[384,2048]{1,0:T(8,128)(2,1)S(1)} %copy-done.29), channel_id=1, source_target_pairs={{0,1},{1,2},{2,3},{3,0},{4,5},{5,6},{6,7},{7,4},{8,9},{9,10},{10,1... | collective-permute-start | bytes 4718600 | tf_op jit(solution)/shard_map/ppermute | solution.py:91
  320.7 57.7 %collective-permute-start.63 = (bf16[384,2048]{1,0:T(8,128)(2,1)S(1)}, bf16[384,2048]{1,0:T(8,128)(2,1)}, u32[]{:S(2)}, u32[]{:S(2)}) collective-permute-start(bf16[384,2048]{1,0:T(8,128)(2,1)S(1)} %copy-done.29), channel_id=1, source_target_pairs={{0,4},{4,0},{1,5},{5,1},{2,6},{6,2},{3,7},{7,3},{8,12},{12,8},{9,1... | collective-permute-start | bytes 4718600 | tf_op jit(solution)/shard_map/ppermute | solution.py:78
  332.7 57.3 %collective-permute-start.66 = (bf16[384,2048]{1,0:T(8,128)(2,1)}, bf16[384,2048]{1,0:T(8,128)(2,1)}, u32[]{:S(2)}, u32[]{:S(2)}) collective-permute-start(bf16[384,2048]{1,0:T(8,128)(2,1)} %collective-permute-done.64), channel_id=1, source_target_pairs={{0,1},{1,2},{2,3},{3,0},{4,5},{5,6},{6,7},{7,4},{8,9},{9,10},{10,1... | collective-permute-start | bytes 4718600 | tf_op jit(solution)/shard_map/ppermute | solution.py:91
  339.4 52.1 %collective-permute-start.65 = (bf16[384,2048]{1,0:T(8,128)(2,1)}, bf16[384,2048]{1,0:T(8,128)(2,1)}, u32[]{:S(2)}, u32[]{:S(2)}) collective-permute-start(bf16[384,2048]{1,0:T(8,128)(2,1)} %collective-permute-done.64), channel_id=1, source_target_pairs={{0,4},{4,0},{1,5},{5,1},{2,6},{6,2},{3,7},{7,3},{8,12},{12,8},{9,1... | collective-permute-start | bytes 4718600 | tf_op jit(solution)/shard_map/ppermute | solution.py:78
  339.5 46.6 %collective-permute-start.33 = (bf16[384,2048]{1,0:T(8,128)(2,1)}, bf16[384,2048]{1,0:T(8,128)(2,1)}, u32[]{:S(2)}, u32[]{:S(2)}) collective-permute-start(bf16[384,2048]{1,0:T(8,128)(2,1)} %slice.444), channel_id=1, source_target_pairs={{0,4},{4,0},{1,5},{5,1},{2,6},{6,2},{3,7},{7,3},{8,12},{12,8},{9,1... | collective-permute-start | bytes 4718600 | tf_op jit(solution)/shard_map/ppermute | solution.py:78
  386.1 57.8 %collective-permute-start.47 = (bf16[512,1408]{0,1:T(8,128)(2,1)S(1)}, bf16[512,1408]{0,1:T(8,128)(2,1)S(1)}, u32[]{:S(2)}, u32[]{:S(2)}) collective-permute-start(bf16[512,1408]{0,1:T(8,128)(2,1)S(1)} %copy-done.33), channel_id=1, source_target_pairs={{0,16},{8,24},{16,0},{24,8},{1,17},{9,25},{17,1},{25,9},{2,18},{10... | collective-permute-start | bytes 4325384 | tf_op jit(solution)/shard_map/ppermute | solution.py:86
  390.0 58.2 %collective-permute-start.46 = (bf16[512,1408]{0,1:T(8,128)(2,1)S(1)}, bf16[512,1408]{0,1:T(8,128)(2,1)S(1)}, u32[]{:S(2)}, u32[]{:S(2)}) collective-permute-start(bf16[512,1408]{0,1:T(8,128)(2,1)S(1)} %copy-done.33), channel_id=1, source_target_pairs={{0,8},{8,0},{16,24},{24,16},{1,9},{9,1},{17,25},{25,17},{2,10},{10... | collective-permute-start | bytes 4325384 | tf_op jit(solution)/shard_map/ppermute | solution.py:82
  391.5 57.5 %collective-permute-start.68 = (bf16[384,2048]{1,0:T(8,128)(2,1)}, bf16[384,2048]{1,0:T(8,128)(2,1)S(1)}, u32[]{:S(2)}, u32[]{:S(2)}) collective-permute-start(bf16[384,2048]{1,0:T(8,128)(2,1)} %collective-permute-done.66), channel_id=1, source_target_pairs={{0,1},{1,2},{2,3},{3,0},{4,5},{5,6},{6,7},{7,4},{8,9},{9,10},{10,1... | collective-permute-start | bytes 4718600 | tf_op jit(solution)/shard_map/ppermute | solution.py:91
  463.9 61.8 %collective-permute-start.34 = (bf16[384,2048]{1,0:T(8,128)(2,1)S(1)}, bf16[384,2048]{1,0:T(8,128)(2,1)S(1)}, u32[]{:S(2)}, u32[]{:S(2)}) collective-permute-start(bf16[384,2048]{1,0:T(8,128)(2,1)S(1)} %get-tuple-element.93), channel_id=1, source_target_pairs={{0,4},{4,0},{1,5},{5,1},{2,6},{6,2},{3,7},{7,3},{8,12},{12,8},{9,1... | collective-permute-start | bytes 4718600 | tf_op jit(solution)/shard_map/ppermute | solution.py:78
  478.3 50.2 %collective-permute-start.36 = (bf16[384,2048]{1,0:T(8,128)(2,1)S(1)}, bf16[384,2048]{1,0:T(8,128)(2,1)S(1)}, u32[]{:S(2)}, u32[]{:S(2)}) collective-permute-start(bf16[384,2048]{1,0:T(8,128)(2,1)S(1)} %collective-permute-done.35), channel_id=1, source_target_pairs={{0,4},{4,0},{1,5},{5,1},{2,6},{6,2},{3,7},{7,3},{8,12},{12,8},{9,1... | collective-permute-start | bytes 4718600 | tf_op jit(solution)/shard_map/ppermute | solution.py:78
  707.7 58.5 %collective-permute-start.129 = (bf16[704,512]{1,0:T(8,128)(2,1)S(1)}, bf16[704,512]{1,0:T(8,128)(2,1)}, u32[]{:S(2)}, u32[]{:S(2)}) collective-permute-start(bf16[704,512]{1,0:T(8,128)(2,1)S(1)} %slice.532), channel_id=1, source_target_pairs={{0,8},{8,0},{16,24},{24,16},{1,9},{9,1},{17,25},{25,17},{2,10},{10... | collective-permute-start | bytes 2162696 | tf_op jit(solution)/shard_map/ppermute | solution.py:82
  708.4 75.2 %collective-permute-start.126 = (bf16[704,512]{1,0:T(8,128)(2,1)S(1)}, bf16[704,512]{1,0:T(8,128)(2,1)}, u32[]{:S(2)}, u32[]{:S(2)}) collective-permute-start(bf16[704,512]{1,0:T(8,128)(2,1)S(1)} %slice.526), channel_id=1, source_target_pairs={{0,16},{8,24},{16,0},{24,8},{1,17},{9,25},{17,1},{25,9},{2,18},{10... | collective-permute-start | bytes 2162696 | tf_op jit(solution)/shard_map/ppermute | solution.py:86
  711.1 50.9 %collective-permute-start.127 = (bf16[704,512]{1,0:T(8,128)(2,1)}, bf16[704,512]{1,0:T(8,128)(2,1)S(1)}, u32[]{:S(2)}, u32[]{:S(2)}) collective-permute-start(bf16[704,512]{1,0:T(8,128)(2,1)} %get-tuple-element.124), channel_id=1, source_target_pairs={{0,16},{8,24},{16,0},{24,8},{1,17},{9,25},{17,1},{25,9},{2,18},{10... | collective-permute-start | bytes 2162696 | tf_op jit(solution)/shard_map/ppermute | solution.py:86
  711.7 52.7 %collective-permute-start.130 = (bf16[704,512]{1,0:T(8,128)(2,1)}, bf16[704,512]{1,0:T(8,128)(2,1)S(1)}, u32[]{:S(2)}, u32[]{:S(2)}) collective-permute-start(bf16[704,512]{1,0:T(8,128)(2,1)} %get-tuple-element.125), channel_id=1, source_target_pairs={{0,8},{8,0},{16,24},{24,16},{1,9},{9,1},{17,25},{25,17},{2,10},{10... | collective-permute-start | bytes 2162696 | tf_op jit(solution)/shard_map/ppermute | solution.py:82
  713.1 91.1 %collective-permute-start.123 = (bf16[512,1408]{1,0:T(8,128)(2,1)}, bf16[512,1408]{1,0:T(8,128)(2,1)}, u32[]{:S(2)}, u32[]{:S(2)}) collective-permute-start(bf16[512,1408]{1,0:T(8,128)(2,1)} %convolution_convert_fusion.13), channel_id=1, source_target_pairs={{0,8},{8,0},{16,24},{24,16},{1,9},{9,1},{17,25},{25,17},{2,10},{10... | collective-permute-start | bytes 4325384 | tf_op jit(solution)/shard_map/ppermute | solution.py:82
  783.5 98.1 %collective-permute-start.122 = (bf16[512,1408]{1,0:T(8,128)(2,1)}, bf16[512,1408]{1,0:T(8,128)(2,1)}, u32[]{:S(2)}, u32[]{:S(2)}) collective-permute-start(bf16[512,1408]{1,0:T(8,128)(2,1)} %convolution_convert_fusion.15), channel_id=1, source_target_pairs={{0,8},{8,0},{16,24},{24,16},{1,9},{9,1},{17,25},{25,17},{2,10},{10... | collective-permute-start | bytes 4325384 | tf_op jit(solution)/shard_map/ppermute | solution.py:82
  814.9 66.9 %collective-permute-start.60 = (bf16[384,2048]{1,0:T(8,128)(2,1)S(1)}, bf16[384,2048]{1,0:T(8,128)(2,1)S(1)}, u32[]{:S(2)}, u32[]{:S(2)}) collective-permute-start(bf16[384,2048]{1,0:T(8,128)(2,1)S(1)} %copy-done.69), channel_id=1, source_target_pairs={{0,4},{4,0},{1,5},{5,1},{2,6},{6,2},{3,7},{7,3},{8,12},{12,8},{9,1... | collective-permute-start | bytes 4718600 | tf_op jit(solution)/shard_map/ppermute | solution.py:78
  821.6 60.7 %collective-permute-start.124 = (bf16[512,1408]{1,0:T(8,128)(2,1)}, bf16[512,1408]{1,0:T(8,128)(2,1)}, u32[]{:S(2)}, u32[]{:S(2)}) collective-permute-start(bf16[512,1408]{1,0:T(8,128)(2,1)} %fusion.37), channel_id=1, source_target_pairs={{0,16},{8,24},{16,0},{24,8},{1,17},{9,25},{17,1},{25,9},{2,18},{10... | collective-permute-start | bytes 4325384 | tf_op jit(solution)/shard_map/ppermute | solution.py:86
  854.6 98.8 %collective-permute-start.118 = (bf16[512,1408]{1,0:T(8,128)(2,1)S(1)}, bf16[512,1408]{1,0:T(8,128)(2,1)S(1)}, u32[]{:S(2)}, u32[]{:S(2)}) collective-permute-start(bf16[512,1408]{1,0:T(8,128)(2,1)S(1)} %copy-done.130), channel_id=1, source_target_pairs={{0,16},{8,24},{16,0},{24,8},{1,17},{9,25},{17,1},{25,9},{2,18},{10... | collective-permute-start | bytes 4325384 | tf_op jit(solution)/shard_map/ppermute | solution.py:86
  881.8 71.7 %collective-permute-start.120 = (bf16[512,1408]{1,0:T(8,128)(2,1)S(1)}, bf16[512,1408]{1,0:T(8,128)(2,1)}, u32[]{:S(2)}, u32[]{:S(2)}) collective-permute-start(bf16[512,1408]{1,0:T(8,128)(2,1)S(1)} %fusion.44), channel_id=1, source_target_pairs={{0,8},{8,0},{16,24},{24,16},{1,9},{9,1},{17,25},{25,17},{2,10},{10... | collective-permute-start | bytes 4325384 | tf_op jit(solution)/shard_map/ppermute | solution.py:82
  882.4 69.1 %collective-permute-start.73 = (bf16[384,2048]{1,0:T(8,128)(2,1)S(1)}, bf16[384,2048]{1,0:T(8,128)(2,1)S(1)}, u32[]{:S(2)}, u32[]{:S(2)}) collective-permute-start(bf16[384,2048]{1,0:T(8,128)(2,1)S(1)} %add_convert_fusion.9), channel_id=1, source_target_pairs={{0,1},{1,2},{2,3},{3,0},{4,5},{5,6},{6,7},{7,4},{8,9},{9,10},{10,1... | collective-permute-start | bytes 4718600 | tf_op jit(solution)/shard_map/ppermute | solution.py:91
  919.9 110.6 %collective-permute-start.62 = (bf16[384,2048]{1,0:T(8,128)(2,1)}, bf16[384,2048]{1,0:T(8,128)(2,1)}, u32[]{:S(2)}, u32[]{:S(2)}) collective-permute-start(bf16[384,2048]{1,0:T(8,128)(2,1)} %slice.459), channel_id=1, source_target_pairs={{0,4},{4,0},{1,5},{5,1},{2,6},{6,2},{3,7},{7,3},{8,12},{12,8},{9,1... | collective-permute-start | bytes 4718600 | tf_op jit(solution)/shard_map/ppermute | solution.py:78
  922.0 50.0 %collective-permute-start.76 = (bf16[384,2048]{1,0:T(8,128)(2,1)}, bf16[384,2048]{1,0:T(8,128)(2,1)S(1)}, u32[]{:S(2)}, u32[]{:S(2)}) collective-permute-start(bf16[384,2048]{1,0:T(8,128)(2,1)} %slice.475), channel_id=1, source_target_pairs={{0,4},{4,0},{1,5},{5,1},{2,6},{6,2},{3,7},{7,3},{8,12},{12,8},{9,1... | collective-permute-start | bytes 4718600 | tf_op jit(solution)/shard_map/ppermute | solution.py:78
  951.4 86.3 %collective-permute-start.132 = (bf16[1408,256]{1,0:T(8,128)(2,1)}, bf16[1408,256]{1,0:T(8,128)(2,1)}, u32[]{:S(2)}, u32[]{:S(2)}) collective-permute-start(bf16[1408,256]{1,0:T(8,128)(2,1)} %bitcast.243), channel_id=1, source_target_pairs={{0,4},{4,0},{1,5},{5,1},{2,6},{6,2},{3,7},{7,3},{8,12},{12,8},{9,1... | collective-permute-start | bytes 2162696 | tf_op jit(solution)/shard_map/ppermute | solution.py:78
  953.4 77.1 %collective-permute-start.61 = (bf16[384,2048]{1,0:T(8,128)(2,1)}, bf16[384,2048]{1,0:T(8,128)(2,1)}, u32[]{:S(2)}, u32[]{:S(2)}) collective-permute-start(bf16[384,2048]{1,0:T(8,128)(2,1)} %add_convert_fusion.14), channel_id=1, source_target_pairs={{0,1},{1,2},{2,3},{3,0},{4,5},{5,6},{6,7},{7,4},{8,9},{9,10},{10,1... | collective-permute-start | bytes 4718600 | tf_op jit(solution)/shard_map/ppermute | solution.py:91
  953.4 72.6 %collective-permute-start.75 = (bf16[384,2048]{1,0:T(8,128)(2,1)}, bf16[384,2048]{1,0:T(8,128)(2,1)}, u32[]{:S(2)}, u32[]{:S(2)}) collective-permute-start(bf16[384,2048]{1,0:T(8,128)(2,1)} %add_convert_fusion.7), channel_id=1, source_target_pairs={{0,1},{1,2},{2,3},{3,0},{4,5},{5,6},{6,7},{7,4},{8,9},{9,10},{10,1... | collective-permute-start | bytes 4718600 | tf_op jit(solution)/shard_map/ppermute | solution.py:91
  972.1 70.7 %collective-permute-start.125 = (bf16[256,1408]{0,1:T(8,128)(2,1)}, bf16[256,1408]{0,1:T(8,128)(2,1)}, u32[]{:S(2)}, u32[]{:S(2)}) collective-permute-start(bf16[256,1408]{0,1:T(8,128)(2,1)} %bitcast.320), channel_id=1, source_target_pairs={{0,4},{4,0},{1,5},{5,1},{2,6},{6,2},{3,7},{7,3},{8,12},{12,8},{9,1... | collective-permute-start | bytes 2162696 | tf_op jit(solution)/shard_map/ppermute | solution.py:78
  1125.5 53.8 %collective-permute-start.104 = (bf16[128,2048]{1,0:T(8,128)(2,1)}, bf16[128,2048]{1,0:T(8,128)(2,1)S(1)}, u32[]{:S(2)}, u32[]{:S(2)}) collective-permute-start(bf16[128,2048]{1,0:T(8,128)(2,1)} %convolution_convert_fusion.23), channel_id=1, source_target_pairs={{0,8},{8,0},{16,24},{24,16},{1,9},{9,1},{17,25},{25,17},{2,10},{10... | collective-permute-start | bytes 1572872 | tf_op jit(solution)/shard_map/ppermute | solution.py:82
  1130.7 62.8 %collective-permute-start.112 = (bf16[1024,512]{0,1:T(8,128)(2,1)}, bf16[1024,512]{0,1:T(8,128)(2,1)}, u32[]{:S(2)}, u32[]{:S(2)}) collective-permute-start(bf16[1024,512]{0,1:T(8,128)(2,1)} %convolution_convert_fusion.25), channel_id=1, source_target_pairs={{0,8},{8,0},{16,24},{24,16},{1,9},{9,1},{17,25},{25,17},{2,10},{10... | collective-permute-start | bytes 3145736 | tf_op jit(solution)/shard_map/ppermute | solution.py:82
  1134.4 74.0 %collective-permute-start.111 = (bf16[1024,512]{0,1:T(8,128)(2,1)}, bf16[1024,512]{0,1:T(8,128)(2,1)}, u32[]{:S(2)}, u32[]{:S(2)}) collective-permute-start(bf16[1024,512]{0,1:T(8,128)(2,1)} %convolution_convert_fusion.27), channel_id=1, source_target_pairs={{0,8},{8,0},{16,24},{24,16},{1,9},{9,1},{17,25},{25,17},{2,10},{10... | collective-permute-start | bytes 3145736 | tf_op jit(solution)/shard_map/ppermute | solution.py:82
  1139.7 177.7 %collective-permute-start.90 = (bf16[512,1536]{1,0:T(8,128)(2,1)}, bf16[512,1536]{1,0:T(8,128)(2,1)}, u32[]{:S(2)}, u32[]{:S(2)}) collective-permute-start(bf16[512,1536]{1,0:T(8,128)(2,1)} %convolution_convert_fusion.11), channel_id=1, source_target_pairs={{0,16},{8,24},{16,0},{24,8},{1,17},{9,25},{17,1},{25,9},{2,18},{10... | collective-permute-start | bytes 4718600 | tf_op jit(solution)/shard_map/ppermute | solution.py:86
  1207.1 55.6 %collective-permute-start.91 = (bf16[512,1536]{1,0:T(8,128)(2,1)}, bf16[512,1536]{1,0:T(8,128)(2,1)}, u32[]{:S(2)}, u32[]{:S(2)}) collective-permute-start(bf16[512,1536]{1,0:T(8,128)(2,1)} %convolution_convert_fusion.9), channel_id=1, source_target_pairs={{0,16},{8,24},{16,0},{24,8},{1,17},{9,25},{17,1},{25,9},{2,18},{10... | collective-permute-start | bytes 4718600 | tf_op jit(solution)/shard_map/ppermute | solution.py:86
  1207.7 79.9 %collective-permute-start.82 = (bf16[384,2048]{1,0:T(8,128)(2,1)}, bf16[384,2048]{1,0:T(8,128)(2,1)}, u32[]{:S(2)}, u32[]{:S(2)}) collective-permute-start(bf16[384,2048]{1,0:T(8,128)(2,1)} %slice.480), channel_id=1, source_target_pairs={{0,4},{4,0},{1,5},{5,1},{2,6},{6,2},{3,7},{7,3},{8,12},{12,8},{9,1... | collective-permute-start | bytes 4718600 | tf_op jit(solution)/shard_map/ppermute | solution.py:78
  1265.7 51.7 %collective-permute-start.92 = (bf16[512,1536]{1,0:T(8,128)(2,1)}, bf16[512,1536]{1,0:T(8,128)(2,1)}, u32[]{:S(2)}, u32[]{:S(2)}) collective-permute-start(bf16[512,1536]{1,0:T(8,128)(2,1)} %add_convert_fusion.5), channel_id=1, source_target_pairs={{0,8},{8,0},{16,24},{24,16},{1,9},{9,1},{17,25},{25,17},{2,10},{10... | collective-permute-start | bytes 4718600 | tf_op jit(solution)/shard_map/ppermute | solution.py:82
  (250 other events, 4786.9 us)

commit v2 on v1

--- a/solution.py
+++ b/solution.py
@@ -74,6 +74,19 @@
     return lax.optimization_barrier((value, *others))[0]
 
 
+class Line:
+    def __init__(self):
+        self.last = None
+
+    def send(self, move, value, *needs, free=False):
+        if self.last is not None and not free:
+            needs = (*needs, self.last)
+        if needs:
+            value = after(value, *needs)
+        self.last = move(value)
+        return self.last
+
+
 def swap_core(value):
     return lax.ppermute(value, "ctx", [(0, 1), (1, 0)])
 
@@ -91,43 +104,36 @@
     return lax.ppermute(value, "tp", [(i, (i + 1) % size) for i in range(size)])
 
 
-def gather_z(value):
-    pieces = [value]
-    for _ in range(lax.axis_size("tp") - 1):
-        pieces.append(step_z(pieces[-1]))
-    return pieces
-
-
-def gather_xfirst(value):
-    one = swap_x(value)
-    return [value, one, swap_y(value), swap_y(one)]
-
-
-def gather_yfirst(value):
-    two = swap_y(value)
-    return [value, swap_x(value), two, swap_x(two)]
-
-
-def scatter_yfirst(blocks, last=bf16):
-    three, two = swap_y(blocks[3]), swap_y(blocks[2])
-    other = swap_x(add16(blocks[1], three))
+def gather_xy(line_x, line_y, x_first, y_first):
+    ax = line_x.send(swap_x, x_first)
+    by = line_y.send(swap_y, y_first)
+    ay = line_y.send(swap_y, x_first)
+    bx = line_x.send(swap_x, y_first)
+    axy = line_y.send(swap_y, ax)
+    byx = line_x.send(swap_x, by)
+    return [x_first, ax, ay, axy], [y_first, bx, by, byx]
+
+
+def scatter_yfirst(line_x, line_y, blocks, last=bf16):
+    three, two = line_y.send(swap_y, blocks[3]), line_y.send(swap_y, blocks[2])
+    other = line_x.send(swap_x, add16(blocks[1], three))
     total = blocks[0].astype(f32) + two.astype(f32) + other.astype(f32)
     return total.astype(last)
 
 
-def scatter_xfirst(blocks, last=bf16):
-    three, one = swap_x(blocks[3]), swap_x(blocks[1])
-    other = swap_y(add16(blocks[2], three))
+def scatter_xfirst(line_x, line_y, blocks, last=bf16):
+    three, one = line_x.send(swap_x, blocks[3]), line_x.send(swap_x, blocks[1])
+    other = line_y.send(swap_y, add16(blocks[2], three))
     total = blocks[0].astype(f32) + one.astype(f32) + other.astype(f32)
     return total.astype(last)
 
 
-def scatter_z(block_of, last=bf16, add=add16):
+def scatter_z(line_z, block_of, last=bf16, add=add16):
     size = lax.axis_size("tp")
     total = block_of(1)
     for j in range(2, size):
-        total = add(step_z(total), block_of(j))
-    return (step_z(total).astype(f32) + block_of(0).astype(f32)).astype(last)
+        total = add(line_z.send(step_z, total), block_of(j))
+    return (line_z.send(step_z, total).astype(f32) + block_of(0).astype(f32)).astype(last)
 
 
 def in_order(core, mine, other, axis):
@@ -136,6 +142,77 @@
         jnp.concatenate([mine, other], axis=axis),
         jnp.concatenate([other, mine], axis=axis),
     )
+
+
+def assemble(sources, moves, shapes, place):
+    depth = min(32, len(moves))
+
+    def kernel(place_ref, *refs):
+        given, made, sems = refs[: len(sources)], refs[len(sources) : -1], refs[-1]
+        flight = []
+        for i, (src, row, rows, column, columns, dst, to_row, to_column) in enumerate(moves):
+            if i >= depth:
+                flight[i - depth].wait()
+            if not isinstance(to_row, int):
+                to_row = pl.multiple_of(to_row[1](place_ref), to_row[0])
+            copy = pltpu.make_async_copy(
+                given[src].at[pl.ds(row, rows), pl.ds(column, columns)],
+                made[dst].at[pl.ds(to_row, rows), pl.ds(to_column, columns)],
+                sems.at[i % depth],
+            )
+            copy.start()
+            flight.append(copy)
+        for copy in flight[-depth:]:
+            copy.wait()
+
+    return pl.pallas_call(
+        kernel,
+        out_shape=[jax.ShapeDtypeStruct(shape, bf16) for shape in shapes],
+        grid_spec=pltpu.PrefetchScalarGridSpec(
+            num_scalar_prefetch=1,
+            in_specs=[pl.BlockSpec(memory_space=pl.ANY)] * len(sources),
+            out_specs=[pl.BlockSpec(memory_space=pltpu.VMEM)] * len(shapes),
+            scratch_shapes=[pltpu.SemaphoreType.DMA((depth,))],
+        ),
+        compiler_params=pltpu.CompilerParams(vmem_limit_bytes=48 << 20),
+        cost_estimate=pl.CostEstimate(
+            flops=0,
+            transcendentals=0,
+            bytes_accessed=4 * sum(a * b for a, b in shapes),
+        ),
+        name="assemble",
+    )(place, *sources)
+
+
+def lay_out_kernel(places, *refs):
+    pieces, (latent, rope) = refs[:-2], refs[-2:]
+    rows = pieces[0].shape[1]
+    for i, piece in enumerate(pieces):
+        at = pl.ds(pl.multiple_of(places[i], rows), rows)
+        latent[:, at, :] = piece[:, :, :KVRANK]
+        keys = piece[:, :, KVRANK:]
+        rope[:, at, :] = jnp.concatenate([keys, keys], axis=-1)
+
+
+def lay_out(places, pieces, length):
+    micro = pieces[0].shape[0]
+    in_vmem = pl.BlockSpec(memory_space=pltpu.VMEM)
+    return pl.pallas_call(
+        lay_out_kernel,
+        out_shape=[
+            jax.ShapeDtypeStruct((micro, length, KVRANK), bf16),
+            jax.ShapeDtypeStruct((micro, length, 2 * ROPE), bf16),
+        ],
+        grid_spec=pltpu.PrefetchScalarGridSpec(
+            num_scalar_prefetch=1,
+            in_specs=[in_vmem] * len(pieces),
+            out_specs=[in_vmem] * 2,
+        ),
+        cost_estimate=pl.CostEstimate(
+            flops=0, transcendentals=0, bytes_accessed=4 * micro * length * (KVRANK + 2 * ROPE)
+        ),
+        name="lay_out",
+    )(places, *pieces)
 
 
 def swap_halves(values, lane):
@@ -340,6 +417,246 @@
     )(place, q_lin, kv, rope_keys, seg_query, seg_key, cos, sin, d_o)
 
 
+def spans(total, step):
+    return [(at, min(step, total - at)) for at in range(0, total, step)]
+
+
+def feed_kernel(part, rows, offset, place, *refs):
+    given, refs = refs[:20], refs[20:]
+    refs = refs[4:] if offset else refs
+    back_own, back_other, out_own, out_other, act_all, hid_all, norm_all, grad_all = refs[:8]
+    w_hid, w_down, norm, grad, d_act, act, hid, sems = refs[8:]
+    norm_own, norm_other, grad_own, grad_other = given[:4]
+    slice_rows = given[4].shape[0]
+
+    def at_core(i):
+        core = place[0] if i < 4 else 1 - place[0]
+        return pl.ds(pl.multiple_of((2 * (i % 4) + core) * slice_rows, slice_rows), slice_rows)
+
+    early = [
+        pltpu.make_async_copy(grad_own, grad.at[pl.ds(0, rows)], sems.at[0]),
+        pltpu.make_async_copy(grad_other, grad.at[pl.ds(rows, rows)], sems.at[1]),
+    ] + [
+        pltpu.make_async_copy(given[12 + i], w_down.at[at_core(i)], sems.at[2 + i])
+        for i in range(8)
+    ]
+    later = [
+        pltpu.make_async_copy(norm_own, norm.at[pl.ds(0, rows)], sems.at[10]),
+        pltpu.make_async_copy(norm_other, norm.at[pl.ds(rows, rows)], sems.at[11]),
+    ] + [
+        pltpu.make_async_copy(given[4 + i], w_hid.at[at_core(i)], sems.at[12 + i])
+        for i in range(8)
+    ]
+    for copy in early + later:
+        copy.start()
+    for copy in early:
+        copy.wait()
+
+    def for_chunks(total, body):
+        whole = total // 256
+
+        def step(i, carry):
+            body(pl.multiple_of(i * 256, 256), 256)
+            return carry
+
+        lax.fori_loop(0, whole, step, 0)
+        if total % 256:
+            body(whole * 256, total % 256)
+
+    def act_back(start, size):
+        d_act[:, pl.ds(start, size)] = dot(grad[...], w_down[:, pl.ds(start, size)])
+
+    for_chunks(part, act_back)
+    for copy in later:
+        copy.wait()
+
+    def forward(start, size):
+        gate = dot(norm[...], w_hid[:, pl.ds(start, size)])
+        up_at = start + part
+        if not isinstance(start, int):
+            up_at = pl.multiple_of(up_at, LANES)
+        up = dot(norm[...], w_hid[:, pl.ds(up_at, size)])
+        back = d_act[:, pl.ds(start, size)]
+        sigma = jax.nn.sigmoid(gate)
+        swish = gate * sigma
+        act[:, pl.ds(start, size)] = (swish * up).astype(bf16)
+        hid[:, pl.ds(start, size)] = (
+            back * up * sigma * (1.0 + gate * (1.0 - sigma))
+        ).astype(bf16)
+        hid[:, pl.ds(up_at, size)] = (back * swish).astype(bf16)
+
+    for_chunks(part, forward)
+    here = pl.ds(offset * 2 * rows, 2 * rows)
+    saves = [
+        pltpu.make_async_copy(source, target.at[here], sems.at[20 + i])
+        for i, (source, target) in enumerate(
+            ((act, act_all), (hid, hid_all), (norm, norm_all), (grad, grad_all))
+        )
+    ]
+    for copy in saves:
+        copy.start()
+
+    def backward(start, size):
+        back = dot_rt(hid[...], w_hid[pl.ds(start, size), :], bf16)
+        back_own[:, pl.ds(start, size)] = back[:rows]
+        back_other[:, pl.ds(start, size)] = back[rows:]
+        out = dot_rt(act[...], w_down[pl.ds(start, size), :], bf16)
+        out_own[:, pl.ds(start, size)] = out[:rows]
+        out_other[:, pl.ds(start, size)] = out[rows:]
+
+    for_chunks(w_hid.shape[0], backward)
+    for copy in saves:
+        copy.wait()
+
+
+def feed(place, offset, blocks, tokens, hidden_pieces, down_pieces, whole):
+    rows, width = tokens[0].shape
+    part = down_pieces[0].shape[1]
+    anywhere = pl.BlockSpec(memory_space=pl.ANY)
+    in_vmem = pl.BlockSpec(memory_space=pltpu.VMEM)
+    total = 2 * rows * blocks
+    operands = [*tokens, *hidden_pieces, *down_pieces, *whole]
+    return pl.pallas_call(
+        functools.partial(feed_kernel, part, rows, offset),
+        out_shape=[jax.ShapeDtypeStruct((rows, width), bf16)] * 4
+        + [
+            jax.ShapeDtypeStruct((total, columns), bf16)
+            for columns in (part, 2 * part, width, width)
+        ],
+        grid_spec=pltpu.PrefetchScalarGridSpec(
+            num_scalar_prefetch=1,
+            in_specs=[anywhere] * len(operands),
+            out_specs=[in_vmem] * 4 + [anywhere] * 4,
+            scratch_shapes=[
+                pltpu.VMEM((width, 2 * part), bf16),
+                pltpu.VMEM((width, part), bf16),
+                pltpu.VMEM((2 * rows, width), bf16),
+                pltpu.VMEM((2 * rows, width), bf16),
+                pltpu.VMEM((2 * rows, part), f32),
+                pltpu.VMEM((2 * rows, part), bf16),
+                pltpu.VMEM((2 * rows, 2 * part), bf16),
+                pltpu.SemaphoreType.DMA((24,)),
+            ],
+        ),
+        input_output_aliases={21 + i: 4 + i for i in range(len(whole))},
+        compiler_params=pltpu.CompilerParams(vmem_limit_bytes=58 << 20),
+        cost_estimate=pl.CostEstimate(
+            flops=2 * 2 * rows * width * part * 6,
+            transcendentals=2 * rows * part,
+            bytes_accessed=2 * (3 * width * part + 2 * rows * (6 * width + 3 * part)),
+        ),
+        name="feed",
+    )(place, *operands)
+
+
+def pack_kernel(part, place, gate, up, down, hid_mine, hid_other, down_mine, down_other):
+    slice_rows, hidden_here = gate.shape
+    rest = hidden_here - part
+
+    def put(at, low, high, value):
+        low[:, at : at + part] = value[:, :part]
+        if rest < part:
+            edge = rest // LANES * LANES
+            high[:, at + edge : at + part] = jnp.zeros((slice_rows, part - edge), bf16)
+        high[:, at : at + rest] = value[:, part:]
+
+    def write(hid_low, hid_high, down_low, down_high):
+        put(0, hid_low, hid_high, gate[...])
+        put(part, hid_low, hid_high, up[...])
+        put(0, down_low, down_high, down[...].T)
+
+    @pl.when(place[0] == 0)
+    def _():
+        write(hid_mine, hid_other, down_mine, down_other)
+
+    @pl.when(place[0] != 0)
+    def _():
+        write(hid_other, hid_mine, down_other, down_mine)
+
+
+def pack(place, part, gate, up, down):
+    slice_rows = gate.shape[0]
+    in_vmem = pl.BlockSpec(memory_space=pltpu.VMEM)
+    return pl.pallas_call(
+        functools.partial(pack_kernel, part),
+        out_shape=[jax.ShapeDtypeStruct((slice_rows, n * part), bf16) for n in (2, 2, 1, 1)],
+        grid_spec=pltpu.PrefetchScalarGridSpec(
+            num_scalar_prefetch=1, in_specs=[in_vmem] * 3, out_specs=[in_vmem] * 4
+        ),
+        compiler_params=pltpu.CompilerParams(vmem_limit_bytes=48 << 20),
+        cost_estimate=pl.CostEstimate(
+            flops=0, transcendentals=0, bytes_accessed=24 * slice_rows * part
+        ),
+        name="pack",
+    )(place, gate, up, down)
+
+
+def weight_grad_kernel(blocks, place, left, right_ref, *refs):
+    outs, (turned, buffer, sems) = refs[:-3], refs[-3:]
+    slice_rows, tokens = outs[0].shape[0], turned.shape[1]
+
+    def fetch(i):
+        half, k = blocks[i]
+        core = place[0] if half == 0 else 1 - place[0]
+        start = pl.multiple_of((2 * k + core) * slice_rows, slice_rows)
+        return pltpu.make_async_copy(
+            left.at[:, pl.ds(start, slice_rows)], buffer.at[i % 2], sems.at[i % 2]
+        )
+
+    @pl.when(pl.program_id(0) == 0)
+    def _():
+        fetch(0).start()
+        for i in range(len(outs)):
+            fetch(i).wait()
+            if i + 1 < len(outs):
+                fetch(i + 1).start()
+
+            def turn(j, carry, i=i):
+                at = pl.ds(pl.multiple_of(j * 256, 256), 256)
+                turned[pl.ds(i * slice_rows, slice_rows), at] = buffer[i % 2, at, :].T
+                return carry
+
+            lax.fori_loop(0, tokens // 256, turn, 0)
+
+    for half in range(0, len(outs), 4):
+        rows = pl.ds(half * slice_rows, 4 * slice_rows)
+        grads = dot(turned[rows, :], right_ref[...], bf16)
+        for i in range(4):
+            outs[half + i][...] = grads[i * slice_rows : (i + 1) * slice_rows]
+
+
+def weight_grad(place, blocks, slice_rows, left, right):
+    tokens, columns = right.shape
+    count = len(blocks)
+    return pl.pallas_call(
+        functools.partial(weight_grad_kernel, blocks),
+        out_shape=[jax.ShapeDtypeStruct((slice_rows, columns), bf16)] * count,
+        grid_spec=pltpu.PrefetchScalarGridSpec(
+            num_scalar_prefetch=1,
+            grid=(-(-columns // 256),),
+            in_specs=[
+                pl.BlockSpec(memory_space=pl.ANY),
+                pl.BlockSpec((tokens, 256), lambda n, place: (0, n)),
+            ],
+            out_specs=[pl.BlockSpec((slice_rows, 256), lambda n, place: (0, n))] * count,
+            scratch_shapes=[
+                pltpu.VMEM((count * slice_rows, tokens), bf16),
+                pltpu.VMEM((2, tokens, slice_rows), bf16),
+                pltpu.SemaphoreType.DMA((2,)),
+            ],
+        ),
+        compiler_params=pltpu.CompilerParams(
+            dimension_semantics=("arbitrary",), vmem_limit_bytes=48 << 20
+        ),
+        cost_estimate=pl.CostEstimate(
+            flops=2 * tokens * columns * count * slice_rows,
+            transcendentals=0,
+            bytes_accessed=2 * (tokens * columns + count * slice_rows * (tokens + columns)),
+        ),
+        name="weight_grad",
+    )(place, left, right)
+
+
 def shards(
     hidden,
     segments,
@@ -374,6 +691,8 @@
     part = -(-hidden_here // (cores * LANES)) * LANES
     window = min(length, -(-(DOC_MOST + rows) // LANES) * LANES)
 
+    line_x, line_y, line_z, line_c = Line(), Line(), Line(), Line()
+
     def features(values):
         size = values.shape[-1] // 4
         return jnp.concatenate(
@@ -384,15 +703,17 @@
             axis=-1,
         )
 
+    def columns(values, k):
+        return values[:, block * k : block * (k + 1)]
+
     def mine(values, axis):
         return lax.dynamic_index_in_dim(values, core, axis, keepdims=False)
 
     def others(values, axis):
         return lax.dynamic_index_in_dim(values, 1 - core, axis, keepdims=False)
 
-    def halves(values, axis, pick, joined):
-        del axis
-        return in_order(core, mine(values, pick), swap_core(others(values, pick)), joined)
+    def to_core(value):
+        return line_c.send(swap_core, value)
 
     small_rows = latent_weight.shape[0]
     gain_rows, latent_gains = attn_gain.shape[0], latent_gain.shape[0]
@@ -400,27 +721,21 @@
     gains_row = jnp.concatenate([attn_gain, mlp_gain, latent_gain])
     gains_row = jnp.pad(gains_row, (0, kv_cols - gains_row.shape[0]))
     small = jnp.concatenate([latent_weight, jnp.pad(gains_row[None], ((0, 15), (0, 0)))])
-    line = jnp.zeros((tp_size, small_rows + 16, kv_cols), bf16)
-    for j, piece in enumerate(gather_z(small)):
-        line = lax.dynamic_update_index_in_dim(line, piece, (place_z - j) % tp_size, 0)
-    plane = jnp.stack(gather_xfirst(line))
-    small_all = in_order(core, plane[:, None], swap_core(plane)[:, None], 1)
-    w_latent = small_all[:, :, :, :small_rows].reshape(width, kv_cols)
-    gain_all = small_all[:, :, :, small_rows].astype(f32)
-    gain_one = gain_all[..., :gain_rows].reshape(width)
-    gain_two = gain_all[..., gain_rows : 2 * gain_rows].reshape(width)
-    gain_kv = features(
-        gain_all[..., 2 * gain_rows : 2 * gain_rows + latent_gains].reshape(KVRANK)
-    )
-
-    down_pad = jnp.pad(down_weight, ((0, cores * part - hidden_here), (0, 0)))
-    down_piece = halves(down_pad.reshape(cores, part, slice_rows), 0, 0, 1)
-    half_part = part // 2 // 16 * 16
-    down_top = gather_xfirst(down_piece[:half_part])
-    down_low = gather_yfirst(down_piece[half_part:])
-    w_down = jnp.concatenate(
-        [jnp.concatenate(down_top, axis=1), jnp.concatenate(down_low, axis=1)], axis=0
-    )
+    small_all = lax.all_gather(small, ("shard", "ctx", "tp"), axis=0)
+    devices = 4 * cores * tp_size
+
+    def own_first(values):
+        size = values.shape[0] // 4
+        return jnp.concatenate(
+            [lax.dynamic_slice_in_dim(values, (shard ^ k) * size, size, 0) for k in range(4)]
+        )
+
+    w_latent = own_first(small_all[:, :small_rows].reshape(width, kv_cols))
+    gain_all = small_all[:, small_rows].astype(f32)
+    gain_one = own_first(gain_all[:, :gain_rows].reshape(width))
+    gain_two = own_first(gain_all[:, gain_rows : 2 * gain_rows].reshape(width))
+    gain_kv = gain_all[:, 2 * gain_rows : 2 * gain_rows + latent_gains].reshape(KVRANK)
+    del devices
 
     def q_order(values):
         groups = values.shape[1] // (heads * (NOPE + ROPE))
@@ -436,47 +751,89 @@
         rope = values[..., heads * NOPE : heads * (NOPE + ROPE)].reshape(*lead, heads, ROPE)
         return jnp.concatenate([plain, rope], axis=-1).reshape(lead[0], -1)
 
-    q_local = q_order(q_weight)
     expand_rows = expand_weight.shape[0]
     kv_width = heads * (NOPE + VHEAD)
-    expand_local = expand_weight.reshape(expand_rows, -1, kv_width)
-    out_local = out_weight.reshape(-1, heads * VHEAD, slice_rows)
-    if split:
-        q_piece = halves(q_local, 0, 1, 0)
-        expand_piece = halves(expand_local, 0, 1, 0)
-        out_piece = halves(out_local, 1, 0, 1)
-    else:
-        q_piece = in_order(core, q_local[:, 0], swap_core(q_local[:, 0]), 0)
-        expand_piece = in_order(core, expand_local[:, 0], swap_core(expand_local[:, 0]), 0)
-        out_piece = in_order(core, out_local[0], swap_core(out_local[0]), 1)
-    q_line = jnp.concatenate(gather_z(q_piece), axis=1)
-    expand_line = jnp.concatenate(gather_z(expand_piece), axis=1)
-    out_line = jnp.concatenate(gather_z(out_piece), axis=0)
-    q_blocks = gather_xfirst(q_line)
-    expand_blocks = gather_yfirst(expand_line)
-    out_blocks = gather_yfirst(out_line)
-    w_query = jnp.concatenate(q_blocks, axis=0)
-    w_expand = jnp.concatenate(expand_blocks, axis=0)
-    w_expand = jnp.concatenate(
+    out_width = heads * VHEAD
+    stack = slice_rows // expand_rows
+    blocks_kv = kv_width // LANES
+    expand_cols = -(-blocks_kv // stack)
+    groups = cores if split else 1
+
+    def expand_stack(values):
+        tiles = [values[:, LANES * i : LANES * (i + 1)] for i in range(blocks_kv)]
+        tiles += [jnp.zeros_like(tiles[0])] * (expand_cols * stack - blocks_kv)
+        return jnp.concatenate(
+            [jnp.concatenate(tiles[stack * i : stack * (i + 1)]) for i in range(expand_cols)],
+            axis=1,
+        )
+
+    q_local = q_order(q_weight)
+    out_local = out_weight.T
+    packs = jnp.stack(
         [
-            lax.dynamic_slice_in_dim(w_expand, (shard ^ k) * (KVRANK // 4), KVRANK // 4, 0)
-            for k in range(4)
-        ],
-        axis=0,
-    )
-    w_out = jnp.concatenate(out_blocks, axis=1)
-
-    def hidden_piece(weight):
-        padded = jnp.pad(weight, ((0, 0), (0, cores * part - hidden_here)))
-        return halves(padded.reshape(slice_rows, cores, part), 0, 1, 0)
-
-    gate_piece, up_piece = lax.optimization_barrier(
-        (hidden_piece(gate_weight), hidden_piece(up_weight), q_blocks[3], out_blocks[3])
-    )[:2]
-    w_gate = jnp.concatenate(gather_xfirst(gate_piece), axis=0)
-    w_up = jnp.concatenate(gather_yfirst(up_piece), axis=0)
-
-    seg_all = segments[:, 0]
+            jnp.concatenate(
+                [
+                    q_local[:, g],
+                    out_local[:, out_width * g : out_width * (g + 1)],
+                    expand_stack(expand_weight[:, kv_width * g : kv_width * (g + 1)]),
+                ],
+                axis=1,
+            )
+            for g in range(groups)
+        ]
+    )
+    pack_mine, pack_other = (mine(packs, 0), others(packs, 0)) if split else (packs[0], packs[0])
+    attn_piece = jnp.concatenate([pack_mine, to_core(pack_other)])
+
+    shift = jnp.stack([core, shard]).astype(jnp.int32)
+
+    tokens = ()
+
+    def now(value):
+        return after(value, *tokens) if tokens else value
+
+    def send(line, move, value, free=False):
+        return line.send(move, now(value), free=free)
+
+    def close(*arrived):
+        nonlocal tokens
+        tokens = arrived
+
+    attn_z, held = [attn_piece], {}
+    wanted = []
+    for j in range(tp_size):
+        lead, tail = (1, 2) if j % 2 == 0 else (2, 1)
+        wanted.append((j, lead, 0, lead == 1, True))
+        wanted.append((j, tail, 0, tail == 1, False))
+        wanted.append((j, 3, lead, lead == 2, False))
+
+    def attention_round():
+        for j, piece in enumerate(attn_z):
+            held.setdefault((j, 0), piece)
+        keys, arrived = [], []
+        for over_x in (True, False):
+            ready = [w for w in wanted if w[3] == over_x and (w[0], w[2]) in held]
+            ready.sort(key=lambda w: not w[4])
+            if ready:
+                j, k, source = ready[0][:3]
+                wanted.remove(ready[0])
+                line, move = (line_x, swap_x) if over_x else (line_y, swap_y)
+                arrived.append(send(line, move, held[j, source]))
+                keys.append((j, k))
+        held.update(zip(keys, arrived))
+        if len(attn_z) < tp_size:
+            attn_z.append(send(line_z, step_z, attn_z[-1]))
+            arrived.append(attn_z[-1])
+        return arrived
+
+    close(*attention_round())
+    hid_a, hid_other, down_a, down_other = pack(
+        now(shift), part, gate_weight, up_weight, down_weight
+    )
+    grad_own = features(now(cotangent).reshape(own, width))
+    inputs16 = features(now(hidden).reshape(own, width))
+    inputs = inputs16.astype(f32)
+    seg_all = now(segments)[:, 0]
     bases = [core * span + place_z * rows, (1 - core) * span + place_z * rows][:slots]
     starts = [jnp.maximum(base + rows - window, 0) for base in bases]
     place = jnp.stack([jnp.stack([a, b]) for a, b in zip(starts, bases)]).astype(jnp.int32)
@@ -502,215 +859,415 @@
     attention = (heads, tp_size, window, scale, place)
     tables = (seg_query[..., None], seg_key, cos_lanes, sin_lanes)
 
-    inputs = features(hidden.reshape(own, width)).astype(f32)
-    factor_one = norm_scale(inputs)
+    close(*attention_round(), hid_a, grad_own, inputs16)
+    for _ in range(tp_size - 3):
+        close(*attention_round())
+    half_own = own // 2
+    grad_half = send(line_z, step_z, grad_own[:half_own])
+    hid_b = send(line_c, swap_core, hid_other)
+    factor_one = norm_scale(now(inputs))
     normed_own = (inputs * factor_one * gain_one).astype(bf16)
-    normed_chip = normed_own
-    if split:
-        normed_chip = jnp.concatenate([normed_own, swap_core(normed_own)])
     latent_raw = dot(normed_own, w_latent)
     latent_part = latent_raw[:, :KVRANK]
     factor_latent = norm_scale(latent_part)
     latent_own = (latent_part * factor_latent * gain_kv).astype(bf16)
     rope_own = rotate(latent_raw[:, KVRANK:], cos_own, sin_own).astype(bf16)
     latent_pack = jnp.concatenate([latent_own, rope_own], axis=1).reshape(micro, rows, kv_cols)
-    latent_half = jnp.zeros((micro, span, kv_cols), bf16)
-    for j, piece in enumerate(gather_z(latent_pack)):
-        latent_half = lax.dynamic_update_slice_in_dim(
-            latent_half, piece, (place_z - j) % tp_size * rows, 1
-        )
-    latent_full = in_order(core, latent_half, swap_core(latent_half), 1)
-    latent_all = latent_full[..., :KVRANK].reshape(micro * length, KVRANK)
-    rope_keys = jnp.concatenate([latent_full[..., KVRANK:]] * 2, axis=-1)
-
+    close(*attention_round(), latent_pack, grad_half, hid_b)
+    normed_chip = normed_own
+    if split:
+        normed_chip = jnp.concatenate([normed_own, send(line_c, swap_core, normed_own)])
+    down_b = send(line_c, swap_core, down_other)
+    grad_half = jnp.concatenate([grad_half, send(line_z, step_z, grad_own[half_own:])])
+    grad_z = [grad_own, grad_half]
+    while len(wanted) > 2:
+        close(*attention_round(), normed_chip, grad_half, down_b)
+    latent_z, latent_far = [latent_pack], [send(line_c, swap_core, latent_pack)]
+
+    def latents_ahead(count):
+        for _ in range(count):
+            latent_z.append(send(line_z, step_z, latent_z[-1]))
+            latent_far.append(to_core(latent_z[-1]))
+
+    latents_ahead(2)
+    close(*attention_round(), latent_z[-1], latent_far[0])
+    attn_xy = [[held[j, k] for k in range(4)] for j in range(tp_size)]
+
+    hid_a1, hid_b2 = send(line_x, swap_x, hid_a), send(line_y, swap_y, hid_b)
+    latents_ahead(tp_size - 3)
+    q_cols, out_cols = q_width, q_width + out_width
+
+    def core_row(k, half):
+        def row(ref):
+            at = ref[0] if half == 0 else 1 - ref[0]
+            return (2 * k + at) * slice_rows
+
+        return (slice_rows, row)
+
+    def expand_row(k, half):
+        def row(ref):
+            at = ref[0] if half == 0 else 1 - ref[0]
+            return (2 * (ref[1] ^ k) + at) * expand_rows
+
+        return (expand_rows, row)
+
+    moves = []
+    for j in range(tp_size):
+        for k in range(4):
+            for half in range(2):
+                source, top = 4 * j + k, half * slice_rows
+                moves.append(
+                    (source, top, slice_rows, 0, q_width, 0, core_row(k, half), j * q_width)
+                )
+                moves.append(
+                    (source, top, slice_rows, q_cols, out_width, 1, core_row(k, half), j * out_width)
+                )
+                for i in range(blocks_kv):
+                    moves.append(
+                        (
+                            source,
+                            top + i % stack * expand_rows,
+                            expand_rows,
+                            out_cols + i // stack * LANES,
+                            LANES,
+                            2,
+                            expand_row(k, half),
+                            j * kv_width + i * LANES,
+                        )
+                    )
+    w_query, w_out, w_expand = assemble(
+        [piece for pieces in attn_xy for piece in pieces],
+        moves,
+        [(width, tp_size * q_width), (width, tp_size * out_width), (KVRANK, tp_size * kv_width)],
+        now(shift),
+    )
     q_lin = dot(normed_chip, w_query).reshape(slots, micro, rows, tp_size * q_width)
+    close(hid_a1, hid_b2, latent_z[-1], q_lin)
+
+    hid_b1, hid_a2 = send(line_x, swap_x, hid_b), send(line_y, swap_y, hid_a)
+    more = (tp_size - 2) // 2
+
+    def grads_ahead(count):
+        for _ in range(count):
+            grad_z.append(send(line_z, step_z, grad_z[-1]))
+
+    latent_rows = [
+        [(at * span + (place_z - j) % tp_size * rows) for j in range(tp_size)]
+        for at in (core, 1 - core)
+    ]
+    latent_all, rope_keys = lay_out(
+        jnp.stack([row for each in latent_rows for row in each]).astype(jnp.int32),
+        [now(piece) for piece in latent_z + latent_far],
+        length,
+    )
+    latent_all = latent_all.reshape(micro * length, KVRANK)
+    grads_ahead(more)
     kv_all = dot(latent_all, w_expand, bf16).reshape(micro, length, tp_size * kv_width)
     mixed = attend(*attention, q_lin, kv_all, rope_keys, *tables)
-    mixed = mixed.reshape(slots * own, tp_size * heads * VHEAD)
+    mixed = mixed.reshape(slots * own, tp_size * out_width)
+    grad_far = [to_core(grad_z[0])]
+    close(hid_b1, hid_a2, grad_z[-1], grad_far[-1], mixed)
+
+    hid_b3, hid_a3 = send(line_x, swap_x, hid_b2), send(line_y, swap_y, hid_a1)
+    grads_ahead(tp_size - 2 - more)
+    mixed = now(mixed)
     if split:
-        mixed_out = dot(mixed, w_out, bf16)
-        middle = inputs + mixed_out[:own].astype(f32) + swap_core(mixed_out[own:]).astype(f32)
+        mixed_out = dot_rt(mixed, w_out, bf16)
+        middle = inputs + mixed_out[:own].astype(f32) + to_core(mixed_out[own:]).astype(f32)
     else:
-        middle = inputs + dot(mixed, w_out)
+        middle = inputs + dot_rt(mixed, w_out)
     factor_two = norm_scale(middle)
     normed_two = (middle * factor_two * gain_two).astype(bf16)
-
-    def to_group(values):
-        pieces = []
-        for piece in gather_z(values):
-            pieces += [piece, swap_core(piece)]
-        return jnp.concatenate(pieces)
-
-    grad_own = features(cotangent.reshape(own, width))
-    grad_all = to_group(after(grad_own, q_line, expand_line, out_line))
-    normed_all = to_group(normed_two)
-    grad_act = dot_rt(grad_all, w_down)
-    gate_val = dot(normed_all, w_gate)
-    up_val = dot(normed_all, w_up)
-    sigma = jax.nn.sigmoid(gate_val)
-    swish = gate_val * sigma
-    hidden_act = (swish * up_val).astype(bf16)
-    grad_gate = (grad_act * up_val * sigma * (1.0 + gate_val * (1.0 - sigma))).astype(bf16)
-    grad_up = (grad_act * swish).astype(bf16)
-
-    def rows_of(values, j):
-        return values[2 * own * j : 2 * own * (j + 1)]
-
-    def from_group(product):
-        def block_of(j):
-            both = lax.optimization_barrier(product(j))
-            return add16(both[:own], swap_core(both[own:]))
-
-        return scatter_z(block_of, f32)
-
-    grad_normed_two = from_group(
-        lambda j: (
-            dot_rt(rows_of(grad_gate, j), w_gate) + dot_rt(rows_of(grad_up, j), w_up)
-        ).astype(bf16)
-    )
-    down_out = from_group(lambda j: dot(rows_of(hidden_act, j), w_down, bf16))
-    output = (middle + down_out).astype(bf16)
-
-    def columns(values, k):
-        return values[:, block * k : block * (k + 1)]
-
-    gate_back = scatter_yfirst(
-        [dot_lt(columns(normed_all, k), grad_gate, bf16) for k in range(4)]
-    )
-    up_back = scatter_xfirst([dot_lt(columns(normed_all, k), grad_up, bf16) for k in range(4)])
-    down_blocks = [dot_lt(hidden_act, columns(grad_all, k), bf16) for k in range(4)]
-    down_back = jnp.concatenate(
-        [
-            scatter_yfirst([piece[:half_part] for piece in down_blocks]),
-            scatter_xfirst([piece[half_part:] for piece in down_blocks]),
-        ]
-    )
-
-    def hidden_grad(value):
-        by_core = value.reshape(cores, slice_rows, part)
-        both = in_order(core, mine(by_core, 0), swap_core(others(by_core, 0)), 1)
-        return both[:, :hidden_here].astype(f32)
-
-    grad_wgate, grad_wup = hidden_grad(gate_back), hidden_grad(up_back)
-    by_core = down_back.reshape(part, cores, slice_rows)
-    grad_wdown = in_order(core, mine(by_core, 1), swap_core(others(by_core, 1)), 0)
-    grad_wdown = grad_wdown[:hidden_here].astype(f32)
-
-    grad_mid_norm, grad_gain_two = norm_back(middle, factor_two, gain_two, grad_normed_two)
+    grad_far.append(send(line_c, swap_core, grad_z[1]))
+    close(hid_b3, hid_a3, grad_z[-1], grad_far[-1], normed_two)
+
+    down_a1, down_b2 = send(line_x, swap_x, down_a), send(line_y, swap_y, down_b)
+    down_b1 = send(line_x, swap_x, down_b, free=True)
+    down_a2 = send(line_y, swap_y, down_a, free=True)
+    down_b3, down_a3 = send(line_x, swap_x, down_b2), send(line_y, swap_y, down_a1)
+    norm_z = [normed_two, send(line_z, step_z, normed_two)]
+    norm_far = [send(line_c, swap_core, normed_two)]
+    for piece in grad_z[2:]:
+        grad_far.append(send(line_c, swap_core, piece, free=True))
+    close(down_b3, down_a3, norm_z[-1], norm_far[-1], grad_far[-1])
+
+    hidden_pieces = [hid_a, hid_a1, hid_a2, hid_a3, hid_b, hid_b1, hid_b2, hid_b3]
+    down_pieces = [down_a, down_a1, down_a2, down_a3, down_b, down_b1, down_b2, down_b3]
+    whole, back_parts, out_parts = [], [], []
+
+    class Ring:
+        def __init__(self, parts):
+            self.parts, self.at, self.total, self.seen = parts, 0, None, {}
+
+        def block(self, j):
+            if j not in self.seen:
+                own_part, far_part = self.parts[j]
+                self.seen[j] = add16(own_part, send(line_c, swap_core, far_part))
+            return self.seen[j]
+
+        def step(self):
+            if self.at == tp_size - 1:
+                return ()
+            self.at += 1
+            total = self.block(self.at)
+            if self.total is not None:
+                total = add16(total, self.total)
+            self.total = send(line_z, step_z, total)
+            return (self.total,)
+
+        def result(self):
+            while self.step():
+                pass
+            return self.total.astype(f32) + self.block(0).astype(f32)
+
+    back_ring, out_ring = Ring(back_parts), Ring(out_parts)
+    for j in range(tp_size):
+        arrived = []
+        if len(norm_z) < tp_size:
+            norm_z.append(send(line_z, step_z, norm_z[-1]))
+            arrived.append(norm_z[-1])
+        elif back_ring.at + 1 < len(back_parts):
+            arrived += back_ring.step()
+        if j + 1 < tp_size:
+            norm_far.append(send(line_c, swap_core, norm_z[j + 1]))
+            arrived.append(norm_far[-1])
+        made = feed(
+            now(shift),
+            j,
+            tp_size,
+            [norm_z[j], norm_far[j], grad_z[j], grad_far[j]],
+            hidden_pieces,
+            down_pieces,
+            whole,
+        )
+        back_parts.append(made[:2])
+        out_parts.append(made[2:4])
+        whole = made[4:]
+        close(*arrived, made[0])
+    act_all, hidden_all, normed_all, grad_all = whole
+
+    first, second = ((0, 3), (0, 2), (1, 3), (1, 1)), ((0, 1), (0, 0), (1, 2), (1, 0))
+    arrived = []
+    while back_ring.at < tp_size - 1:
+        arrived += back_ring.step()
+    hid_grads = dict(
+        zip(first, weight_grad(now(shift), first, slice_rows, normed_all, hidden_all))
+    )
+    grad_normed_two = back_ring.result()
+    close(*arrived, hid_grads[first[0]], grad_normed_two)
+
+    half_ring = (tp_size - 1) // 2
+    own3 = send(line_y, swap_y, hid_grads[0, 3])
+    far3 = send(line_x, swap_x, hid_grads[1, 3])
+    arrived = [own3, far3]
+    for _ in range(half_ring):
+        arrived += out_ring.step()
+    hid_grads.update(
+        zip(second, weight_grad(now(shift), second, slice_rows, normed_all, hidden_all))
+    )
+    close(*arrived, hid_grads[second[0]])
+
+    own2 = send(line_y, swap_y, hid_grads[0, 2])
+    far1 = send(line_x, swap_x, hid_grads[1, 1])
+    arrived = [own2, far1]
+    for _ in range(half_ring):
+        arrived += out_ring.step()
+    blocks = first + second
+    down_grads = dict(
+        zip(blocks, weight_grad(now(shift), blocks, slice_rows, grad_all, act_all))
+    )
+    own1, far2 = add16(hid_grads[0, 1], own3), add16(hid_grads[1, 2], far3)
+    close(*arrived, down_grads[blocks[0]], own1, far2)
+
+    own1, far2 = send(line_x, swap_x, own1), send(line_y, swap_y, far2)
+    down3 = send(line_y, swap_y, down_grads[0, 3], free=True)
+    downf3 = send(line_x, swap_x, down_grads[1, 3], free=True)
+    arrived = [own1, far2, down3, downf3]
+    hid_own = add16(hid_grads[0, 0], own2, own1)
+    hid_other = add16(hid_grads[1, 0], far1, far2)
+
+    grad_mid_norm, grad_gain_two = norm_back(middle, factor_two, gain_two, now(grad_normed_two))
     grad_middle = grad_own.astype(f32) + grad_mid_norm
     grad_attn = grad_middle.astype(bf16)
     if split:
-        grad_attn = jnp.concatenate([grad_attn, swap_core(grad_attn)])
-    grad_mixed = dot_rt(grad_attn, w_out, bf16)
+        grad_attn = jnp.concatenate([grad_attn, to_core(grad_attn)])
+    grad_mixed = dot(grad_attn, w_out, bf16)
+    out_blocks = [dot_lt(columns(grad_attn, k), mixed, bf16) for k in range(4)]
+    down1, downf2 = add16(down_grads[0, 1], down3), add16(down_grads[1, 2], downf3)
+    close(*arrived, grad_mixed, down1, downf2, *out_blocks)
+
+    down2 = send(line_y, swap_y, down_grads[0, 2])
+    downf1 = send(line_x, swap_x, down_grads[1, 1])
+    down1 = send(line_x, swap_x, down1, free=True)
+    downf2 = send(line_y, swap_y, downf2, free=True)
+    hid_far = send(line_c, swap_core, hid_other)
+    output = (middle + out_ring.result()).astype(bf16)
     grad_qlin, grad_kv, grad_ropes = attend_back(
-        *attention,
+        heads,
+        tp_size,
+        window,
+        scale,
+        now(place),
         q_lin,
         kv_all,
         rope_keys,
         *tables,
-        grad_mixed.reshape(slots, micro, rows, tp_size * heads * VHEAD),
+        grad_mixed.reshape(slots, micro, rows, tp_size * out_width),
     )
     grad_qlin = grad_qlin.reshape(slots * own, tp_size * q_width)
     grad_kv = grad_kv.reshape(micro * length, tp_size * kv_width)
-
+    close(down2, downf1, down1, downf2, hid_far, grad_ropes)
+
+    def stage_one(blocks):
+        middle_row = blocks[0].shape[0] // 2
+        top, low = zip(*((each[:middle_row], each[middle_row:]) for each in blocks))
+        return (
+            top,
+            low,
+            send(line_y, swap_y, top[3], free=True),
+            send(line_x, swap_x, low[3], free=True),
+            send(line_y, swap_y, top[2], free=True),
+            send(line_x, swap_x, low[1], free=True),
+        )
+
+    def stage_two(top, low, top3, low3, top2, low1):
+        top1 = send(line_x, swap_x, add16(top[1], top3), free=True)
+        low2 = send(line_y, swap_y, add16(low[2], low3), free=True)
+        return top, low, top2, low1, top1, low2
+
+    def stage_sum(top, low, top2, low1, top1, low2):
+        return jnp.concatenate([add16(top[0], top2, top1), add16(low[0], low1, low2)])
+
+    out_stage = stage_one(out_blocks)
+    latent_block = KVRANK // 4
+    kv_now = now(grad_kv)
+    expand_blocks = [
+        dot_lt(
+            lax.dynamic_slice_in_dim(latent_all, (shard ^ k) * latent_block, latent_block, 1),
+            kv_now,
+            bf16,
+        )
+        for k in range(4)
+    ]
     grad_latent = jnp.concatenate(
         [
-            dot_rt(grad_kv, w_expand, bf16).reshape(micro, length, KVRANK),
+            dot_rt(kv_now, w_expand, bf16).reshape(micro, length, KVRANK),
             (grad_ropes[..., :ROPE] + grad_ropes[..., ROPE:]).astype(bf16),
         ],
         axis=-1,
     ).reshape(micro, cores, span, kv_cols)
-    latent_sum = add16(mine(grad_latent, 1), swap_core(others(grad_latent, 1)))
+    close(*out_stage[2:], grad_latent, *expand_blocks)
+
+    out_stage = stage_two(*out_stage)
+    expand_stage = stage_one(expand_blocks)
+    latent_sum = add16(mine(grad_latent, 1), send(line_c, swap_core, others(grad_latent, 1)))
+    qlin_now = now(grad_qlin)
+    query_blocks = [dot_lt(columns(normed_chip, k), qlin_now, bf16) for k in range(4)]
+    close(*out_stage[4:], *expand_stage[2:], latent_sum, *query_blocks)
+
+    query_stage = stage_one(query_blocks)
+    expand_stage = stage_two(*expand_stage)
     grad_latent_own = scatter_z(
-        lambda j: lax.dynamic_slice_in_dim(latent_sum, (place_z - j) % tp_size * rows, rows, 1), f32
+        line_z,
+        lambda j: lax.dynamic_slice_in_dim(
+            now(latent_sum), (place_z - j) % tp_size * rows, rows, 1
+        ),
+        f32,
     ).reshape(own, kv_cols)
+    out_back = stage_sum(*out_stage)
+    if split:
+        query_part = dot_rt(now(grad_qlin), w_query, bf16)
+        grad_normed_one = query_part[:own].astype(f32) + to_core(query_part[own:]).astype(f32)
+    else:
+        grad_normed_one = dot_rt(now(grad_qlin), w_query)
+    close(*query_stage[2:], *expand_stage[4:], grad_latent_own)
+
+    query_stage = stage_two(*query_stage)
+    down_own = add16(down_grads[0, 0], down2, down1)
+    down_other = add16(down_grads[1, 0], downf1, downf2)
+    down_far = to_core(down_other)
+    grad_wgate, grad_wup, grad_wdown = (
+        in_order(core, near, far, 1)[:, :hidden_here].astype(f32)
+        for near, far in (
+            (hid_own[:, :part], hid_far[:, :part]),
+            (hid_own[:, part:], hid_far[:, part:]),
+            (down_own, down_far),
+        )
+    )
+    grad_wdown = grad_wdown.T
+
+    out_here = scatter_z(line_z, lambda j: out_back[:, out_width * j : out_width * (j + 1)])
+    expand_back = stage_sum(*expand_stage)
+    expand_here = scatter_z(line_z, lambda j: expand_back[:, kv_width * j : kv_width * (j + 1)])
+    query_back = stage_sum(*query_stage)
+    query_here = scatter_z(line_z, lambda j: query_back[:, q_width * j : q_width * (j + 1)])
+    out_cores = out_here.reshape(cores, slice_rows, out_width)
+    query_cores = query_here.reshape(cores, slice_rows, q_width)
+    expand_cores = expand_here.reshape(cores, expand_rows, kv_width)
+
+    def finish(by_core):
+        kept, given = mine(by_core, 0), to_core(others(by_core, 0))
+        if split:
+            return in_order(core, kept[:, None], given[:, None], 1).astype(f32)
+        return (kept.astype(f32) + given.astype(f32))[:, None]
+
+    grad_wout = finish(out_cores).reshape(slice_rows, -1).T
+    grad_wexpand = finish(expand_cores).reshape(expand_rows, -1)
+    grad_wquery = q_disorder(finish(query_cores))
+
     grad_latent_part, grad_gain_latent = norm_back(
         latent_part, factor_latent, gain_kv, grad_latent_own[:, :KVRANK]
     )
     grad_raw = jnp.concatenate(
         [grad_latent_part, rotate(grad_latent_own[:, KVRANK:], cos_own, -sin_own)], axis=-1
     ).astype(bf16)
-    grad_normed_one = dot_rt(grad_raw, w_latent)
-    if split:
-        query_back = dot_rt(grad_qlin, w_query, bf16)
-        grad_normed_one = (
-            grad_normed_one
-            + query_back[:own].astype(f32)
-            + swap_core(query_back[own:]).astype(f32)
-        )
-    else:
-        grad_normed_one = grad_normed_one + dot_rt(grad_qlin, w_query)
+    grad_normed_one = grad_normed_one + dot_rt(grad_raw, w_latent)
     grad_in_norm, grad_gain_one = norm_back(inputs, factor_one, gain_one, grad_normed_one)
     input_grad = (grad_middle + grad_in_norm).astype(bf16)
 
-    out_back = scatter_xfirst([dot_lt(mixed, columns(grad_attn, k), bf16) for k in range(4)])
-    query_back = scatter_yfirst(
-        [dot_lt(columns(normed_chip, k), grad_qlin, bf16) for k in range(4)]
-    )
-    latent_block = KVRANK // 4
-    expand_back = scatter_xfirst(
-        [
-            dot_lt(
-                lax.dynamic_slice_in_dim(latent_all, (shard ^ k) * latent_block, latent_block, 1),
-                grad_kv,
-                bf16,
-            )
-            for k in range(4)
-        ]
-    )
-    out_here = scatter_z(
-        lambda j: out_back[heads * VHEAD * j : heads * VHEAD * (j + 1)]
-    )
-    query_here = scatter_z(lambda j: query_back[:, q_width * j : q_width * (j + 1)])
-    expand_here = scatter_z(lambda j: expand_back[:, kv_width * j : kv_width * (j + 1)])
-    out_cores = out_here.reshape(heads * VHEAD, cores, slice_rows)
-    query_cores = query_here.reshape(cores, slice_rows, q_width)
-    expand_cores = expand_here.reshape(cores, expand_rows, kv_width)
-    if split:
-        grad_wout = in_order(core, mine(out_cores, 1), swap_core(others(out_cores, 1)), 0)
-        grad_wquery = in_order(
-            core, mine(query_cores, 0)[:, None], swap_core(others(query_cores, 0))[:, None], 1
-        )
-        grad_wexpand = in_order(core, mine(expand_cores, 0), swap_core(others(expand_cores, 0)), 1)
-    else:
-        grad_wout = mine(out_cores, 1).astype(f32) + swap_core(others(out_cores, 1)).astype(f32)
-        grad_wquery = mine(query_cores, 0).astype(f32) + swap_core(others(query_cores, 0)).astype(
-            f32
-        )
-        grad_wquery = grad_wquery[:, None]
-        grad_wexpand = mine(expand_cores, 0).astype(f32) + swap_core(
-            others(expand_cores, 0)
-        ).astype(f32)
-    grad_wquery = q_disorder(grad_wquery).astype(f32)
-    grad_wout, grad_wexpand = grad_wout.astype(f32), grad_wexpand.astype(f32)
-
-    def scatter_small(values, add):
-        kept = add(mine(values, 1), swap_core(others(values, 1)))
-        three, two = swap_y(kept[3]), swap_y(kept[2])
-        kept = add(add(kept[0], two), swap_x(add(kept[1], three)))
-        return scatter_z(
-            lambda j: lax.dynamic_index_in_dim(
-                kept, (place_z - j) % tp_size, 0, keepdims=False
-            ),
-            f32,
-            add,
-        )
-
-    grad_wlatent = dot_lt(normed_own, grad_raw, bf16)
-    grad_wlatent = scatter_small(
-        grad_wlatent.reshape(4, cores, tp_size, small_rows, kv_cols), add16
-    )
-    gain_grads = scatter_small(
-        jnp.concatenate(
+    core_rows = width // 4 // cores
+
+    def core_features(values, at, size):
+        return jnp.concatenate(
             [
-                grad_gain_one.reshape(4, cores, tp_size, gain_rows),
-                grad_gain_two.reshape(4, cores, tp_size, gain_rows),
-                features(grad_gain_latent).reshape(4, cores, tp_size, latent_gains),
+                lax.dynamic_slice_in_dim(values, (cores * k + at) * size, size, values.ndim - 1)
+                for k in range(4)
             ],
             axis=-1,
-        ),
-        jnp.add,
-    )
+        )
+
+    def gains_of(at):
+        pieces = [
+            core_features(grads, at, grads.shape[0] // (4 * cores)).reshape(4, tp_size, -1)
+            for grads in (grad_gain_one, grad_gain_two, features(grad_gain_latent))
+        ]
+        return jnp.concatenate(pieces, axis=-1)
+
+    def over_all(kept, given, rounded):
+        kept = kept.astype(f32) + swap_core(given.astype(rounded)).astype(f32)
+        sent = kept.astype(rounded)
+        total = kept[0]
+        for k in (1, 2, 3):
+            gone = lax.ppermute(sent[k], "shard", [(i, i ^ k) for i in range(4)])
+            total = total + gone.astype(f32)
+        sent = total.astype(rounded)
+        here = lax.dynamic_index_in_dim(total, place_z, 0, keepdims=False)
+        for j in range(1, tp_size):
+            gone = lax.dynamic_index_in_dim(sent, (place_z + j) % tp_size, 0, keepdims=False)
+            gone = lax.ppermute(gone, "tp", [(i, (i + j) % tp_size) for i in range(tp_size)])
+            here = here + gone.astype(f32)
+        return here
+
+    grad_wlatent = over_all(
+        *(
+            dot_lt(core_features(normed_own, at, core_rows), grad_raw).reshape(
+                4, tp_size, small_rows, kv_cols
+            )
+            for at in (core, 1 - core)
+        ),
+        bf16,
+    )
+    gain_grads = over_all(gains_of(core), gains_of(1 - core), f32)
     like = (micro, 1, rows, width)
     return (
         features(output).reshape(like),

time: 1380 us -> 1110 us (0.80)
  matrix products: 411 us -> 91.7 us
  Pallas kernels: 71.8 us -> 349 us
  waiting for transfers between devices: 515 us -> 364 us
  local copies, waits for them, and re-layouts: 149 us -> 92.1 us
  other arithmetic: 148 us -> 95.4 us
  starting transfers between devices: 72.4 us -> 93.9 us
    pallas_call x0 -> x10, Pallas kernels: none -> 277 us  [the longest x4 161 us: feed(): pl.pallas_call(functools.partial(feed_kernel, part, rows, offset), out_sh...]
    ppermute x45 -> x31, waiting for transfers between devices: 344 us -> 160 us  [step_z(): return lax.ppermute(value, 'tp', [(i, (i + 1) % size) for i in range(size)])]
    dot_general x25 -> x14, matrix products: 155 us -> 36.6 us  [dot_lt(): lax.dot_general(left, right, (((0,), (0,)), ((), ())), preferred_element_...]
    dot_general x13 -> x4, matrix products: 131 us -> 27.1 us  [dot_rt(): lax.dot_general(left, right, (((1,), (1,)), ((), ())), preferred_element_...]
    dot_general x10 -> x4, matrix products: 125 us -> 28 us  [dot(): return jnp.dot(left, right, preferred_element_type=f32).astype(kind)]
    ppermute x25 -> x27, waiting for transfers between devices: 43.5 us -> 82.4 us  [swap_x(): return lax.ppermute(value, 'shard', [(i, i ^ 1) for i in range(4)])]
    concatenate x8 -> x7, other arithmetic: 39.6 us -> 3.66 us  [the longest x3 2.19 us: stage_sum(): jnp.concatenate([add16(top[0], top2, top1), add16(low[0], low1, low2)])]
    ppermute x26 -> x27, waiting for transfers between devices: 125 us -> 98 us  [swap_y(): return lax.ppermute(value, 'shard', [(i, i ^ 2) for i in range(4)])]
  transfers between devices with their start and end apart: 133 -> 133, of which waited for: 54 -> 62; matrix products, arithmetic and copies ran while one was open for 36% -> 19% of each run, Pallas kernels for 2% -> 32%
where the time goes in v2:
time: 1110 us; the launch traced here: 1100 us
  waiting for transfers between devices  364 us (33%)
  Pallas kernels  349 us (31%)
  other arithmetic  95.4 us (9%)
  starting transfers between devices  93.9 us (8%)
  local copies, waits for them, and re-layouts  92.1 us (8%)
  matrix products  91.7 us (8%)
  between operations  17.8 us (2%)
    pallas_call x4, Pallas kernels, feed(): pl.pallas_call(functools.partial(feed_kernel, part, rows, offset), out_sh...  161 us
    ppermute x31, waiting for transfers between devices, step_z(): return lax.ppermute(value, 'tp', [(i, (i + 1) % size) for i in range(size)])  160 us
    ppermute x27, waiting for transfers between devices, swap_y(): return lax.ppermute(value, 'shard', [(i, i ^ 2) for i in range(4)])  98 us
    pallas_call x3, Pallas kernels, weight_grad(): pl.pallas_call(functools.partial(weight_grad_kernel, blocks), out_shape=[...  95.6 us
    ppermute x27, waiting for transfers between devices, swap_x(): return lax.ppermute(value, 'shard', [(i, i ^ 1) for i in range(4)])  82.4 us
    convert_element_type x32, other arithmetic, add16(): return total.astype(bf16)  45 us
    pallas_call x1, Pallas kernels, attend_back(): pl.pallas_call(functools.partial(attend_back_kernel, heads, width, scale)...  44.2 us
    dot_general x14, matrix products, dot_lt(): lax.dot_general(left, right, (((0,), (0,)), ((), ())), preferred_element_...  36.6 us
  transfers between devices with their start and end apart: 133, of which 62 were waited for; matrix products, arithmetic and copies ran while one was open for 19% of the time, Pallas kernels for 32%

profile of v2, /device:TPU:0, one launch (start us, length us, event | category | flops | bytes accessed | tf_op | source)
XLA Modules:
  0.0 1103.9 jit_solution(16816126054074637701)
XLA Ops:
  24.2 11.2 %collective-permute-done.1.refs_1_ = bf16[512,768]{1,0:T(8,128)(2,1)S(1)} collective-permute-done((bf16[512,768]{1,0:T(8,128)(2,1)S(1)}, bf16[512,768]{1,0:T(8,128)(2,1)S(1)}, u32[]{:S(2)}, u32[]{:S(2)}) %collective-permute-start.1) | collective-permute-done | bytes 786464 | tf_op jit(solution)/shard_map/ppermute | solution.py:95
  36.9 4.6 collective-permute-done.3.refs_4_
  44.7 4.0 pack.1
  52.7 8.6 collective-permute-done.6.refs_6_
  75.9 14.3 %collective-permute-done.8.refs_3_ = bf16[512,768]{1,0:T(8,128)(2,1)} collective-permute-done((bf16[512,768]{1,0:T(8,128)(2,1)S(1)}, bf16[512,768]{1,0:T(8,128)(2,1)}, u32[]{:S(2)}, u32[]{:S(2)}) %collective-permute-start.8) | collective-permute-done | bytes 786464 | tf_op jit(solution)/shard_map/ppermute | solution.py:99
  91.2 6.3 collective-permute-done.9.refs_12_
  113.5 6.0 collective-permute-done.12
  125.6 16.0 %collective-permute-done.17 = bf16[192,2048]{1,0:T(8,128)(2,1)S(1)} collective-permute-done((bf16[192,2048]{1,0:T(8,128)(2,1)}, bf16[192,2048]{1,0:T(8,128)(2,1)S(1)}, u32[]{:S(2)}, u32[]{:S(2)}) %collective-permute-start.17) | collective-permute-done | bytes 786464 | tf_op jit(solution)/shard_map/ppermute | solution.py:104
  144.3 13.0 %collective-permute-done.21.refs_1_ = bf16[3,128,576]{2,1,0:T(8,128)(2,1)} collective-permute-done((bf16[3,128,576]{2,1,0:T(8,128)(2,1)S(1)}, bf16[3,128,576]{2,1,0:T(8,128)(2,1)}, u32[]{:S(2)}, u32[]{:S(2)}) %collective-permute-start.21) | collective-permute-done | bytes 442400 | tf_op jit(solution)/shard_map/ppermute | solution.py:104
  163.2 8.1 collective-permute-done.22.refs_2_
  177.7 11.6 %assemble.1 = (bf16[2048,1536]{1,0:T(8,128)(2,1)}, bf16[2048,1024]{1,0:T(8,128)(2,1)}, bf16[512,2048]{1,0:T(8,128)(2,1)}) custom-call(s32[2]{0:T(128)S(1)} %pad_add_fusion.3.place.place_ref, bf16[512,768]{1,0:T(8,128)(2,1)S(1)} %pad_maximum_fusion.17.refs_0_, bf16[512,768]{1,0:T(8,128)(2,1)S(1)} %collective-permute-done.1.refs_1_, ...), custom_call_target="tpu_custom_call" | custom-call | bytes 25165824 | tf_op jit(solution)/shard_map/assemble/pallas_call | solution.py:168
  189.4 9.4 fusion.114
  199.2 7.0 collective-permute-done.25.refs_10_
  208.6 5.0 lay_out.1
  213.5 11.8 %convolution_convert_fusion = bf16[3072,2048]{1,0:T(8,128)(2,1)} fusion(bf16[3072,512]{1,0:T(8,128)(2,1)} %bitcast.218, bf16[512,2048]{1,0:T(8,128)(2,1)} %get-tuple-element.334), kind=kOutput, calls=%fused_computation | convolution fusion | flops 6448742400 | bytes 17825792 | tf_op jit(solution)/shard_map/dot_general | solution.py:51
  225.4 27.2 %attend.1 = bf16[2,3,128,1024]{3,2,1,0:T(8,128)(2,1)S(1)} custom-call(s32[2,2]{1,0:T(2,128)S(1)} %pad_add_fusion.2.place, f32[2,3,128,1536]{3,2,1,0:T(8,128)S(1)} %bitcast.191, bf16[3,1024,2048]{2,1,0:T(8,128)(2,1)} %bitcast.213, bf16[3,1024,128]{2,1,0:T(8,128)(2,1)S(1)} %copy-done.5, s32[3,256,1]{2,1,0:T(8,128)S(1)} %copy.186.segq_ref, ...), custom_call_target="tpu_custom_call" | custom-call | flops 3019898880 | bytes 19660800 | tf_op jit(solution)/shard_map/attend/pallas_call | solution.py:359
  265.6 28.5 %collective-permute-done.36.refs_7_ = bf16[256,2816]{1,0:T(8,128)(2,1)S(1)} collective-permute-done((bf16[256,2816]{1,0:T(8,128)(2,1)S(1)}, bf16[256,2816]{1,0:T(8,128)(2,1)S(1)}, u32[]{:S(2)}, u32[]{:S(2)}) %collective-permute-start.36) | collective-permute-done | bytes 1441824 | tf_op jit(solution)/shard_map/ppermute | solution.py:99
  299.6 14.2 %collective-permute-done.43.refs_13_ = bf16[256,1408]{1,0:T(8,128)(2,1)S(1)} collective-permute-done((bf16[256,1408]{1,0:T(8,128)(2,1)S(1)}, bf16[256,1408]{1,0:T(8,128)(2,1)S(1)}, u32[]{:S(2)}, u32[]{:S(2)}) %collective-permute-start.43) | collective-permute-done | bytes 720928 | tf_op jit(solution)/shard_map/ppermute | solution.py:95
  316.4 14.4 %collective-permute-done.40.refs_18_ = bf16[256,1408]{1,0:T(8,128)(2,1)S(1)} collective-permute-done((bf16[256,1408]{1,0:T(8,128)(2,1)S(1)}, bf16[256,1408]{1,0:T(8,128)(2,1)S(1)}, u32[]{:S(2)}, u32[]{:S(2)}) %collective-permute-start.40) | collective-permute-done | bytes 720928 | tf_op jit(solution)/shard_map/ppermute | solution.py:99
  333.5 13.5 %collective-permute-done.45.refs_15_ = bf16[256,1408]{1,0:T(8,128)(2,1)S(1)} collective-permute-done((bf16[256,1408]{1,0:T(8,128)(2,1)S(1)}, bf16[256,1408]{1,0:T(8,128)(2,1)S(1)}, u32[]{:S(2)}, u32[]{:S(2)}) %collective-permute-start.45) | collective-permute-done | bytes 720928 | tf_op jit(solution)/shard_map/ppermute | solution.py:99
  349.4 40.3 %feed.4 = (bf16[384,2048]{1,0:T(8,128)(2,1)}, bf16[384,2048]{1,0:T(8,128)(2,1)}, bf16[384,2048]{1,0:T(8,128)(2,1)}, bf16[384,2048]{1,0:T(8,128)(2,1)}, bf16[3072...) custom-call(s32[2]{0:T(128)} %copy-done.21, ...), custom_call_target="tpu_custom_call" | custom-call | flops 26575110144 | bytes 42663936 | tf_op jit(solution)/shard_map/feed/pallas_call | solution.py:519
  392.2 40.2 %feed.5 = (bf16[384,2048]{1,0:T(8,128)(2,1)}, bf16[384,2048]{1,0:T(8,128)(2,1)}, bf16[384,2048]{1,0:T(8,128)(2,1)}, bf16[384,2048]{1,0:T(8,128)(2,1)}, bf16[3072...) custom-call(s32[2]{0:T(128)} %copy-done.21, ...), custom_call_target="tpu_custom_call", output_to_operand_aliasing={{4}: (21, {}), {5}: (22, {}), {6}: (23, {}), {7}: (24, {})} | custom-call | flops 26575110144 | bytes 42663936 | tf_op jit(solution)/shard_map/feed/pallas_call | solution.py:519
  439.6 40.3 %feed.6 = (bf16[384,2048]{1,0:T(8,128)(2,1)}, bf16[384,2048]{1,0:T(8,128)(2,1)}, bf16[384,2048]{1,0:T(8,128)(2,1)}, bf16[384,2048]{1,0:T(8,128)(2,1)}, bf16[3072...) custom-call(s32[2]{0:T(128)} %copy-done.21, ...), custom_call_target="tpu_custom_call", output_to_operand_aliasing={{4}: (21, {}), {5}: (22, {}), {6}: (23, {}), {7}: (24, {})} | custom-call | flops 26575110144 | bytes 42663936 | tf_op jit(solution)/shard_map/feed/pallas_call | solution.py:519
  488.5 40.3 %feed.7 = (bf16[384,2048]{1,0:T(8,128)(2,1)}, bf16[384,2048]{1,0:T(8,128)(2,1)}, bf16[384,2048]{1,0:T(8,128)(2,1)}, bf16[384,2048]{1,0:T(8,128)(2,1)}, bf16[3072...) custom-call(s32[2]{0:T(128)} %copy-done.21, ...), custom_call_target="tpu_custom_call", output_to_operand_aliasing={{4}: (21, {}), {5}: (22, {}), {6}: (23, {}), {7}: (24, {})} | custom-call | flops 26575110144 | bytes 42663936 | tf_op jit(solution)/shard_map/feed/pallas_call | solution.py:519
  535.2 29.5 %weight_grad.3 = (bf16[256,2816]{1,0:T(8,128)(2,1)}, bf16[256,2816]{1,0:T(8,128)(2,1)S(1)}, bf16[256,2816]{1,0:T(8,128)(2,1)}, bf16[256,2816]{1,0:T(8,128)(2,1)S(1)}) custom-call(s32[2]{0:T(128)S(1)} %copy-done.22, bf16[3072,2048]{1,0:T(8,128)(2,1)} %get-tuple-element.414.left, bf16[3072,2816]{1,0:T(8,128)(2,1)} %get-tuple-element.415.right_ref), custom_call_target="tpu_custom_call" | custom-call | flops 17716740096 | bytes 29360128 | tf_op jit(solution)/shard_map/weight_grad/pallas_call | solution.py:631
  564.7 8.8 collective-permute-done.59
  582.0 29.0 %weight_grad.4 = (bf16[256,2816]{1,0:T(8,128)(2,1)S(1)}, bf16[256,2816]{1,0:T(8,128)(2,1)S(1)}, bf16[256,2816]{1,0:T(8,128)(2,1)S(1)}, bf16[256,2816]{1,0:T(8,128)(2,1)S(1)}) custom-call(s32[2]{0:T(128)S(1)} %copy-done.22, bf16[3072,2048]{1,0:T(8,128)(2,1)} %get-tuple-element.414.left, bf16[3072,2816]{1,0:T(8,128)(2,1)} %get-tuple-element.415.right_ref), custom_call_target="tpu_custom_call" | custom-call | flops 17716740096 | bytes 29360128 | tf_op jit(solution)/shard_map/weight_grad/pallas_call | solution.py:631
  612.7 7.6 collective-permute-done.64
  629.1 37.1 %weight_grad.5 = (bf16[256,1408]{1,0:T(8,128)(2,1)}, bf16[256,1408]{1,0:T(8,128)(2,1)S(1)}, bf16[256,1408]{1,0:T(8,128)(2,1)}, bf16[256,1408]{1,0:T(8,128)(2,1)S...) custom-call(s32[2]{0:T(128)S(1)} %copy-done.22, ...), custom_call_target="tpu_custom_call" | custom-call | flops 17716740096 | bytes 27000832 | tf_op jit(solution)/shard_map/weight_grad/pallas_call | solution.py:631
  684.3 6.7 collective-permute-done.72
  695.7 24.4 %collective-permute-done.69 = bf16[256,2816]{1,0:T(8,128)(2,1)} collective-permute-done((bf16[256,2816]{1,0:T(8,128)(2,1)}, bf16[256,2816]{1,0:T(8,128)(2,1)}, u32[]{:S(2)}, u32[]{:S(2)}) %collective-permute-start.69) | collective-permute-done | bytes 1441824 | tf_op jit(solution)/shard_map/ppermute | solution.py:95
  739.9 5.4 fusion.16
  749.5 44.2 %attend_back.1 = (bf16[2,3,128,1536]{3,2,1,0:T(8,128)(2,1)S(1)}, bf16[3,1024,2048]{2,1,0:T(8,128)(2,1)}, f32[3,1024,128]{2,1,0:T(8,128)S(1)}) custom-call(s32[2,2]{1,0:T(2,128)S(1)} %copy-done.20, f32[2,3,128,1536]{3,2,1,0:T(8,128)S(1)} %bitcast.194, bf16[3,1024,2048]{2,1,0:T(8,128)(2,1)} %bitcast.214, bf16[3,1024,128]{2,1,0:T(8,128)(2,1)S(1)} %copy-done.6, ...), custom_call_target="tpu_custom_call" | custom-call | flops 8053063680 | bytes 34603008 | tf_op jit(solution)/shard_map/attend_back/pallas_call | solution.py:389
  803.7 11.1 %convolution_convert_fusion.1 = bf16[3072,512]{1,0:T(8,128)(2,1)} fusion(bf16[3072,2048]{1,0:T(8,128)(2,1)} %bitcast.206, bf16[512,2048]{1,0:T(8,128)(2,1)S(1)} %copy-done.175), kind=kOutput, calls=%fused_computation.22 | convolution fusion | flops 6444023808 | bytes 17825792 | tf_op jit(solution)/shard_map/dot_general | solution.py:55
  848.9 5.8 collective-permute-done.83
  882.0 11.1 %collective-permute-done.86 = bf16[256,1024]{1,0:T(8,128)(2,1)S(1)} collective-permute-done((bf16[256,1024]{1,0:T(8,128)(2,1)S(1)}, bf16[256,1024]{1,0:T(8,128)(2,1)S(1)}, u32[]{:S(2)}, u32[]{:S(2)}) %collective-permute-start.86) | collective-permute-done | bytes 524320 | tf_op jit(solution)/shard_map/ppermute | solution.py:95
  896.5 16.4 %collective-permute-done.76 = bf16[384,2048]{1,0:T(8,128)(2,1)S(1)} collective-permute-done((bf16[384,2048]{1,0:T(8,128)(2,1)S(1)}, bf16[384,2048]{1,0:T(8,128)(2,1)S(1)}, u32[]{:S(2)}, u32[]{:S(2)}) %collective-permute-start.76) | collective-permute-done | bytes 1572896 | tf_op jit(solution)/shard_map/ppermute | solution.py:104
  918.0 5.5 convolution_convert_fusion.3
  930.3 9.1 collective-permute-done.94
  941.0 4.4 collective-permute-done.105
  946.9 11.7 %collective-permute-done.95 = bf16[3,128,576]{1,2,0:T(8,128)(2,1)S(1)} collective-permute-done((bf16[3,128,576]{1,2,0:T(8,128)(2,1)S(1)}, bf16[3,128,576]{1,2,0:T(8,128)(2,1)S(1)}, u32[]{:S(2)}, u32[]{:S(2)}) %collective-permute-start.95) | collective-permute-done | bytes 442400 | tf_op jit(solution)/shard_map/ppermute | solution.py:104
  963.8 7.3 collective-permute-done.96
  989.7 6.8 fusion.10
  1016.7 4.4 collective-permute-start.102
  1029.5 7.8 collective-permute-done.114
  1045.3 5.9 collective-permute-done.116
  1062.2 7.7 collective-permute-done.118
  1076.3 5.5 collective-permute-done.119
  (884 shorter events, 376.9 us)
Async XLA Ops:
  7.2 92.7 %all-gather.3.cloned.1.call-start = ((), (), s32[]{:S(2)}) async-start(), calls=%async_computation | async-start | bytes 3379200 | tf_op jit(solution)/shard_map/all_gather | solution.py:724
  172.0 34.3 %collective-permute-start.25 = (bf16[256,2816]{1,0:T(8,128)(2,1)}, bf16[256,2816]{1,0:T(8,128)(2,1)S(1)}, u32[]{:S(2)}, u32[]{:S(2)}) collective-permute-start(bf16[256,2816]{1,0:T(8,128)(2,1)} %collective-permute-done.13.refs_8_), channel_id=1, source_target_pairs={{0,16},{8,24},{16,0},{24,8},{1,17},{9,25},{17,1},{25,9},{2,18},{10... | collective-permute-start | bytes 4325384 | tf_op jit(solution)/shard_map/ppermute | solution.py:99
  172.5 33.9 %collective-permute-start.24 = (bf16[256,2816]{1,0:T(8,128)(2,1)}, bf16[256,2816]{1,0:T(8,128)(2,1)S(1)}, u32[]{:S(2)}, u32[]{:S(2)}) collective-permute-start(bf16[256,2816]{1,0:T(8,128)(2,1)} %copy-done.23), channel_id=1, source_target_pairs={{0,8},{8,0},{16,24},{24,16},{1,9},{9,1},{17,25},{25,17},{2,10},{10... | collective-permute-start | bytes 4325384 | tf_op jit(solution)/shard_map/ppermute | solution.py:95
  198.8 53.8 %collective-permute-start.33 = (bf16[384,2048]{1,0:T(8,128)(2,1)}, bf16[384,2048]{1,0:T(8,128)(2,1)}, u32[]{:S(2)}, u32[]{:S(2)}) collective-permute-start(bf16[384,2048]{1,0:T(8,128)(2,1)} %pad_maximum_fusion.8.refs_2_), channel_id=1, source_target_pairs={{0,4},{4,0},{1,5},{5,1},{2,6},{6,2},{3,7},{7,3},{8,12},{12,8},{9,1... | collective-permute-start | bytes 4718600 | tf_op jit(solution)/shard_map/ppermute | solution.py:91
  206.4 46.2 %collective-permute-start.32 = (bf16[384,2048]{1,0:T(8,128)(2,1)}, bf16[384,2048]{1,0:T(8,128)(2,1)}, u32[]{:S(2)}, u32[]{:S(2)}) collective-permute-start(bf16[384,2048]{1,0:T(8,128)(2,1)} %constant_dynamic-update-slice_fusion.refs_2_), channel_id=1, source_target_pairs={{0,1},{1,2},{2,3},{3,0},{4,5},{5,6},{6,7},{7,4},{8,9},{9,10},{10,1... | collective-permute-start | bytes 4718600 | tf_op jit(solution)/shard_map/ppermute | solution.py:104
  206.4 46.2 %collective-permute-start.31 = (bf16[256,2816]{1,0:T(8,128)(2,1)S(1)}, bf16[256,2816]{1,0:T(8,128)(2,1)}, u32[]{:S(2)}, u32[]{:S(2)}) collective-permute-start(bf16[256,2816]{1,0:T(8,128)(2,1)S(1)} %copy-done.24), channel_id=1, source_target_pairs={{0,16},{8,24},{16,0},{24,8},{1,17},{9,25},{17,1},{25,9},{2,18},{10... | collective-permute-start | bytes 4325384 | tf_op jit(solution)/shard_map/ppermute | solution.py:99
  208.1 44.6 %collective-permute-start.30 = (bf16[256,2816]{1,0:T(8,128)(2,1)}, bf16[256,2816]{1,0:T(8,128)(2,1)}, u32[]{:S(2)}, u32[]{:S(2)}) collective-permute-start(bf16[256,2816]{1,0:T(8,128)(2,1)} %collective-permute-done.13.refs_8_), channel_id=1, source_target_pairs={{0,8},{8,0},{16,24},{24,16},{1,9},{9,1},{17,25},{25,17},{2,10},{10... | collective-permute-start | bytes 4325384 | tf_op jit(solution)/shard_map/ppermute | solution.py:95
  256.7 39.2 %collective-permute-start.37 = (bf16[384,2048]{1,0:T(8,128)(2,1)}, bf16[384,2048]{1,0:T(8,128)(2,1)S(1)}, u32[]{:S(2)}, u32[]{:S(2)}) collective-permute-start(bf16[384,2048]{1,0:T(8,128)(2,1)} %collective-permute-done.32.refs_2_), channel_id=1, source_target_pairs={{0,1},{1,2},{2,3},{3,0},{4,5},{5,6},{6,7},{7,4},{8,9},{9,10},{10,1... | collective-permute-start | bytes 4718600 | tf_op jit(solution)/shard_map/ppermute | solution.py:104
  260.1 35.8 %collective-permute-start.38 = (bf16[384,2048]{1,0:T(8,128)(2,1)}, bf16[384,2048]{1,0:T(8,128)(2,1)S(1)}, u32[]{:S(2)}, u32[]{:S(2)}) collective-permute-start(bf16[384,2048]{1,0:T(8,128)(2,1)} %constant_dynamic-update-slice_fusion.refs_2_), channel_id=1, source_target_pairs={{0,4},{4,0},{1,5},{5,1},{2,6},{6,2},{3,7},{7,3},{8,12},{12,8},{9,1... | collective-permute-start | bytes 4718600 | tf_op jit(solution)/shard_map/ppermute | solution.py:91
  260.2 33.9 %collective-permute-start.36 = (bf16[256,2816]{1,0:T(8,128)(2,1)S(1)}, bf16[256,2816]{1,0:T(8,128)(2,1)S(1)}, u32[]{:S(2)}, u32[]{:S(2)}) collective-permute-start(bf16[256,2816]{1,0:T(8,128)(2,1)S(1)} %copy-done.186), channel_id=1, source_target_pairs={{0,16},{8,24},{16,0},{24,8},{1,17},{9,25},{17,1},{25,9},{2,18},{10... | collective-permute-start | bytes 4325384 | tf_op jit(solution)/shard_map/ppermute | solution.py:99
  261.3 33.6 %collective-permute-start.35 = (bf16[256,2816]{1,0:T(8,128)(2,1)S(1)}, bf16[256,2816]{1,0:T(8,128)(2,1)S(1)}, u32[]{:S(2)}, u32[]{:S(2)}) collective-permute-start(bf16[256,2816]{1,0:T(8,128)(2,1)S(1)} %copy-done.184), channel_id=1, source_target_pairs={{0,8},{8,0},{16,24},{24,16},{1,9},{9,1},{17,25},{25,17},{2,10},{10... | collective-permute-start | bytes 4325384 | tf_op jit(solution)/shard_map/ppermute | solution.py:95
  298.5 49.6 %collective-permute-start.47 = (bf16[384,2048]{1,0:T(8,128)(2,1)S(1)}, bf16[384,2048]{1,0:T(8,128)(2,1)S(1)}, u32[]{:S(2)}, u32[]{:S(2)}) collective-permute-start(bf16[384,2048]{1,0:T(8,128)(2,1)S(1)} %collective-permute-done.37.refs_2_), channel_id=1, source_target_pairs={{0,4},{4,0},{1,5},{5,1},{2,6},{6,2},{3,7},{7,3},{8,12},{12,8},{9,1... | collective-permute-start | bytes 4718600 | tf_op jit(solution)/shard_map/ppermute | solution.py:91
  298.5 49.6 %collective-permute-start.46 = (bf16[384,2048]{1,0:T(8,128)(2,1)S(1)}, bf16[384,2048]{1,0:T(8,128)(2,1)S(1)}, u32[]{:S(2)}, u32[]{:S(2)}) collective-permute-start(bf16[384,2048]{1,0:T(8,128)(2,1)S(1)} %multiply_convert_fusion.refs_0_), channel_id=1, source_target_pairs={{0,4},{4,0},{1,5},{5,1},{2,6},{6,2},{3,7},{7,3},{8,12},{12,8},{9,1... | collective-permute-start | bytes 4718600 | tf_op jit(solution)/shard_map/ppermute | solution.py:91
  299.0 49.1 %collective-permute-start.39 = (bf16[384,2048]{1,0:T(8,128)(2,1)S(1)}, bf16[384,2048]{1,0:T(8,128)(2,1)}, u32[]{:S(2)}, u32[]{:S(2)}) collective-permute-start(bf16[384,2048]{1,0:T(8,128)(2,1)S(1)} %multiply_convert_fusion.refs_0_), channel_id=1, source_target_pairs={{0,1},{1,2},{2,3},{3,0},{4,5},{5,6},{6,7},{7,4},{8,9},{9,10},{10,1... | collective-permute-start | bytes 4718600 | tf_op jit(solution)/shard_map/ppermute | solution.py:104
  348.1 41.6 %collective-permute-start.49 = (bf16[384,2048]{1,0:T(8,128)(2,1)}, bf16[384,2048]{1,0:T(8,128)(2,1)}, u32[]{:S(2)}, u32[]{:S(2)}) collective-permute-start(bf16[384,2048]{1,0:T(8,128)(2,1)} %collective-permute-done.39.refs_0_), channel_id=1, source_target_pairs={{0,4},{4,0},{1,5},{5,1},{2,6},{6,2},{3,7},{7,3},{8,12},{12,8},{9,1... | collective-permute-start | bytes 4718600 | tf_op jit(solution)/shard_map/ppermute | solution.py:91
  349.2 40.5 %collective-permute-start.48 = (bf16[384,2048]{1,0:T(8,128)(2,1)}, bf16[384,2048]{1,0:T(8,128)(2,1)}, u32[]{:S(2)}, u32[]{:S(2)}) collective-permute-start(bf16[384,2048]{1,0:T(8,128)(2,1)} %collective-permute-done.39.refs_0_), channel_id=1, source_target_pairs={{0,1},{1,2},{2,3},{3,0},{4,5},{5,6},{6,7},{7,4},{8,9},{9,10},{10,1... | collective-permute-start | bytes 4718600 | tf_op jit(solution)/shard_map/ppermute | solution.py:104
  389.7 42.7 %collective-permute-start.51 = (bf16[384,2048]{1,0:T(8,128)(2,1)}, bf16[384,2048]{1,0:T(8,128)(2,1)S(1)}, u32[]{:S(2)}, u32[]{:S(2)}) collective-permute-start(bf16[384,2048]{1,0:T(8,128)(2,1)} %collective-permute-done.48.refs_0_), channel_id=1, source_target_pairs={{0,4},{4,0},{1,5},{5,1},{2,6},{6,2},{3,7},{7,3},{8,12},{12,8},{9,1... | collective-permute-start | bytes 4718600 | tf_op jit(solution)/shard_map/ppermute | solution.py:91
  389.8 42.7 %collective-permute-start.50 = (bf16[384,2048]{1,0:T(8,128)(2,1)}, bf16[384,2048]{1,0:T(8,128)(2,1)S(1)}, u32[]{:S(2)}, u32[]{:S(2)}) collective-permute-start(bf16[384,2048]{1,0:T(8,128)(2,1)} %collective-permute-done.48.refs_0_), channel_id=1, source_target_pairs={{0,1},{1,2},{2,3},{3,0},{4,5},{5,6},{6,7},{7,4},{8,9},{9,10},{10,1... | collective-permute-start | bytes 4718600 | tf_op jit(solution)/shard_map/ppermute | solution.py:104
  436.9 43.0 %collective-permute-start.54 = (bf16[384,2048]{1,0:T(8,128)(2,1)S(1)}, bf16[384,2048]{1,0:T(8,128)(2,1)}, u32[]{:S(2)}, u32[]{:S(2)}) collective-permute-start(bf16[384,2048]{1,0:T(8,128)(2,1)S(1)} %collective-permute-done.50.refs_0_), channel_id=1, source_target_pairs={{0,4},{4,0},{1,5},{5,1},{2,6},{6,2},{3,7},{7,3},{8,12},{12,8},{9,1... | collective-permute-start | bytes 4718600 | tf_op jit(solution)/shard_map/ppermute | solution.py:91
  439.0 40.9 %collective-permute-start.53 = (bf16[384,2048]{1,0:T(8,128)(2,1)S(1)}, bf16[384,2048]{1,0:T(8,128)(2,1)S(1)}, u32[]{:S(2)}, u32[]{:S(2)}) collective-permute-start(bf16[384,2048]{1,0:T(8,128)(2,1)S(1)} %add_convert_fusion.12), channel_id=1, source_target_pairs={{0,1},{1,2},{2,3},{3,0},{4,5},{5,6},{6,7},{7,4},{8,9},{9,10},{10,1... | collective-permute-start | bytes 4718600 | tf_op jit(solution)/shard_map/ppermute | solution.py:104
  485.9 43.0 %collective-permute-start.57 = (bf16[384,2048]{1,0:T(8,128)(2,1)S(1)}, bf16[384,2048]{1,0:T(8,128)(2,1)S(1)}, u32[]{:S(2)}, u32[]{:S(2)}) collective-permute-start(bf16[384,2048]{1,0:T(8,128)(2,1)S(1)} %add_convert_fusion.10), channel_id=1, source_target_pairs={{0,1},{1,2},{2,3},{3,0},{4,5},{5,6},{6,7},{7,4},{8,9},{9,10},{10,1... | collective-permute-start | bytes 4718600 | tf_op jit(solution)/shard_map/ppermute | solution.py:104
  534.9 38.5 %collective-permute-start.59 = (bf16[384,2048]{1,0:T(8,128)(2,1)S(1)}, bf16[384,2048]{1,0:T(8,128)(2,1)S(1)}, u32[]{:S(2)}, u32[]{:S(2)}) collective-permute-start(bf16[384,2048]{1,0:T(8,128)(2,1)S(1)} %add_convert_fusion.8), channel_id=1, source_target_pairs={{0,1},{1,2},{2,3},{3,0},{4,5},{5,6},{6,7},{7,4},{8,9},{9,10},{10,1... | collective-permute-start | bytes 4718600 | tf_op jit(solution)/shard_map/ppermute | solution.py:104
  577.4 34.1 %collective-permute-start.62 = (bf16[256,2816]{1,0:T(8,128)(2,1)}, bf16[256,2816]{1,0:T(8,128)(2,1)S(1)}, u32[]{:S(2)}, u32[]{:S(2)}) collective-permute-start(bf16[256,2816]{1,0:T(8,128)(2,1)} %get-tuple-element.427), channel_id=1, source_target_pairs={{0,8},{8,0},{16,24},{24,16},{1,9},{9,1},{17,25},{25,17},{2,10},{10... | collective-permute-start | bytes 4325384 | tf_op jit(solution)/shard_map/ppermute | solution.py:95
  578.9 33.8 %collective-permute-start.61 = (bf16[256,2816]{1,0:T(8,128)(2,1)}, bf16[256,2816]{1,0:T(8,128)(2,1)S(1)}, u32[]{:S(2)}, u32[]{:S(2)}) collective-permute-start(bf16[256,2816]{1,0:T(8,128)(2,1)} %get-tuple-element.423), channel_id=1, source_target_pairs={{0,16},{8,24},{16,0},{24,8},{1,17},{9,25},{17,1},{25,9},{2,18},{10... | collective-permute-start | bytes 4325384 | tf_op jit(solution)/shard_map/ppermute | solution.py:99
  581.8 38.5 %collective-permute-start.64 = (bf16[384,2048]{1,0:T(8,128)(2,1)S(1)}, bf16[384,2048]{1,0:T(8,128)(2,1)S(1)}, u32[]{:S(2)}, u32[]{:S(2)}) collective-permute-start(bf16[384,2048]{1,0:T(8,128)(2,1)S(1)} %add_convert_fusion.6), channel_id=1, source_target_pairs={{0,1},{1,2},{2,3},{3,0},{4,5},{5,6},{6,7},{7,4},{8,9},{9,10},{10,1... | collective-permute-start | bytes 4718600 | tf_op jit(solution)/shard_map/ppermute | solution.py:104
  624.8 41.5 %collective-permute-start.66 = (bf16[256,2816]{1,0:T(8,128)(2,1)S(1)}, bf16[256,2816]{1,0:T(8,128)(2,1)}, u32[]{:S(2)}, u32[]{:S(2)}) collective-permute-start(bf16[256,2816]{1,0:T(8,128)(2,1)S(1)} %copy-done.28), channel_id=1, source_target_pairs={{0,8},{8,0},{16,24},{24,16},{1,9},{9,1},{17,25},{25,17},{2,10},{10... | collective-permute-start | bytes 4325384 | tf_op jit(solution)/shard_map/ppermute | solution.py:95
  626.3 40.0 %collective-permute-start.65 = (bf16[256,2816]{1,0:T(8,128)(2,1)S(1)}, bf16[256,2816]{1,0:T(8,128)(2,1)}, u32[]{:S(2)}, u32[]{:S(2)}) collective-permute-start(bf16[256,2816]{1,0:T(8,128)(2,1)S(1)} %copy-done.26), channel_id=1, source_target_pairs={{0,16},{8,24},{16,0},{24,8},{1,17},{9,25},{17,1},{25,9},{2,18},{10... | collective-permute-start | bytes 4325384 | tf_op jit(solution)/shard_map/ppermute | solution.py:99
  629.1 38.3 %collective-permute-start.68 = (bf16[384,2048]{1,0:T(8,128)(2,1)}, bf16[384,2048]{1,0:T(8,128)(2,1)S(1)}, u32[]{:S(2)}, u32[]{:S(2)}) collective-permute-start(bf16[384,2048]{1,0:T(8,128)(2,1)} %add_convert_fusion.4), channel_id=1, source_target_pairs={{0,1},{1,2},{2,3},{3,0},{4,5},{5,6},{6,7},{7,4},{8,9},{9,10},{10,1... | collective-permute-start | bytes 4718600 | tf_op jit(solution)/shard_map/ppermute | solution.py:104
  673.4 46.7 %collective-permute-start.69 = (bf16[256,2816]{1,0:T(8,128)(2,1)}, bf16[256,2816]{1,0:T(8,128)(2,1)}, u32[]{:S(2)}, u32[]{:S(2)}) collective-permute-start(bf16[256,2816]{1,0:T(8,128)(2,1)} %add_convert_fusion.16), channel_id=1, source_target_pairs={{0,8},{8,0},{16,24},{24,16},{1,9},{9,1},{17,25},{25,17},{2,10},{10... | collective-permute-start | bytes 4325384 | tf_op jit(solution)/shard_map/ppermute | solution.py:95
  678.0 49.3 %collective-permute-start.73 = (bf16[384,2048]{1,0:T(8,128)(2,1)}, bf16[384,2048]{1,0:T(8,128)(2,1)}, u32[]{:S(2)}, u32[]{:S(2)}) collective-permute-start(bf16[384,2048]{1,0:T(8,128)(2,1)} %get-tuple-element.458), channel_id=1, source_target_pairs={{0,4},{4,0},{1,5},{5,1},{2,6},{6,2},{3,7},{7,3},{8,12},{12,8},{9,1... | collective-permute-start | bytes 4718600 | tf_op jit(solution)/shard_map/ppermute | solution.py:91
  678.1 45.7 %collective-permute-start.70 = (bf16[256,2816]{1,0:T(8,128)(2,1)}, bf16[256,2816]{1,0:T(8,128)(2,1)}, u32[]{:S(2)}, u32[]{:S(2)}) collective-permute-start(bf16[256,2816]{1,0:T(8,128)(2,1)} %add_convert_fusion.15), channel_id=1, source_target_pairs={{0,16},{8,24},{16,0},{24,8},{1,17},{9,25},{17,1},{25,9},{2,18},{10... | collective-permute-start | bytes 4325384 | tf_op jit(solution)/shard_map/ppermute | solution.py:99
  745.3 53.2 %collective-permute-start.80 = (bf16[256,1408]{1,0:T(8,128)(2,1)}, bf16[256,1408]{1,0:T(8,128)(2,1)}, u32[]{:S(2)}, u32[]{:S(2)}) collective-permute-start(bf16[256,1408]{1,0:T(8,128)(2,1)} %add_convert_fusion.25), channel_id=1, source_target_pairs={{0,8},{8,0},{16,24},{24,16},{1,9},{9,1},{17,25},{25,17},{2,10},{10... | collective-permute-start | bytes 2162696 | tf_op jit(solution)/shard_map/ppermute | solution.py:95
  746.0 52.5 %collective-permute-start.78 = (bf16[256,1408]{1,0:T(8,128)(2,1)S(1)}, bf16[256,1408]{1,0:T(8,128)(2,1)}, u32[]{:S(2)}, u32[]{:S(2)}) collective-permute-start(bf16[256,1408]{1,0:T(8,128)(2,1)S(1)} %copy-done.35), channel_id=1, source_target_pairs={{0,16},{8,24},{16,0},{24,8},{1,17},{9,25},{17,1},{25,9},{2,18},{10... | collective-permute-start | bytes 2162696 | tf_op jit(solution)/shard_map/ppermute | solution.py:99
  747.1 53.8 %collective-permute-start.81 = (bf16[256,1408]{1,0:T(8,128)(2,1)}, bf16[256,1408]{1,0:T(8,128)(2,1)}, u32[]{:S(2)}, u32[]{:S(2)}) collective-permute-start(bf16[256,1408]{1,0:T(8,128)(2,1)} %add_convert_fusion.24), channel_id=1, source_target_pairs={{0,16},{8,24},{16,0},{24,8},{1,17},{9,25},{17,1},{25,9},{2,18},{10... | collective-permute-start | bytes 2162696 | tf_op jit(solution)/shard_map/ppermute | solution.py:99
  748.0 53.0 %collective-permute-start.79 = (bf16[256,1408]{1,0:T(8,128)(2,1)S(1)}, bf16[256,1408]{1,0:T(8,128)(2,1)}, u32[]{:S(2)}, u32[]{:S(2)}) collective-permute-start(bf16[256,1408]{1,0:T(8,128)(2,1)S(1)} %copy-done.33), channel_id=1, source_target_pairs={{0,8},{8,0},{16,24},{24,16},{1,9},{9,1},{17,25},{25,17},{2,10},{10... | collective-permute-start | bytes 2162696 | tf_op jit(solution)/shard_map/ppermute | solution.py:95
  749.4 54.2 %collective-permute-start.74 = (bf16[256,2816]{1,0:T(8,128)(2,1)}, bf16[256,2816]{1,0:T(8,128)(2,1)}, u32[]{:S(2)}, u32[]{:S(2)}) collective-permute-start(bf16[256,2816]{1,0:T(8,128)(2,1)} %add_convert_fusion.14), channel_id=1, source_target_pairs={{0,4},{4,0},{1,5},{5,1},{2,6},{6,2},{3,7},{7,3},{8,12},{12,8},{9,1... | collective-permute-start | bytes 4325384 | tf_op jit(solution)/shard_map/ppermute | solution.py:91
  832.9 34.7 %collective-permute-start.75 = (bf16[384,2048]{1,0:T(8,128)(2,1)}, bf16[384,2048]{1,0:T(8,128)(2,1)}, u32[]{:S(2)}, u32[]{:S(2)}) collective-permute-start(bf16[384,2048]{1,0:T(8,128)(2,1)} %get-tuple-element.465), channel_id=1, source_target_pairs={{0,4},{4,0},{1,5},{5,1},{2,6},{6,2},{3,7},{7,3},{8,12},{12,8},{9,1... | collective-permute-start | bytes 4718600 | tf_op jit(solution)/shard_map/ppermute | solution.py:91
  874.6 38.3 %collective-permute-start.76 = (bf16[384,2048]{1,0:T(8,128)(2,1)S(1)}, bf16[384,2048]{1,0:T(8,128)(2,1)S(1)}, u32[]{:S(2)}, u32[]{:S(2)}) collective-permute-start(bf16[384,2048]{1,0:T(8,128)(2,1)S(1)} %add_convert_fusion.2), channel_id=1, source_target_pairs={{0,1},{1,2},{2,3},{3,0},{4,5},{5,6},{6,7},{7,4},{8,9},{9,10},{10,1... | collective-permute-start | bytes 4718600 | tf_op jit(solution)/shard_map/ppermute | solution.py:104
  879.1 37.1 %collective-permute-start.91 = (bf16[64,2048]{1,0:T(8,128)(2,1)S(1)}, bf16[64,2048]{1,0:T(8,128)(2,1)S(1)}, u32[]{:S(2)}, u32[]{:S(2)}) collective-permute-start(bf16[64,2048]{1,0:T(8,128)(2,1)S(1)} %copy-done.131), channel_id=1, source_target_pairs={{0,8},{8,0},{16,24},{24,16},{1,9},{9,1},{17,25},{25,17},{2,10},{10... | collective-permute-start | bytes 786440 | tf_op jit(solution)/shard_map/ppermute | solution.py:95
  880.6 35.0 %collective-permute-start.92 = (bf16[3,512,576]{1,2,0:T(8,128)(2,1)S(1)}, bf16[3,512,576]{1,2,0:T(8,128)(2,1)S(1)}, u32[]{:S(2)}, u32[]{:S(2)}) collective-permute-start(bf16[3,512,576]{1,2,0:T(8,128)(2,1)S(1)} %copy-done.95), channel_id=1, source_target_pairs={{0,4},{4,0},{1,5},{5,1},{2,6},{6,2},{3,7},{7,3},{8,12},{12,8},{9,1... | collective-permute-start | bytes 5308424 | tf_op jit(solution)/shard_map/ppermute | solution.py:91
  880.7 35.5 %collective-permute-start.90 = (bf16[64,2048]{1,0:T(8,128)(2,1)S(1)}, bf16[64,2048]{1,0:T(8,128)(2,1)S(1)}, u32[]{:S(2)}, u32[]{:S(2)}) collective-permute-start(bf16[64,2048]{1,0:T(8,128)(2,1)S(1)} %copy-done.130), channel_id=1, source_target_pairs={{0,16},{8,24},{16,0},{24,8},{1,17},{9,25},{17,1},{25,9},{2,18},{10... | collective-permute-start | bytes 786440 | tf_op jit(solution)/shard_map/ppermute | solution.py:99
  924.8 64.1 %collective-permute-start.93 = (bf16[384,2048]{1,0:T(8,128)(2,1)}, bf16[384,2048]{1,0:T(8,128)(2,1)}, u32[]{:S(2)}, u32[]{:S(2)}) collective-permute-start(bf16[384,2048]{1,0:T(8,128)(2,1)} %slice.459), channel_id=1, source_target_pairs={{0,4},{4,0},{1,5},{5,1},{2,6},{6,2},{3,7},{7,3},{8,12},{12,8},{9,1... | collective-permute-start | bytes 4718600 | tf_op jit(solution)/shard_map/ppermute | solution.py:91
  926.0 53.1 %collective-permute-start.107 = (bf16[256,1536]{1,0:T(8,128)(2,1)}, bf16[256,1536]{1,0:T(8,128)(2,1)S(1)}, u32[]{:S(2)}, u32[]{:S(2)}) collective-permute-start(bf16[256,1536]{1,0:T(8,128)(2,1)} %slice.472), channel_id=1, source_target_pairs={{0,8},{8,0},{16,24},{24,16},{1,9},{9,1},{17,25},{25,17},{2,10},{10... | collective-permute-start | bytes 2359304 | tf_op jit(solution)/shard_map/ppermute | solution.py:95
  927.3 51.7 %collective-permute-start.104 = (bf16[256,1536]{1,0:T(8,128)(2,1)}, bf16[256,1536]{1,0:T(8,128)(2,1)}, u32[]{:S(2)}, u32[]{:S(2)}) collective-permute-start(bf16[256,1536]{1,0:T(8,128)(2,1)} %slice.468), channel_id=1, source_target_pairs={{0,16},{8,24},{16,0},{24,8},{1,17},{9,25},{17,1},{25,9},{2,18},{10... | collective-permute-start | bytes 2359304 | tf_op jit(solution)/shard_map/ppermute | solution.py:99
  972.5 40.5 %collective-permute-start.112 = (bf16[512,256]{1,0:T(8,128)(2,1)}, bf16[512,256]{1,0:T(8,128)(2,1)}, u32[]{:S(2)}, u32[]{:S(2)}) collective-permute-start(bf16[512,256]{1,0:T(8,128)(2,1)} %fusion.71), channel_id=1, source_target_pairs={{0,1},{1,2},{2,3},{3,0},{4,5},{5,6},{6,7},{7,4},{8,9},{9,10},{10,1... | collective-permute-start | bytes 786440 | tf_op jit(solution)/shard_map/ppermute | solution.py:104
  979.1 58.5 %collective-permute-start.110 = (bf16[256,1536]{1,0:T(8,128)(2,1)}, bf16[256,1536]{1,0:T(8,128)(2,1)}, u32[]{:S(2)}, u32[]{:S(2)}) collective-permute-start(bf16[256,1536]{1,0:T(8,128)(2,1)} %add_convert_fusion.20), channel_id=1, source_target_pairs={{0,8},{8,0},{16,24},{24,16},{1,9},{9,1},{17,25},{25,17},{2,10},{10... | collective-permute-start | bytes 2359304 | tf_op jit(solution)/shard_map/ppermute | solution.py:95
  980.7 56.9 %collective-permute-start.111 = (bf16[256,1536]{1,0:T(8,128)(2,1)}, bf16[256,1536]{1,0:T(8,128)(2,1)}, u32[]{:S(2)}, u32[]{:S(2)}) collective-permute-start(bf16[256,1536]{1,0:T(8,128)(2,1)} %add_convert_fusion.18), channel_id=1, source_target_pairs={{0,16},{8,24},{16,0},{24,8},{1,17},{9,25},{17,1},{25,9},{2,18},{10... | collective-permute-start | bytes 2359304 | tf_op jit(solution)/shard_map/ppermute | solution.py:99
  1026.6 43.4 %collective-permute-start.125 = (bf16[4,4,64,576]{3,2,1,0:T(8,128)(2,1)}, bf16[4,4,64,576]{3,2,1,0:T(8,128)(2,1)}, u32[]{:S(2)}, u32[]{:S(2)}) collective-permute-start(bf16[4,4,64,576]{3,2,1,0:T(8,128)(2,1)} %bitcast.75), channel_id=1, source_target_pairs={{0,4},{4,0},{1,5},{5,1},{2,6},{6,2},{3,7},{7,3},{8,12},{12,8},{9,1... | collective-permute-start | bytes 3538952 | tf_op jit(solution)/shard_map/ppermute | solution.py:91
  (291 other events, 3698.8 us)
Sparse Core Ops, SparseCore 0:
  11.4 84.8 all-gather.2

commit v3 on v2

--- a/solution.py
+++ b/solution.py
@@ -185,17 +185,17 @@
 
 
 def lay_out_kernel(places, *refs):
-    pieces, (latent, rope) = refs[:-2], refs[-2:]
-    rows = pieces[0].shape[1]
-    for i, piece in enumerate(pieces):
-        at = pl.ds(pl.multiple_of(places[i], rows), rows)
+    given, (latent, rope) = refs[:-2], refs[-2:]
+    micro, rows = latent.shape[0], given[0].shape[1]
+    pieces = [each[i : i + micro] for each in given for i in range(0, each.shape[0], micro)]
+    for place, piece in zip(range(len(pieces)), pieces):
+        at = pl.ds(pl.multiple_of(places[place], rows), rows)
         latent[:, at, :] = piece[:, :, :KVRANK]
         keys = piece[:, :, KVRANK:]
         rope[:, at, :] = jnp.concatenate([keys, keys], axis=-1)
 
 
-def lay_out(places, pieces, length):
-    micro = pieces[0].shape[0]
+def lay_out(places, pieces, micro, length):
     in_vmem = pl.BlockSpec(memory_space=pltpu.VMEM)
     return pl.pallas_call(
         lay_out_kernel,
@@ -213,6 +213,9 @@
         ),
         name="lay_out",
     )(places, *pieces)
+
+
+SENT_BLOCKS = (((3, 0), (2, 0)), ((3, 1), (1, 1)), ((1, 0), (0, 0), (2, 1), (0, 1)))
 
 
 def swap_halves(values, lane):
@@ -277,6 +280,7 @@
     heads,
     width,
     scale,
+    groups,
     place,
     q_ref,
     kv_ref,
@@ -286,17 +290,28 @@
     cos_ref,
     sin_ref,
     do_ref,
-    dq_ref,
-    dkv_ref,
-    dkr_ref,
-    total,
+    norm_ref,
+    latent_ref,
+    wq_ref,
+    wkv_ref,
+    *refs,
 ):
     slots, rows = q_ref.shape[0], q_ref.shape[2]
+    q_width, kv_width = q_ref.shape[3], kv_ref.shape[2]
+    query_outs, expand_outs, latent_outs = refs[:3], refs[3:6], refs[6:8]
+    parts, (total, rope_total, kv_grads, q_grads, expand_grads) = refs[8:-5], refs[-5:]
+    group, m = pl.program_id(0), pl.program_id(1)
+    micro = pl.num_programs(1)
     lane = lax.broadcasted_iota(jnp.int32, (rows, LANES), 1)
-
-    @pl.when(pl.program_id(1) == 0)
+    q_first = pl.multiple_of(group * q_width, LANES)
+    kv_first = pl.multiple_of(group * kv_width, LANES)
+
+    def q_rows(slot):
+        return pl.ds(pl.multiple_of((slot * micro + m) * rows, rows), rows)
+
+    @pl.when(group == 0)
     def _():
-        dkr_ref[...] = jnp.zeros_like(dkr_ref)
+        rope_total[m] = jnp.zeros(rope_total.shape[1:], f32)
 
     total[...] = jnp.zeros_like(total)
     for slot in range(slots):
@@ -327,29 +342,66 @@
             grad_key = dot_lt(grad_scores, query)
             at = head * (NOPE + VHEAD)
             total[window, at : at + NOPE] += grad_key[:, :NOPE]
-            dkr_ref[0, window, :] += grad_key[:, NOPE:]
+            rope_total[m, window, :] += grad_key[:, NOPE:]
             total[window, at + NOPE : at + NOPE + VHEAD] += dot_lt(probs.astype(bf16), grad_mixed)
-            dq_ref[slot, 0, :, head * NOPE : (head + 1) * NOPE] = grad_query[:, :NOPE].astype(bf16)
+            q_grads[q_rows(slot), pl.ds(q_first + head * NOPE, NOPE)] = grad_query[:, :NOPE].astype(
+                bf16
+            )
             if head % 2 == 0:
                 rope_grads = jnp.where(lane < ROPE, grad_query[:, NOPE:], 0.0)
             else:
                 rope_grads = jnp.where(lane < ROPE, rope_grads, grad_query[:, NOPE:])
             if head % 2 == 1 or head == heads - 1:
                 turned = rope_grads * cos_ref[slot, 0] - swap_halves(rope_grads, lane) * sin_ref[slot, 0]
-                first = heads * NOPE + head // 2 * LANES
-                dq_ref[slot, 0, :, first : first + LANES] = turned.astype(bf16)
-    dkv_ref[0] = total[...].astype(bf16)
-
-
-def attention_specs(heads, slots, rows, length, width, q_width):
+                first = q_first + heads * NOPE + head // 2 * LANES
+                q_grads[q_rows(slot), pl.ds(first, LANES)] = turned.astype(bf16)
+    kv_grads[m, :, pl.ds(kv_first, kv_width)] = total[...].astype(bf16)
+
+    @pl.when(m == micro - 1)
+    def _():
+        grads = dot_lt(norm_ref[...], q_grads[:, pl.ds(q_first, q_width)], bf16)
+        size = grads.shape[0] // 8
+        for out, blocks in zip(query_outs, SENT_BLOCKS):
+            for i, (k, half) in enumerate(blocks):
+                out[i * size : (i + 1) * size, :] = grads[(2 * k + half) * size :][:size]
+        back = kv_grads[:, :, pl.ds(kv_first, kv_width)]
+        expand_grads[...] = dot_lt(
+            latent_ref[...], back.reshape(latent_ref.shape[0], kv_width), bf16
+        )
+        size = expand_grads.shape[0] // 8
+        shard = place[slots, 0]
+        for out, blocks in zip(expand_outs, SENT_BLOCKS):
+            for i, (k, half) in enumerate(blocks):
+                at = pl.multiple_of((2 * (shard ^ k) + half) * size, size)
+                out[i * size : (i + 1) * size, :] = expand_grads[pl.ds(at, size), :]
+
+    @pl.when(group == groups - 1)
+    def _():
+        span = latent_outs[0].shape[1]
+        for out, half in zip(latent_outs, (place[slots, 1], 1 - place[slots, 1])):
+            at = pl.ds(pl.multiple_of(half * span, span), span)
+            out[0, :, :KVRANK] = dot_rt(kv_grads[m, at, :], wkv_ref[...], bf16)
+            ropes = rope_total[m, at, :]
+            ropes = ropes + pltpu.roll(ropes, ROPE, 1)
+            out[0, :, KVRANK:] = ropes[:, :ROPE].astype(bf16)
+        for slot, out in enumerate(parts):
+            out[0] = dot_rt(q_grads[q_rows(slot), :], wq_ref[...], bf16)
+
+
+def attention_specs(heads, slots, rows, length, width, q_width, order):
+    def at(*index):
+        return lambda a, b, place: tuple(
+            {"m": (a, b)[order], "j": (a, b)[1 - order]}.get(i, i) for i in index
+        )
+
     return [
-        pl.BlockSpec((slots, 1, rows, q_width), lambda m, j, place: (0, m, 0, j)),
-        pl.BlockSpec((1, length, heads * (NOPE + VHEAD)), lambda m, j, place: (m, 0, j)),
-        pl.BlockSpec((1, length, LANES), lambda m, j, place: (m, 0, 0)),
-        pl.BlockSpec((1, slots * rows, 1), lambda m, j, place: (m, 0, 0)),
-        pl.BlockSpec((1, slots, width), lambda m, j, place: (m, 0, 0)),
-        pl.BlockSpec((slots, 1, rows, LANES), lambda m, j, place: (0, m, 0, 0)),
-        pl.BlockSpec((slots, 1, rows, LANES), lambda m, j, place: (0, m, 0, 0)),
+        pl.BlockSpec((slots, 1, rows, q_width), at(0, "m", 0, "j")),
+        pl.BlockSpec((1, length, heads * (NOPE + VHEAD)), at("m", 0, "j")),
+        pl.BlockSpec((1, length, LANES), at("m", 0, 0)),
+        pl.BlockSpec((1, slots * rows, 1), at("m", 0, 0)),
+        pl.BlockSpec((1, slots, width), at("m", 0, 0)),
+        pl.BlockSpec((slots, 1, rows, LANES), at(0, "m", 0, 0)),
+        pl.BlockSpec((slots, 1, rows, LANES), at(0, "m", 0, 0)),
     ]
 
 
@@ -362,7 +414,7 @@
         grid_spec=pltpu.PrefetchScalarGridSpec(
             num_scalar_prefetch=1,
             grid=(micro, groups),
-            in_specs=attention_specs(heads, slots, rows, length, width, q_all // groups),
+            in_specs=attention_specs(heads, slots, rows, length, width, q_all // groups, 0),
             out_specs=pl.BlockSpec(
                 (slots, 1, rows, heads * VHEAD), lambda m, j, place: (0, m, 0, j)
             ),
@@ -380,41 +432,103 @@
 
 
 def attend_back(
-    heads, groups, width, scale, place, q_lin, kv, rope_keys, seg_query, seg_key, cos, sin, d_o
+    heads,
+    groups,
+    width,
+    scale,
+    place,
+    q_lin,
+    kv,
+    rope_keys,
+    seg_query,
+    seg_key,
+    cos,
+    sin,
+    d_o,
+    normed,
+    latents,
+    w_query,
+    w_expand,
 ):
     slots, micro, rows, q_all = q_lin.shape
     length = kv.shape[1]
-    q_width = q_all // groups
-    kv_width = heads * (NOPE + VHEAD)
+    tokens, model = normed.shape
+    q_width, kv_width = q_all // groups, kv.shape[2] // groups
+    latent_width = KVRANK + ROPE
+
+    def last(j, m, place):
+        return (jnp.where(j == groups - 1, m, 0), 0, 0)
+
+    def whole(shape):
+        return pl.BlockSpec(shape, lambda j, m, place: (0, 0), pipeline_mode=pl.Buffered(1))
+
+    def sent(total, columns):
+        return [
+            (jax.ShapeDtypeStruct((n * total // 8, columns * groups), bf16), n * total // 8, columns)
+            for n in (2, 2, 4)
+        ]
+
+    grads = sent(model, q_width) + sent(KVRANK, kv_width)
     return pl.pallas_call(
-        functools.partial(attend_back_kernel, heads, width, scale),
-        out_shape=(
-            jax.ShapeDtypeStruct(q_lin.shape, bf16),
-            jax.ShapeDtypeStruct(kv.shape, bf16),
-            jax.ShapeDtypeStruct((micro, length, LANES), f32),
-        ),
+        functools.partial(attend_back_kernel, heads, width, scale, groups),
+        out_shape=[
+            *(shape for shape, _, _ in grads),
+            *[jax.ShapeDtypeStruct((micro, length // 2, latent_width), bf16)] * 2,
+            *[jax.ShapeDtypeStruct((micro, rows, model), bf16)] * slots,
+        ],
         grid_spec=pltpu.PrefetchScalarGridSpec(
             num_scalar_prefetch=1,
-            grid=(micro, groups),
-            in_specs=attention_specs(heads, slots, rows, length, width, q_width)
-            + [pl.BlockSpec((slots, 1, rows, heads * VHEAD), lambda m, j, place: (0, m, 0, j))],
+            grid=(groups, micro),
+            in_specs=attention_specs(heads, slots, rows, length, width, q_width, 1)
+            + [
+                pl.BlockSpec((slots, 1, rows, heads * VHEAD), lambda j, m, place: (0, m, 0, j)),
+                whole(normed.shape),
+                whole(latents.shape),
+                whole(w_query.shape),
+                whole(w_expand.shape),
+            ],
             out_specs=[
-                pl.BlockSpec((slots, 1, rows, q_width), lambda m, j, place: (0, m, 0, j)),
-                pl.BlockSpec((1, length, kv_width), lambda m, j, place: (m, 0, j)),
-                pl.BlockSpec((1, length, LANES), lambda m, j, place: (m, 0, 0)),
+                *(
+                    pl.BlockSpec((height, columns), lambda j, m, place: (0, j))
+                    for _, height, columns in grads
+                ),
+                *[pl.BlockSpec((1, length // 2, latent_width), last)] * 2,
+                *[pl.BlockSpec((1, rows, model), last)] * slots,
             ],
-            scratch_shapes=[pltpu.VMEM((length, kv_width), f32)],
+            scratch_shapes=[
+                pltpu.VMEM((length, kv_width), f32),
+                pltpu.VMEM((micro, length, LANES), f32),
+                pltpu.VMEM(kv.shape, bf16),
+                pltpu.VMEM((tokens, q_all), bf16),
+                pltpu.VMEM((KVRANK, kv_width), bf16),
+            ],
         ),
         compiler_params=pltpu.CompilerParams(
-            dimension_semantics=("arbitrary", "arbitrary"), vmem_limit_bytes=40 << 20
+            dimension_semantics=("arbitrary", "arbitrary"), vmem_limit_bytes=60 << 20
         ),
         cost_estimate=pl.CostEstimate(
-            flops=2 * slots * rows * micro * groups * heads * width * 1024,
+            flops=2 * slots * rows * micro * groups * heads * width * 1024
+            + 4 * tokens * model * q_all
+            + 4 * micro * length * KVRANK * kv.shape[2],
             transcendentals=slots * rows * micro * groups * heads * width,
-            bytes_accessed=4 * kv.size + 8 * q_lin.size,
+            bytes_accessed=2 * kv.size + 4 * q_lin.size + 8 * w_query.size,
         ),
         name="attend_back",
-    )(place, q_lin, kv, rope_keys, seg_query, seg_key, cos, sin, d_o)
+    )(
+        place,
+        q_lin,
+        kv,
+        rope_keys,
+        seg_query,
+        seg_key,
+        cos,
+        sin,
+        d_o,
+        normed,
+        latents,
+        w_query,
+        w_expand,
+    )
 
 
 def spans(total, step):
@@ -591,12 +705,18 @@
     )(place, gate, up, down)
 
 
-def weight_grad_kernel(blocks, place, left, right_ref, *refs):
-    outs, (turned, buffer, sems) = refs[:-3], refs[-3:]
-    slice_rows, tokens = outs[0].shape[0], turned.shape[1]
+def weight_grad_kernel(packs, place, left, right_ref, *refs):
+    packed, (turned, buffer, sems) = refs[:-3], refs[-3:]
+    slice_rows, tokens = packed[0].shape[0] // len(packs[0]), turned.shape[1]
+    blocks = [block for pack in packs for block in pack]
+    outs = [
+        out.at[pl.ds(i * slice_rows, slice_rows)]
+        for out, pack in zip(packed, packs)
+        for i in range(len(pack))
+    ]
 
     def fetch(i):
-        half, k = blocks[i]
+        k, half = blocks[i]
         core = place[0] if half == 0 else 1 - place[0]
         start = pl.multiple_of((2 * k + core) * slice_rows, slice_rows)
         return pltpu.make_async_copy(
@@ -625,12 +745,13 @@
             outs[half + i][...] = grads[i * slice_rows : (i + 1) * slice_rows]
 
 
-def weight_grad(place, blocks, slice_rows, left, right):
+def weight_grad(place, packs, slice_rows, left, right):
     tokens, columns = right.shape
-    count = len(blocks)
+    count = sum(len(pack) for pack in packs)
+    heights = [len(pack) * slice_rows for pack in packs]
     return pl.pallas_call(
-        functools.partial(weight_grad_kernel, blocks),
-        out_shape=[jax.ShapeDtypeStruct((slice_rows, columns), bf16)] * count,
+        functools.partial(weight_grad_kernel, packs),
+        out_shape=[jax.ShapeDtypeStruct((height, columns), bf16) for height in heights],
         grid_spec=pltpu.PrefetchScalarGridSpec(
             num_scalar_prefetch=1,
             grid=(-(-columns // 256),),
@@ -638,7 +759,7 @@
                 pl.BlockSpec(memory_space=pl.ANY),
                 pl.BlockSpec((tokens, 256), lambda n, place: (0, n)),
             ],
-            out_specs=[pl.BlockSpec((slice_rows, 256), lambda n, place: (0, n))] * count,
+            out_specs=[pl.BlockSpec((height, 256), lambda n, place: (0, n)) for height in heights],
             scratch_shapes=[
                 pltpu.VMEM((count * slice_rows, tokens), bf16),
                 pltpu.VMEM((2, tokens, slice_rows), bf16),
@@ -827,16 +948,20 @@
         return arrived
 
     close(*attention_round())
+    arrived = attention_round()
     hid_a, hid_other, down_a, down_other = pack(
         now(shift), part, gate_weight, up_weight, down_weight
     )
+    down_b, hid_b = to_core(down_other), to_core(hid_other)
     grad_own = features(now(cotangent).reshape(own, width))
     inputs16 = features(now(hidden).reshape(own, width))
     inputs = inputs16.astype(f32)
     seg_all = now(segments)[:, 0]
     bases = [core * span + place_z * rows, (1 - core) * span + place_z * rows][:slots]
     starts = [jnp.maximum(base + rows - window, 0) for base in bases]
-    place = jnp.stack([jnp.stack([a, b]) for a, b in zip(starts, bases)]).astype(jnp.int32)
+    place = jnp.stack(
+        [jnp.stack([a, b]) for a, b in zip(starts + [shard], bases + [core])]
+    ).astype(jnp.int32)
     seg_query = jnp.concatenate(
         [lax.dynamic_slice_in_dim(seg_all, base, rows, 1) for base in bases], axis=1
     )
@@ -856,15 +981,14 @@
     sin_own = sin_rows[0].reshape(own, ROPE // 2)
     cos_lanes = jnp.concatenate([cos_rows] * 4, axis=-1)
     sin_lanes = jnp.concatenate([-sin_rows, sin_rows] * 2, axis=-1)
-    attention = (heads, tp_size, window, scale, place)
     tables = (seg_query[..., None], seg_key, cos_lanes, sin_lanes)
 
-    close(*attention_round(), hid_a, grad_own, inputs16)
-    for _ in range(tp_size - 3):
+    close(*arrived, down_b, hid_b, grad_own, inputs16)
+    while len(attn_z) < tp_size - 1:
         close(*attention_round())
-    half_own = own // 2
-    grad_half = send(line_z, step_z, grad_own[:half_own])
-    hid_b = send(line_c, swap_core, hid_other)
+    arrived = attention_round()
+    down_a1 = send(line_x, swap_x, down_a, free=True)
+    down_b2 = send(line_y, swap_y, down_b, free=True)
     factor_one = norm_scale(now(inputs))
     normed_own = (inputs * factor_one * gain_one).astype(bf16)
     latent_raw = dot(normed_own, w_latent)
@@ -873,28 +997,42 @@
     latent_own = (latent_part * factor_latent * gain_kv).astype(bf16)
     rope_own = rotate(latent_raw[:, KVRANK:], cos_own, sin_own).astype(bf16)
     latent_pack = jnp.concatenate([latent_own, rope_own], axis=1).reshape(micro, rows, kv_cols)
-    close(*attention_round(), latent_pack, grad_half, hid_b)
+    close(*arrived, down_a1, down_b2, latent_pack)
+    latent_z, grad_z = [latent_pack], [grad_own]
+
+    def latents_ahead():
+        if len(latent_z) < tp_size:
+            latent_z.append(send(line_z, step_z, latent_z[-1]))
+        return latent_z[-1]
+
+    def grads_ahead(count):
+        for _ in range(count):
+            grad_z.append(send(line_z, step_z, grad_z[-1]))
+
+    arrived = attention_round()
+    down_b1 = send(line_x, swap_x, down_b, free=True)
+    down_a2 = send(line_y, swap_y, down_a, free=True)
+    close(*arrived, down_b1, down_a2, latents_ahead())
+    arrived = attention_round()
+    down_b3 = send(line_x, swap_x, down_b2, free=True)
+    down_a3 = send(line_y, swap_y, down_a1, free=True)
+    close(*arrived, down_b3, down_a3, latents_ahead())
+    while len(wanted) > 2:
+        close(*attention_round(), latents_ahead())
+    arrived = attention_round()
     normed_chip = normed_own
     if split:
         normed_chip = jnp.concatenate([normed_own, send(line_c, swap_core, normed_own)])
-    down_b = send(line_c, swap_core, down_other)
-    grad_half = jnp.concatenate([grad_half, send(line_z, step_z, grad_own[half_own:])])
-    grad_z = [grad_own, grad_half]
-    while len(wanted) > 2:
-        close(*attention_round(), normed_chip, grad_half, down_b)
-    latent_z, latent_far = [latent_pack], [send(line_c, swap_core, latent_pack)]
-
-    def latents_ahead(count):
-        for _ in range(count):
-            latent_z.append(send(line_z, step_z, latent_z[-1]))
-            latent_far.append(to_core(latent_z[-1]))
-
-    latents_ahead(2)
-    close(*attention_round(), latent_z[-1], latent_far[0])
+    half_tp = tp_size // 2
+    latent_far = [send(line_c, swap_core, jnp.concatenate(latent_z[:half_tp]))]
+    while len(latent_z) < tp_size:
+        latents_ahead()
+    close(*arrived, normed_chip, latent_far[0], latent_z[-1])
     attn_xy = [[held[j, k] for k in range(4)] for j in range(tp_size)]
 
     hid_a1, hid_b2 = send(line_x, swap_x, hid_a), send(line_y, swap_y, hid_b)
-    latents_ahead(tp_size - 3)
+    grads_ahead(1)
+    latent_far.append(send(line_c, swap_core, jnp.concatenate(latent_z[half_tp:])))
     q_cols, out_cols = q_width, q_width + out_width
 
     def core_row(k, half):
@@ -942,34 +1080,29 @@
         now(shift),
     )
     q_lin = dot(normed_chip, w_query).reshape(slots, micro, rows, tp_size * q_width)
-    close(hid_a1, hid_b2, latent_z[-1], q_lin)
-
-    hid_b1, hid_a2 = send(line_x, swap_x, hid_b), send(line_y, swap_y, hid_a)
-    more = (tp_size - 2) // 2
-
-    def grads_ahead(count):
-        for _ in range(count):
-            grad_z.append(send(line_z, step_z, grad_z[-1]))
-
     latent_rows = [
         [(at * span + (place_z - j) % tp_size * rows) for j in range(tp_size)]
         for at in (core, 1 - core)
     ]
     latent_all, rope_keys = lay_out(
         jnp.stack([row for each in latent_rows for row in each]).astype(jnp.int32),
-        [now(piece) for piece in latent_z + latent_far],
+        latent_z + latent_far,
+        micro,
         length,
     )
     latent_all = latent_all.reshape(micro * length, KVRANK)
+    kv_all = dot(latent_all, w_expand, bf16).reshape(micro, length, tp_size * kv_width)
+    close(hid_a1, hid_b2, grad_z[-1], q_lin, kv_all)
+
+    hid_b1, hid_a2 = send(line_x, swap_x, hid_b), send(line_y, swap_y, hid_a)
+    more = tp_size - 3
     grads_ahead(more)
-    kv_all = dot(latent_all, w_expand, bf16).reshape(micro, length, tp_size * kv_width)
-    mixed = attend(*attention, q_lin, kv_all, rope_keys, *tables)
+    grad_far = [send(line_c, swap_core, piece, free=True) for piece in grad_z[:2]]
+    mixed = attend(heads, tp_size, window, scale, now(place), q_lin, kv_all, rope_keys, *tables)
     mixed = mixed.reshape(slots * own, tp_size * out_width)
-    grad_far = [to_core(grad_z[0])]
-    close(hid_b1, hid_a2, grad_z[-1], grad_far[-1], mixed)
+    close(hid_b1, hid_a2, grad_z[-1], *grad_far, mixed)
 
     hid_b3, hid_a3 = send(line_x, swap_x, hid_b2), send(line_y, swap_y, hid_a1)
-    grads_ahead(tp_size - 2 - more)
     mixed = now(mixed)
     if split:
         mixed_out = dot_rt(mixed, w_out, bf16)
@@ -978,18 +1111,11 @@
         middle = inputs + dot_rt(mixed, w_out)
     factor_two = norm_scale(middle)
     normed_two = (middle * factor_two * gain_two).astype(bf16)
-    grad_far.append(send(line_c, swap_core, grad_z[1]))
-    close(hid_b3, hid_a3, grad_z[-1], grad_far[-1], normed_two)
-
-    down_a1, down_b2 = send(line_x, swap_x, down_a), send(line_y, swap_y, down_b)
-    down_b1 = send(line_x, swap_x, down_b, free=True)
-    down_a2 = send(line_y, swap_y, down_a, free=True)
-    down_b3, down_a3 = send(line_x, swap_x, down_b2), send(line_y, swap_y, down_a1)
     norm_z = [normed_two, send(line_z, step_z, normed_two)]
     norm_far = [send(line_c, swap_core, normed_two)]
     for piece in grad_z[2:]:
-        grad_far.append(send(line_c, swap_core, piece, free=True))
-    close(down_b3, down_a3, norm_z[-1], norm_far[-1], grad_far[-1])
+        grad_far.append(send(line_c, swap_core, piece))
+    close(hid_b3, hid_a3, norm_z[-1], *norm_far, *grad_far[2:])
 
     hidden_pieces = [hid_a, hid_a1, hid_a2, hid_a3, hid_b, hid_b1, hid_b2, hid_b3]
     down_pieces = [down_a, down_a1, down_a2, down_a3, down_b, down_b1, down_b2, down_b3]
@@ -1026,11 +1152,16 @@
         if len(norm_z) < tp_size:
             norm_z.append(send(line_z, step_z, norm_z[-1]))
             arrived.append(norm_z[-1])
+        elif len(grad_z) < tp_size:
+            grads_ahead(1 if j + 2 < tp_size else tp_size - len(grad_z))
+            arrived.append(grad_z[-1])
         elif back_ring.at + 1 < len(back_parts):
             arrived += back_ring.step()
         if j + 1 < tp_size:
             norm_far.append(send(line_c, swap_core, norm_z[j + 1]))
             arrived.append(norm_far[-1])
+        while len(grad_far) <= j:
+            grad_far.append(send(line_c, swap_core, grad_z[len(grad_far)], free=True))
         made = feed(
             now(shift),
             j,
@@ -1046,45 +1177,32 @@
         close(*arrived, made[0])
     act_all, hidden_all, normed_all, grad_all = whole
 
-    first, second = ((0, 3), (0, 2), (1, 3), (1, 1)), ((0, 1), (0, 0), (1, 2), (1, 0))
+    first, second = ((3, 0), (2, 0), (3, 1), (1, 1)), ((1, 0), (0, 0), (2, 1), (0, 1))
+    arrived = back_ring.step()
+    down_y, down_x, down_kept = weight_grad(
+        now(shift), SENT_BLOCKS, slice_rows, grad_all, act_all
+    )
+    close(*arrived, down_y)
+
+    down_y, down_x = send(line_y, swap_y, down_y), send(line_x, swap_x, down_x)
     arrived = []
     while back_ring.at < tp_size - 1:
         arrived += back_ring.step()
-    hid_grads = dict(
-        zip(first, weight_grad(now(shift), first, slice_rows, normed_all, hidden_all))
-    )
+    back_ring.block(0)
+    own3, own2, far3, far1 = weight_grad(
+        now(shift), [(block,) for block in first], slice_rows, normed_all, hidden_all
+    )
+    close(*arrived, down_y, down_x, own3)
+
+    own3, far3 = send(line_y, swap_y, own3), send(line_x, swap_x, far3)
+    arrived = out_ring.step()
     grad_normed_two = back_ring.result()
-    close(*arrived, hid_grads[first[0]], grad_normed_two)
-
-    half_ring = (tp_size - 1) // 2
-    own3 = send(line_y, swap_y, hid_grads[0, 3])
-    far3 = send(line_x, swap_x, hid_grads[1, 3])
-    arrived = [own3, far3]
-    for _ in range(half_ring):
-        arrived += out_ring.step()
-    hid_grads.update(
-        zip(second, weight_grad(now(shift), second, slice_rows, normed_all, hidden_all))
-    )
-    close(*arrived, hid_grads[second[0]])
-
-    own2 = send(line_y, swap_y, hid_grads[0, 2])
-    far1 = send(line_x, swap_x, hid_grads[1, 1])
-    arrived = [own2, far1]
-    for _ in range(half_ring):
-        arrived += out_ring.step()
-    blocks = first + second
-    down_grads = dict(
-        zip(blocks, weight_grad(now(shift), blocks, slice_rows, grad_all, act_all))
-    )
-    own1, far2 = add16(hid_grads[0, 1], own3), add16(hid_grads[1, 2], far3)
-    close(*arrived, down_grads[blocks[0]], own1, far2)
-
-    own1, far2 = send(line_x, swap_x, own1), send(line_y, swap_y, far2)
-    down3 = send(line_y, swap_y, down_grads[0, 3], free=True)
-    downf3 = send(line_x, swap_x, down_grads[1, 3], free=True)
-    arrived = [own1, far2, down3, downf3]
-    hid_own = add16(hid_grads[0, 0], own2, own1)
-    hid_other = add16(hid_grads[1, 0], far1, far2)
+    own1, own0, far2, far0 = weight_grad(
+        now(shift), [(block,) for block in second], slice_rows, normed_all, hidden_all
+    )
+    close(*arrived, own3, far3, own1)
+
+    own2, far1 = send(line_y, swap_y, own2), send(line_x, swap_x, far1)
 
     grad_mid_norm, grad_gain_two = norm_back(middle, factor_two, gain_two, now(grad_normed_two))
     grad_middle = grad_own.astype(f32) + grad_mid_norm
@@ -1093,16 +1211,45 @@
         grad_attn = jnp.concatenate([grad_attn, to_core(grad_attn)])
     grad_mixed = dot(grad_attn, w_out, bf16)
     out_blocks = [dot_lt(columns(grad_attn, k), mixed, bf16) for k in range(4)]
-    down1, downf2 = add16(down_grads[0, 1], down3), add16(down_grads[1, 2], downf3)
-    close(*arrived, grad_mixed, down1, downf2, *out_blocks)
-
-    down2 = send(line_y, swap_y, down_grads[0, 2])
-    downf1 = send(line_x, swap_x, down_grads[1, 1])
-    down1 = send(line_x, swap_x, down1, free=True)
-    downf2 = send(line_y, swap_y, downf2, free=True)
-    hid_far = send(line_c, swap_core, hid_other)
-    output = (middle + out_ring.result()).astype(bf16)
-    grad_qlin, grad_kv, grad_ropes = attend_back(
+    close(own2, far1, grad_mixed, *out_blocks)
+
+    def cut(value):
+        middle_row = value.shape[0] // 2
+        return value[:middle_row], value[middle_row:]
+
+    def block_of(blocks, k, half):
+        return cut(blocks[k])[half]
+
+    def sent_of(blocks):
+        return [jnp.concatenate([block_of(blocks, *at) for at in pair]) for pair in SENT_BLOCKS[:2]]
+
+    def kept_of(blocks):
+        return jnp.concatenate([block_of(blocks, *at) for at in SENT_BLOCKS[2]])
+
+    def stage_one(over_y, over_x):
+        return send(line_y, swap_y, over_y, free=True), send(line_x, swap_x, over_x, free=True)
+
+    def stage_two(kept, sent):
+        (top1, top0), (low2, low0) = (cut(each) for each in cut(kept))
+        (top3, top2), (low3, low1) = cut(now(sent[0])), cut(now(sent[1]))
+        top1 = send(line_x, swap_x, add16(top1, top3), free=True)
+        low2 = send(line_y, swap_y, add16(low2, low3), free=True)
+        return (top0, top2, top1), (low0, low1, low2)
+
+    def stage_sum(tops, lows):
+        return jnp.concatenate([add16(*tops), add16(*lows)])
+
+    (down3, down2), (downf3, downf1) = cut(down_y), cut(down_x)
+    (down1, down0), (downf2, downf0) = (cut(each) for each in cut(down_kept))
+    over_x = send(
+        line_x, swap_x, jnp.concatenate([add16(own1, now(own3)), add16(down1, down3)], axis=1)
+    )
+    over_y = send(
+        line_y, swap_y, jnp.concatenate([add16(far2, now(far3)), add16(downf2, downf3)], axis=1)
+    )
+    arrived = out_ring.step()
+    out_sent = stage_one(*sent_of(out_blocks))
+    made = attend_back(
         heads,
         tp_size,
         window,
@@ -1113,79 +1260,53 @@
         rope_keys,
         *tables,
         grad_mixed.reshape(slots, micro, rows, tp_size * out_width),
-    )
-    grad_qlin = grad_qlin.reshape(slots * own, tp_size * q_width)
-    grad_kv = grad_kv.reshape(micro * length, tp_size * kv_width)
-    close(down2, downf1, down1, downf2, hid_far, grad_ropes)
-
-    def stage_one(blocks):
-        middle_row = blocks[0].shape[0] // 2
-        top, low = zip(*((each[:middle_row], each[middle_row:]) for each in blocks))
-        return (
-            top,
-            low,
-            send(line_y, swap_y, top[3], free=True),
-            send(line_x, swap_x, low[3], free=True),
-            send(line_y, swap_y, top[2], free=True),
-            send(line_x, swap_x, low[1], free=True),
-        )
-
-    def stage_two(top, low, top3, low3, top2, low1):
-        top1 = send(line_x, swap_x, add16(top[1], top3), free=True)
-        low2 = send(line_y, swap_y, add16(low[2], low3), free=True)
-        return top, low, top2, low1, top1, low2
-
-    def stage_sum(top, low, top2, low1, top1, low2):
-        return jnp.concatenate([add16(top[0], top2, top1), add16(low[0], low1, low2)])
-
-    out_stage = stage_one(out_blocks)
-    latent_block = KVRANK // 4
-    kv_now = now(grad_kv)
-    expand_blocks = [
-        dot_lt(
-            lax.dynamic_slice_in_dim(latent_all, (shard ^ k) * latent_block, latent_block, 1),
-            kv_now,
-            bf16,
-        )
-        for k in range(4)
-    ]
-    grad_latent = jnp.concatenate(
-        [
-            dot_rt(kv_now, w_expand, bf16).reshape(micro, length, KVRANK),
-            (grad_ropes[..., :ROPE] + grad_ropes[..., ROPE:]).astype(bf16),
-        ],
-        axis=-1,
-    ).reshape(micro, cores, span, kv_cols)
-    close(*out_stage[2:], grad_latent, *expand_blocks)
-
-    out_stage = stage_two(*out_stage)
-    expand_stage = stage_one(expand_blocks)
-    latent_sum = add16(mine(grad_latent, 1), send(line_c, swap_core, others(grad_latent, 1)))
-    qlin_now = now(grad_qlin)
-    query_blocks = [dot_lt(columns(normed_chip, k), qlin_now, bf16) for k in range(4)]
-    close(*out_stage[4:], *expand_stage[2:], latent_sum, *query_blocks)
-
-    query_stage = stage_one(query_blocks)
-    expand_stage = stage_two(*expand_stage)
-    grad_latent_own = scatter_z(
-        line_z,
-        lambda j: lax.dynamic_slice_in_dim(
-            now(latent_sum), (place_z - j) % tp_size * rows, rows, 1
-        ),
-        f32,
-    ).reshape(own, kv_cols)
-    out_back = stage_sum(*out_stage)
+        normed_chip,
+        latent_all,
+        w_query,
+        w_expand,
+    )
+    sums, (latent_mine, latent_others), parts = made[:6], made[6:8], made[8:]
+    close(over_x, over_y, *arrived, *out_sent, sums[0])
+
+    query_sent = stage_one(*sums[:2])
+    latent_far = send(line_c, swap_core, latent_others)
+    arrived = []
+    while out_ring.at < tp_size - 1:
+        arrived += out_ring.step()
+    close(*query_sent, *arrived, latent_far)
+
+    latent_sum = add16(latent_mine, now(latent_far))
+
+    def latent_block(j):
+        return lax.dynamic_slice_in_dim(latent_sum, (place_z - j) % tp_size * rows, rows, 1)
+
+    latent_step = send(line_z, step_z, latent_block(1))
+    out_sums = stage_two(kept_of(out_blocks), out_sent)
+    grad_normed_one = parts[0].reshape(own, width).astype(f32)
     if split:
-        query_part = dot_rt(now(grad_qlin), w_query, bf16)
-        grad_normed_one = query_part[:own].astype(f32) + to_core(query_part[own:]).astype(f32)
-    else:
-        grad_normed_one = dot_rt(now(grad_qlin), w_query)
-    close(*query_stage[2:], *expand_stage[4:], grad_latent_own)
-
-    query_stage = stage_two(*query_stage)
-    down_own = add16(down_grads[0, 0], down2, down1)
-    down_other = add16(down_grads[1, 0], downf1, downf2)
-    down_far = to_core(down_other)
+        far = send(line_c, swap_core, parts[1].reshape(own, width), free=True)
+        grad_normed_one = grad_normed_one + far.astype(f32)
+    close(latent_step, out_sums[0][2], out_sums[1][2])
+
+    for j in range(2, tp_size - 1):
+        latent_step = send(line_z, step_z, add16(now(latent_step), latent_block(j)))
+    expand_sent = stage_one(*sums[3:5])
+    close(latent_step, *expand_sent)
+
+    latent_step = send(line_z, step_z, add16(now(latent_step), latent_block(tp_size - 1)))
+    query_sums = stage_two(sums[2], query_sent)
+    close(latent_step, query_sums[0][2], query_sums[1][2])
+
+    expand_sums = stage_two(sums[5], expand_sent)
+    grad_latent_own = (now(latent_step).astype(f32) + latent_block(0).astype(f32)).reshape(
+        own, kv_cols
+    )
+    output = (middle + out_ring.result()).astype(bf16)
+    hid_own = add16(own0, own2, over_x[:, : 2 * part])
+    hid_other = add16(far0, far1, over_y[:, : 2 * part])
+    down_own = add16(down0, down2, over_x[:, 2 * part :])
+    down_other = add16(downf0, downf1, over_y[:, 2 * part :])
+    hid_far, down_far = to_core(hid_other), to_core(down_other)
     grad_wgate, grad_wup, grad_wdown = (
         in_order(core, near, far, 1)[:, :hidden_here].astype(f32)
         for near, far in (
@@ -1196,11 +1317,12 @@
     )
     grad_wdown = grad_wdown.T
 
-    out_here = scatter_z(line_z, lambda j: out_back[:, out_width * j : out_width * (j + 1)])
-    expand_back = stage_sum(*expand_stage)
-    expand_here = scatter_z(line_z, lambda j: expand_back[:, kv_width * j : kv_width * (j + 1)])
-    query_back = stage_sum(*query_stage)
-    query_here = scatter_z(line_z, lambda j: query_back[:, q_width * j : q_width * (j + 1)])
+    def over_z(value, columns):
+        return scatter_z(Line(), lambda j: value[:, columns * j : columns * (j + 1)])
+
+    out_here = over_z(stage_sum(*out_sums), out_width)
+    query_here = over_z(stage_sum(*query_sums), q_width)
+    expand_here = over_z(stage_sum(*expand_sums), kv_width)
     out_cores = out_here.reshape(cores, slice_rows, out_width)
     query_cores = query_here.reshape(cores, slice_rows, q_width)
     expand_cores = expand_here.reshape(cores, expand_rows, kv_width)

time: 1110 us -> 1060 us (0.955)
  matrix products: 91.7 us -> 46.3 us
  waiting for transfers between devices: 364 us -> 322 us
  Pallas kernels: 349 us -> 386 us
    ppermute x27 -> x22, waiting for transfers between devices: 98 us -> 46.3 us  [swap_y(): return lax.ppermute(value, 'shard', [(i, i ^ 2) for i in range(4)])]
    pallas_call x4, Pallas kernels: 140 us -> 176 us  [the longest x3 93.8 us: weight_grad(): pl.pallas_call(functools.partial(weight_grad_kernel, packs), out_shape=[j...]
    dot_general x14 -> x6, matrix products: 36.6 us -> 10.7 us  [dot_lt(): lax.dot_general(left, right, (((0,), (0,)), ((), ())), preferred_element_...]
    dot_general x4 -> x2, matrix products: 27.1 us -> 8.04 us  [dot_rt(): lax.dot_general(left, right, (((1,), (1,)), ((), ())), preferred_element_...]
    ppermute x31 -> x30, waiting for transfers between devices: 160 us -> 145 us  [step_z(): return lax.ppermute(value, 'tp', [(i, (i + 1) % size) for i in range(size)])]
    ppermute x31 -> x30, starting transfers between devices: 10.6 us -> 23.5 us  [step_z(): return lax.ppermute(value, 'tp', [(i, (i + 1) % size) for i in range(size)])]
    slice x11 -> x5, local copies, waits for them, and re-layouts: 13 us -> 0.26 us  [cut(): return (value[:middle_row], value[middle_row:])]
    optimization_barrier x0 -> x4, local copies, waits for them, and re-layouts: none -> 12.2 us  [after(): return lax.optimization_barrier((value, *others))[0]]
  transfers between devices with their start and end apart: 133 -> 120, of which waited for: 62 -> 55; matrix products, arithmetic and copies ran while one was open for 19% -> 18% of each run, Pallas kernels for 32% -> 37%
where the time goes in v3:
time: 1060 us; the launch traced here: 1050 us
  Pallas kernels  386 us (36%)
  waiting for transfers between devices  322 us (30%)
  other arithmetic  99.2 us (9%)
  local copies, waits for them, and re-layouts  93.1 us (9%)
  starting transfers between devices  85.1 us (8%)
  matrix products  46.3 us (4%)
  between operations  17.1 us (2%)
    pallas_call x4, Pallas kernels, feed(): pl.pallas_call(functools.partial(feed_kernel, part, rows, offset), out_sh...  161 us
    ppermute x30, waiting for transfers between devices, step_z(): return lax.ppermute(value, 'tp', [(i, (i + 1) % size) for i in range(size)])  145 us
    pallas_call x3, Pallas kernels, weight_grad(): pl.pallas_call(functools.partial(weight_grad_kernel, packs), out_shape=[j...  93.8 us
    ppermute x22, waiting for transfers between devices, swap_x(): return lax.ppermute(value, 'shard', [(i, i ^ 1) for i in range(4)])  92.9 us
    pallas_call x1, Pallas kernels, attend_back(): pl.pallas_call(functools.partial(attend_back_kernel, heads, width, scale,...  82.6 us
    ppermute x22, waiting for transfers between devices, swap_y(): return lax.ppermute(value, 'shard', [(i, i ^ 2) for i in range(4)])  46.3 us
    convert_element_type x29, other arithmetic, add16(): return total.astype(bf16)  41.7 us
    unnamed x308, local copies, waits for them, and re-layouts  30.6 us
  transfers between devices with their start and end apart: 120, of which 55 were waited for; matrix products, arithmetic and copies ran while one was open for 18% of the time, Pallas kernels for 37%

profile of v3, /device:TPU:0, one launch (start us, length us, event | category | flops | bytes accessed | tf_op | source)
XLA Modules:
  0.0 1049.1 jit_solution(18208092113586600859)
XLA Ops:
  24.3 11.1 %collective-permute-done.1.refs_1_ = bf16[512,768]{1,0:T(8,128)(2,1)S(1)} collective-permute-done((bf16[512,768]{1,0:T(8,128)(2,1)S(1)}, bf16[512,768]{1,0:T(8,128)(2,1)S(1)}, u32[]{:S(2)}, u32[]{:S(2)}) %collective-permute-start.1) | collective-permute-done | bytes 786464 | tf_op jit(solution)/shard_map/ppermute | solution.py:95
  36.9 4.6 collective-permute-done.3.refs_4_
  41.4 4.3 pack.1
  60.9 18.2 %collective-permute-done.4.refs_8_ = bf16[512,768]{1,0:T(8,128)(2,1)} collective-permute-done((bf16[512,768]{1,0:T(8,128)(2,1)}, bf16[512,768]{1,0:T(8,128)(2,1)}, u32[]{:S(2)}, u32[]{:S(2)}) %collective-permute-start.4) | collective-permute-done | bytes 786464 | tf_op jit(solution)/shard_map/ppermute | solution.py:104
  104.4 9.8 collective-permute-done.12.refs_13_
  118.8 12.5 %collective-permute-done.18.refs_1_ = bf16[3,128,576]{2,1,0:T(8,128)(2,1)S(1)} collective-permute-done((bf16[3,128,576]{2,1,0:T(8,128)(2,1)}, bf16[3,128,576]{2,1,0:T(8,128)(2,1)S(1)}, u32[]{:S(2)}, u32[]{:S(2)}) %collective-permute-start.18) | collective-permute-done | bytes 442400 | tf_op jit(solution)/shard_map/ppermute | solution.py:104
  131.3 17.2 %collective-permute-done.16.refs_17_ = bf16[256,1408]{1,0:T(8,128)(2,1)S(1)} collective-permute-done((bf16[256,1408]{1,0:T(8,128)(2,1)}, bf16[256,1408]{1,0:T(8,128)(2,1)S(1)}, u32[]{:S(2)}, u32[]{:S(2)}) %collective-permute-start.16) | collective-permute-done | bytes 720928 | tf_op jit(solution)/shard_map/ppermute | solution.py:95
  152.7 11.2 %collective-permute-done.23.refs_2_ = bf16[3,128,576]{2,1,0:T(8,128)(2,1)S(1)} collective-permute-done((bf16[3,128,576]{2,1,0:T(8,128)(2,1)S(1)}, bf16[3,128,576]{2,1,0:T(8,128)(2,1)S(1)}, u32[]{:S(2)}, u32[]{:S(2)}) %collective-permute-start.23) | collective-permute-done | bytes 442400 | tf_op jit(solution)/shard_map/ppermute | solution.py:104
  163.9 17.2 %collective-permute-done.21.refs_19_ = bf16[256,1408]{1,0:T(8,128)(2,1)S(1)} collective-permute-done((bf16[256,1408]{1,0:T(8,128)(2,1)}, bf16[256,1408]{1,0:T(8,128)(2,1)S(1)}, u32[]{:S(2)}, u32[]{:S(2)}) %collective-permute-start.21) | collective-permute-done | bytes 720928 | tf_op jit(solution)/shard_map/ppermute | solution.py:95
  192.2 12.2 %collective-permute-done.28.refs_3_ = bf16[3,128,576]{2,1,0:T(8,128)(2,1)} collective-permute-done((bf16[3,128,576]{2,1,0:T(8,128)(2,1)S(1)}, bf16[3,128,576]{2,1,0:T(8,128)(2,1)}, u32[]{:S(2)}, u32[]{:S(2)}) %collective-permute-start.28) | collective-permute-done | bytes 442400 | tf_op jit(solution)/shard_map/ppermute | solution.py:104
  214.9 11.8 %assemble.1 = (bf16[2048,1536]{1,0:T(8,128)(2,1)}, bf16[2048,1024]{1,0:T(8,128)(2,1)}, bf16[512,2048]{1,0:T(8,128)(2,1)}) custom-call(s32[2]{0:T(128)S(1)} %pad_add_fusion.3.place.place_ref, bf16[512,768]{1,0:T(8,128)(2,1)S(1)} %pad_maximum_fusion.22.refs_0_, bf16[512,768]{1,0:T(8,128)(2,1)S(1)} %collective-permute-done.1.refs_1_, ...), custom_call_target="tpu_custom_call" | custom-call | bytes 25165824 | tf_op jit(solution)/shard_map/assemble/pallas_call | solution.py:168
  226.7 9.0 fusion.90
  240.2 5.2 lay_out.1
  245.4 11.7 %convolution_convert_fusion = bf16[3072,2048]{1,0:T(8,128)(2,1)} fusion(bf16[3072,512]{1,0:T(8,128)(2,1)} %bitcast.212, bf16[512,2048]{1,0:T(8,128)(2,1)} %get-tuple-element.314.wkv_ref), kind=kOutput, calls=%fused_computation | convolution fusion | flops 6448742400 | bytes 17825792 | tf_op jit(solution)/shard_map/dot_general | solution.py:51
  257.1 3.9 collective-permute-start.35
  266.9 27.3 %attend.1 = bf16[2,3,128,1024]{3,2,1,0:T(8,128)(2,1)S(1)} custom-call(s32[3,2]{1,0:T(4,128)S(1)} %pad_add_fusion.2.place, f32[2,3,128,1536]{3,2,1,0:T(8,128)S(1)} %bitcast.171, bf16[3,1024,2048]{2,1,0:T(8,128)(2,1)} %bitcast.177, bf16[3,1024,128]{2,1,0:T(8,128)(2,1)S(1)} %copy-done.10, s32[3,256,1]{2,1,0:T(8,128)S(1)} %copy.190.segq_ref, ...), custom_call_target="tpu_custom_call" | custom-call | flops 3019898880 | bytes 19660800 | tf_op jit(solution)/shard_map/attend/pallas_call | solution.py:411
  296.7 3.7 convolution_convert_fusion.1
  312.0 32.4 %collective-permute-done.40.refs_11_ = bf16[256,2816]{1,0:T(8,128)(2,1)S(1)} collective-permute-done((bf16[256,2816]{1,0:T(8,128)(2,1)}, bf16[256,2816]{1,0:T(8,128)(2,1)S(1)}, u32[]{:S(2)}, u32[]{:S(2)}) %collective-permute-start.40) | collective-permute-done | bytes 1441824 | tf_op jit(solution)/shard_map/ppermute | solution.py:95
  346.6 40.2 %feed.4 = (bf16[384,2048]{1,0:T(8,128)(2,1)}, bf16[384,2048]{1,0:T(8,128)(2,1)}, bf16[384,2048]{1,0:T(8,128)(2,1)}, bf16[384,2048]{1,0:T(8,128)(2,1)}, bf16[3072...) custom-call(s32[2]{0:T(128)} %copy-done.13, ...), custom_call_target="tpu_custom_call" | custom-call | flops 26575110144 | bytes 42663936 | tf_op jit(solution)/shard_map/feed/pallas_call | solution.py:633
  388.3 40.3 %feed.5 = (bf16[384,2048]{1,0:T(8,128)(2,1)}, bf16[384,2048]{1,0:T(8,128)(2,1)}, bf16[384,2048]{1,0:T(8,128)(2,1)}, bf16[384,2048]{1,0:T(8,128)(2,1)}, bf16[3072...) custom-call(s32[2]{0:T(128)} %copy-done.13, ...), custom_call_target="tpu_custom_call", output_to_operand_aliasing={{4}: (21, {}), {5}: (22, {}), {6}: (23, {}), {7}: (24, {})} | custom-call | flops 26575110144 | bytes 42663936 | tf_op jit(solution)/shard_map/feed/pallas_call | solution.py:633
  429.8 40.4 %feed.6 = (bf16[384,2048]{1,0:T(8,128)(2,1)}, bf16[384,2048]{1,0:T(8,128)(2,1)}, bf16[384,2048]{1,0:T(8,128)(2,1)}, bf16[384,2048]{1,0:T(8,128)(2,1)}, bf16[3072...) custom-call(s32[2]{0:T(128)} %copy-done.13, ...), custom_call_target="tpu_custom_call", output_to_operand_aliasing={{4}: (21, {}), {5}: (22, {}), {6}: (23, {}), {7}: (24, {})} | custom-call | flops 26575110144 | bytes 42663936 | tf_op jit(solution)/shard_map/feed/pallas_call | solution.py:633
  477.9 40.4 %feed.7 = (bf16[384,2048]{1,0:T(8,128)(2,1)}, bf16[384,2048]{1,0:T(8,128)(2,1)}, bf16[384,2048]{1,0:T(8,128)(2,1)}, bf16[384,2048]{1,0:T(8,128)(2,1)}, bf16[3072...) custom-call(s32[2]{0:T(128)} %copy-done.13, ...), custom_call_target="tpu_custom_call", output_to_operand_aliasing={{4}: (21, {}), {5}: (22, {}), {6}: (23, {}), {7}: (24, {})} | custom-call | flops 26575110144 | bytes 42663936 | tf_op jit(solution)/shard_map/feed/pallas_call | solution.py:633
  524.3 35.8 %weight_grad.3 = (bf16[512,1408]{1,0:T(8,128)(2,1)S(1)}, bf16[512,1408]{1,0:T(8,128)(2,1)S(1)}, bf16[1024,1408]{1,0:T(8,128)(2,1)S(1)}) custom-call(s32[2]{0:T(128)S(1)} %copy-done.14, bf16[3072,2048]{1,0:T(8,128)(2,1)} %get-tuple-element.381.left, bf16[3072,1408]{1,0:T(8,128)(2,1)} %get-tuple-element.382.right_ref), custom_call_target="tpu_custom_call" | custom-call | flops 17716740096 | bytes 27000832 | tf_op jit(solution)/shard_map/weight_grad/pallas_call | solution.py:752
  566.0 29.0 %weight_grad.4 = (bf16[256,2816]{1,0:T(8,128)(2,1)S(1)}, bf16[256,2816]{1,0:T(8,128)(2,1)S(1)}, bf16[256,2816]{1,0:T(8,128)(2,1)S(1)}, bf16[256,2816]{1,0:T(8,128)(2,1)S(1)}) custom-call(s32[2]{0:T(128)S(1)} %copy-done.14, bf16[3072,2048]{1,0:T(8,128)(2,1)} %get-tuple-element.394.left, bf16[3072,2816]{1,0:T(8,128)(2,1)} %get-tuple-element.395.right_ref), custom_call_target="tpu_custom_call" | custom-call | flops 17716740096 | bytes 29360128 | tf_op jit(solution)/shard_map/weight_grad/pallas_call | solution.py:752
  595.7 8.4 collective-permute-done.56
  605.7 4.3 convert_add_fusion.2
  612.2 29.0 %weight_grad.5 = (bf16[256,2816]{1,0:T(8,128)(2,1)S(1)}, bf16[256,2816]{1,0:T(8,128)(2,1)S(1)}, bf16[256,2816]{1,0:T(8,128)(2,1)S(1)}, bf16[256,2816]{1,0:T(8,128)(2,1)S(1)}) custom-call(s32[2]{0:T(128)S(1)} %copy-done.14, bf16[3072,2048]{1,0:T(8,128)(2,1)} %get-tuple-element.394.left, bf16[3072,2816]{1,0:T(8,128)(2,1)} %get-tuple-element.395.right_ref), custom_call_target="tpu_custom_call" | custom-call | flops 17716740096 | bytes 29360128 | tf_op jit(solution)/shard_map/weight_grad/pallas_call | solution.py:752
  641.3 9.3 collective-permute-done.62
  650.6 3.8 multiply_reduce_fusion
  668.2 5.4 fusion.12
  673.6 19.9 %collective-permute-done.64 = bf16[256,2816]{1,0:T(8,128)(2,1)S(1)} collective-permute-done((bf16[256,2816]{1,0:T(8,128)(2,1)S(1)}, bf16[256,2816]{1,0:T(8,128)(2,1)S(1)}, u32[]{:S(2)}, u32[]{:S(2)}) %collective-permute-start.64) | collective-permute-done | bytes 1441824 | tf_op jit(solution)/shard_map/ppermute | solution.py:99
  711.5 82.6 %attend_back.1 = (bf16[512,1536]{1,0:T(8,128)(2,1)}, bf16[512,1536]{1,0:T(8,128)(2,1)}, bf16[1024,1536]{1,0:T(8,128)(2,1)}, bf16[128,2048]{1,0:T(8,128)(2,1)}, b...) custom-call(s32[3,2]{1,0:T(4,128)} %copy-done.12, ...), custom_call_target="tpu_custom_call" | custom-call | flops 30601641984 | bytes 42467328 | tf_op jit(solution)/shard_map/attend_back/pallas_call | solution.py:472
  794.2 3.9 copy.192
  798.1 4.0 collective-permute-done.73
  805.7 3.9 add_convert_fusion.3
  815.5 3.8 add_convert_fusion.15
  819.3 19.9 %collective-permute-done.76 = bf16[512,1536]{1,0:T(8,128)(2,1)} collective-permute-done((bf16[512,1536]{1,0:T(8,128)(2,1)}, bf16[512,1536]{1,0:T(8,128)(2,1)}, u32[]{:S(2)}, u32[]{:S(2)}) %collective-permute-start.76) | collective-permute-done | bytes 1572896 | tf_op jit(solution)/shard_map/ppermute | solution.py:99
  839.9 8.7 collective-permute-done.75
  848.6 3.9 copy.193
  862.1 7.8 collective-permute-done.78
  882.1 9.2 collective-permute-done.104
  895.7 6.7 collective-permute-done.105
  903.9 11.2 %collective-permute-done.106 = bf16[512,256]{1,0:T(8,128)(2,1)S(1)} collective-permute-done((bf16[512,256]{1,0:T(8,128)(2,1)S(1)}, bf16[512,256]{1,0:T(8,128)(2,1)S(1)}, u32[]{:S(2)}, u32[]{:S(2)}) %collective-permute-start.106) | collective-permute-done | bytes 262176 | tf_op jit(solution)/shard_map/ppermute | solution.py:104
  920.8 4.3 fusion.9
  969.3 6.7 collective-permute-done.96
  979.5 9.2 collective-permute-done.102
  990.9 5.2 collective-permute-done.103
  1000.4 4.7 collective-permute-done.115
  (725 shorter events, 306.9 us)
Async XLA Ops:
  7.2 77.1 %all-gather.3.cloned.1.call-start = ((), (), s32[]{:S(2)}) async-start(), calls=%async_computation | async-start | bytes 3379200 | tf_op jit(solution)/shard_map/all_gather | solution.py:845
  79.2 35.5 %collective-permute-start.9 = (bf16[512,768]{1,0:T(8,128)(2,1)}, bf16[512,768]{1,0:T(8,128)(2,1)}, u32[]{:S(2)}, u32[]{:S(2)}) collective-permute-start(bf16[512,768]{1,0:T(8,128)(2,1)} %collective-permute-done.4.refs_8_), channel_id=1, source_target_pairs={{0,1},{1,2},{2,3},{3,0},{4,5},{5,6},{6,7},{7,4},{8,9},{9,10},{10,1... | collective-permute-start | bytes 2359304 | tf_op jit(solution)/shard_map/ppermute | solution.py:104
  79.2 35.4 %collective-permute-start.10 = (bf16[512,768]{1,0:T(8,128)(2,1)}, bf16[512,768]{1,0:T(8,128)(2,1)}, u32[]{:S(2)}, u32[]{:S(2)}) collective-permute-start(bf16[512,768]{1,0:T(8,128)(2,1)} %collective-permute-done.4.refs_8_), channel_id=1, source_target_pairs={{0,8},{8,0},{16,24},{24,16},{1,9},{9,1},{17,25},{25,17},{2,10},{10... | collective-permute-start | bytes 2359304 | tf_op jit(solution)/shard_map/ppermute | solution.py:95
  80.2 34.4 %collective-permute-start.11 = (bf16[512,768]{1,0:T(8,128)(2,1)S(1)}, bf16[512,768]{1,0:T(8,128)(2,1)}, u32[]{:S(2)}, u32[]{:S(2)}) collective-permute-start(bf16[512,768]{1,0:T(8,128)(2,1)S(1)} %collective-permute-done.1.refs_1_), channel_id=1, source_target_pairs={{0,16},{8,24},{16,0},{24,8},{1,17},{9,25},{17,1},{25,9},{2,18},{10... | collective-permute-start | bytes 2359304 | tf_op jit(solution)/shard_map/ppermute | solution.py:99
  80.8 33.3 %collective-permute-start.12 = (bf16[256,1408]{1,0:T(8,128)(2,1)S(1)}, bf16[256,1408]{1,0:T(8,128)(2,1)}, u32[]{:S(2)}, u32[]{:S(2)}) collective-permute-start(bf16[256,1408]{1,0:T(8,128)(2,1)S(1)} %copy-done.17), channel_id=1, source_target_pairs={{0,8},{8,0},{16,24},{24,16},{1,9},{9,1},{17,25},{25,17},{2,10},{10... | collective-permute-start | bytes 2162696 | tf_op jit(solution)/shard_map/ppermute | solution.py:95
  82.2 32.4 %collective-permute-start.13 = (bf16[256,1408]{1,0:T(8,128)(2,1)}, bf16[256,1408]{1,0:T(8,128)(2,1)}, u32[]{:S(2)}, u32[]{:S(2)}) collective-permute-start(bf16[256,1408]{1,0:T(8,128)(2,1)} %collective-permute-done.7.refs_16_), channel_id=1, source_target_pairs={{0,16},{8,24},{16,0},{24,8},{1,17},{9,25},{17,1},{25,9},{2,18},{10... | collective-permute-start | bytes 2162696 | tf_op jit(solution)/shard_map/ppermute | solution.py:99
  114.7 33.8 %collective-permute-start.14 = (bf16[512,768]{1,0:T(8,128)(2,1)}, bf16[512,768]{1,0:T(8,128)(2,1)S(1)}, u32[]{:S(2)}, u32[]{:S(2)}) collective-permute-start(bf16[512,768]{1,0:T(8,128)(2,1)} %collective-permute-done.9.refs_12_), channel_id=1, source_target_pairs={{0,16},{8,24},{16,0},{24,8},{1,17},{9,25},{17,1},{25,9},{2,18},{10... | collective-permute-start | bytes 2359304 | tf_op jit(solution)/shard_map/ppermute | solution.py:99
  115.0 33.5 %collective-permute-start.15 = (bf16[512,768]{1,0:T(8,128)(2,1)}, bf16[512,768]{1,0:T(8,128)(2,1)S(1)}, u32[]{:S(2)}, u32[]{:S(2)}) collective-permute-start(bf16[512,768]{1,0:T(8,128)(2,1)} %collective-permute-done.6.refs_6_), channel_id=1, source_target_pairs={{0,8},{8,0},{16,24},{24,16},{1,9},{9,1},{17,25},{25,17},{2,10},{10... | collective-permute-start | bytes 2359304 | tf_op jit(solution)/shard_map/ppermute | solution.py:95
  148.5 33.3 %collective-permute-start.19 = (bf16[512,768]{1,0:T(8,128)(2,1)}, bf16[512,768]{1,0:T(8,128)(2,1)}, u32[]{:S(2)}, u32[]{:S(2)}) collective-permute-start(bf16[512,768]{1,0:T(8,128)(2,1)} %collective-permute-done.9.refs_12_), channel_id=1, source_target_pairs={{0,8},{8,0},{16,24},{24,16},{1,9},{9,1},{17,25},{25,17},{2,10},{10... | collective-permute-start | bytes 2359304 | tf_op jit(solution)/shard_map/ppermute | solution.py:95
  210.2 46.9 %collective-permute-start.29 = (bf16[256,2816]{1,0:T(8,128)(2,1)}, bf16[256,2816]{1,0:T(8,128)(2,1)}, u32[]{:S(2)}, u32[]{:S(2)}) collective-permute-start(bf16[256,2816]{1,0:T(8,128)(2,1)} %get-tuple-element.320.refs_4_), channel_id=1, source_target_pairs={{0,8},{8,0},{16,24},{24,16},{1,9},{9,1},{17,25},{25,17},{2,10},{10... | collective-permute-start | bytes 4325384 | tf_op jit(solution)/shard_map/ppermute | solution.py:95
  211.3 45.8 %collective-permute-start.30 = (bf16[256,2816]{1,0:T(8,128)(2,1)}, bf16[256,2816]{1,0:T(8,128)(2,1)}, u32[]{:S(2)}, u32[]{:S(2)}) collective-permute-start(bf16[256,2816]{1,0:T(8,128)(2,1)} %collective-permute-done.8.refs_8_), channel_id=1, source_target_pairs={{0,16},{8,24},{16,0},{24,8},{1,17},{9,25},{17,1},{25,9},{2,18},{10... | collective-permute-start | bytes 4325384 | tf_op jit(solution)/shard_map/ppermute | solution.py:99
  212.7 44.4 %collective-permute-start.31 = (bf16[384,2048]{1,0:T(8,128)(2,1)}, bf16[384,2048]{1,0:T(8,128)(2,1)}, u32[]{:S(2)}, u32[]{:S(2)}) collective-permute-start(bf16[384,2048]{1,0:T(8,128)(2,1)} %pad_maximum_fusion.9.refs_2_), channel_id=1, source_target_pairs={{0,1},{1,2},{2,3},{3,0},{4,5},{5,6},{6,7},{7,4},{8,9},{9,10},{10,1... | collective-permute-start | bytes 4718600 | tf_op jit(solution)/shard_map/ppermute | solution.py:104
  257.1 39.6 %collective-permute-start.35 = (bf16[384,2048]{1,0:T(8,128)(2,1)}, bf16[384,2048]{1,0:T(8,128)(2,1)}, u32[]{:S(2)}, u32[]{:S(2)}) collective-permute-start(bf16[384,2048]{1,0:T(8,128)(2,1)} %collective-permute-done.31.refs_2_), channel_id=1, source_target_pairs={{0,1},{1,2},{2,3},{3,0},{4,5},{5,6},{6,7},{7,4},{8,9},{9,10},{10,1... | collective-permute-start | bytes 4718600 | tf_op jit(solution)/shard_map/ppermute | solution.py:104
  261.0 35.7 %collective-permute-start.36 = (bf16[384,2048]{1,0:T(8,128)(2,1)}, bf16[384,2048]{1,0:T(8,128)(2,1)}, u32[]{:S(2)}, u32[]{:S(2)}) collective-permute-start(bf16[384,2048]{1,0:T(8,128)(2,1)} %pad_maximum_fusion.9.refs_2_), channel_id=1, source_target_pairs={{0,4},{4,0},{1,5},{5,1},{2,6},{6,2},{3,7},{7,3},{8,12},{12,8},{9,1... | collective-permute-start | bytes 4718600 | tf_op jit(solution)/shard_map/ppermute | solution.py:91
  261.2 35.5 %collective-permute-start.37 = (bf16[384,2048]{1,0:T(8,128)(2,1)}, bf16[384,2048]{1,0:T(8,128)(2,1)}, u32[]{:S(2)}, u32[]{:S(2)}) collective-permute-start(bf16[384,2048]{1,0:T(8,128)(2,1)} %collective-permute-done.31.refs_2_), channel_id=1, source_target_pairs={{0,4},{4,0},{1,5},{5,1},{2,6},{6,2},{3,7},{7,3},{8,12},{12,8},{9,1... | collective-permute-start | bytes 4718600 | tf_op jit(solution)/shard_map/ppermute | solution.py:91
  261.5 34.0 %collective-permute-start.33 = (bf16[256,2816]{1,0:T(8,128)(2,1)}, bf16[256,2816]{1,0:T(8,128)(2,1)}, u32[]{:S(2)}, u32[]{:S(2)}) collective-permute-start(bf16[256,2816]{1,0:T(8,128)(2,1)} %collective-permute-done.8.refs_8_), channel_id=1, source_target_pairs={{0,8},{8,0},{16,24},{24,16},{1,9},{9,1},{17,25},{25,17},{2,10},{10... | collective-permute-start | bytes 4325384 | tf_op jit(solution)/shard_map/ppermute | solution.py:95
  262.4 33.7 %collective-permute-start.34 = (bf16[256,2816]{1,0:T(8,128)(2,1)}, bf16[256,2816]{1,0:T(8,128)(2,1)}, u32[]{:S(2)}, u32[]{:S(2)}) collective-permute-start(bf16[256,2816]{1,0:T(8,128)(2,1)} %get-tuple-element.320.refs_4_), channel_id=1, source_target_pairs={{0,16},{8,24},{16,0},{24,8},{1,17},{9,25},{17,1},{25,9},{2,18},{10... | collective-permute-start | bytes 4325384 | tf_op jit(solution)/shard_map/ppermute | solution.py:99
  307.0 38.5 %collective-permute-start.39 = (bf16[384,2048]{1,0:T(8,128)(2,1)S(1)}, bf16[384,2048]{1,0:T(8,128)(2,1)S(1)}, u32[]{:S(2)}, u32[]{:S(2)}) collective-permute-start(bf16[384,2048]{1,0:T(8,128)(2,1)S(1)} %multiply_convert_fusion.refs_0_), channel_id=1, source_target_pairs={{0,1},{1,2},{2,3},{3,0},{4,5},{5,6},{6,7},{7,4},{8,9},{9,10},{10,1... | collective-permute-start | bytes 4718600 | tf_op jit(solution)/shard_map/ppermute | solution.py:104
  310.3 35.2 %collective-permute-start.43 = (bf16[384,2048]{1,0:T(8,128)(2,1)}, bf16[384,2048]{1,0:T(8,128)(2,1)S(1)}, u32[]{:S(2)}, u32[]{:S(2)}) collective-permute-start(bf16[384,2048]{1,0:T(8,128)(2,1)} %collective-permute-done.35.refs_2_), channel_id=1, source_target_pairs={{0,4},{4,0},{1,5},{5,1},{2,6},{6,2},{3,7},{7,3},{8,12},{12,8},{9,1... | collective-permute-start | bytes 4718600 | tf_op jit(solution)/shard_map/ppermute | solution.py:91
  310.4 34.1 %collective-permute-start.40 = (bf16[256,2816]{1,0:T(8,128)(2,1)}, bf16[256,2816]{1,0:T(8,128)(2,1)S(1)}, u32[]{:S(2)}, u32[]{:S(2)}) collective-permute-start(bf16[256,2816]{1,0:T(8,128)(2,1)} %collective-permute-done.30.refs_10_), channel_id=1, source_target_pairs={{0,8},{8,0},{16,24},{24,16},{1,9},{9,1},{17,25},{25,17},{2,10},{10... | collective-permute-start | bytes 4325384 | tf_op jit(solution)/shard_map/ppermute | solution.py:95
  311.5 33.8 %collective-permute-start.41 = (bf16[256,2816]{1,0:T(8,128)(2,1)}, bf16[256,2816]{1,0:T(8,128)(2,1)S(1)}, u32[]{:S(2)}, u32[]{:S(2)}) collective-permute-start(bf16[256,2816]{1,0:T(8,128)(2,1)} %collective-permute-done.29.refs_5_), channel_id=1, source_target_pairs={{0,16},{8,24},{16,0},{24,8},{1,17},{9,25},{17,1},{25,9},{2,18},{10... | collective-permute-start | bytes 4325384 | tf_op jit(solution)/shard_map/ppermute | solution.py:99
  345.5 41.3 %collective-permute-start.44 = (bf16[384,2048]{1,0:T(8,128)(2,1)S(1)}, bf16[384,2048]{1,0:T(8,128)(2,1)}, u32[]{:S(2)}, u32[]{:S(2)}) collective-permute-start(bf16[384,2048]{1,0:T(8,128)(2,1)S(1)} %collective-permute-done.39.refs_0_), channel_id=1, source_target_pairs={{0,1},{1,2},{2,3},{3,0},{4,5},{5,6},{6,7},{7,4},{8,9},{9,10},{10,1... | collective-permute-start | bytes 4718600 | tf_op jit(solution)/shard_map/ppermute | solution.py:104
  346.6 40.3 %collective-permute-start.45 = (bf16[384,2048]{1,0:T(8,128)(2,1)S(1)}, bf16[384,2048]{1,0:T(8,128)(2,1)}, u32[]{:S(2)}, u32[]{:S(2)}) collective-permute-start(bf16[384,2048]{1,0:T(8,128)(2,1)S(1)} %collective-permute-done.39.refs_0_), channel_id=1, source_target_pairs={{0,4},{4,0},{1,5},{5,1},{2,6},{6,2},{3,7},{7,3},{8,12},{12,8},{9,1... | collective-permute-start | bytes 4718600 | tf_op jit(solution)/shard_map/ppermute | solution.py:91
  386.8 41.8 %collective-permute-start.46 = (bf16[384,2048]{1,0:T(8,128)(2,1)}, bf16[384,2048]{1,0:T(8,128)(2,1)S(1)}, u32[]{:S(2)}, u32[]{:S(2)}) collective-permute-start(bf16[384,2048]{1,0:T(8,128)(2,1)} %collective-permute-done.44.refs_0_), channel_id=1, source_target_pairs={{0,1},{1,2},{2,3},{3,0},{4,5},{5,6},{6,7},{7,4},{8,9},{9,10},{10,1... | collective-permute-start | bytes 4718600 | tf_op jit(solution)/shard_map/ppermute | solution.py:104
  388.1 40.5 %collective-permute-start.47 = (bf16[384,2048]{1,0:T(8,128)(2,1)}, bf16[384,2048]{1,0:T(8,128)(2,1)S(1)}, u32[]{:S(2)}, u32[]{:S(2)}) collective-permute-start(bf16[384,2048]{1,0:T(8,128)(2,1)} %collective-permute-done.44.refs_0_), channel_id=1, source_target_pairs={{0,4},{4,0},{1,5},{5,1},{2,6},{6,2},{3,7},{7,3},{8,12},{12,8},{9,1... | collective-permute-start | bytes 4718600 | tf_op jit(solution)/shard_map/ppermute | solution.py:91
  428.7 41.6 %collective-permute-start.48 = (bf16[384,2048]{1,0:T(8,128)(2,1)}, bf16[384,2048]{1,0:T(8,128)(2,1)}, u32[]{:S(2)}, u32[]{:S(2)}) collective-permute-start(bf16[384,2048]{1,0:T(8,128)(2,1)} %collective-permute-done.35.refs_2_), channel_id=1, source_target_pairs={{0,1},{1,2},{2,3},{3,0},{4,5},{5,6},{6,7},{7,4},{8,9},{9,10},{10,1... | collective-permute-start | bytes 4718600 | tf_op jit(solution)/shard_map/ppermute | solution.py:104
  429.7 40.5 %collective-permute-start.49 = (bf16[384,2048]{1,0:T(8,128)(2,1)S(1)}, bf16[384,2048]{1,0:T(8,128)(2,1)S(1)}, u32[]{:S(2)}, u32[]{:S(2)}) collective-permute-start(bf16[384,2048]{1,0:T(8,128)(2,1)S(1)} %collective-permute-done.46.refs_0_), channel_id=1, source_target_pairs={{0,4},{4,0},{1,5},{5,1},{2,6},{6,2},{3,7},{7,3},{8,12},{12,8},{9,1... | collective-permute-start | bytes 4718600 | tf_op jit(solution)/shard_map/ppermute | solution.py:91
  474.6 43.8 %collective-permute-start.52 = (bf16[384,2048]{1,0:T(8,128)(2,1)S(1)}, bf16[384,2048]{1,0:T(8,128)(2,1)S(1)}, u32[]{:S(2)}, u32[]{:S(2)}) collective-permute-start(bf16[384,2048]{1,0:T(8,128)(2,1)S(1)} %add_convert_fusion.13), channel_id=1, source_target_pairs={{0,1},{1,2},{2,3},{3,0},{4,5},{5,6},{6,7},{7,4},{8,9},{9,10},{10,1... | collective-permute-start | bytes 4718600 | tf_op jit(solution)/shard_map/ppermute | solution.py:104
  522.9 38.3 %collective-permute-start.54 = (bf16[384,2048]{1,0:T(8,128)(2,1)S(1)}, bf16[384,2048]{1,0:T(8,128)(2,1)S(1)}, u32[]{:S(2)}, u32[]{:S(2)}) collective-permute-start(bf16[384,2048]{1,0:T(8,128)(2,1)S(1)} %add_convert_fusion.11), channel_id=1, source_target_pairs={{0,1},{1,2},{2,3},{3,0},{4,5},{5,6},{6,7},{7,4},{8,9},{9,10},{10,1... | collective-permute-start | bytes 4718600 | tf_op jit(solution)/shard_map/ppermute | solution.py:104
  561.2 34.1 %collective-permute-start.57 = (bf16[512,1408]{1,0:T(8,128)(2,1)S(1)}, bf16[512,1408]{1,0:T(8,128)(2,1)}, u32[]{:S(2)}, u32[]{:S(2)}) collective-permute-start(bf16[512,1408]{1,0:T(8,128)(2,1)S(1)} %get-tuple-element.389), channel_id=1, source_target_pairs={{0,16},{8,24},{16,0},{24,8},{1,17},{9,25},{17,1},{25,9},{2,18},{10... | collective-permute-start | bytes 4325384 | tf_op jit(solution)/shard_map/ppermute | solution.py:99
  561.8 33.8 %collective-permute-start.58 = (bf16[512,1408]{1,0:T(8,128)(2,1)S(1)}, bf16[512,1408]{1,0:T(8,128)(2,1)}, u32[]{:S(2)}, u32[]{:S(2)}) collective-permute-start(bf16[512,1408]{1,0:T(8,128)(2,1)S(1)} %get-tuple-element.392), channel_id=1, source_target_pairs={{0,8},{8,0},{16,24},{24,16},{1,9},{9,1},{17,25},{25,17},{2,10},{10... | collective-permute-start | bytes 4325384 | tf_op jit(solution)/shard_map/ppermute | solution.py:95
  565.7 38.4 %collective-permute-start.56 = (bf16[384,2048]{1,0:T(8,128)(2,1)S(1)}, bf16[384,2048]{1,0:T(8,128)(2,1)}, u32[]{:S(2)}, u32[]{:S(2)}) collective-permute-start(bf16[384,2048]{1,0:T(8,128)(2,1)S(1)} %add_convert_fusion.9), channel_id=1, source_target_pairs={{0,1},{1,2},{2,3},{3,0},{4,5},{5,6},{6,7},{7,4},{8,9},{9,10},{10,1... | collective-permute-start | bytes 4718600 | tf_op jit(solution)/shard_map/ppermute | solution.py:104
  565.8 38.3 %collective-permute-start.60 = (bf16[384,2048]{1,0:T(8,128)(2,1)}, bf16[384,2048]{1,0:T(8,128)(2,1)}, u32[]{:S(2)}, u32[]{:S(2)}) collective-permute-start(bf16[384,2048]{1,0:T(8,128)(2,1)} %get-tuple-element.407), channel_id=1, source_target_pairs={{0,4},{4,0},{1,5},{5,1},{2,6},{6,2},{3,7},{7,3},{8,12},{12,8},{9,1... | collective-permute-start | bytes 4718600 | tf_op jit(solution)/shard_map/ppermute | solution.py:91
  604.1 37.2 %collective-permute-start.59 = (bf16[256,2816]{1,0:T(8,128)(2,1)S(1)}, bf16[256,2816]{1,0:T(8,128)(2,1)}, u32[]{:S(2)}, u32[]{:S(2)}) collective-permute-start(bf16[256,2816]{1,0:T(8,128)(2,1)S(1)} %get-tuple-element.400), channel_id=1, source_target_pairs={{0,16},{8,24},{16,0},{24,8},{1,17},{9,25},{17,1},{25,9},{2,18},{10... | collective-permute-start | bytes 4325384 | tf_op jit(solution)/shard_map/ppermute | solution.py:99
  604.7 36.5 %collective-permute-start.63 = (bf16[256,2816]{1,0:T(8,128)(2,1)S(1)}, bf16[256,2816]{1,0:T(8,128)(2,1)}, u32[]{:S(2)}, u32[]{:S(2)}) collective-permute-start(bf16[256,2816]{1,0:T(8,128)(2,1)S(1)} %get-tuple-element.413), channel_id=1, source_target_pairs={{0,8},{8,0},{16,24},{24,16},{1,9},{9,1},{17,25},{25,17},{2,10},{10... | collective-permute-start | bytes 4325384 | tf_op jit(solution)/shard_map/ppermute | solution.py:95
  611.8 38.7 %collective-permute-start.62 = (bf16[384,2048]{1,0:T(8,128)(2,1)}, bf16[384,2048]{1,0:T(8,128)(2,1)}, u32[]{:S(2)}, u32[]{:S(2)}) collective-permute-start(bf16[384,2048]{1,0:T(8,128)(2,1)} %add_convert_fusion.8), channel_id=1, source_target_pairs={{0,1},{1,2},{2,3},{3,0},{4,5},{5,6},{6,7},{7,4},{8,9},{9,10},{10,1... | collective-permute-start | bytes 4718600 | tf_op jit(solution)/shard_map/ppermute | solution.py:104
  659.4 34.1 %collective-permute-start.64 = (bf16[256,2816]{1,0:T(8,128)(2,1)S(1)}, bf16[256,2816]{1,0:T(8,128)(2,1)S(1)}, u32[]{:S(2)}, u32[]{:S(2)}) collective-permute-start(bf16[256,2816]{1,0:T(8,128)(2,1)S(1)} %get-tuple-element.415), channel_id=1, source_target_pairs={{0,16},{8,24},{16,0},{24,8},{1,17},{9,25},{17,1},{25,9},{2,18},{10... | collective-permute-start | bytes 4325384 | tf_op jit(solution)/shard_map/ppermute | solution.py:99
  661.0 33.7 %collective-permute-start.65 = (bf16[256,2816]{1,0:T(8,128)(2,1)S(1)}, bf16[256,2816]{1,0:T(8,128)(2,1)S(1)}, u32[]{:S(2)}, u32[]{:S(2)}) collective-permute-start(bf16[256,2816]{1,0:T(8,128)(2,1)S(1)} %get-tuple-element.418), channel_id=1, source_target_pairs={{0,8},{8,0},{16,24},{24,16},{1,9},{9,1},{17,25},{25,17},{2,10},{10... | collective-permute-start | bytes 4325384 | tf_op jit(solution)/shard_map/ppermute | solution.py:95
  698.5 95.7 %collective-permute-start.67 = (bf16[256,4224]{1,0:T(8,128)(2,1)}, bf16[256,4224]{1,0:T(8,128)(2,1)}, u32[]{:S(2)}, u32[]{:S(2)}) collective-permute-start(bf16[256,4224]{1,0:T(8,128)(2,1)} %pad_maximum_fusion.4), channel_id=1, source_target_pairs={{0,8},{8,0},{16,24},{24,16},{1,9},{9,1},{17,25},{25,17},{2,10},{10... | collective-permute-start | bytes 6488072 | tf_op jit(solution)/shard_map/ppermute | solution.py:95
  702.7 91.5 %collective-permute-start.68 = (bf16[256,4224]{1,0:T(8,128)(2,1)}, bf16[256,4224]{1,0:T(8,128)(2,1)}, u32[]{:S(2)}, u32[]{:S(2)}) collective-permute-start(bf16[256,4224]{1,0:T(8,128)(2,1)} %pad_maximum_fusion.5), channel_id=1, source_target_pairs={{0,16},{8,24},{16,0},{24,8},{1,17},{9,25},{17,1},{25,9},{2,18},{10... | collective-permute-start | bytes 6488072 | tf_op jit(solution)/shard_map/ppermute | solution.py:99
  704.8 89.4 %collective-permute-start.71 = (bf16[512,1024]{1,0:T(8,128)(2,1)}, bf16[512,1024]{1,0:T(8,128)(2,1)}, u32[]{:S(2)}, u32[]{:S(2)}) collective-permute-start(bf16[512,1024]{1,0:T(8,128)(2,1)} %pad_maximum_fusion.18), channel_id=1, source_target_pairs={{0,16},{8,24},{16,0},{24,8},{1,17},{9,25},{17,1},{25,9},{2,18},{10... | collective-permute-start | bytes 3145736 | tf_op jit(solution)/shard_map/ppermute | solution.py:99
  706.9 87.3 %collective-permute-start.72 = (bf16[512,1024]{1,0:T(8,128)(2,1)}, bf16[512,1024]{1,0:T(8,128)(2,1)}, u32[]{:S(2)}, u32[]{:S(2)}) collective-permute-start(bf16[512,1024]{1,0:T(8,128)(2,1)} %pad_maximum_fusion.19), channel_id=1, source_target_pairs={{0,8},{8,0},{16,24},{24,16},{1,9},{9,1},{17,25},{25,17},{2,10},{10... | collective-permute-start | bytes 3145736 | tf_op jit(solution)/shard_map/ppermute | solution.py:95
  711.4 82.8 %collective-permute-start.70 = (bf16[384,2048]{1,0:T(8,128)(2,1)}, bf16[384,2048]{1,0:T(8,128)(2,1)}, u32[]{:S(2)}, u32[]{:S(2)}) collective-permute-start(bf16[384,2048]{1,0:T(8,128)(2,1)} %add_convert_fusion.5), channel_id=1, source_target_pairs={{0,1},{1,2},{2,3},{3,0},{4,5},{5,6},{6,7},{7,4},{8,9},{9,10},{10,1... | collective-permute-start | bytes 4718600 | tf_op jit(solution)/shard_map/ppermute | solution.py:104
  802.2 37.0 %collective-permute-start.76 = (bf16[512,1536]{1,0:T(8,128)(2,1)}, bf16[512,1536]{1,0:T(8,128)(2,1)}, u32[]{:S(2)}, u32[]{:S(2)}) collective-permute-start(bf16[512,1536]{1,0:T(8,128)(2,1)} %get-tuple-element.449), channel_id=1, source_target_pairs={{0,16},{8,24},{16,0},{24,8},{1,17},{9,25},{17,1},{25,9},{2,18},{10... | collective-permute-start | bytes 4718600 | tf_op jit(solution)/shard_map/ppermute | solution.py:99
  803.2 36.7 %collective-permute-start.77 = (bf16[512,1536]{1,0:T(8,128)(2,1)}, bf16[512,1536]{1,0:T(8,128)(2,1)}, u32[]{:S(2)}, u32[]{:S(2)}) collective-permute-start(bf16[512,1536]{1,0:T(8,128)(2,1)} %get-tuple-element.451), channel_id=1, source_target_pairs={{0,8},{8,0},{16,24},{24,16},{1,9},{9,1},{17,25},{25,17},{2,10},{10... | collective-permute-start | bytes 4718600 | tf_op jit(solution)/shard_map/ppermute | solution.py:95
  809.6 39.0 %collective-permute-start.75 = (bf16[384,2048]{1,0:T(8,128)(2,1)}, bf16[384,2048]{1,0:T(8,128)(2,1)}, u32[]{:S(2)}, u32[]{:S(2)}) collective-permute-start(bf16[384,2048]{1,0:T(8,128)(2,1)} %add_convert_fusion.3), channel_id=1, source_target_pairs={{0,1},{1,2},{2,3},{3,0},{4,5},{5,6},{6,7},{7,4},{8,9},{9,10},{10,1... | collective-permute-start | bytes 4718600 | tf_op jit(solution)/shard_map/ppermute | solution.py:104
  882.1 34.9 %collective-permute-start.87 = (bf16[384,2048]{1,0:T(8,128)(2,1)S(1)}, bf16[384,2048]{1,0:T(8,128)(2,1)S(1)}, u32[]{:S(2)}, u32[]{:S(2)}) collective-permute-start(bf16[384,2048]{1,0:T(8,128)(2,1)S(1)} %bitcast.214), channel_id=1, source_target_pairs={{0,4},{4,0},{1,5},{5,1},{2,6},{6,2},{3,7},{7,3},{8,12},{12,8},{9,1... | collective-permute-start | bytes 4718600 | tf_op jit(solution)/shard_map/ppermute | solution.py:91
  917.0 94.4 %collective-permute-start.88 = (bf16[384,2048]{1,0:T(8,128)(2,1)}, bf16[384,2048]{1,0:T(8,128)(2,1)}, u32[]{:S(2)}, u32[]{:S(2)}) collective-permute-start(bf16[384,2048]{1,0:T(8,128)(2,1)} %get-tuple-element.477), channel_id=1, source_target_pairs={{0,4},{4,0},{1,5},{5,1},{2,6},{6,2},{3,7},{7,3},{8,12},{12,8},{9,1... | collective-permute-start | bytes 4718600 | tf_op jit(solution)/shard_map/ppermute | solution.py:91
  (222 other events, 3060.6 us)
Sparse Core Ops, SparseCore 0:
  11.4 72.3 all-gather.2

commit v4 on v3

--- a/solution.py
+++ b/solution.py
@@ -102,30 +102,6 @@
 def step_z(value):
     size = lax.axis_size("tp")
     return lax.ppermute(value, "tp", [(i, (i + 1) % size) for i in range(size)])
-
-
-def gather_xy(line_x, line_y, x_first, y_first):
-    ax = line_x.send(swap_x, x_first)
-    by = line_y.send(swap_y, y_first)
-    ay = line_y.send(swap_y, x_first)
-    bx = line_x.send(swap_x, y_first)
-    axy = line_y.send(swap_y, ax)
-    byx = line_x.send(swap_x, by)
-    return [x_first, ax, ay, axy], [y_first, bx, by, byx]
-
-
-def scatter_yfirst(line_x, line_y, blocks, last=bf16):
-    three, two = line_y.send(swap_y, blocks[3]), line_y.send(swap_y, blocks[2])
-    other = line_x.send(swap_x, add16(blocks[1], three))
-    total = blocks[0].astype(f32) + two.astype(f32) + other.astype(f32)
-    return total.astype(last)
-
-
-def scatter_xfirst(line_x, line_y, blocks, last=bf16):
-    three, one = line_x.send(swap_x, blocks[3]), line_x.send(swap_x, blocks[1])
-    other = line_y.send(swap_y, add16(blocks[2], three))
-    total = blocks[0].astype(f32) + one.astype(f32) + other.astype(f32)
-    return total.astype(last)
 
 
 def scatter_z(line_z, block_of, last=bf16, add=add16):
@@ -213,6 +189,102 @@
         ),
         name="lay_out",
     )(places, *pieces)
+
+
+def begin_kernel(place, hidden, gain, w_latent, gain_kv, cos_ref, sin_ref, normed, raw, packed, scale_one, scale_kv):
+    values = hidden[...].astype(f32)
+    factor = norm_scale(values)
+    scale_one[...] = factor
+    normed[...] = (values * factor * gain[...]).astype(bf16)
+    latent = dot(normed[...], w_latent[...])
+    own = latent[:, :KVRANK]
+    raw[...] = own
+    factor = norm_scale(own)
+    scale_kv[...] = factor
+    ropes = latent[:, KVRANK:]
+    ropes = jnp.concatenate([ropes, ropes], axis=1)
+    lane = lax.broadcasted_iota(jnp.int32, ropes.shape, 1)
+    ropes = ropes * cos_ref[...] + swap_halves(ropes, lane) * sin_ref[...]
+    packed[:, :KVRANK] = (own * factor * gain_kv[...]).astype(bf16)
+    packed[:, KVRANK:] = ropes[:, :ROPE].astype(bf16)
+
+
+def in_one(kernel, name, outs, place, *operands, scratch=()):
+    in_vmem = pl.BlockSpec(memory_space=pltpu.VMEM)
+    moved = sum(x.size * x.dtype.itemsize for x in operands)
+    return pl.pallas_call(
+        kernel,
+        out_shape=[jax.ShapeDtypeStruct(shape, kind) for shape, kind in outs],
+        grid_spec=pltpu.PrefetchScalarGridSpec(
+            num_scalar_prefetch=1,
+            in_specs=[in_vmem] * len(operands),
+            out_specs=[in_vmem] * len(outs),
+            scratch_shapes=[pltpu.VMEM(shape, kind) for shape, kind in scratch],
+        ),
+        compiler_params=pltpu.CompilerParams(vmem_limit_bytes=58 << 20),
+        cost_estimate=pl.CostEstimate(flops=0, transcendentals=0, bytes_accessed=moved),
+        name=name,
+    )(place, *operands)
+
+
+def finish_kernel(
+    place,
+    latent_far,
+    latent_here,
+    raw,
+    scale_kv,
+    gain_kv,
+    cos_ref,
+    sin_ref,
+    own_part,
+    far_part,
+    w_latent,
+    hidden,
+    scale_one,
+    gain,
+    grad_middle,
+    normed,
+    grad_gain_two,
+    input_grad,
+    w_mine,
+    w_other,
+    grad_gain,
+    grad_gain_kv,
+    grad_w,
+):
+    grads = latent_far[...].astype(f32) + latent_here[...].astype(f32)
+    grad_part, total = norm_back(raw[...], scale_kv[...], gain_kv[...], grads[:, :KVRANK])
+    grad_gain_kv[...] = total[None]
+    ropes = grads[:, KVRANK:]
+    ropes = jnp.concatenate([ropes, ropes], axis=1)
+    lane = lax.broadcasted_iota(jnp.int32, ropes.shape, 1)
+    ropes = ropes * cos_ref[...] - swap_halves(ropes, lane) * sin_ref[...]
+    grad_raw = jnp.concatenate([grad_part, ropes[:, :ROPE]], axis=1).astype(bf16)
+    grad_w[...] = dot_lt(normed[...], grad_raw, bf16)
+    grad_normed = dot_rt(grad_raw, w_latent[...]) + own_part[...].astype(f32)
+    if far_part is not None:
+        grad_normed = grad_normed + far_part[...].astype(f32)
+    grad_in, total = norm_back(
+        hidden[...].astype(f32), scale_one[...], gain[...], grad_normed
+    )
+    grad_gain[...] = total[None]
+    input_grad[...] = (grad_middle[...] + grad_in).astype(bf16)
+    size, kv_size = grad_w.shape[0] // 8, KVRANK // 8
+    for out, half in ((w_mine, place[0]), (w_other, 1 - place[0])):
+        for k in range(4):
+            at = pl.multiple_of((2 * k + half) * size, size)
+            top = k * (size + 16)
+            out[top : top + size, :] = grad_w[pl.ds(at, size), :]
+            both = pl.multiple_of((place[1] ^ k) * 2 * kv_size, 2 * kv_size)
+            kv_row = jnp.broadcast_to(grad_gain_kv[:, pl.ds(both, 2 * kv_size)], (16, 2 * kv_size))
+            kv_row = jnp.where(half == 0, kv_row, pltpu.roll(kv_row, kv_size, 1))[:, :kv_size]
+            row = [
+                jnp.broadcast_to(gains[:, pl.ds(at, size)], (16, size))
+                for gains in (grad_gain, grad_gain_two)
+            ]
+            out[top + size : top + size + 16, :] = jnp.concatenate([*row, kv_row], axis=1).astype(
+                bf16
+            )
 
 
 SENT_BLOCKS = (((3, 0), (2, 0)), ((3, 1), (1, 1)), ((1, 0), (0, 0), (2, 1), (0, 1)))
@@ -664,7 +736,7 @@
 
 
 def pack_kernel(part, place, gate, up, down, hid_mine, hid_other, down_mine, down_other):
-    slice_rows, hidden_here = gate.shape
+    hidden_here, slice_rows = gate.shape
     rest = hidden_here - part
 
     def put(at, low, high, value):
@@ -675,8 +747,8 @@
         high[:, at : at + rest] = value[:, part:]
 
     def write(hid_low, hid_high, down_low, down_high):
-        put(0, hid_low, hid_high, gate[...])
-        put(part, hid_low, hid_high, up[...])
+        put(0, hid_low, hid_high, gate[...].T)
+        put(part, hid_low, hid_high, up[...].T)
         put(0, down_low, down_high, down[...].T)
 
     @pl.when(place[0] == 0)
@@ -689,7 +761,7 @@
 
 
 def pack(place, part, gate, up, down):
-    slice_rows = gate.shape[0]
+    slice_rows = gate.shape[1]
     in_vmem = pl.BlockSpec(memory_space=pltpu.VMEM)
     return pl.pallas_call(
         functools.partial(pack_kernel, part),
@@ -703,6 +775,43 @@
         ),
         name="pack",
     )(place, gate, up, down)
+
+
+def spread_kernel(place, hid_own, hid_far, down_own, down_far, *outs):
+    part = down_own.shape[1]
+    rest = outs[0].shape[0] - part
+
+    def write(low, high):
+        for out, i in zip(outs, (0, 1, 0)):
+            hid, down = (low[0], low[1]) if out is not outs[2] else (low[1], low[1])
+            out[:part, :] = hid[:, i * part : (i + 1) * part].T.astype(f32)
+            hid = high[0] if out is not outs[2] else high[1]
+            out[part:, :] = hid[:, i * part : (i + 1) * part].T.astype(f32)[:rest]
+
+    @pl.when(place[0] == 0)
+    def _():
+        write((hid_own, down_own), (hid_far, down_far))
+
+    @pl.when(place[0] != 0)
+    def _():
+        write((hid_far, down_far), (hid_own, down_own))
+
+
+def spread(place, hidden_here, *halves):
+    slice_rows = halves[0].shape[0]
+    in_vmem = pl.BlockSpec(memory_space=pltpu.VMEM)
+    return pl.pallas_call(
+        spread_kernel,
+        out_shape=[jax.ShapeDtypeStruct((hidden_here, slice_rows), f32)] * 3,
+        grid_spec=pltpu.PrefetchScalarGridSpec(
+            num_scalar_prefetch=1, in_specs=[in_vmem] * 4, out_specs=[in_vmem] * 3
+        ),
+        compiler_params=pltpu.CompilerParams(vmem_limit_bytes=48 << 20),
+        cost_estimate=pl.CostEstimate(
+            flops=0, transcendentals=0, bytes_accessed=20 * slice_rows * hidden_here
+        ),
+        name="spread",
+    )(place, *halves)
 
 
 def weight_grad_kernel(packs, place, left, right_ref, *refs):
@@ -908,17 +1017,22 @@
 
     shift = jnp.stack([core, shard]).astype(jnp.int32)
 
-    tokens = ()
+    tokens, sending = (), []
 
     def now(value):
         return after(value, *tokens) if tokens else value
 
+    def behind(value):
+        return after(value, *tokens, *sending)
+
     def send(line, move, value, free=False):
-        return line.send(move, now(value), free=free)
+        sending.append(now(value))
+        return line.send(move, sending[-1], free=free)
 
     def close(*arrived):
         nonlocal tokens
         tokens = arrived
+        sending.clear()
 
     attn_z, held = [attn_piece], {}
     wanted = []
@@ -947,12 +1061,14 @@
             arrived.append(attn_z[-1])
         return arrived
 
-    close(*attention_round())
     arrived = attention_round()
     hid_a, hid_other, down_a, down_other = pack(
-        now(shift), part, gate_weight, up_weight, down_weight
-    )
-    down_b, hid_b = to_core(down_other), to_core(hid_other)
+        behind(shift), part, gate_weight.T, up_weight.T, down_weight
+    )
+    close(*arrived, hid_a)
+    arrived = attention_round()
+    down_b = send(line_c, swap_core, down_other)
+    hid_b = send(line_c, swap_core, hid_other, free=True)
     grad_own = features(now(cotangent).reshape(own, width))
     inputs16 = features(now(hidden).reshape(own, width))
     inputs = inputs16.astype(f32)
@@ -977,8 +1093,6 @@
     freqs = THETA_BASE ** (-2.0 * jnp.arange(ROPE // 2, dtype=f32) / ROPE)
     angles = positions.astype(f32)[..., None] * freqs
     cos_rows, sin_rows = jnp.cos(angles), jnp.sin(angles)
-    cos_own = cos_rows[0].reshape(own, ROPE // 2)
-    sin_own = sin_rows[0].reshape(own, ROPE // 2)
     cos_lanes = jnp.concatenate([cos_rows] * 4, axis=-1)
     sin_lanes = jnp.concatenate([-sin_rows, sin_rows] * 2, axis=-1)
     tables = (seg_query[..., None], seg_key, cos_lanes, sin_lanes)
@@ -989,14 +1103,25 @@
     arrived = attention_round()
     down_a1 = send(line_x, swap_x, down_a, free=True)
     down_b2 = send(line_y, swap_y, down_b, free=True)
-    factor_one = norm_scale(now(inputs))
-    normed_own = (inputs * factor_one * gain_one).astype(bf16)
-    latent_raw = dot(normed_own, w_latent)
-    latent_part = latent_raw[:, :KVRANK]
-    factor_latent = norm_scale(latent_part)
-    latent_own = (latent_part * factor_latent * gain_kv).astype(bf16)
-    rope_own = rotate(latent_raw[:, KVRANK:], cos_own, sin_own).astype(bf16)
-    latent_pack = jnp.concatenate([latent_own, rope_own], axis=1).reshape(micro, rows, kv_cols)
+    own_lanes = [lanes[0].reshape(own, LANES) for lanes in (cos_lanes, sin_lanes)]
+    normed_own, latent_part, latent_pack, factor_one, factor_latent = in_one(
+        begin_kernel,
+        "begin",
+        [
+            ((own, width), bf16),
+            ((own, KVRANK), f32),
+            ((own, kv_cols), bf16),
+            ((own, 1), f32),
+            ((own, 1), f32),
+        ],
+        shift,
+        behind(inputs16),
+        gain_one[None],
+        w_latent,
+        gain_kv[None],
+        *own_lanes,
+    )
+    latent_pack = latent_pack.reshape(micro, rows, kv_cols)
     close(*arrived, down_a1, down_b2, latent_pack)
     latent_z, grad_z = [latent_pack], [grad_own]
 
@@ -1098,7 +1223,7 @@
     more = tp_size - 3
     grads_ahead(more)
     grad_far = [send(line_c, swap_core, piece, free=True) for piece in grad_z[:2]]
-    mixed = attend(heads, tp_size, window, scale, now(place), q_lin, kv_all, rope_keys, *tables)
+    mixed = attend(heads, tp_size, window, scale, behind(place), q_lin, kv_all, rope_keys, *tables)
     mixed = mixed.reshape(slots * own, tp_size * out_width)
     close(hid_b1, hid_a2, grad_z[-1], *grad_far, mixed)
 
@@ -1163,7 +1288,7 @@
         while len(grad_far) <= j:
             grad_far.append(send(line_c, swap_core, grad_z[len(grad_far)], free=True))
         made = feed(
-            now(shift),
+            behind(shift),
             j,
             tp_size,
             [norm_z[j], norm_far[j], grad_z[j], grad_far[j]],
@@ -1180,7 +1305,7 @@
     first, second = ((3, 0), (2, 0), (3, 1), (1, 1)), ((1, 0), (0, 0), (2, 1), (0, 1))
     arrived = back_ring.step()
     down_y, down_x, down_kept = weight_grad(
-        now(shift), SENT_BLOCKS, slice_rows, grad_all, act_all
+        behind(shift), SENT_BLOCKS, slice_rows, grad_all, act_all
     )
     close(*arrived, down_y)
 
@@ -1190,25 +1315,25 @@
         arrived += back_ring.step()
     back_ring.block(0)
     own3, own2, far3, far1 = weight_grad(
-        now(shift), [(block,) for block in first], slice_rows, normed_all, hidden_all
+        behind(shift), [(block,) for block in first], slice_rows, normed_all, hidden_all
     )
     close(*arrived, down_y, down_x, own3)
 
     own3, far3 = send(line_y, swap_y, own3), send(line_x, swap_x, far3)
     arrived = out_ring.step()
-    grad_normed_two = back_ring.result()
-    own1, own0, far2, far0 = weight_grad(
-        now(shift), [(block,) for block in second], slice_rows, normed_all, hidden_all
-    )
-    close(*arrived, own3, far3, own1)
-
-    own2, far1 = send(line_y, swap_y, own2), send(line_x, swap_x, far1)
-
-    grad_mid_norm, grad_gain_two = norm_back(middle, factor_two, gain_two, now(grad_normed_two))
+    grad_mid_norm, grad_gain_two = norm_back(middle, factor_two, gain_two, back_ring.result())
     grad_middle = grad_own.astype(f32) + grad_mid_norm
     grad_attn = grad_middle.astype(bf16)
+    attn_far = send(line_c, swap_core, grad_attn, free=True)
+    own1, own0, far2, far0 = weight_grad(
+        behind(shift), [(block,) for block in second], slice_rows, normed_all, hidden_all
+    )
+    close(*arrived, own3, far3, attn_far, own1)
+
+    own2, far1 = send(line_y, swap_y, own2), send(line_x, swap_x, far1)
+
     if split:
-        grad_attn = jnp.concatenate([grad_attn, to_core(grad_attn)])
+        grad_attn = jnp.concatenate([grad_attn, attn_far])
     grad_mixed = dot(grad_attn, w_out, bf16)
     out_blocks = [dot_lt(columns(grad_attn, k), mixed, bf16) for k in range(4)]
     close(own2, far1, grad_mixed, *out_blocks)
@@ -1254,7 +1379,7 @@
         tp_size,
         window,
         scale,
-        now(place),
+        behind(place),
         q_lin,
         kv_all,
         rope_keys,
@@ -1273,134 +1398,163 @@
     arrived = []
     while out_ring.at < tp_size - 1:
         arrived += out_ring.step()
-    close(*query_sent, *arrived, latent_far)
-
-    latent_sum = add16(latent_mine, now(latent_far))
-
-    def latent_block(j):
-        return lax.dynamic_slice_in_dim(latent_sum, (place_z - j) % tp_size * rows, rows, 1)
-
-    latent_step = send(line_z, step_z, latent_block(1))
-    out_sums = stage_two(kept_of(out_blocks), out_sent)
-    grad_normed_one = parts[0].reshape(own, width).astype(f32)
-    if split:
-        far = send(line_c, swap_core, parts[1].reshape(own, width), free=True)
-        grad_normed_one = grad_normed_one + far.astype(f32)
-    close(latent_step, out_sums[0][2], out_sums[1][2])
-
-    for j in range(2, tp_size - 1):
-        latent_step = send(line_z, step_z, add16(now(latent_step), latent_block(j)))
-    expand_sent = stage_one(*sums[3:5])
-    close(latent_step, *expand_sent)
-
-    latent_step = send(line_z, step_z, add16(now(latent_step), latent_block(tp_size - 1)))
-    query_sums = stage_two(sums[2], query_sent)
-    close(latent_step, query_sums[0][2], query_sums[1][2])
-
-    expand_sums = stage_two(sums[5], expand_sent)
-    grad_latent_own = (now(latent_step).astype(f32) + latent_block(0).astype(f32)).reshape(
-        own, kv_cols
-    )
-    output = (middle + out_ring.result()).astype(bf16)
     hid_own = add16(own0, own2, over_x[:, : 2 * part])
     hid_other = add16(far0, far1, over_y[:, : 2 * part])
     down_own = add16(down0, down2, over_x[:, 2 * part :])
     down_other = add16(downf0, downf1, over_y[:, 2 * part :])
-    hid_far, down_far = to_core(hid_other), to_core(down_other)
-    grad_wgate, grad_wup, grad_wdown = (
-        in_order(core, near, far, 1)[:, :hidden_here].astype(f32)
-        for near, far in (
-            (hid_own[:, :part], hid_far[:, :part]),
-            (hid_own[:, part:], hid_far[:, part:]),
-            (down_own, down_far),
-        )
-    )
-    grad_wdown = grad_wdown.T
-
-    def over_z(value, columns):
-        return scatter_z(Line(), lambda j: value[:, columns * j : columns * (j + 1)])
-
-    out_here = over_z(stage_sum(*out_sums), out_width)
-    query_here = over_z(stage_sum(*query_sums), q_width)
-    expand_here = over_z(stage_sum(*expand_sums), kv_width)
-    out_cores = out_here.reshape(cores, slice_rows, out_width)
-    query_cores = query_here.reshape(cores, slice_rows, q_width)
-    expand_cores = expand_here.reshape(cores, expand_rows, kv_width)
-
-    def finish(by_core):
-        kept, given = mine(by_core, 0), to_core(others(by_core, 0))
+    close(*query_sent, *arrived, latent_far, hid_own, hid_other, down_own, down_other)
+
+    latent_sum = add16(latent_mine, now(latent_far))
+
+    def latent_block(j):
+        return lax.dynamic_slice_in_dim(latent_sum, (place_z - j) % tp_size * rows, rows, 1)
+
+    latent_step = send(line_z, step_z, latent_block(1))
+    out_sums = stage_two(kept_of(out_blocks), out_sent)
+    expand_sent = stage_one(*sums[3:5])
+    output = (middle + out_ring.result()).astype(bf16)
+    close(latent_step, out_sums[0][2], out_sums[1][2], *expand_sent, output)
+
+    class Columns:
+        def __init__(self, sums, count):
+            self.value, self.count, self.at = stage_sum(*sums), count, 1
+            self.total = self.block(1)
+
+        def block(self, j):
+            return self.value[:, self.count * j : self.count * (j + 1)]
+
+        def step(self):
+            if self.at > tp_size - 1:
+                return ()
+            self.total = line_z.send(step_z, now(self.total), free=True)
+            self.at += 1
+            return (self.total,)
+
+        def add(self):
+            if self.at <= tp_size:
+                self.total = add16(now(self.total), self.block(self.at % tp_size))
+                if self.at == tp_size:
+                    self.at += 1
+
+    for j in range(2, tp_size - 1):
+        latent_step = send(line_z, step_z, add16(now(latent_step), latent_block(j)))
+    expand_sums = stage_two(sums[5], expand_sent)
+    out_columns = Columns(out_sums, out_width)
+    arrived = out_columns.step()
+    hid_far = send(line_c, swap_core, hid_other)
+    close(latent_step, expand_sums[0][2], expand_sums[1][2], *arrived, hid_far)
+
+    latent_step = send(line_z, step_z, add16(now(latent_step), latent_block(tp_size - 1)))
+    query_sums = stage_two(sums[2], query_sent)
+    out_columns.add()
+    expand_columns = Columns(expand_sums, kv_width)
+    arrived = [*out_columns.step(), *expand_columns.step()]
+    far_part = None
+    if split:
+        far_part = send(line_c, swap_core, parts[1].reshape(own, width))
+    down_far = send(line_c, swap_core, down_other, free=True)
+    close(latent_step, query_sums[0][2], query_sums[1][2], *arrived, down_far, far_part)
+
+    query_columns = Columns(query_sums, q_width)
+    out_columns.add()
+    expand_columns.add()
+    arrived = [*query_columns.step(), *expand_columns.step(), *out_columns.step()]
+    grad_wgate, grad_wup, grad_wdown = spread(
+        behind(shift), hidden_here, hid_own, hid_far, down_own, down_far
+    )
+    grad_wgate, grad_wup = grad_wgate.T, grad_wup.T
+    others_of = [] if far_part is None else [far_part]
+    kernel = finish_kernel
+    if far_part is None:
+        kernel = lambda *refs: finish_kernel(*refs[:9], None, *refs[9:])
+    gathered_rows = 4 * (width // 8 + 16)
+    input_grad, w_mine, w_other = in_one(
+        kernel,
+        "finish",
+        [((own, width), bf16), *[((gathered_rows, kv_cols), bf16)] * 2],
+        shift,
+        behind(latent_step).reshape(own, kv_cols),
+        latent_block(0).reshape(own, kv_cols),
+        latent_part,
+        factor_latent,
+        gain_kv[None],
+        *own_lanes,
+        parts[0].reshape(own, width),
+        *others_of,
+        w_latent,
+        inputs16,
+        factor_one,
+        gain_one[None],
+        grad_middle,
+        normed_own,
+        grad_gain_two[None],
+        scratch=[((1, width), f32), ((1, KVRANK), f32), ((width, kv_cols), bf16)],
+    )
+    close(*arrived, input_grad, grad_wdown)
+
+    rings = [query_columns, expand_columns]
+    for ring in rings:
+        ring.add()
+    arrived = [step for ring in rings for step in ring.step()]
+    w_sum = add16(w_mine, send(line_c, swap_core, w_other, free=True))
+    high = w_sum.shape[0] // 4
+    w_far = [
+        lax.ppermute(w_sum[high * k : high * (k + 1)], "shard", [(i, i ^ k) for i in range(4)])
+        for k in (1, 2, 3)
+    ]
+    close(*arrived, *w_far)
+
+    w_sum = add16(w_sum[:high], *(now(each) for each in w_far))
+    for ring in rings:
+        ring.add()
+    arrived = [step for ring in rings for step in ring.step()]
+
+    def rows_for(at):
+        rows_at = lax.dynamic_slice_in_dim(w_sum, at * small_rows, small_rows, 0)
+        return jnp.concatenate([rows_at, w_sum[high - 16 :]])
+
+    w_here = rows_for(place_z).astype(f32)
+    for j in range(1, tp_size):
+        pairs = [(i, (i + j) % tp_size) for i in range(tp_size)]
+        w_here = w_here + lax.ppermute(rows_for((place_z + j) % tp_size), "tp", pairs).astype(f32)
+    grad_wlatent, gains = w_here[:small_rows], w_here[small_rows]
+
+    def own_gains(start, count):
+        each = count // tp_size
+        return lax.dynamic_slice_in_dim(gains[start : start + count], place_z * each, each, 0)
+
+    grad_gain_one, grad_gain_two = own_gains(0, width // 8), own_gains(width // 8, width // 8)
+    grad_gain_latent = own_gains(width // 4, KVRANK // 8)
+    close(*arrived)
+    for ring in (*rings, out_columns):
+        while ring.at <= tp_size:
+            ring.add()
+            if ring.at < tp_size:
+                ring.total = step_z(ring.total)
+                ring.at += 1
+    query_here, expand_here, out_here = (ring.total for ring in (*rings, out_columns))
+
+    def finished(value, here_rows):
+        halves = value.reshape(cores, here_rows, value.shape[1])
+        kept, given = mine(halves, 0), swap_core(others(halves, 0))
         if split:
             return in_order(core, kept[:, None], given[:, None], 1).astype(f32)
         return (kept.astype(f32) + given.astype(f32))[:, None]
 
-    grad_wout = finish(out_cores).reshape(slice_rows, -1).T
-    grad_wexpand = finish(expand_cores).reshape(expand_rows, -1)
-    grad_wquery = q_disorder(finish(query_cores))
-
-    grad_latent_part, grad_gain_latent = norm_back(
-        latent_part, factor_latent, gain_kv, grad_latent_own[:, :KVRANK]
-    )
-    grad_raw = jnp.concatenate(
-        [grad_latent_part, rotate(grad_latent_own[:, KVRANK:], cos_own, -sin_own)], axis=-1
-    ).astype(bf16)
-    grad_normed_one = grad_normed_one + dot_rt(grad_raw, w_latent)
-    grad_in_norm, grad_gain_one = norm_back(inputs, factor_one, gain_one, grad_normed_one)
-    input_grad = (grad_middle + grad_in_norm).astype(bf16)
-
-    core_rows = width // 4 // cores
-
-    def core_features(values, at, size):
-        return jnp.concatenate(
-            [
-                lax.dynamic_slice_in_dim(values, (cores * k + at) * size, size, values.ndim - 1)
-                for k in range(4)
-            ],
-            axis=-1,
-        )
-
-    def gains_of(at):
-        pieces = [
-            core_features(grads, at, grads.shape[0] // (4 * cores)).reshape(4, tp_size, -1)
-            for grads in (grad_gain_one, grad_gain_two, features(grad_gain_latent))
-        ]
-        return jnp.concatenate(pieces, axis=-1)
-
-    def over_all(kept, given, rounded):
-        kept = kept.astype(f32) + swap_core(given.astype(rounded)).astype(f32)
-        sent = kept.astype(rounded)
-        total = kept[0]
-        for k in (1, 2, 3):
-            gone = lax.ppermute(sent[k], "shard", [(i, i ^ k) for i in range(4)])
-            total = total + gone.astype(f32)
-        sent = total.astype(rounded)
-        here = lax.dynamic_index_in_dim(total, place_z, 0, keepdims=False)
-        for j in range(1, tp_size):
-            gone = lax.dynamic_index_in_dim(sent, (place_z + j) % tp_size, 0, keepdims=False)
-            gone = lax.ppermute(gone, "tp", [(i, (i + j) % tp_size) for i in range(tp_size)])
-            here = here + gone.astype(f32)
-        return here
-
-    grad_wlatent = over_all(
-        *(
-            dot_lt(core_features(normed_own, at, core_rows), grad_raw).reshape(
-                4, tp_size, small_rows, kv_cols
-            )
-            for at in (core, 1 - core)
-        ),
-        bf16,
-    )
-    gain_grads = over_all(gains_of(core), gains_of(1 - core), f32)
+    grad_wout = finished(out_here, slice_rows).reshape(slice_rows, -1).T
+    grad_wexpand = finished(expand_here, expand_rows).reshape(expand_rows, -1)
+    grad_wquery = q_disorder(finished(query_here, slice_rows))
     like = (micro, 1, rows, width)
     return (
         features(output).reshape(like),
         features(input_grad).reshape(like),
-        gain_grads[:gain_rows],
+        grad_gain_one,
         grad_wquery,
         grad_wlatent,
-        gain_grads[2 * gain_rows :],
+        grad_gain_latent,
         grad_wexpand,
         grad_wout,
-        gain_grads[gain_rows : 2 * gain_rows],
+        grad_gain_two,
         grad_wgate,
         grad_wup,
         grad_wdown,

time: 1060 us -> 1040 us (0.981)
  Pallas kernels: 386 us -> 412 us
  local copies, waits for them, and re-layouts: 93.1 us -> 69.8 us
    ppermute x22, waiting for transfers between devices: 46.3 us -> 99.5 us  [swap_y(): return lax.ppermute(value, 'shard', [(i, i ^ 2) for i in range(4)])]
    ppermute x22, waiting for transfers between devices: 92.9 us -> 58.6 us  [swap_x(): return lax.ppermute(value, 'shard', [(i, i ^ 1) for i in range(4)])]
    ppermute x30, waiting for transfers between devices: 145 us -> 114 us  [step_z(): return lax.ppermute(value, 'tp', [(i, (i + 1) % size) for i in range(size)])]
    pallas_call x0 -> x3, Pallas kernels: none -> 25.7 us  [the longest x2 18.9 us: in_one(): pl.pallas_call(kernel, out_shape=[jax.ShapeDtypeStruct(shape, kind) for s...]
    concatenate x25 -> x1, local copies, waits for them, and re-layouts: 15.8 us -> 2.79 us  [shards(): jnp.concatenate([normed_own, send(line_c, swap_core, normed_own)])]
    convert_element_type x29 -> x33, other arithmetic: 41.7 us -> 53.4 us  [add16(): return total.astype(bf16)]
    all_gather x1, waiting for transfers between devices: 0.01 us -> 11 us  [shards(): small_all = lax.all_gather(small, ('shard', 'ctx', 'tp'), axis=0)]
    ppermute x33 -> x32, waiting for transfers between devices: 25.4 us -> 20.9 us  [swap_core(): return lax.ppermute(value, 'ctx', [(0, 1), (1, 0)])]
  transfers between devices with their start and end apart: 120 -> 113, of which waited for: 55 -> 51; matrix products, arithmetic and copies ran while one was open for 18% -> 15% of each run, Pallas kernels for 37% -> 40%
where the time goes in v4:
time: 1040 us; the launch traced here: 1030 us
  Pallas kernels  412 us (40%)
  waiting for transfers between devices  324 us (31%)
  other arithmetic  95.4 us (9%)
  starting transfers between devices  76.9 us (7%)
  local copies, waits for them, and re-layouts  69.8 us (7%)
  matrix products  37.3 us (4%)
  between operations  16.5 us (2%)
    pallas_call x4, Pallas kernels, feed(): pl.pallas_call(functools.partial(feed_kernel, part, rows, offset), out_sh...  161 us
    ppermute x30, waiting for transfers between devices, step_z(): return lax.ppermute(value, 'tp', [(i, (i + 1) % size) for i in range(size)])  114 us
    ppermute x22, waiting for transfers between devices, swap_y(): return lax.ppermute(value, 'shard', [(i, i ^ 2) for i in range(4)])  99.5 us
    pallas_call x3, Pallas kernels, weight_grad(): pl.pallas_call(functools.partial(weight_grad_kernel, packs), out_shape=[j...  94.5 us
    pallas_call x1, Pallas kernels, attend_back(): pl.pallas_call(functools.partial(attend_back_kernel, heads, width, scale,...  82.6 us
    ppermute x22, waiting for transfers between devices, swap_x(): return lax.ppermute(value, 'shard', [(i, i ^ 1) for i in range(4)])  58.6 us
    convert_element_type x33, other arithmetic, add16(): return total.astype(bf16)  53.4 us
    unnamed x260, local copies, waits for them, and re-layouts  27.7 us
  transfers between devices with their start and end apart: 113, of which 51 were waited for; matrix products, arithmetic and copies ran while one was open for 15% of the time, Pallas kernels for 40%

profile of v4, /device:TPU:0, one launch (start us, length us, event | category | flops | bytes accessed | tf_op | source)
XLA Modules:
  0.0 1032.1 jit_solution(4548331743892602801)
XLA Ops:
  26.5 9.1 collective-permute-done.1.refs_1_
  37.1 4.6 collective-permute-done.3.refs_4_
  51.5 12.1 %collective-permute-done.6.refs_6_ = bf16[512,768]{1,0:T(8,128)(2,1)S(1)} collective-permute-done((bf16[512,768]{1,0:T(8,128)(2,1)}, bf16[512,768]{1,0:T(8,128)(2,1)S(1)}, u32[]{:S(2)}, u32[]{:S(2)}) %collective-permute-start.6) | collective-permute-done | bytes 786464 | tf_op jit(solution)/shard_map/ppermute | solution.py:99
  66.0 4.4 collective-permute-done.4.refs_8_
  74.7 11.0 %all-gather.3.cloned.1.call-done = bf16[2560,576]{1,0:T(8,128)(2,1)} async-done(((bf16[80,576]{1,0:T(8,128)(2,1)}), bf16[2560,576]{1,0:T(8,128)(2,1)}) %all-gather.3.cloned.1.call-update) | async-done | bytes 2949136 | tf_op jit(solution)/shard_map/all_gather | solution.py:954
  93.7 7.2 pad_maximum_fusion.2.w_latent
  100.9 6.3 begin.1
  111.5 14.2 %collective-permute-done.18.refs_1_ = bf16[3,128,576]{2,1,0:T(8,128)(2,1)S(1)} collective-permute-done((bf16[3,128,576]{2,1,0:T(8,128)(2,1)}, bf16[3,128,576]{2,1,0:T(8,128)(2,1)S(1)}, u32[]{:S(2)}, u32[]{:S(2)}) %collective-permute-start.18) | collective-permute-done | bytes 442400 | tf_op jit(solution)/shard_map/ppermute | solution.py:104
  125.7 18.3 %collective-permute-done.17.refs_14_ = bf16[256,1408]{1,0:T(8,128)(2,1)S(1)} collective-permute-done((bf16[256,1408]{1,0:T(8,128)(2,1)}, bf16[256,1408]{1,0:T(8,128)(2,1)S(1)}, u32[]{:S(2)}, u32[]{:S(2)}) %collective-permute-start.17) | collective-permute-done | bytes 720928 | tf_op jit(solution)/shard_map/ppermute | solution.py:99
  149.3 12.9 %collective-permute-done.23.refs_2_ = bf16[3,128,576]{2,1,0:T(8,128)(2,1)S(1)} collective-permute-done((bf16[3,128,576]{2,1,0:T(8,128)(2,1)S(1)}, bf16[3,128,576]{2,1,0:T(8,128)(2,1)S(1)}, u32[]{:S(2)}, u32[]{:S(2)}) %collective-permute-start.23) | collective-permute-done | bytes 442400 | tf_op jit(solution)/shard_map/ppermute | solution.py:104
  162.2 17.0 %collective-permute-done.22.refs_15_ = bf16[256,1408]{1,0:T(8,128)(2,1)S(1)} collective-permute-done((bf16[256,1408]{1,0:T(8,128)(2,1)}, bf16[256,1408]{1,0:T(8,128)(2,1)S(1)}, u32[]{:S(2)}, u32[]{:S(2)}) %collective-permute-start.22) | collective-permute-done | bytes 720928 | tf_op jit(solution)/shard_map/ppermute | solution.py:99
  191.8 10.2 collective-permute-done.28.refs_3_
  213.7 11.6 %assemble.1 = (bf16[2048,1536]{1,0:T(8,128)(2,1)}, bf16[2048,1024]{1,0:T(8,128)(2,1)}, bf16[512,2048]{1,0:T(8,128)(2,1)}) custom-call(s32[2]{0:T(128)S(1)} %copy-done.20, bf16[512,768]{1,0:T(8,128)(2,1)S(1)} %pad_maximum_fusion.15.refs_0_, bf16[512,768]{1,0:T(8,128)(2,1)S(1)} %collective-permute-done.1.refs_1_, ...), custom_call_target="tpu_custom_call" | custom-call | bytes 25165824 | tf_op jit(solution)/shard_map/assemble/pallas_call | solution.py:144
  225.3 9.6 fusion.58
  238.4 5.2 lay_out.1
  243.6 11.7 %convolution_convert_fusion = bf16[3072,2048]{1,0:T(8,128)(2,1)} fusion(bf16[3072,512]{1,0:T(8,128)(2,1)} %bitcast.184, bf16[512,2048]{1,0:T(8,128)(2,1)} %get-tuple-element.344.wkv_ref), kind=kOutput, calls=%fused_computation | convolution fusion | flops 6448742400 | bytes 17825792 | tf_op jit(solution)/shard_map/dot_general | solution.py:51
  262.2 27.3 %attend.1 = bf16[2,3,128,1024]{3,2,1,0:T(8,128)(2,1)S(1)} custom-call(s32[3,2]{1,0:T(4,128)S(1)} %pad_add_fusion.2.place, f32[2,3,128,1536]{3,2,1,0:T(8,128)S(1)} %bitcast.135, bf16[3,1024,2048]{2,1,0:T(8,128)(2,1)} %bitcast.143, bf16[3,1024,128]{2,1,0:T(8,128)(2,1)S(1)} %copy-done.12, s32[3,256,1]{2,1,0:T(8,128)S(1)} %copy.108.segq_ref, ...), custom_call_target="tpu_custom_call" | custom-call | flops 3019898880 | bytes 19660800 | tf_op jit(solution)/shard_map/attend/pallas_call | solution.py:483
  310.2 31.4 %collective-permute-done.41.refs_7_ = bf16[256,2816]{1,0:T(8,128)(2,1)S(1)} collective-permute-done((bf16[256,2816]{1,0:T(8,128)(2,1)}, bf16[256,2816]{1,0:T(8,128)(2,1)S(1)}, u32[]{:S(2)}, u32[]{:S(2)}) %collective-permute-start.41) | collective-permute-done | bytes 1441824 | tf_op jit(solution)/shard_map/ppermute | solution.py:99
  344.3 40.5 %feed.4 = (bf16[384,2048]{1,0:T(8,128)(2,1)}, bf16[384,2048]{1,0:T(8,128)(2,1)}, bf16[384,2048]{1,0:T(8,128)(2,1)}, bf16[384,2048]{1,0:T(8,128)(2,1)}, bf16[3072...) custom-call(s32[2]{0:T(128)} %copy-done.19, ...), custom_call_target="tpu_custom_call" | custom-call | flops 26575110144 | bytes 42663936 | tf_op jit(solution)/shard_map/feed/pallas_call | solution.py:705
  386.5 40.3 %feed.5 = (bf16[384,2048]{1,0:T(8,128)(2,1)}, bf16[384,2048]{1,0:T(8,128)(2,1)}, bf16[384,2048]{1,0:T(8,128)(2,1)}, bf16[384,2048]{1,0:T(8,128)(2,1)}, bf16[3072...) custom-call(s32[2]{0:T(128)} %copy-done.19, ...), custom_call_target="tpu_custom_call", output_to_operand_aliasing={{4}: (21, {}), {5}: (22, {}), {6}: (23, {}), {7}: (24, {})} | custom-call | flops 26575110144 | bytes 42663936 | tf_op jit(solution)/shard_map/feed/pallas_call | solution.py:705
  427.9 40.3 %feed.6 = (bf16[384,2048]{1,0:T(8,128)(2,1)}, bf16[384,2048]{1,0:T(8,128)(2,1)}, bf16[384,2048]{1,0:T(8,128)(2,1)}, bf16[384,2048]{1,0:T(8,128)(2,1)}, bf16[3072...) custom-call(s32[2]{0:T(128)} %copy-done.19, ...), custom_call_target="tpu_custom_call", output_to_operand_aliasing={{4}: (21, {}), {5}: (22, {}), {6}: (23, {}), {7}: (24, {})} | custom-call | flops 26575110144 | bytes 42663936 | tf_op jit(solution)/shard_map/feed/pallas_call | solution.py:705
  476.0 40.4 %feed.7 = (bf16[384,2048]{1,0:T(8,128)(2,1)}, bf16[384,2048]{1,0:T(8,128)(2,1)}, bf16[384,2048]{1,0:T(8,128)(2,1)}, bf16[384,2048]{1,0:T(8,128)(2,1)}, bf16[3072...) custom-call(s32[2]{0:T(128)} %copy-done.19, ...), custom_call_target="tpu_custom_call", output_to_operand_aliasing={{4}: (21, {}), {5}: (22, {}), {6}: (23, {}), {7}: (24, {})} | custom-call | flops 26575110144 | bytes 42663936 | tf_op jit(solution)/shard_map/feed/pallas_call | solution.py:705
  522.4 36.0 %weight_grad.3 = (bf16[512,1408]{1,0:T(8,128)(2,1)S(1)}, bf16[512,1408]{1,0:T(8,128)(2,1)S(1)}, bf16[1024,1408]{1,0:T(8,128)(2,1)S(1)}) custom-call(s32[2]{0:T(128)S(1)} %copy-done.21, bf16[3072,2048]{1,0:T(8,128)(2,1)} %get-tuple-element.411.left, bf16[3072,1408]{1,0:T(8,128)(2,1)} %get-tuple-element.412.right_ref), custom_call_target="tpu_custom_call" | custom-call | flops 17716740096 | bytes 27000832 | tf_op jit(solution)/shard_map/weight_grad/pallas_call | solution.py:861
  565.5 29.4 %weight_grad.4 = (bf16[256,2816]{1,0:T(8,128)(2,1)S(1)}, bf16[256,2816]{1,0:T(8,128)(2,1)S(1)}, bf16[256,2816]{1,0:T(8,128)(2,1)S(1)}, bf16[256,2816]{1,0:T(8,128)(2,1)S(1)}) custom-call(s32[2]{0:T(128)S(1)} %copy-done.21, bf16[3072,2048]{1,0:T(8,128)(2,1)} %get-tuple-element.426.left, bf16[3072,2816]{1,0:T(8,128)(2,1)} %get-tuple-element.427.right_ref), custom_call_target="tpu_custom_call" | custom-call | flops 17716740096 | bytes 29360128 | tf_op jit(solution)/shard_map/weight_grad/pallas_call | solution.py:861
  595.0 9.1 collective-permute-done.56
  608.0 4.3 fusion.49
  623.7 29.0 %weight_grad.5 = (bf16[256,2816]{1,0:T(8,128)(2,1)S(1)}, bf16[256,2816]{1,0:T(8,128)(2,1)S(1)}, bf16[256,2816]{1,0:T(8,128)(2,1)S(1)}, bf16[256,2816]{1,0:T(8,128)(2,1)S(1)}) custom-call(s32[2]{0:T(128)S(1)} %copy-done.21, bf16[3072,2048]{1,0:T(8,128)(2,1)} %get-tuple-element.426.left, bf16[3072,2816]{1,0:T(8,128)(2,1)} %get-tuple-element.427.right_ref), custom_call_target="tpu_custom_call" | custom-call | flops 17716740096 | bytes 29360128 | tf_op jit(solution)/shard_map/weight_grad/pallas_call | solution.py:861
  652.7 4.3 collective-permute-done.62
  666.6 5.4 fusion.2
  672.1 17.4 %collective-permute-done.66 = bf16[256,2816]{1,0:T(8,128)(2,1)S(1)} collective-permute-done((bf16[256,2816]{1,0:T(8,128)(2,1)S(1)}, bf16[256,2816]{1,0:T(8,128)(2,1)S(1)}, u32[]{:S(2)}, u32[]{:S(2)}) %collective-permute-start.66) | collective-permute-done | bytes 1441824 | tf_op jit(solution)/shard_map/ppermute | solution.py:95
  704.7 82.6 %attend_back.1 = (bf16[512,1536]{1,0:T(8,128)(2,1)}, bf16[512,1536]{1,0:T(8,128)(2,1)}, bf16[1024,1536]{1,0:T(8,128)(2,1)}, bf16[128,2048]{1,0:T(8,128)(2,1)}, b...) custom-call(s32[3,2]{1,0:T(4,128)} %copy-done.22, ...), custom_call_target="tpu_custom_call" | custom-call | flops 30601641984 | bytes 42467328 | tf_op jit(solution)/shard_map/attend_back/pallas_call | solution.py:544
  787.4 4.2 copy.110
  811.1 26.2 %collective-permute-done.77 = bf16[512,1536]{1,0:T(8,128)(2,1)} collective-permute-done((bf16[512,1536]{1,0:T(8,128)(2,1)S(1)}, bf16[512,1536]{1,0:T(8,128)(2,1)}, u32[]{:S(2)}, u32[]{:S(2)}) %collective-permute-start.77) | collective-permute-done | bytes 1572896 | tf_op jit(solution)/shard_map/ppermute | solution.py:95
  838.2 5.7 collective-permute-done.75
  860.9 4.1 add_convert_fusion.1
  865.0 9.5 collective-permute-done.79
  883.7 5.4 collective-permute-done.87
  891.6 7.5 collective-permute-done.84
  907.2 14.2 %collective-permute-done.91 = bf16[256,1536]{1,0:T(8,128)(2,1)S(1)} collective-permute-done((bf16[256,1536]{1,0:T(8,128)(2,1)S(1)}, bf16[256,1536]{1,0:T(8,128)(2,1)S(1)}, u32[]{:S(2)}, u32[]{:S(2)}) %collective-permute-start.91) | collective-permute-done | bytes 786464 | tf_op jit(solution)/shard_map/ppermute | solution.py:99
  924.7 7.8 collective-permute-done.92
  932.4 9.3 collective-permute-done.89
  942.7 6.7 spread.1
  949.4 12.6 %finish.1 = (bf16[384,2048]{1,0:T(8,128)(2,1)}, bf16[1088,576]{1,0:T(8,128)(2,1)}, bf16[1088,576]{1,0:T(8,128)(2,1)}) custom-call(s32[2]{0:T(128)} %copy-done.19, bf16[384,576]{1,0:T(8,128)(2,1)} %bitcast.172, bf16[384,576]{1,0:T(8,128)(2,1)} %bitcast.150, f32[384,512]{1,0:T(8,128)} %get-tuple-element.523.raw, f32[384,1]{1,0:T(8,128)} %get-tuple-element.524.scale_kv, ...), custom_call_target="tpu_custom_call" | custom-call | bytes 13882368 | tf_op jit(solution)/shard_map/finish/pallas_call | solution.py:215
  970.5 4.3 collective-permute-start.101
  984.7 5.4 collective-permute-done.102
  990.7 7.3 collective-permute-done.103
  999.9 4.1 collective-permute-start.106
  1004.8 10.5 %collective-permute-done.105 = bf16[80,576]{1,0:T(8,128)(2,1)S(1)} collective-permute-done((bf16[80,576]{1,0:T(8,128)(2,1)S(1)}, bf16[80,576]{1,0:T(8,128)(2,1)S(1)}, u32[]{:S(2)}, u32[]{:S(2)}) %collective-permute-start.105) | collective-permute-done | bytes 92192 | tf_op jit(solution)/shard_map/ppermute | solution.py:1519
  (607 shorter events, 268.0 us)
Async XLA Ops:
  7.2 78.5 %all-gather.3.cloned.1.call-start = ((), (), s32[]{:S(2)}) async-start(), calls=%async_computation | async-start | bytes 3379200 | tf_op jit(solution)/shard_map/all_gather | solution.py:954
  70.4 36.8 %collective-permute-start.13 = (bf16[256,1408]{1,0:T(8,128)(2,1)}, bf16[256,1408]{1,0:T(8,128)(2,1)}, u32[]{:S(2)}, u32[]{:S(2)}) collective-permute-start(bf16[256,1408]{1,0:T(8,128)(2,1)} %collective-permute-done.7.refs_16_), channel_id=1, source_target_pairs={{0,16},{8,24},{16,0},{24,8},{1,17},{9,25},{17,1},{25,9},{2,18},{10... | collective-permute-start | bytes 2162696 | tf_op jit(solution)/shard_map/ppermute | solution.py:99
  71.9 35.3 %collective-permute-start.12 = (bf16[256,1408]{1,0:T(8,128)(2,1)}, bf16[256,1408]{1,0:T(8,128)(2,1)}, u32[]{:S(2)}, u32[]{:S(2)}) collective-permute-start(bf16[256,1408]{1,0:T(8,128)(2,1)} %get-tuple-element.311.refs_12_), channel_id=1, source_target_pairs={{0,8},{8,0},{16,24},{24,16},{1,9},{9,1},{17,25},{25,17},{2,10},{10... | collective-permute-start | bytes 2162696 | tf_op jit(solution)/shard_map/ppermute | solution.py:95
  73.4 33.8 %collective-permute-start.11 = (bf16[512,768]{1,0:T(8,128)(2,1)S(1)}, bf16[512,768]{1,0:T(8,128)(2,1)}, u32[]{:S(2)}, u32[]{:S(2)}) collective-permute-start(bf16[512,768]{1,0:T(8,128)(2,1)S(1)} %collective-permute-done.1.refs_1_), channel_id=1, source_target_pairs={{0,16},{8,24},{16,0},{24,8},{1,17},{9,25},{17,1},{25,9},{2,18},{10... | collective-permute-start | bytes 2359304 | tf_op jit(solution)/shard_map/ppermute | solution.py:99
  73.9 33.4 %collective-permute-start.10 = (bf16[512,768]{1,0:T(8,128)(2,1)S(1)}, bf16[512,768]{1,0:T(8,128)(2,1)}, u32[]{:S(2)}, u32[]{:S(2)}) collective-permute-start(bf16[512,768]{1,0:T(8,128)(2,1)S(1)} %collective-permute-done.4.refs_8_), channel_id=1, source_target_pairs={{0,8},{8,0},{16,24},{24,16},{1,9},{9,1},{17,25},{25,17},{2,10},{10... | collective-permute-start | bytes 2359304 | tf_op jit(solution)/shard_map/ppermute | solution.py:95
  74.5 32.8 %collective-permute-start.9 = (bf16[512,768]{1,0:T(8,128)(2,1)S(1)}, bf16[512,768]{1,0:T(8,128)(2,1)}, u32[]{:S(2)}, u32[]{:S(2)}) collective-permute-start(bf16[512,768]{1,0:T(8,128)(2,1)S(1)} %collective-permute-done.4.refs_8_), channel_id=1, source_target_pairs={{0,1},{1,2},{2,3},{3,0},{4,5},{5,6},{6,7},{7,4},{8,9},{9,10},{10,1... | collective-permute-start | bytes 2359304 | tf_op jit(solution)/shard_map/ppermute | solution.py:104
  107.3 36.7 %collective-permute-start.15 = (bf16[512,768]{1,0:T(8,128)(2,1)S(1)}, bf16[512,768]{1,0:T(8,128)(2,1)S(1)}, u32[]{:S(2)}, u32[]{:S(2)}) collective-permute-start(bf16[512,768]{1,0:T(8,128)(2,1)S(1)} %copy-done.14), channel_id=1, source_target_pairs={{0,8},{8,0},{16,24},{24,16},{1,9},{9,1},{17,25},{25,17},{2,10},{10... | collective-permute-start | bytes 2359304 | tf_op jit(solution)/shard_map/ppermute | solution.py:95
  108.9 36.2 %collective-permute-start.14 = (bf16[512,768]{1,0:T(8,128)(2,1)}, bf16[512,768]{1,0:T(8,128)(2,1)S(1)}, u32[]{:S(2)}, u32[]{:S(2)}) collective-permute-start(bf16[512,768]{1,0:T(8,128)(2,1)} %collective-permute-done.9.refs_12_), channel_id=1, source_target_pairs={{0,16},{8,24},{16,0},{24,8},{1,17},{9,25},{17,1},{25,9},{2,18},{10... | collective-permute-start | bytes 2359304 | tf_op jit(solution)/shard_map/ppermute | solution.py:99
  108.9 35.1 %collective-permute-start.17 = (bf16[256,1408]{1,0:T(8,128)(2,1)}, bf16[256,1408]{1,0:T(8,128)(2,1)S(1)}, u32[]{:S(2)}, u32[]{:S(2)}) collective-permute-start(bf16[256,1408]{1,0:T(8,128)(2,1)} %get-tuple-element.311.refs_12_), channel_id=1, source_target_pairs={{0,16},{8,24},{16,0},{24,8},{1,17},{9,25},{17,1},{25,9},{2,18},{10... | collective-permute-start | bytes 2162696 | tf_op jit(solution)/shard_map/ppermute | solution.py:99
  110.9 33.1 %collective-permute-start.16 = (bf16[256,1408]{1,0:T(8,128)(2,1)}, bf16[256,1408]{1,0:T(8,128)(2,1)S(1)}, u32[]{:S(2)}, u32[]{:S(2)}) collective-permute-start(bf16[256,1408]{1,0:T(8,128)(2,1)} %collective-permute-done.7.refs_16_), channel_id=1, source_target_pairs={{0,8},{8,0},{16,24},{24,16},{1,9},{9,1},{17,25},{25,17},{2,10},{10... | collective-permute-start | bytes 2162696 | tf_op jit(solution)/shard_map/ppermute | solution.py:95
  145.1 34.6 %collective-permute-start.20 = (bf16[512,768]{1,0:T(8,128)(2,1)S(1)}, bf16[512,768]{1,0:T(8,128)(2,1)S(1)}, u32[]{:S(2)}, u32[]{:S(2)}) collective-permute-start(bf16[512,768]{1,0:T(8,128)(2,1)S(1)} %collective-permute-done.4.refs_8_), channel_id=1, source_target_pairs={{0,16},{8,24},{16,0},{24,8},{1,17},{9,25},{17,1},{25,9},{2,18},{10... | collective-permute-start | bytes 2359304 | tf_op jit(solution)/shard_map/ppermute | solution.py:99
  145.5 34.3 %collective-permute-start.19 = (bf16[512,768]{1,0:T(8,128)(2,1)}, bf16[512,768]{1,0:T(8,128)(2,1)S(1)}, u32[]{:S(2)}, u32[]{:S(2)}) collective-permute-start(bf16[512,768]{1,0:T(8,128)(2,1)} %collective-permute-done.9.refs_12_), channel_id=1, source_target_pairs={{0,8},{8,0},{16,24},{24,16},{1,9},{9,1},{17,25},{25,17},{2,10},{10... | collective-permute-start | bytes 2359304 | tf_op jit(solution)/shard_map/ppermute | solution.py:95
  209.0 46.3 %collective-permute-start.31 = (bf16[384,2048]{1,0:T(8,128)(2,1)}, bf16[384,2048]{1,0:T(8,128)(2,1)}, u32[]{:S(2)}, u32[]{:S(2)}) collective-permute-start(bf16[384,2048]{1,0:T(8,128)(2,1)} %pad_maximum_fusion.8.refs_2_), channel_id=1, source_target_pairs={{0,1},{1,2},{2,3},{3,0},{4,5},{5,6},{6,7},{7,4},{8,9},{9,10},{10,1... | collective-permute-start | bytes 4718600 | tf_op jit(solution)/shard_map/ppermute | solution.py:104
  210.0 45.2 %collective-permute-start.30 = (bf16[256,2816]{1,0:T(8,128)(2,1)}, bf16[256,2816]{1,0:T(8,128)(2,1)}, u32[]{:S(2)}, u32[]{:S(2)}) collective-permute-start(bf16[256,2816]{1,0:T(8,128)(2,1)} %collective-permute-done.8.refs_8_), channel_id=1, source_target_pairs={{0,16},{8,24},{16,0},{24,8},{1,17},{9,25},{17,1},{25,9},{2,18},{10... | collective-permute-start | bytes 4325384 | tf_op jit(solution)/shard_map/ppermute | solution.py:99
  210.6 44.6 %collective-permute-start.29 = (bf16[256,2816]{1,0:T(8,128)(2,1)}, bf16[256,2816]{1,0:T(8,128)(2,1)}, u32[]{:S(2)}, u32[]{:S(2)}) collective-permute-start(bf16[256,2816]{1,0:T(8,128)(2,1)} %get-tuple-element.352.refs_4_), channel_id=1, source_target_pairs={{0,8},{8,0},{16,24},{24,16},{1,9},{9,1},{17,25},{25,17},{2,10},{10... | collective-permute-start | bytes 4325384 | tf_op jit(solution)/shard_map/ppermute | solution.py:95
  255.3 38.6 %collective-permute-start.35 = (bf16[384,2048]{1,0:T(8,128)(2,1)}, bf16[384,2048]{1,0:T(8,128)(2,1)}, u32[]{:S(2)}, u32[]{:S(2)}) collective-permute-start(bf16[384,2048]{1,0:T(8,128)(2,1)} %collective-permute-done.31.refs_2_), channel_id=1, source_target_pairs={{0,1},{1,2},{2,3},{3,0},{4,5},{5,6},{6,7},{7,4},{8,9},{9,10},{10,1... | collective-permute-start | bytes 4718600 | tf_op jit(solution)/shard_map/ppermute | solution.py:104
  256.1 37.8 %collective-permute-start.36 = (bf16[384,2048]{1,0:T(8,128)(2,1)}, bf16[384,2048]{1,0:T(8,128)(2,1)}, u32[]{:S(2)}, u32[]{:S(2)}) collective-permute-start(bf16[384,2048]{1,0:T(8,128)(2,1)} %pad_maximum_fusion.8.refs_2_), channel_id=1, source_target_pairs={{0,4},{4,0},{1,5},{5,1},{2,6},{6,2},{3,7},{7,3},{8,12},{12,8},{9,1... | collective-permute-start | bytes 4718600 | tf_op jit(solution)/shard_map/ppermute | solution.py:91
  256.1 37.8 %collective-permute-start.37 = (bf16[384,2048]{1,0:T(8,128)(2,1)}, bf16[384,2048]{1,0:T(8,128)(2,1)}, u32[]{:S(2)}, u32[]{:S(2)}) collective-permute-start(bf16[384,2048]{1,0:T(8,128)(2,1)} %collective-permute-done.31.refs_2_), channel_id=1, source_target_pairs={{0,4},{4,0},{1,5},{5,1},{2,6},{6,2},{3,7},{7,3},{8,12},{12,8},{9,1... | collective-permute-start | bytes 4718600 | tf_op jit(solution)/shard_map/ppermute | solution.py:91
  256.6 33.8 %collective-permute-start.34 = (bf16[256,2816]{1,0:T(8,128)(2,1)}, bf16[256,2816]{1,0:T(8,128)(2,1)}, u32[]{:S(2)}, u32[]{:S(2)}) collective-permute-start(bf16[256,2816]{1,0:T(8,128)(2,1)} %get-tuple-element.352.refs_4_), channel_id=1, source_target_pairs={{0,16},{8,24},{16,0},{24,8},{1,17},{9,25},{17,1},{25,9},{2,18},{10... | collective-permute-start | bytes 4325384 | tf_op jit(solution)/shard_map/ppermute | solution.py:99
  257.7 33.5 %collective-permute-start.33 = (bf16[256,2816]{1,0:T(8,128)(2,1)}, bf16[256,2816]{1,0:T(8,128)(2,1)}, u32[]{:S(2)}, u32[]{:S(2)}) collective-permute-start(bf16[256,2816]{1,0:T(8,128)(2,1)} %collective-permute-done.8.refs_8_), channel_id=1, source_target_pairs={{0,8},{8,0},{16,24},{24,16},{1,9},{9,1},{17,25},{25,17},{2,10},{10... | collective-permute-start | bytes 4325384 | tf_op jit(solution)/shard_map/ppermute | solution.py:95
  304.2 38.5 %collective-permute-start.39 = (bf16[384,2048]{1,0:T(8,128)(2,1)S(1)}, bf16[384,2048]{1,0:T(8,128)(2,1)S(1)}, u32[]{:S(2)}, u32[]{:S(2)}) collective-permute-start(bf16[384,2048]{1,0:T(8,128)(2,1)S(1)} %multiply_convert_fusion.refs_0_), channel_id=1, source_target_pairs={{0,1},{1,2},{2,3},{3,0},{4,5},{5,6},{6,7},{7,4},{8,9},{9,10},{10,1... | collective-permute-start | bytes 4718600 | tf_op jit(solution)/shard_map/ppermute | solution.py:104
  307.4 35.2 %collective-permute-start.43 = (bf16[384,2048]{1,0:T(8,128)(2,1)}, bf16[384,2048]{1,0:T(8,128)(2,1)S(1)}, u32[]{:S(2)}, u32[]{:S(2)}) collective-permute-start(bf16[384,2048]{1,0:T(8,128)(2,1)} %collective-permute-done.35.refs_2_), channel_id=1, source_target_pairs={{0,4},{4,0},{1,5},{5,1},{2,6},{6,2},{3,7},{7,3},{8,12},{12,8},{9,1... | collective-permute-start | bytes 4718600 | tf_op jit(solution)/shard_map/ppermute | solution.py:91
  307.6 34.1 %collective-permute-start.41 = (bf16[256,2816]{1,0:T(8,128)(2,1)}, bf16[256,2816]{1,0:T(8,128)(2,1)S(1)}, u32[]{:S(2)}, u32[]{:S(2)}) collective-permute-start(bf16[256,2816]{1,0:T(8,128)(2,1)} %collective-permute-done.29.refs_5_), channel_id=1, source_target_pairs={{0,16},{8,24},{16,0},{24,8},{1,17},{9,25},{17,1},{25,9},{2,18},{10... | collective-permute-start | bytes 4325384 | tf_op jit(solution)/shard_map/ppermute | solution.py:99
  308.7 33.8 %collective-permute-start.40 = (bf16[256,2816]{1,0:T(8,128)(2,1)}, bf16[256,2816]{1,0:T(8,128)(2,1)S(1)}, u32[]{:S(2)}, u32[]{:S(2)}) collective-permute-start(bf16[256,2816]{1,0:T(8,128)(2,1)} %collective-permute-done.30.refs_10_), channel_id=1, source_target_pairs={{0,8},{8,0},{16,24},{24,16},{1,9},{9,1},{17,25},{25,17},{2,10},{10... | collective-permute-start | bytes 4325384 | tf_op jit(solution)/shard_map/ppermute | solution.py:95
  342.7 42.2 %collective-permute-start.45 = (bf16[384,2048]{1,0:T(8,128)(2,1)S(1)}, bf16[384,2048]{1,0:T(8,128)(2,1)}, u32[]{:S(2)}, u32[]{:S(2)}) collective-permute-start(bf16[384,2048]{1,0:T(8,128)(2,1)S(1)} %collective-permute-done.39.refs_0_), channel_id=1, source_target_pairs={{0,4},{4,0},{1,5},{5,1},{2,6},{6,2},{3,7},{7,3},{8,12},{12,8},{9,1... | collective-permute-start | bytes 4718600 | tf_op jit(solution)/shard_map/ppermute | solution.py:91
  343.6 41.2 %collective-permute-start.44 = (bf16[384,2048]{1,0:T(8,128)(2,1)S(1)}, bf16[384,2048]{1,0:T(8,128)(2,1)}, u32[]{:S(2)}, u32[]{:S(2)}) collective-permute-start(bf16[384,2048]{1,0:T(8,128)(2,1)S(1)} %collective-permute-done.39.refs_0_), channel_id=1, source_target_pairs={{0,1},{1,2},{2,3},{3,0},{4,5},{5,6},{6,7},{7,4},{8,9},{9,10},{10,1... | collective-permute-start | bytes 4718600 | tf_op jit(solution)/shard_map/ppermute | solution.py:104
  384.8 41.9 %collective-permute-start.47 = (bf16[384,2048]{1,0:T(8,128)(2,1)}, bf16[384,2048]{1,0:T(8,128)(2,1)S(1)}, u32[]{:S(2)}, u32[]{:S(2)}) collective-permute-start(bf16[384,2048]{1,0:T(8,128)(2,1)} %collective-permute-done.44.refs_0_), channel_id=1, source_target_pairs={{0,4},{4,0},{1,5},{5,1},{2,6},{6,2},{3,7},{7,3},{8,12},{12,8},{9,1... | collective-permute-start | bytes 4718600 | tf_op jit(solution)/shard_map/ppermute | solution.py:91
  384.9 41.9 %collective-permute-start.46 = (bf16[384,2048]{1,0:T(8,128)(2,1)}, bf16[384,2048]{1,0:T(8,128)(2,1)S(1)}, u32[]{:S(2)}, u32[]{:S(2)}) collective-permute-start(bf16[384,2048]{1,0:T(8,128)(2,1)} %collective-permute-done.44.refs_0_), channel_id=1, source_target_pairs={{0,1},{1,2},{2,3},{3,0},{4,5},{5,6},{6,7},{7,4},{8,9},{9,10},{10,1... | collective-permute-start | bytes 4718600 | tf_op jit(solution)/shard_map/ppermute | solution.py:104
  426.8 41.4 %collective-permute-start.49 = (bf16[384,2048]{1,0:T(8,128)(2,1)S(1)}, bf16[384,2048]{1,0:T(8,128)(2,1)S(1)}, u32[]{:S(2)}, u32[]{:S(2)}) collective-permute-start(bf16[384,2048]{1,0:T(8,128)(2,1)S(1)} %collective-permute-done.46.refs_0_), channel_id=1, source_target_pairs={{0,4},{4,0},{1,5},{5,1},{2,6},{6,2},{3,7},{7,3},{8,12},{12,8},{9,1... | collective-permute-start | bytes 4718600 | tf_op jit(solution)/shard_map/ppermute | solution.py:91
  427.0 41.2 %collective-permute-start.48 = (bf16[384,2048]{1,0:T(8,128)(2,1)}, bf16[384,2048]{1,0:T(8,128)(2,1)}, u32[]{:S(2)}, u32[]{:S(2)}) collective-permute-start(bf16[384,2048]{1,0:T(8,128)(2,1)} %collective-permute-done.35.refs_2_), channel_id=1, source_target_pairs={{0,1},{1,2},{2,3},{3,0},{4,5},{5,6},{6,7},{7,4},{8,9},{9,10},{10,1... | collective-permute-start | bytes 4718600 | tf_op jit(solution)/shard_map/ppermute | solution.py:104
  472.5 43.8 %collective-permute-start.52 = (bf16[384,2048]{1,0:T(8,128)(2,1)S(1)}, bf16[384,2048]{1,0:T(8,128)(2,1)S(1)}, u32[]{:S(2)}, u32[]{:S(2)}) collective-permute-start(bf16[384,2048]{1,0:T(8,128)(2,1)S(1)} %add_convert_fusion.13), channel_id=1, source_target_pairs={{0,1},{1,2},{2,3},{3,0},{4,5},{5,6},{6,7},{7,4},{8,9},{9,10},{10,1... | collective-permute-start | bytes 4718600 | tf_op jit(solution)/shard_map/ppermute | solution.py:104
  520.9 38.3 %collective-permute-start.54 = (bf16[384,2048]{1,0:T(8,128)(2,1)S(1)}, bf16[384,2048]{1,0:T(8,128)(2,1)S(1)}, u32[]{:S(2)}, u32[]{:S(2)}) collective-permute-start(bf16[384,2048]{1,0:T(8,128)(2,1)S(1)} %add_convert_fusion.11), channel_id=1, source_target_pairs={{0,1},{1,2},{2,3},{3,0},{4,5},{5,6},{6,7},{7,4},{8,9},{9,10},{10,1... | collective-permute-start | bytes 4718600 | tf_op jit(solution)/shard_map/ppermute | solution.py:104
  559.2 48.6 %collective-permute-start.58 = (bf16[512,1408]{1,0:T(8,128)(2,1)S(1)}, bf16[512,1408]{1,0:T(8,128)(2,1)}, u32[]{:S(2)}, u32[]{:S(2)}) collective-permute-start(bf16[512,1408]{1,0:T(8,128)(2,1)S(1)} %get-tuple-element.422), channel_id=1, source_target_pairs={{0,8},{8,0},{16,24},{24,16},{1,9},{9,1},{17,25},{25,17},{2,10},{10... | collective-permute-start | bytes 4325384 | tf_op jit(solution)/shard_map/ppermute | solution.py:95
  560.8 47.1 %collective-permute-start.57 = (bf16[512,1408]{1,0:T(8,128)(2,1)S(1)}, bf16[512,1408]{1,0:T(8,128)(2,1)}, u32[]{:S(2)}, u32[]{:S(2)}) collective-permute-start(bf16[512,1408]{1,0:T(8,128)(2,1)S(1)} %get-tuple-element.419), channel_id=1, source_target_pairs={{0,16},{8,24},{16,0},{24,8},{1,17},{9,25},{17,1},{25,9},{2,18},{10... | collective-permute-start | bytes 4325384 | tf_op jit(solution)/shard_map/ppermute | solution.py:99
  564.9 39.2 %collective-permute-start.56 = (bf16[384,2048]{1,0:T(8,128)(2,1)}, bf16[384,2048]{1,0:T(8,128)(2,1)}, u32[]{:S(2)}, u32[]{:S(2)}) collective-permute-start(bf16[384,2048]{1,0:T(8,128)(2,1)} %add_convert_fusion.9), channel_id=1, source_target_pairs={{0,1},{1,2},{2,3},{3,0},{4,5},{5,6},{6,7},{7,4},{8,9},{9,10},{10,1... | collective-permute-start | bytes 4718600 | tf_op jit(solution)/shard_map/ppermute | solution.py:104
  614.6 38.1 %collective-permute-start.63 = (bf16[256,2816]{1,0:T(8,128)(2,1)S(1)}, bf16[256,2816]{1,0:T(8,128)(2,1)}, u32[]{:S(2)}, u32[]{:S(2)}) collective-permute-start(bf16[256,2816]{1,0:T(8,128)(2,1)S(1)} %get-tuple-element.444), channel_id=1, source_target_pairs={{0,8},{8,0},{16,24},{24,16},{1,9},{9,1},{17,25},{25,17},{2,10},{10... | collective-permute-start | bytes 4325384 | tf_op jit(solution)/shard_map/ppermute | solution.py:95
  616.2 36.5 %collective-permute-start.61 = (bf16[256,2816]{1,0:T(8,128)(2,1)S(1)}, bf16[256,2816]{1,0:T(8,128)(2,1)}, u32[]{:S(2)}, u32[]{:S(2)}) collective-permute-start(bf16[256,2816]{1,0:T(8,128)(2,1)S(1)} %get-tuple-element.441), channel_id=1, source_target_pairs={{0,16},{8,24},{16,0},{24,8},{1,17},{9,25},{17,1},{25,9},{2,18},{10... | collective-permute-start | bytes 4325384 | tf_op jit(solution)/shard_map/ppermute | solution.py:99
  618.6 38.3 %collective-permute-start.62 = (bf16[384,2048]{1,0:T(8,128)(2,1)}, bf16[384,2048]{1,0:T(8,128)(2,1)}, u32[]{:S(2)}, u32[]{:S(2)}) collective-permute-start(bf16[384,2048]{1,0:T(8,128)(2,1)} %add_convert_fusion.8), channel_id=1, source_target_pairs={{0,1},{1,2},{2,3},{3,0},{4,5},{5,6},{6,7},{7,4},{8,9},{9,10},{10,1... | collective-permute-start | bytes 4718600 | tf_op jit(solution)/shard_map/ppermute | solution.py:104
  693.7 93.6 %collective-permute-start.68 = (bf16[256,4224]{1,0:T(8,128)(2,1)}, bf16[256,4224]{1,0:T(8,128)(2,1)}, u32[]{:S(2)}, u32[]{:S(2)}) collective-permute-start(bf16[256,4224]{1,0:T(8,128)(2,1)} %pad_maximum_fusion.4), channel_id=1, source_target_pairs={{0,16},{8,24},{16,0},{24,8},{1,17},{9,25},{17,1},{25,9},{2,18},{10... | collective-permute-start | bytes 6488072 | tf_op jit(solution)/shard_map/ppermute | solution.py:99
  698.3 89.1 %collective-permute-start.67 = (bf16[256,4224]{1,0:T(8,128)(2,1)}, bf16[256,4224]{1,0:T(8,128)(2,1)}, u32[]{:S(2)}, u32[]{:S(2)}) collective-permute-start(bf16[256,4224]{1,0:T(8,128)(2,1)} %pad_maximum_fusion.3), channel_id=1, source_target_pairs={{0,8},{8,0},{16,24},{24,16},{1,9},{9,1},{17,25},{25,17},{2,10},{10... | collective-permute-start | bytes 6488072 | tf_op jit(solution)/shard_map/ppermute | solution.py:95
  699.5 87.8 %collective-permute-start.72 = (bf16[512,1024]{1,0:T(8,128)(2,1)}, bf16[512,1024]{1,0:T(8,128)(2,1)S(1)}, u32[]{:S(2)}, u32[]{:S(2)}) collective-permute-start(bf16[512,1024]{1,0:T(8,128)(2,1)} %pad_maximum_fusion.12), channel_id=1, source_target_pairs={{0,8},{8,0},{16,24},{24,16},{1,9},{9,1},{17,25},{25,17},{2,10},{10... | collective-permute-start | bytes 3145736 | tf_op jit(solution)/shard_map/ppermute | solution.py:95
  700.3 87.1 %collective-permute-start.71 = (bf16[512,1024]{1,0:T(8,128)(2,1)}, bf16[512,1024]{1,0:T(8,128)(2,1)}, u32[]{:S(2)}, u32[]{:S(2)}) collective-permute-start(bf16[512,1024]{1,0:T(8,128)(2,1)} %pad_maximum_fusion.11), channel_id=1, source_target_pairs={{0,16},{8,24},{16,0},{24,8},{1,17},{9,25},{17,1},{25,9},{2,18},{10... | collective-permute-start | bytes 3145736 | tf_op jit(solution)/shard_map/ppermute | solution.py:99
  704.5 82.8 %collective-permute-start.70 = (bf16[384,2048]{1,0:T(8,128)(2,1)}, bf16[384,2048]{1,0:T(8,128)(2,1)}, u32[]{:S(2)}, u32[]{:S(2)}) collective-permute-start(bf16[384,2048]{1,0:T(8,128)(2,1)} %add_convert_fusion.5), channel_id=1, source_target_pairs={{0,1},{1,2},{2,3},{3,0},{4,5},{5,6},{6,7},{7,4},{8,9},{9,10},{10,1... | collective-permute-start | bytes 4718600 | tf_op jit(solution)/shard_map/ppermute | solution.py:104
  800.5 36.8 %collective-permute-start.77 = (bf16[512,1536]{1,0:T(8,128)(2,1)S(1)}, bf16[512,1536]{1,0:T(8,128)(2,1)}, u32[]{:S(2)}, u32[]{:S(2)}) collective-permute-start(bf16[512,1536]{1,0:T(8,128)(2,1)S(1)} %copy-done.112), channel_id=1, source_target_pairs={{0,8},{8,0},{16,24},{24,16},{1,9},{9,1},{17,25},{25,17},{2,10},{10... | collective-permute-start | bytes 4718600 | tf_op jit(solution)/shard_map/ppermute | solution.py:95
  801.7 36.5 %collective-permute-start.76 = (bf16[512,1536]{1,0:T(8,128)(2,1)S(1)}, bf16[512,1536]{1,0:T(8,128)(2,1)}, u32[]{:S(2)}, u32[]{:S(2)}) collective-permute-start(bf16[512,1536]{1,0:T(8,128)(2,1)S(1)} %copy-done.111), channel_id=1, source_target_pairs={{0,16},{8,24},{16,0},{24,8},{1,17},{9,25},{17,1},{25,9},{2,18},{10... | collective-permute-start | bytes 4718600 | tf_op jit(solution)/shard_map/ppermute | solution.py:99
  805.4 38.5 %collective-permute-start.75 = (bf16[384,2048]{1,0:T(8,128)(2,1)S(1)}, bf16[384,2048]{1,0:T(8,128)(2,1)}, u32[]{:S(2)}, u32[]{:S(2)}) collective-permute-start(bf16[384,2048]{1,0:T(8,128)(2,1)S(1)} %add_convert_fusion.3), channel_id=1, source_target_pairs={{0,1},{1,2},{2,3},{3,0},{4,5},{5,6},{6,7},{7,4},{8,9},{9,10},{10,1... | collective-permute-start | bytes 4718600 | tf_op jit(solution)/shard_map/ppermute | solution.py:104
  899.1 42.6 %collective-permute-start.95 = (bf16[384,2048]{1,0:T(8,128)(2,1)}, bf16[384,2048]{1,0:T(8,128)(2,1)S(1)}, u32[]{:S(2)}, u32[]{:S(2)}) collective-permute-start(bf16[384,2048]{1,0:T(8,128)(2,1)} %bitcast.188), channel_id=1, source_target_pairs={{0,4},{4,0},{1,5},{5,1},{2,6},{6,2},{3,7},{7,3},{8,12},{12,8},{9,1... | collective-permute-start | bytes 4718600 | tf_op jit(solution)/shard_map/ppermute | solution.py:91
  904.4 37.3 %collective-permute-start.94 = (bf16[256,1408]{1,0:T(8,128)(2,1)S(1)}, bf16[256,1408]{1,0:T(8,128)(2,1)S(1)}, u32[]{:S(2)}, u32[]{:S(2)}) collective-permute-start(bf16[256,1408]{1,0:T(8,128)(2,1)S(1)} %copy-done.90), channel_id=1, source_target_pairs={{0,4},{4,0},{1,5},{5,1},{2,6},{6,2},{3,7},{7,3},{8,12},{12,8},{9,1... | collective-permute-start | bytes 2162696 | tf_op jit(solution)/shard_map/ppermute | solution.py:91
  (194 other events, 3060.1 us)
Sparse Core Ops, SparseCore 0:
  11.4 74.1 all-gather.2

commit v5 on v4

--- a/solution.py
+++ b/solution.py
@@ -1459,10 +1459,6 @@
     out_columns.add()
     expand_columns.add()
     arrived = [*query_columns.step(), *expand_columns.step(), *out_columns.step()]
-    grad_wgate, grad_wup, grad_wdown = spread(
-        behind(shift), hidden_here, hid_own, hid_far, down_own, down_far
-    )
-    grad_wgate, grad_wup = grad_wgate.T, grad_wup.T
     others_of = [] if far_part is None else [far_part]
     kernel = finish_kernel
     if far_part is None:
@@ -1490,7 +1486,7 @@
         grad_gain_two[None],
         scratch=[((1, width), f32), ((1, KVRANK), f32), ((width, kv_cols), bf16)],
     )
-    close(*arrived, input_grad, grad_wdown)
+    close(*arrived, input_grad)
 
     rings = [query_columns, expand_columns]
     for ring in rings:
@@ -1502,7 +1498,11 @@
         lax.ppermute(w_sum[high * k : high * (k + 1)], "shard", [(i, i ^ k) for i in range(4)])
         for k in (1, 2, 3)
     ]
-    close(*arrived, *w_far)
+    grad_wgate, grad_wup, grad_wdown = spread(
+        behind(shift), hidden_here, hid_own, hid_far, down_own, down_far
+    )
+    grad_wgate, grad_wup = grad_wgate.T, grad_wup.T
+    close(*arrived, *w_far, grad_wdown)
 
     w_sum = add16(w_sum[:high], *(now(each) for each in w_far))
     for ring in rings:

time: 1040 us -> 1040 us (level)
    unnamed x260 -> x264, local copies, waits for them, and re-layouts: 27.7 us -> 27.5 us
  transfers between devices with their start and end apart: 113 -> 113, of which waited for: 51 -> 50; matrix products, arithmetic and copies ran while one was open for 15% -> 15% of each run, Pallas kernels for 40% -> 40%
where the time goes in v5:
time: 1040 us; the launch traced here: 1030 us
  Pallas kernels  412 us (40%)
  waiting for transfers between devices  322 us (31%)
  other arithmetic  94.9 us (9%)
  starting transfers between devices  75.5 us (7%)
  local copies, waits for them, and re-layouts  70.7 us (7%)
  matrix products  37.5 us (4%)
  between operations  16.5 us (2%)
    pallas_call x4, Pallas kernels, feed(): pl.pallas_call(functools.partial(feed_kernel, part, rows, offset), out_sh...  162 us
    ppermute x30, waiting for transfers between devices, step_z(): return lax.ppermute(value, 'tp', [(i, (i + 1) % size) for i in range(size)])  114 us
    ppermute x22, waiting for transfers between devices, swap_y(): return lax.ppermute(value, 'shard', [(i, i ^ 2) for i in range(4)])  99.6 us
    pallas_call x3, Pallas kernels, weight_grad(): pl.pallas_call(functools.partial(weight_grad_kernel, packs), out_shape=[j...  94.5 us
    pallas_call x1, Pallas kernels, attend_back(): pl.pallas_call(functools.partial(attend_back_kernel, heads, width, scale,...  82.7 us
    ppermute x22, waiting for transfers between devices, swap_x(): return lax.ppermute(value, 'shard', [(i, i ^ 1) for i in range(4)])  59 us
    convert_element_type x33, other arithmetic, add16(): return total.astype(bf16)  52.9 us
    unnamed x264, local copies, waits for them, and re-layouts  27.5 us
  transfers between devices with their start and end apart: 113, of which 50 were waited for; matrix products, arithmetic and copies ran while one was open for 15% of the time, Pallas kernels for 40%

profile of v5, /device:TPU:0, one launch (start us, length us, event | category | flops | bytes accessed | tf_op | source)
XLA Modules:
  0.0 1028.8 jit_solution(17510404099066197349)
XLA Ops:
  26.5 9.1 collective-permute-done.1.refs_1_
  37.1 4.6 collective-permute-done.3.refs_4_
  51.5 12.1 %collective-permute-done.6.refs_6_ = bf16[512,768]{1,0:T(8,128)(2,1)S(1)} collective-permute-done((bf16[512,768]{1,0:T(8,128)(2,1)}, bf16[512,768]{1,0:T(8,128)(2,1)S(1)}, u32[]{:S(2)}, u32[]{:S(2)}) %collective-permute-start.6) | collective-permute-done | bytes 786464 | tf_op jit(solution)/shard_map/ppermute | solution.py:99
  66.0 4.4 collective-permute-done.4.refs_8_
  74.7 11.0 %all-gather.3.cloned.1.call-done = bf16[2560,576]{1,0:T(8,128)(2,1)} async-done(((bf16[80,576]{1,0:T(8,128)(2,1)}), bf16[2560,576]{1,0:T(8,128)(2,1)}) %all-gather.3.cloned.1.call-update) | async-done | bytes 2949136 | tf_op jit(solution)/shard_map/all_gather | solution.py:954
  93.7 7.2 pad_maximum_fusion.2.w_latent
  100.9 6.3 begin.1
  111.5 14.2 %collective-permute-done.18.refs_1_ = bf16[3,128,576]{2,1,0:T(8,128)(2,1)S(1)} collective-permute-done((bf16[3,128,576]{2,1,0:T(8,128)(2,1)}, bf16[3,128,576]{2,1,0:T(8,128)(2,1)S(1)}, u32[]{:S(2)}, u32[]{:S(2)}) %collective-permute-start.18) | collective-permute-done | bytes 442400 | tf_op jit(solution)/shard_map/ppermute | solution.py:104
  125.7 18.3 %collective-permute-done.17.refs_14_ = bf16[256,1408]{1,0:T(8,128)(2,1)S(1)} collective-permute-done((bf16[256,1408]{1,0:T(8,128)(2,1)}, bf16[256,1408]{1,0:T(8,128)(2,1)S(1)}, u32[]{:S(2)}, u32[]{:S(2)}) %collective-permute-start.17) | collective-permute-done | bytes 720928 | tf_op jit(solution)/shard_map/ppermute | solution.py:99
  149.3 12.9 %collective-permute-done.23.refs_2_ = bf16[3,128,576]{2,1,0:T(8,128)(2,1)S(1)} collective-permute-done((bf16[3,128,576]{2,1,0:T(8,128)(2,1)S(1)}, bf16[3,128,576]{2,1,0:T(8,128)(2,1)S(1)}, u32[]{:S(2)}, u32[]{:S(2)}) %collective-permute-start.23) | collective-permute-done | bytes 442400 | tf_op jit(solution)/shard_map/ppermute | solution.py:104
  162.2 17.0 %collective-permute-done.22.refs_15_ = bf16[256,1408]{1,0:T(8,128)(2,1)S(1)} collective-permute-done((bf16[256,1408]{1,0:T(8,128)(2,1)}, bf16[256,1408]{1,0:T(8,128)(2,1)S(1)}, u32[]{:S(2)}, u32[]{:S(2)}) %collective-permute-start.22) | collective-permute-done | bytes 720928 | tf_op jit(solution)/shard_map/ppermute | solution.py:99
  191.8 10.1 collective-permute-done.28.refs_3_
  213.8 11.5 %assemble.1 = (bf16[2048,1536]{1,0:T(8,128)(2,1)}, bf16[2048,1024]{1,0:T(8,128)(2,1)}, bf16[512,2048]{1,0:T(8,128)(2,1)}) custom-call(s32[2]{0:T(128)S(1)} %copy-done.20, bf16[512,768]{1,0:T(8,128)(2,1)S(1)} %pad_maximum_fusion.15.refs_0_, bf16[512,768]{1,0:T(8,128)(2,1)S(1)} %collective-permute-done.1.refs_1_, ...), custom_call_target="tpu_custom_call" | custom-call | bytes 25165824 | tf_op jit(solution)/shard_map/assemble/pallas_call | solution.py:144
  225.3 9.5 fusion.58
  238.4 5.2 lay_out.1
  243.6 11.7 %convolution_convert_fusion = bf16[3072,2048]{1,0:T(8,128)(2,1)} fusion(bf16[3072,512]{1,0:T(8,128)(2,1)} %bitcast.184, bf16[512,2048]{1,0:T(8,128)(2,1)} %get-tuple-element.344.wkv_ref), kind=kOutput, calls=%fused_computation | convolution fusion | flops 6448742400 | bytes 17825792 | tf_op jit(solution)/shard_map/dot_general | solution.py:51
  262.2 27.2 %attend.1 = bf16[2,3,128,1024]{3,2,1,0:T(8,128)(2,1)S(1)} custom-call(s32[3,2]{1,0:T(4,128)S(1)} %pad_add_fusion.2.place, f32[2,3,128,1536]{3,2,1,0:T(8,128)S(1)} %bitcast.135, bf16[3,1024,2048]{2,1,0:T(8,128)(2,1)} %bitcast.143, bf16[3,1024,128]{2,1,0:T(8,128)(2,1)S(1)} %copy-done.12, s32[3,256,1]{2,1,0:T(8,128)S(1)} %copy.108.segq_ref, ...), custom_call_target="tpu_custom_call" | custom-call | flops 3019898880 | bytes 19660800 | tf_op jit(solution)/shard_map/attend/pallas_call | solution.py:483
  310.2 31.4 %collective-permute-done.41.refs_7_ = bf16[256,2816]{1,0:T(8,128)(2,1)S(1)} collective-permute-done((bf16[256,2816]{1,0:T(8,128)(2,1)}, bf16[256,2816]{1,0:T(8,128)(2,1)S(1)}, u32[]{:S(2)}, u32[]{:S(2)}) %collective-permute-start.41) | collective-permute-done | bytes 1441824 | tf_op jit(solution)/shard_map/ppermute | solution.py:99
  344.3 40.5 %feed.4 = (bf16[384,2048]{1,0:T(8,128)(2,1)}, bf16[384,2048]{1,0:T(8,128)(2,1)}, bf16[384,2048]{1,0:T(8,128)(2,1)}, bf16[384,2048]{1,0:T(8,128)(2,1)}, bf16[3072...) custom-call(s32[2]{0:T(128)} %copy-done.19, ...), custom_call_target="tpu_custom_call" | custom-call | flops 26575110144 | bytes 42663936 | tf_op jit(solution)/shard_map/feed/pallas_call | solution.py:705
  386.5 40.3 %feed.5 = (bf16[384,2048]{1,0:T(8,128)(2,1)}, bf16[384,2048]{1,0:T(8,128)(2,1)}, bf16[384,2048]{1,0:T(8,128)(2,1)}, bf16[384,2048]{1,0:T(8,128)(2,1)}, bf16[3072...) custom-call(s32[2]{0:T(128)} %copy-done.19, ...), custom_call_target="tpu_custom_call", output_to_operand_aliasing={{4}: (21, {}), {5}: (22, {}), {6}: (23, {}), {7}: (24, {})} | custom-call | flops 26575110144 | bytes 42663936 | tf_op jit(solution)/shard_map/feed/pallas_call | solution.py:705
  427.9 40.3 %feed.6 = (bf16[384,2048]{1,0:T(8,128)(2,1)}, bf16[384,2048]{1,0:T(8,128)(2,1)}, bf16[384,2048]{1,0:T(8,128)(2,1)}, bf16[384,2048]{1,0:T(8,128)(2,1)}, bf16[3072...) custom-call(s32[2]{0:T(128)} %copy-done.19, ...), custom_call_target="tpu_custom_call", output_to_operand_aliasing={{4}: (21, {}), {5}: (22, {}), {6}: (23, {}), {7}: (24, {})} | custom-call | flops 26575110144 | bytes 42663936 | tf_op jit(solution)/shard_map/feed/pallas_call | solution.py:705
  476.1 40.4 %feed.7 = (bf16[384,2048]{1,0:T(8,128)(2,1)}, bf16[384,2048]{1,0:T(8,128)(2,1)}, bf16[384,2048]{1,0:T(8,128)(2,1)}, bf16[384,2048]{1,0:T(8,128)(2,1)}, bf16[3072...) custom-call(s32[2]{0:T(128)} %copy-done.19, ...), custom_call_target="tpu_custom_call", output_to_operand_aliasing={{4}: (21, {}), {5}: (22, {}), {6}: (23, {}), {7}: (24, {})} | custom-call | flops 26575110144 | bytes 42663936 | tf_op jit(solution)/shard_map/feed/pallas_call | solution.py:705
  522.4 36.0 %weight_grad.3 = (bf16[512,1408]{1,0:T(8,128)(2,1)S(1)}, bf16[512,1408]{1,0:T(8,128)(2,1)S(1)}, bf16[1024,1408]{1,0:T(8,128)(2,1)S(1)}) custom-call(s32[2]{0:T(128)S(1)} %copy-done.21, bf16[3072,2048]{1,0:T(8,128)(2,1)} %get-tuple-element.411.left, bf16[3072,1408]{1,0:T(8,128)(2,1)} %get-tuple-element.412.right_ref), custom_call_target="tpu_custom_call" | custom-call | flops 17716740096 | bytes 27000832 | tf_op jit(solution)/shard_map/weight_grad/pallas_call | solution.py:861
  565.5 29.4 %weight_grad.4 = (bf16[256,2816]{1,0:T(8,128)(2,1)S(1)}, bf16[256,2816]{1,0:T(8,128)(2,1)S(1)}, bf16[256,2816]{1,0:T(8,128)(2,1)S(1)}, bf16[256,2816]{1,0:T(8,128)(2,1)S(1)}) custom-call(s32[2]{0:T(128)S(1)} %copy-done.21, bf16[3072,2048]{1,0:T(8,128)(2,1)} %get-tuple-element.426.left, bf16[3072,2816]{1,0:T(8,128)(2,1)} %get-tuple-element.427.right_ref), custom_call_target="tpu_custom_call" | custom-call | flops 17716740096 | bytes 29360128 | tf_op jit(solution)/shard_map/weight_grad/pallas_call | solution.py:861
  595.0 9.1 collective-permute-done.56
  608.1 4.3 fusion.49
  624.0 29.0 %weight_grad.5 = (bf16[256,2816]{1,0:T(8,128)(2,1)S(1)}, bf16[256,2816]{1,0:T(8,128)(2,1)S(1)}, bf16[256,2816]{1,0:T(8,128)(2,1)S(1)}, bf16[256,2816]{1,0:T(8,128)(2,1)S(1)}) custom-call(s32[2]{0:T(128)S(1)} %copy-done.21, bf16[3072,2048]{1,0:T(8,128)(2,1)} %get-tuple-element.426.left, bf16[3072,2816]{1,0:T(8,128)(2,1)} %get-tuple-element.427.right_ref), custom_call_target="tpu_custom_call" | custom-call | flops 17716740096 | bytes 29360128 | tf_op jit(solution)/shard_map/weight_grad/pallas_call | solution.py:861
  653.0 4.2 collective-permute-done.62
  666.8 5.5 fusion.2
  672.2 17.5 %collective-permute-done.66 = bf16[256,2816]{1,0:T(8,128)(2,1)S(1)} collective-permute-done((bf16[256,2816]{1,0:T(8,128)(2,1)S(1)}, bf16[256,2816]{1,0:T(8,128)(2,1)S(1)}, u32[]{:S(2)}, u32[]{:S(2)}) %collective-permute-start.66) | collective-permute-done | bytes 1441824 | tf_op jit(solution)/shard_map/ppermute | solution.py:95
  704.9 82.7 %attend_back.1 = (bf16[512,1536]{1,0:T(8,128)(2,1)}, bf16[512,1536]{1,0:T(8,128)(2,1)}, bf16[1024,1536]{1,0:T(8,128)(2,1)}, bf16[128,2048]{1,0:T(8,128)(2,1)}, b...) custom-call(s32[3,2]{1,0:T(4,128)} %copy-done.23, ...), custom_call_target="tpu_custom_call" | custom-call | flops 30601641984 | bytes 42467328 | tf_op jit(solution)/shard_map/attend_back/pallas_call | solution.py:544
  787.7 3.9 copy.110
  791.6 3.9 collective-permute-done.73
  810.8 26.4 %collective-permute-done.77 = bf16[512,1536]{1,0:T(8,128)(2,1)} collective-permute-done((bf16[512,1536]{1,0:T(8,128)(2,1)S(1)}, bf16[512,1536]{1,0:T(8,128)(2,1)}, u32[]{:S(2)}, u32[]{:S(2)}) %collective-permute-start.77) | collective-permute-done | bytes 1572896 | tf_op jit(solution)/shard_map/ppermute | solution.py:95
  838.2 5.7 collective-permute-done.75
  860.3 4.1 add_convert_fusion.1
  864.4 9.5 collective-permute-done.79
  883.1 5.2 collective-permute-done.87
  891.1 7.3 collective-permute-done.84
  906.7 14.1 %collective-permute-done.91 = bf16[256,1536]{1,0:T(8,128)(2,1)S(1)} collective-permute-done((bf16[256,1536]{1,0:T(8,128)(2,1)S(1)}, bf16[256,1536]{1,0:T(8,128)(2,1)S(1)}, u32[]{:S(2)}, u32[]{:S(2)}) %collective-permute-start.91) | collective-permute-done | bytes 786464 | tf_op jit(solution)/shard_map/ppermute | solution.py:99
  924.2 7.7 collective-permute-done.92
  931.8 9.1 collective-permute-done.89
  942.2 12.7 %finish.1 = (bf16[384,2048]{1,0:T(8,128)(2,1)}, bf16[1088,576]{1,0:T(8,128)(2,1)}, bf16[1088,576]{1,0:T(8,128)(2,1)}) custom-call(s32[2]{0:T(128)} %copy-done.19, bf16[384,576]{1,0:T(8,128)(2,1)} %bitcast.172, bf16[384,576]{1,0:T(8,128)(2,1)} %bitcast.150, f32[384,512]{1,0:T(8,128)} %get-tuple-element.523.raw, f32[384,1]{1,0:T(8,128)} %get-tuple-element.524.scale_kv, ...), custom_call_target="tpu_custom_call" | custom-call | bytes 13882368 | tf_op jit(solution)/shard_map/finish/pallas_call | solution.py:215
  954.8 6.2 collective-permute-done.97
  980.8 6.5 spread.1
  987.2 7.1 collective-permute-done.103
  996.3 4.0 collective-permute-start.106
  1003.7 7.9 collective-permute-done.105
  (611 shorter events, 268.0 us)
Async XLA Ops:
  7.2 78.5 %all-gather.3.cloned.1.call-start = ((), (), s32[]{:S(2)}) async-start(), calls=%async_computation | async-start | bytes 3379200 | tf_op jit(solution)/shard_map/all_gather | solution.py:954
  70.4 36.8 %collective-permute-start.13 = (bf16[256,1408]{1,0:T(8,128)(2,1)}, bf16[256,1408]{1,0:T(8,128)(2,1)}, u32[]{:S(2)}, u32[]{:S(2)}) collective-permute-start(bf16[256,1408]{1,0:T(8,128)(2,1)} %collective-permute-done.7.refs_16_), channel_id=1, source_target_pairs={{0,16},{8,24},{16,0},{24,8},{1,17},{9,25},{17,1},{25,9},{2,18},{10... | collective-permute-start | bytes 2162696 | tf_op jit(solution)/shard_map/ppermute | solution.py:99
  71.9 35.3 %collective-permute-start.12 = (bf16[256,1408]{1,0:T(8,128)(2,1)}, bf16[256,1408]{1,0:T(8,128)(2,1)}, u32[]{:S(2)}, u32[]{:S(2)}) collective-permute-start(bf16[256,1408]{1,0:T(8,128)(2,1)} %get-tuple-element.311.refs_12_), channel_id=1, source_target_pairs={{0,8},{8,0},{16,24},{24,16},{1,9},{9,1},{17,25},{25,17},{2,10},{10... | collective-permute-start | bytes 2162696 | tf_op jit(solution)/shard_map/ppermute | solution.py:95
  73.4 33.8 %collective-permute-start.11 = (bf16[512,768]{1,0:T(8,128)(2,1)S(1)}, bf16[512,768]{1,0:T(8,128)(2,1)}, u32[]{:S(2)}, u32[]{:S(2)}) collective-permute-start(bf16[512,768]{1,0:T(8,128)(2,1)S(1)} %collective-permute-done.1.refs_1_), channel_id=1, source_target_pairs={{0,16},{8,24},{16,0},{24,8},{1,17},{9,25},{17,1},{25,9},{2,18},{10... | collective-permute-start | bytes 2359304 | tf_op jit(solution)/shard_map/ppermute | solution.py:99
  73.9 33.4 %collective-permute-start.10 = (bf16[512,768]{1,0:T(8,128)(2,1)S(1)}, bf16[512,768]{1,0:T(8,128)(2,1)}, u32[]{:S(2)}, u32[]{:S(2)}) collective-permute-start(bf16[512,768]{1,0:T(8,128)(2,1)S(1)} %collective-permute-done.4.refs_8_), channel_id=1, source_target_pairs={{0,8},{8,0},{16,24},{24,16},{1,9},{9,1},{17,25},{25,17},{2,10},{10... | collective-permute-start | bytes 2359304 | tf_op jit(solution)/shard_map/ppermute | solution.py:95
  74.5 32.8 %collective-permute-start.9 = (bf16[512,768]{1,0:T(8,128)(2,1)S(1)}, bf16[512,768]{1,0:T(8,128)(2,1)}, u32[]{:S(2)}, u32[]{:S(2)}) collective-permute-start(bf16[512,768]{1,0:T(8,128)(2,1)S(1)} %collective-permute-done.4.refs_8_), channel_id=1, source_target_pairs={{0,1},{1,2},{2,3},{3,0},{4,5},{5,6},{6,7},{7,4},{8,9},{9,10},{10,1... | collective-permute-start | bytes 2359304 | tf_op jit(solution)/shard_map/ppermute | solution.py:104
  107.3 36.7 %collective-permute-start.15 = (bf16[512,768]{1,0:T(8,128)(2,1)S(1)}, bf16[512,768]{1,0:T(8,128)(2,1)S(1)}, u32[]{:S(2)}, u32[]{:S(2)}) collective-permute-start(bf16[512,768]{1,0:T(8,128)(2,1)S(1)} %copy-done.14), channel_id=1, source_target_pairs={{0,8},{8,0},{16,24},{24,16},{1,9},{9,1},{17,25},{25,17},{2,10},{10... | collective-permute-start | bytes 2359304 | tf_op jit(solution)/shard_map/ppermute | solution.py:95
  108.9 36.2 %collective-permute-start.14 = (bf16[512,768]{1,0:T(8,128)(2,1)}, bf16[512,768]{1,0:T(8,128)(2,1)S(1)}, u32[]{:S(2)}, u32[]{:S(2)}) collective-permute-start(bf16[512,768]{1,0:T(8,128)(2,1)} %collective-permute-done.9.refs_12_), channel_id=1, source_target_pairs={{0,16},{8,24},{16,0},{24,8},{1,17},{9,25},{17,1},{25,9},{2,18},{10... | collective-permute-start | bytes 2359304 | tf_op jit(solution)/shard_map/ppermute | solution.py:99
  108.9 35.1 %collective-permute-start.17 = (bf16[256,1408]{1,0:T(8,128)(2,1)}, bf16[256,1408]{1,0:T(8,128)(2,1)S(1)}, u32[]{:S(2)}, u32[]{:S(2)}) collective-permute-start(bf16[256,1408]{1,0:T(8,128)(2,1)} %get-tuple-element.311.refs_12_), channel_id=1, source_target_pairs={{0,16},{8,24},{16,0},{24,8},{1,17},{9,25},{17,1},{25,9},{2,18},{10... | collective-permute-start | bytes 2162696 | tf_op jit(solution)/shard_map/ppermute | solution.py:99
  110.9 33.1 %collective-permute-start.16 = (bf16[256,1408]{1,0:T(8,128)(2,1)}, bf16[256,1408]{1,0:T(8,128)(2,1)S(1)}, u32[]{:S(2)}, u32[]{:S(2)}) collective-permute-start(bf16[256,1408]{1,0:T(8,128)(2,1)} %collective-permute-done.7.refs_16_), channel_id=1, source_target_pairs={{0,8},{8,0},{16,24},{24,16},{1,9},{9,1},{17,25},{25,17},{2,10},{10... | collective-permute-start | bytes 2162696 | tf_op jit(solution)/shard_map/ppermute | solution.py:95
  145.1 34.6 %collective-permute-start.20 = (bf16[512,768]{1,0:T(8,128)(2,1)S(1)}, bf16[512,768]{1,0:T(8,128)(2,1)S(1)}, u32[]{:S(2)}, u32[]{:S(2)}) collective-permute-start(bf16[512,768]{1,0:T(8,128)(2,1)S(1)} %collective-permute-done.4.refs_8_), channel_id=1, source_target_pairs={{0,16},{8,24},{16,0},{24,8},{1,17},{9,25},{17,1},{25,9},{2,18},{10... | collective-permute-start | bytes 2359304 | tf_op jit(solution)/shard_map/ppermute | solution.py:99
  145.5 34.3 %collective-permute-start.19 = (bf16[512,768]{1,0:T(8,128)(2,1)}, bf16[512,768]{1,0:T(8,128)(2,1)S(1)}, u32[]{:S(2)}, u32[]{:S(2)}) collective-permute-start(bf16[512,768]{1,0:T(8,128)(2,1)} %collective-permute-done.9.refs_12_), channel_id=1, source_target_pairs={{0,8},{8,0},{16,24},{24,16},{1,9},{9,1},{17,25},{25,17},{2,10},{10... | collective-permute-start | bytes 2359304 | tf_op jit(solution)/shard_map/ppermute | solution.py:95
  209.0 46.3 %collective-permute-start.31 = (bf16[384,2048]{1,0:T(8,128)(2,1)}, bf16[384,2048]{1,0:T(8,128)(2,1)}, u32[]{:S(2)}, u32[]{:S(2)}) collective-permute-start(bf16[384,2048]{1,0:T(8,128)(2,1)} %pad_maximum_fusion.8.refs_2_), channel_id=1, source_target_pairs={{0,1},{1,2},{2,3},{3,0},{4,5},{5,6},{6,7},{7,4},{8,9},{9,10},{10,1... | collective-permute-start | bytes 4718600 | tf_op jit(solution)/shard_map/ppermute | solution.py:104
  210.1 45.2 %collective-permute-start.30 = (bf16[256,2816]{1,0:T(8,128)(2,1)}, bf16[256,2816]{1,0:T(8,128)(2,1)}, u32[]{:S(2)}, u32[]{:S(2)}) collective-permute-start(bf16[256,2816]{1,0:T(8,128)(2,1)} %collective-permute-done.8.refs_8_), channel_id=1, source_target_pairs={{0,16},{8,24},{16,0},{24,8},{1,17},{9,25},{17,1},{25,9},{2,18},{10... | collective-permute-start | bytes 4325384 | tf_op jit(solution)/shard_map/ppermute | solution.py:99
  210.7 44.6 %collective-permute-start.29 = (bf16[256,2816]{1,0:T(8,128)(2,1)}, bf16[256,2816]{1,0:T(8,128)(2,1)}, u32[]{:S(2)}, u32[]{:S(2)}) collective-permute-start(bf16[256,2816]{1,0:T(8,128)(2,1)} %get-tuple-element.352.refs_4_), channel_id=1, source_target_pairs={{0,8},{8,0},{16,24},{24,16},{1,9},{9,1},{17,25},{25,17},{2,10},{10... | collective-permute-start | bytes 4325384 | tf_op jit(solution)/shard_map/ppermute | solution.py:95
  255.3 38.6 %collective-permute-start.35 = (bf16[384,2048]{1,0:T(8,128)(2,1)}, bf16[384,2048]{1,0:T(8,128)(2,1)}, u32[]{:S(2)}, u32[]{:S(2)}) collective-permute-start(bf16[384,2048]{1,0:T(8,128)(2,1)} %collective-permute-done.31.refs_2_), channel_id=1, source_target_pairs={{0,1},{1,2},{2,3},{3,0},{4,5},{5,6},{6,7},{7,4},{8,9},{9,10},{10,1... | collective-permute-start | bytes 4718600 | tf_op jit(solution)/shard_map/ppermute | solution.py:104
  256.1 37.8 %collective-permute-start.36 = (bf16[384,2048]{1,0:T(8,128)(2,1)}, bf16[384,2048]{1,0:T(8,128)(2,1)}, u32[]{:S(2)}, u32[]{:S(2)}) collective-permute-start(bf16[384,2048]{1,0:T(8,128)(2,1)} %pad_maximum_fusion.8.refs_2_), channel_id=1, source_target_pairs={{0,4},{4,0},{1,5},{5,1},{2,6},{6,2},{3,7},{7,3},{8,12},{12,8},{9,1... | collective-permute-start | bytes 4718600 | tf_op jit(solution)/shard_map/ppermute | solution.py:91
  256.1 37.8 %collective-permute-start.37 = (bf16[384,2048]{1,0:T(8,128)(2,1)}, bf16[384,2048]{1,0:T(8,128)(2,1)}, u32[]{:S(2)}, u32[]{:S(2)}) collective-permute-start(bf16[384,2048]{1,0:T(8,128)(2,1)} %collective-permute-done.31.refs_2_), channel_id=1, source_target_pairs={{0,4},{4,0},{1,5},{5,1},{2,6},{6,2},{3,7},{7,3},{8,12},{12,8},{9,1... | collective-permute-start | bytes 4718600 | tf_op jit(solution)/shard_map/ppermute | solution.py:91
  256.6 33.8 %collective-permute-start.34 = (bf16[256,2816]{1,0:T(8,128)(2,1)}, bf16[256,2816]{1,0:T(8,128)(2,1)}, u32[]{:S(2)}, u32[]{:S(2)}) collective-permute-start(bf16[256,2816]{1,0:T(8,128)(2,1)} %get-tuple-element.352.refs_4_), channel_id=1, source_target_pairs={{0,16},{8,24},{16,0},{24,8},{1,17},{9,25},{17,1},{25,9},{2,18},{10... | collective-permute-start | bytes 4325384 | tf_op jit(solution)/shard_map/ppermute | solution.py:99
  257.7 33.5 %collective-permute-start.33 = (bf16[256,2816]{1,0:T(8,128)(2,1)}, bf16[256,2816]{1,0:T(8,128)(2,1)}, u32[]{:S(2)}, u32[]{:S(2)}) collective-permute-start(bf16[256,2816]{1,0:T(8,128)(2,1)} %collective-permute-done.8.refs_8_), channel_id=1, source_target_pairs={{0,8},{8,0},{16,24},{24,16},{1,9},{9,1},{17,25},{25,17},{2,10},{10... | collective-permute-start | bytes 4325384 | tf_op jit(solution)/shard_map/ppermute | solution.py:95
  304.2 38.5 %collective-permute-start.39 = (bf16[384,2048]{1,0:T(8,128)(2,1)S(1)}, bf16[384,2048]{1,0:T(8,128)(2,1)S(1)}, u32[]{:S(2)}, u32[]{:S(2)}) collective-permute-start(bf16[384,2048]{1,0:T(8,128)(2,1)S(1)} %multiply_convert_fusion.refs_0_), channel_id=1, source_target_pairs={{0,1},{1,2},{2,3},{3,0},{4,5},{5,6},{6,7},{7,4},{8,9},{9,10},{10,1... | collective-permute-start | bytes 4718600 | tf_op jit(solution)/shard_map/ppermute | solution.py:104
  307.4 35.2 %collective-permute-start.43 = (bf16[384,2048]{1,0:T(8,128)(2,1)}, bf16[384,2048]{1,0:T(8,128)(2,1)S(1)}, u32[]{:S(2)}, u32[]{:S(2)}) collective-permute-start(bf16[384,2048]{1,0:T(8,128)(2,1)} %collective-permute-done.35.refs_2_), channel_id=1, source_target_pairs={{0,4},{4,0},{1,5},{5,1},{2,6},{6,2},{3,7},{7,3},{8,12},{12,8},{9,1... | collective-permute-start | bytes 4718600 | tf_op jit(solution)/shard_map/ppermute | solution.py:91
  307.6 34.1 %collective-permute-start.41 = (bf16[256,2816]{1,0:T(8,128)(2,1)}, bf16[256,2816]{1,0:T(8,128)(2,1)S(1)}, u32[]{:S(2)}, u32[]{:S(2)}) collective-permute-start(bf16[256,2816]{1,0:T(8,128)(2,1)} %collective-permute-done.29.refs_5_), channel_id=1, source_target_pairs={{0,16},{8,24},{16,0},{24,8},{1,17},{9,25},{17,1},{25,9},{2,18},{10... | collective-permute-start | bytes 4325384 | tf_op jit(solution)/shard_map/ppermute | solution.py:99
  308.7 33.8 %collective-permute-start.40 = (bf16[256,2816]{1,0:T(8,128)(2,1)}, bf16[256,2816]{1,0:T(8,128)(2,1)S(1)}, u32[]{:S(2)}, u32[]{:S(2)}) collective-permute-start(bf16[256,2816]{1,0:T(8,128)(2,1)} %collective-permute-done.30.refs_10_), channel_id=1, source_target_pairs={{0,8},{8,0},{16,24},{24,16},{1,9},{9,1},{17,25},{25,17},{2,10},{10... | collective-permute-start | bytes 4325384 | tf_op jit(solution)/shard_map/ppermute | solution.py:95
  342.7 42.2 %collective-permute-start.45 = (bf16[384,2048]{1,0:T(8,128)(2,1)S(1)}, bf16[384,2048]{1,0:T(8,128)(2,1)}, u32[]{:S(2)}, u32[]{:S(2)}) collective-permute-start(bf16[384,2048]{1,0:T(8,128)(2,1)S(1)} %collective-permute-done.39.refs_0_), channel_id=1, source_target_pairs={{0,4},{4,0},{1,5},{5,1},{2,6},{6,2},{3,7},{7,3},{8,12},{12,8},{9,1... | collective-permute-start | bytes 4718600 | tf_op jit(solution)/shard_map/ppermute | solution.py:91
  343.6 41.3 %collective-permute-start.44 = (bf16[384,2048]{1,0:T(8,128)(2,1)S(1)}, bf16[384,2048]{1,0:T(8,128)(2,1)}, u32[]{:S(2)}, u32[]{:S(2)}) collective-permute-start(bf16[384,2048]{1,0:T(8,128)(2,1)S(1)} %collective-permute-done.39.refs_0_), channel_id=1, source_target_pairs={{0,1},{1,2},{2,3},{3,0},{4,5},{5,6},{6,7},{7,4},{8,9},{9,10},{10,1... | collective-permute-start | bytes 4718600 | tf_op jit(solution)/shard_map/ppermute | solution.py:104
  384.9 41.9 %collective-permute-start.47 = (bf16[384,2048]{1,0:T(8,128)(2,1)}, bf16[384,2048]{1,0:T(8,128)(2,1)S(1)}, u32[]{:S(2)}, u32[]{:S(2)}) collective-permute-start(bf16[384,2048]{1,0:T(8,128)(2,1)} %collective-permute-done.44.refs_0_), channel_id=1, source_target_pairs={{0,4},{4,0},{1,5},{5,1},{2,6},{6,2},{3,7},{7,3},{8,12},{12,8},{9,1... | collective-permute-start | bytes 4718600 | tf_op jit(solution)/shard_map/ppermute | solution.py:91
  384.9 41.9 %collective-permute-start.46 = (bf16[384,2048]{1,0:T(8,128)(2,1)}, bf16[384,2048]{1,0:T(8,128)(2,1)S(1)}, u32[]{:S(2)}, u32[]{:S(2)}) collective-permute-start(bf16[384,2048]{1,0:T(8,128)(2,1)} %collective-permute-done.44.refs_0_), channel_id=1, source_target_pairs={{0,1},{1,2},{2,3},{3,0},{4,5},{5,6},{6,7},{7,4},{8,9},{9,10},{10,1... | collective-permute-start | bytes 4718600 | tf_op jit(solution)/shard_map/ppermute | solution.py:104
  426.8 41.5 %collective-permute-start.49 = (bf16[384,2048]{1,0:T(8,128)(2,1)S(1)}, bf16[384,2048]{1,0:T(8,128)(2,1)S(1)}, u32[]{:S(2)}, u32[]{:S(2)}) collective-permute-start(bf16[384,2048]{1,0:T(8,128)(2,1)S(1)} %collective-permute-done.46.refs_0_), channel_id=1, source_target_pairs={{0,4},{4,0},{1,5},{5,1},{2,6},{6,2},{3,7},{7,3},{8,12},{12,8},{9,1... | collective-permute-start | bytes 4718600 | tf_op jit(solution)/shard_map/ppermute | solution.py:91
  427.0 41.3 %collective-permute-start.48 = (bf16[384,2048]{1,0:T(8,128)(2,1)}, bf16[384,2048]{1,0:T(8,128)(2,1)}, u32[]{:S(2)}, u32[]{:S(2)}) collective-permute-start(bf16[384,2048]{1,0:T(8,128)(2,1)} %collective-permute-done.35.refs_2_), channel_id=1, source_target_pairs={{0,1},{1,2},{2,3},{3,0},{4,5},{5,6},{6,7},{7,4},{8,9},{9,10},{10,1... | collective-permute-start | bytes 4718600 | tf_op jit(solution)/shard_map/ppermute | solution.py:104
  472.7 43.9 %collective-permute-start.52 = (bf16[384,2048]{1,0:T(8,128)(2,1)S(1)}, bf16[384,2048]{1,0:T(8,128)(2,1)S(1)}, u32[]{:S(2)}, u32[]{:S(2)}) collective-permute-start(bf16[384,2048]{1,0:T(8,128)(2,1)S(1)} %add_convert_fusion.13), channel_id=1, source_target_pairs={{0,1},{1,2},{2,3},{3,0},{4,5},{5,6},{6,7},{7,4},{8,9},{9,10},{10,1... | collective-permute-start | bytes 4718600 | tf_op jit(solution)/shard_map/ppermute | solution.py:104
  521.1 38.3 %collective-permute-start.54 = (bf16[384,2048]{1,0:T(8,128)(2,1)S(1)}, bf16[384,2048]{1,0:T(8,128)(2,1)S(1)}, u32[]{:S(2)}, u32[]{:S(2)}) collective-permute-start(bf16[384,2048]{1,0:T(8,128)(2,1)S(1)} %add_convert_fusion.11), channel_id=1, source_target_pairs={{0,1},{1,2},{2,3},{3,0},{4,5},{5,6},{6,7},{7,4},{8,9},{9,10},{10,1... | collective-permute-start | bytes 4718600 | tf_op jit(solution)/shard_map/ppermute | solution.py:104
  559.4 48.5 %collective-permute-start.58 = (bf16[512,1408]{1,0:T(8,128)(2,1)S(1)}, bf16[512,1408]{1,0:T(8,128)(2,1)}, u32[]{:S(2)}, u32[]{:S(2)}) collective-permute-start(bf16[512,1408]{1,0:T(8,128)(2,1)S(1)} %get-tuple-element.422), channel_id=1, source_target_pairs={{0,8},{8,0},{16,24},{24,16},{1,9},{9,1},{17,25},{25,17},{2,10},{10... | collective-permute-start | bytes 4325384 | tf_op jit(solution)/shard_map/ppermute | solution.py:95
  560.9 47.0 %collective-permute-start.57 = (bf16[512,1408]{1,0:T(8,128)(2,1)S(1)}, bf16[512,1408]{1,0:T(8,128)(2,1)}, u32[]{:S(2)}, u32[]{:S(2)}) collective-permute-start(bf16[512,1408]{1,0:T(8,128)(2,1)S(1)} %get-tuple-element.419), channel_id=1, source_target_pairs={{0,16},{8,24},{16,0},{24,8},{1,17},{9,25},{17,1},{25,9},{2,18},{10... | collective-permute-start | bytes 4325384 | tf_op jit(solution)/shard_map/ppermute | solution.py:99
  564.9 39.2 %collective-permute-start.56 = (bf16[384,2048]{1,0:T(8,128)(2,1)}, bf16[384,2048]{1,0:T(8,128)(2,1)}, u32[]{:S(2)}, u32[]{:S(2)}) collective-permute-start(bf16[384,2048]{1,0:T(8,128)(2,1)} %add_convert_fusion.9), channel_id=1, source_target_pairs={{0,1},{1,2},{2,3},{3,0},{4,5},{5,6},{6,7},{7,4},{8,9},{9,10},{10,1... | collective-permute-start | bytes 4718600 | tf_op jit(solution)/shard_map/ppermute | solution.py:104
  614.7 38.3 %collective-permute-start.63 = (bf16[256,2816]{1,0:T(8,128)(2,1)S(1)}, bf16[256,2816]{1,0:T(8,128)(2,1)}, u32[]{:S(2)}, u32[]{:S(2)}) collective-permute-start(bf16[256,2816]{1,0:T(8,128)(2,1)S(1)} %get-tuple-element.444), channel_id=1, source_target_pairs={{0,8},{8,0},{16,24},{24,16},{1,9},{9,1},{17,25},{25,17},{2,10},{10... | collective-permute-start | bytes 4325384 | tf_op jit(solution)/shard_map/ppermute | solution.py:95
  616.3 36.7 %collective-permute-start.61 = (bf16[256,2816]{1,0:T(8,128)(2,1)S(1)}, bf16[256,2816]{1,0:T(8,128)(2,1)}, u32[]{:S(2)}, u32[]{:S(2)}) collective-permute-start(bf16[256,2816]{1,0:T(8,128)(2,1)S(1)} %get-tuple-element.441), channel_id=1, source_target_pairs={{0,16},{8,24},{16,0},{24,8},{1,17},{9,25},{17,1},{25,9},{2,18},{10... | collective-permute-start | bytes 4325384 | tf_op jit(solution)/shard_map/ppermute | solution.py:99
  618.8 38.3 %collective-permute-start.62 = (bf16[384,2048]{1,0:T(8,128)(2,1)}, bf16[384,2048]{1,0:T(8,128)(2,1)}, u32[]{:S(2)}, u32[]{:S(2)}) collective-permute-start(bf16[384,2048]{1,0:T(8,128)(2,1)} %add_convert_fusion.8), channel_id=1, source_target_pairs={{0,1},{1,2},{2,3},{3,0},{4,5},{5,6},{6,7},{7,4},{8,9},{9,10},{10,1... | collective-permute-start | bytes 4718600 | tf_op jit(solution)/shard_map/ppermute | solution.py:104
  694.0 93.6 %collective-permute-start.68 = (bf16[256,4224]{1,0:T(8,128)(2,1)}, bf16[256,4224]{1,0:T(8,128)(2,1)}, u32[]{:S(2)}, u32[]{:S(2)}) collective-permute-start(bf16[256,4224]{1,0:T(8,128)(2,1)} %pad_maximum_fusion.4), channel_id=1, source_target_pairs={{0,16},{8,24},{16,0},{24,8},{1,17},{9,25},{17,1},{25,9},{2,18},{10... | collective-permute-start | bytes 6488072 | tf_op jit(solution)/shard_map/ppermute | solution.py:99
  698.5 89.1 %collective-permute-start.67 = (bf16[256,4224]{1,0:T(8,128)(2,1)}, bf16[256,4224]{1,0:T(8,128)(2,1)}, u32[]{:S(2)}, u32[]{:S(2)}) collective-permute-start(bf16[256,4224]{1,0:T(8,128)(2,1)} %pad_maximum_fusion.3), channel_id=1, source_target_pairs={{0,8},{8,0},{16,24},{24,16},{1,9},{9,1},{17,25},{25,17},{2,10},{10... | collective-permute-start | bytes 6488072 | tf_op jit(solution)/shard_map/ppermute | solution.py:95
  699.8 87.9 %collective-permute-start.72 = (bf16[512,1024]{1,0:T(8,128)(2,1)}, bf16[512,1024]{1,0:T(8,128)(2,1)}, u32[]{:S(2)}, u32[]{:S(2)}) collective-permute-start(bf16[512,1024]{1,0:T(8,128)(2,1)} %pad_maximum_fusion.12), channel_id=1, source_target_pairs={{0,8},{8,0},{16,24},{24,16},{1,9},{9,1},{17,25},{25,17},{2,10},{10... | collective-permute-start | bytes 3145736 | tf_op jit(solution)/shard_map/ppermute | solution.py:95
  700.6 87.1 %collective-permute-start.71 = (bf16[512,1024]{1,0:T(8,128)(2,1)}, bf16[512,1024]{1,0:T(8,128)(2,1)}, u32[]{:S(2)}, u32[]{:S(2)}) collective-permute-start(bf16[512,1024]{1,0:T(8,128)(2,1)} %pad_maximum_fusion.11), channel_id=1, source_target_pairs={{0,16},{8,24},{16,0},{24,8},{1,17},{9,25},{17,1},{25,9},{2,18},{10... | collective-permute-start | bytes 3145736 | tf_op jit(solution)/shard_map/ppermute | solution.py:99
  704.8 82.9 %collective-permute-start.70 = (bf16[384,2048]{1,0:T(8,128)(2,1)}, bf16[384,2048]{1,0:T(8,128)(2,1)}, u32[]{:S(2)}, u32[]{:S(2)}) collective-permute-start(bf16[384,2048]{1,0:T(8,128)(2,1)} %add_convert_fusion.5), channel_id=1, source_target_pairs={{0,1},{1,2},{2,3},{3,0},{4,5},{5,6},{6,7},{7,4},{8,9},{9,10},{10,1... | collective-permute-start | bytes 4718600 | tf_op jit(solution)/shard_map/ppermute | solution.py:104
  800.4 36.8 %collective-permute-start.77 = (bf16[512,1536]{1,0:T(8,128)(2,1)S(1)}, bf16[512,1536]{1,0:T(8,128)(2,1)}, u32[]{:S(2)}, u32[]{:S(2)}) collective-permute-start(bf16[512,1536]{1,0:T(8,128)(2,1)S(1)} %copy-done.114), channel_id=1, source_target_pairs={{0,8},{8,0},{16,24},{24,16},{1,9},{9,1},{17,25},{25,17},{2,10},{10... | collective-permute-start | bytes 4718600 | tf_op jit(solution)/shard_map/ppermute | solution.py:95
  801.7 36.5 %collective-permute-start.76 = (bf16[512,1536]{1,0:T(8,128)(2,1)S(1)}, bf16[512,1536]{1,0:T(8,128)(2,1)}, u32[]{:S(2)}, u32[]{:S(2)}) collective-permute-start(bf16[512,1536]{1,0:T(8,128)(2,1)S(1)} %copy-done.113), channel_id=1, source_target_pairs={{0,16},{8,24},{16,0},{24,8},{1,17},{9,25},{17,1},{25,9},{2,18},{10... | collective-permute-start | bytes 4718600 | tf_op jit(solution)/shard_map/ppermute | solution.py:99
  805.3 38.5 %collective-permute-start.75 = (bf16[384,2048]{1,0:T(8,128)(2,1)S(1)}, bf16[384,2048]{1,0:T(8,128)(2,1)}, u32[]{:S(2)}, u32[]{:S(2)}) collective-permute-start(bf16[384,2048]{1,0:T(8,128)(2,1)S(1)} %add_convert_fusion.3), channel_id=1, source_target_pairs={{0,1},{1,2},{2,3},{3,0},{4,5},{5,6},{6,7},{7,4},{8,9},{9,10},{10,1... | collective-permute-start | bytes 4718600 | tf_op jit(solution)/shard_map/ppermute | solution.py:104
  898.4 42.5 %collective-permute-start.95 = (bf16[384,2048]{1,0:T(8,128)(2,1)}, bf16[384,2048]{1,0:T(8,128)(2,1)S(1)}, u32[]{:S(2)}, u32[]{:S(2)}) collective-permute-start(bf16[384,2048]{1,0:T(8,128)(2,1)} %bitcast.188), channel_id=1, source_target_pairs={{0,4},{4,0},{1,5},{5,1},{2,6},{6,2},{3,7},{7,3},{8,12},{12,8},{9,1... | collective-permute-start | bytes 4718600 | tf_op jit(solution)/shard_map/ppermute | solution.py:91
  904.0 36.9 %collective-permute-start.94 = (bf16[256,1408]{1,0:T(8,128)(2,1)S(1)}, bf16[256,1408]{1,0:T(8,128)(2,1)S(1)}, u32[]{:S(2)}, u32[]{:S(2)}) collective-permute-start(bf16[256,1408]{1,0:T(8,128)(2,1)S(1)} %copy-done.93), channel_id=1, source_target_pairs={{0,4},{4,0},{1,5},{5,1},{2,6},{6,2},{3,7},{7,3},{8,12},{12,8},{9,1... | collective-permute-start | bytes 2162696 | tf_op jit(solution)/shard_map/ppermute | solution.py:91
  (196 other events, 3015.9 us)
Sparse Core Ops, SparseCore 0:
  11.4 74.1 all-gather.2
